TPU v7x, 256 devices: a whole 4x4x8 slice. The times are simulated.
256 devices in a mesh: wa: 128 (over y, x_lo, z, core), ha: 2 (over x_hi).
Axes of the slice: x: 4 (x_hi: 2, x_lo: 2; x = x_hi * 2 + x_lo), y: 4, z: 8, core: 2. Of those that a mesh axis runs over, the one named last changes fastest.
Arguments:
- tokens: bfloat16 [131072, 4096], P('wa'), may hold values from -6 to 6
- expert_ids: int32 [131072, 8], P('wa'), may hold values from 0 to 127, as said below
- keep_mask: int32 [131072, 8], P('wa'), may hold values from 0 to 1, as said below
- route_weight: float32 [131072, 8], P('wa'), may hold values from 0.2 to 1
- gate_weight: bfloat16 [4096, 1536], P('wa', 'ha'), may hold values from -0.09375 to 0.09375
- up_weight: bfloat16 [4096, 1536], P('wa', 'ha'), may hold values from -0.09375 to 0.09375
- down_weight: bfloat16 [4096, 1536], P('wa', 'ha'), may hold values from -0.15625 to 0.15625
Outputs:
- mixed: bfloat16 [131072, 4096], P('wa', 'ha')
Inputs may be any that keep to these rules, and one draw needn't show every extreme that they name: `expert_ids`: each row names 8 different experts. keep_mask[t, k] is 1 exactly where fewer than 128 earlier tokens of the same block of 1024 rows name expert_ids[t, k]; in some block 128 tokens naming expert 0 are kept.
All inputs are finite; a program needn't handle non-finite values.
Results may differ from a plain program's by a relative error of at most 0.005.
Values may be sent and summed in bfloat16 or wider, within the bound.
No kernel may reach another device: no remote copies, remote signals or barrier semaphores. Data moves between devices by JAX's collectives and lax.ppermute only.
A program may use at most 128 MiB of HBM per device.

v0:
```python
import jax
import jax.numpy as jnp
from jax import lax
from jax.sharding import Mesh
from jax.sharding import PartitionSpec as P

CAP = 128
WA = ("wa_0", "wa_1", "wa_2", "wa_3")


def neutral_like(array, identity):
    return jnp.zeros_like(array) + jnp.asarray(identity, array.dtype)


def carried_in(array, axes, combine, identity):
    before = start = neutral_like(array, identity)
    subtotal = array
    for axis in reversed(axes):
        devices, index = (lax.axis_size(axis), lax.axis_index(axis))
        pieces = lax.all_gather(subtotal, axis)
        inside, subtotal = (start, start)
        for k in range(devices):
            passed = k < index
            subtotal = combine(subtotal, pieces[k])
            inside = jnp.where(passed, subtotal, inside)
        before = combine(inside, before)
    return before


def sent_together(arrays, axis, dim, along):
    widths = [a.shape[along] for a in arrays]
    both = jnp.concatenate(arrays, axis=along)
    filled = lax.all_gather(both, axis, axis=dim, tiled=True)
    return tuple(jnp.split(filled, [sum(widths[:k]) for k in range(1, len(widths))], axis=along))


def split_up(array, dim, devices):
    before, after = (array.shape[:dim], array.shape[dim + 1 :])
    return jnp.moveaxis(array.reshape(*before, devices, -1, *after), dim, 0)


def sent_and_summed(array, axis, dim):
    tiles = split_up(array, dim, lax.axis_size(axis))
    arrived = lax.all_to_all(tiles, axis, split_axis=0, concat_axis=0, tiled=True)
    return arrived.sum(axis=0)


def add_counts(earlier, later):
    return earlier + later


def global_admit(chosen, position):
    counted = jnp.sum(chosen).reshape(1)
    earlier = carried_in(counted, WA, add_counts, jnp.zeros((1,), jnp.int32))
    capacity = lax.axis_size(WA) * CAP // 2
    return chosen * (earlier[0] + position < capacity).astype(jnp.int32)


def slot_table(position, marked):
    slot_ids = jnp.arange(CAP, dtype=jnp.int32)
    return (position[None, :] == slot_ids[:, None]) & (marked[None, :] == 1)


def run_expert(slot_rows, gate_weight, up_weight, down_weight):
    sections = sent_together((gate_weight, up_weight, down_weight), WA, 0, 1)
    gate_next = jnp.dot(slot_rows, sections[0], preferred_element_type=jnp.float32)
    up_next = jnp.dot(slot_rows, sections[1], preferred_element_type=jnp.float32)
    stored = sections[2]
    hidden = (jax.nn.silu(gate_next) * up_next).astype(jnp.bfloat16)
    return lax.dot_general(
        hidden, stored, (((1,), (1,)), ((), ())), preferred_element_type=jnp.float32
    )


def per_device(tokens, expert_ids, keep_mask, route_weight, gate_weight, up_weight, down_weight):
    matches = (expert_ids == 0) & (keep_mask == 1)
    chosen = jnp.any(matches, axis=1).astype(jnp.int32)
    route_sum = jnp.sum(jnp.where(matches, route_weight, jnp.float32(0.0)), axis=1)
    position = jnp.cumsum(chosen) - chosen
    admitted = global_admit(chosen, position)
    dispatch = slot_table(position, admitted)
    slot_rows = jnp.dot(
        dispatch.astype(jnp.bfloat16), tokens, preferred_element_type=jnp.float32
    ).astype(jnp.bfloat16)
    expert_out = run_expert(slot_rows, gate_weight, up_weight, down_weight)
    final_table = slot_table(position, admitted)
    combine_map = jnp.where(final_table.T, route_sum[:, None], jnp.float32(0.0))
    halves = sent_and_summed(expert_out, "ha", 1)
    mixed = jnp.dot(
        combine_map, halves, precision=lax.Precision.HIGHEST, preferred_element_type=jnp.float32
    )
    return mixed.astype(jnp.bfloat16)


def solution(mesh):
    finer = Mesh(
        mesh.devices.reshape(4, 2, 8, 2, mesh.shape["ha"]), ("wa_0", "wa_1", "wa_2", "wa_3", "ha")
    )
    placed = (
        P(WA, None),
        P(WA, None),
        P(WA, None),
        P(WA, None),
        P(WA, "ha"),
        P(WA, "ha"),
        P(WA, "ha"),
    )
    return jax.shard_map(
        per_device, mesh=finer, in_specs=placed, out_specs=P(WA, "ha"), check_vma=False
    )
```

profile of v0, /device:TPU:1, one launch (start us, length us, event | category | flops | bytes accessed | tf_op | source)
XLA Modules:
  0.0 302.4 jit_solution(12403470860558871881)
XLA Ops:
  6.5 1.5 pad_maximum_fusion
  8.1 1.3 dynamic-slice
  9.4 0.8 select_reduce_fusion
  10.9 1.3 dynamic-update-slice
  12.2 4.7 %all-reduce = s32[2]{0:T(128)S(1)} all-reduce(s32[2]{0:T(128)S(1)} %dynamic-update-slice), channel_id=1, replica_groups=mesh['wa_0'=4,'wa_1'=2,'wa_2'=8,'wa_3'=2,'ha'=2] {'wa_3'}, use_global_device_ids=true, to_apply=%add | all-reduce | flops 2 | bytes 16
  16.9 1.3 dynamic-slice.1
  18.8 1.3 dynamic-update-slice.1
  20.1 11.5 %all-reduce.1 = s32[8]{0:T(128)S(1)} all-reduce(s32[8]{0:T(128)S(1)} %dynamic-update-slice.1), channel_id=2, replica_groups=mesh['wa_0'=4,'wa_1'=2,'wa_2'=8,'wa_3'=2,'ha'=2] {'wa_2'}, use_global_device_ids=true, to_apply=%add.1 | all-reduce | flops 8 | bytes 64
  31.6 1.3 dynamic-slice.2
  32.8 0.7 slice_add_fusion.5
  33.5 1.3 fusion.35
  34.8 1.1 slice_add_fusion.2
  35.9 1.3 dynamic-update-slice.2
  37.2 3.5 %all-reduce.2 = s32[2]{0:T(128)S(1)} all-reduce(s32[2]{0:T(128)S(1)} %dynamic-update-slice.2), channel_id=3, replica_groups=mesh['wa_0'=4,'wa_1'=2,'wa_2'=8,'wa_3'=2,'ha'=2] {'wa_1'}, use_global_device_ids=true, to_apply=%add.2 | all-reduce | flops 2 | bytes 16
  40.7 1.3 dynamic-slice.3
  42.6 1.4 dynamic-update-slice.3
  44.0 7.5 %all-reduce.3 = s32[4]{0:T(128)S(1)} all-reduce(s32[4]{0:T(128)S(1)} %dynamic-update-slice.3), channel_id=4, replica_groups=mesh['wa_0'=4,'wa_1'=2,'wa_2'=8,'wa_3'=2,'ha'=2] {'wa_0'}, use_global_device_ids=true, to_apply=%add.3 | all-reduce | flops 4 | bytes 32
  51.8 0.7 fusion.37
  63.5 4.7 %convolution_convert_fusion = bf16[128,4096]{1,0:T(8,128)(2,1)S(1)} fusion(bf16[1024,4096]{1,0:T(8,128)(2,1)} %param.7, s32[1024]{0:T(1024)S(1)} %get-tuple-element.8, pred[1024]{0:T(1024)(128)(4,1)S(1)} %get-tuple-element.7), kind=kOutput, calls=%fused_computation.6 | convolution fusion | flops 1074528256 | bytes 9442304 | tf_op jit(solution)/shard_map/dot_general | solution.py:82
  68.2 178.2 %all-gather.5.cloned.1.call-done = bf16[4096,2304]{1,0:T(8,128)(2,1)} async-done(((bf16[32,2304]{1,0:T(8,128)(2,1)}), bf16[4096,2304]{1,0:T(8,128)(2,1)}) %all-gather.5.cloned.1.call-update) | async-done | bytes 18874384 | tf_op jit(solution)/shard_map/all_gather | solution.py:33
  246.4 4.5 %fusion.4 = f32[128,768]{1,0:T(8,128)} fusion(bf16[128,4096]{1,0:T(8,128)(2,1)S(1)} %convolution_convert_fusion, bf16[4096,2304]{1,0:T(8,128)(2,1)} %all-gather.5.cloned.1.call-done), kind=kOutput, calls=%fused_computation.4 | convolution fusion | flops 805306368 | bytes 7733248 | tf_op jit(solution)/shard_map/dot_general | solution.py:66
  250.9 7.9 %fusion = f32[128,4096]{1,0:T(8,128)S(1)} fusion(bf16[4096,2304]{1,0:T(8,128)(2,1)} %all-gather.5.cloned.1.call-done, bf16[128,4096]{1,0:T(8,128)(2,1)S(1)} %convolution_convert_fusion, f32[128,768]{1,0:T(8,128)} %fusion.4), kind=kOutput, calls=%fused_computation | convolution fusion | flops 1611202560 | bytes 16121856 | tf_op jit(solution)/shard_map/dot_general | solution.py:70
  258.9 27.8 %all_to_all.5 = f32[2,128,2048]{2,1,0:T(8,128)S(1)} all-to-all(f32[2,128,2048]{2,1,0:T(8,128)S(1)} %bitcast.38), channel_id=1, replica_groups=mesh['wa_0'=4,'wa_1'=2,'wa_2'=8,'wa_3'=2,'ha'=2] {'ha'}, dimensions={0} | all-to-all | bytes 4194304 | tf_op jit(solution)/shard_map/all_to_all | solution.py:44
  287.0 8.5 %convolution_convert_fusion.1 = bf16[1024,2048]{1,0:T(8,128)(2,1)} fusion(f32[128,2048]{1,0:T(8,128)S(1)} %reduce_sum.29, f32[1024]{0:T(1024)S(1)} %get-tuple-element.5, s32[1024]{0:T(1024)S(1)} %get-tuple-element.8, pred[1024]{0:T(1024)(128)(4,1)S(1)} %get-tuple-element.7), kind=kOutput, calls=%fused_computation.7 | convolution fusion | flops 3223715840 | bytes 5252096 | tf_op jit(solution)/shard_map/dot_general | solution.py:89
  (18 shorter events, 2.9 us)
Async XLA Ops:
  6.5 239.8 %all-gather.5.cloned.1.call-start = ((), (), s32[]{:S(2)}) async-start(), calls=%async_computation.1 | async-start | bytes 19021824 | tf_op jit(solution)/shard_map/all_gather | solution.py:33
Sparse Core Ops, SparseCore 0:
  9.2 237.1 all-gather.4
where the time goes:
time: 304 us; the launch traced here: 302 us
  waiting for transfers between devices  178 us (59%)
  blocking collectives  55 us (18%)
  matrix products  25.6 us (8%)
  between operations  24.2 us (8%)
  local copies, waits for them, and re-layouts  11.5 us (4%)
  other arithmetic  7.91 us (3%)
    all_gather x1, waiting for transfers between devices, sent_together(): filled = lax.all_gather(both, axis, axis=dim, tiled=True)  178 us
    all_to_all x1, blocking collectives, sent_and_summed(): lax.all_to_all(tiles, axis, split_axis=0, concat_axis=0, tiled=True)  27.8 us
    unnamed x4, blocking collectives  27.2 us
    unnamed x12, local copies, waits for them, and re-layouts  10.5 us
    dot_general x1, matrix products, per_device(): jnp.dot(combine_map, halves, precision=lax.Precision.HIGHEST, preferred_e...  8.52 us
    dot_general x1, matrix products, run_expert(): lax.dot_general(hidden, stored, (((1,), (1,)), ((), ())), preferred_eleme...  7.85 us
  transfers between devices with their start and end apart: 1, of which 1 were waited for; matrix products, arithmetic and copies ran while one was open for 7% of the time, Pallas kernels for 0%

commit v1 on v0

v1 whole, which is shorter than its diff:
```python
import jax
import jax.numpy as jnp
from jax import lax
from jax.experimental import pallas as pl
from jax.experimental.pallas import tpu as pltpu
from jax.sharding import Mesh
from jax.sharding import PartitionSpec as P

CAP = 128
WA = ("y", "xl", "z", "c")
NY, NZ = 4, 8
F32, BF16, I32 = jnp.float32, jnp.bfloat16, jnp.int32
VMEM = pltpu.VMEM
LIMIT = 50 << 20


def whole(memory_space=VMEM):
    return pl.BlockSpec(memory_space=memory_space)


def ring(axis, n, k):
    return lambda a: lax.ppermute(a, axis, [(i, (i + k) % n) for i in range(n)])


def Z(k):
    return ring("z", NZ, k)


def Y(k):
    return ring("y", NY, k)


def C(a):
    return lax.ppermute(a, "c", [(0, 1), (1, 0)])


def XL(a):
    return lax.ppermute(a, "xl", [(0, 1), (1, 0)])


def HA(a):
    return lax.ppermute(a, "ha", [(0, 1), (1, 0)])


def X(k):
    def at(x):
        return (x % 2) * 2 + x // 2

    pairs = [(at(x), at((x + k) % 4)) for x in range(4)]
    return lambda a: lax.ppermute(a, ("xl", "ha"), pairs)


def route_body(ids, keep, rw, info, cnt):
    hit = (ids[...] == 0) & (keep[...] == 1)
    chosen = jnp.max(jnp.where(hit, 1.0, 0.0), axis=0, keepdims=True)
    route = jnp.sum(jnp.where(hit, rw[...], 0.0), axis=0, keepdims=True)
    n = chosen.shape[1]
    row = lax.broadcasted_iota(I32, (n, n), 0)
    col = lax.broadcasted_iota(I32, (n, n), 1)
    before = jnp.where(row < col, 1.0, 0.0).astype(BF16)
    ones = jnp.broadcast_to(chosen, (16, n)).astype(BF16)
    position = jnp.dot(ones, before, preferred_element_type=F32)[:1]
    info[0:1, :] = position
    info[1:2, :] = chosen
    info[2:3, :] = route
    info[3:8, :] = jnp.zeros((5, n), F32)
    total = jnp.sum(chosen, axis=1, keepdims=True)
    cnt[...] = jnp.broadcast_to(total, cnt.shape)


def routing(ids, keep, rw):
    n = ids.shape[1]
    return pl.pallas_call(
        route_body,
        out_shape=(jax.ShapeDtypeStruct((8, n), F32), jax.ShapeDtypeStruct((8, 384), F32)),
        in_specs=[whole()] * 3,
        out_specs=(whole(), whole()),
        cost_estimate=pl.CostEstimate(flops=2 * 16 * n * n, bytes_accessed=4 * 32 * n, transcendentals=0),
        name="routing",
    )(ids, keep, rw)


def table(info):
    slot = lax.broadcasted_iota(I32, (CAP, info.shape[1]), 0).astype(F32)
    return (info[0:1, :] == slot) & (info[1:2, :] > 0.5)


def gather_body(where, tokens, info, out, slot_route):
    block = pl.program_id(0)
    picked = table(info)
    rows = jnp.dot(picked.astype(BF16), tokens[...], preferred_element_type=F32).astype(BF16)
    ky = lax.rem(block - where[0] + NY, NY)
    yi = jnp.where(ky == 0, 0, jnp.where(ky == 3, 1, jnp.where(ky == 1, 2, 3)))
    for z in range(NZ):
        kz = lax.rem(z - where[1] + NZ, NZ)
        zi = jnp.where(kz == 0, 0, jnp.where(kz <= 3, 2 * kz, jnp.where(kz == 4, 7, 15 - 2 * kz)))
        piece = jnp.concatenate([rows[:, z * 64 : z * 64 + 64], rows[:, 512 + z * 64 : 576 + z * 64]], axis=1)
        out[:, pl.ds(pl.multiple_of((yi * NZ + zi) * 128, 128), 128)] = piece

    @pl.when(block == 0)
    def _():
        got = jnp.sum(jnp.where(picked, info[2:3, :], 0.0), axis=1, keepdims=True)
        slot_route[...] = jnp.broadcast_to(got, slot_route.shape)


def gather_rows(where, tokens, info):
    n, d = tokens.shape
    return pl.pallas_call(
        gather_body,
        out_shape=(jax.ShapeDtypeStruct((CAP, d), BF16), jax.ShapeDtypeStruct((CAP, 128), F32)),
        grid_spec=pltpu.PrefetchScalarGridSpec(
            num_scalar_prefetch=1,
            grid=(NY,),
            in_specs=[
                pl.BlockSpec((n, d // NY), lambda i, w: (0, i)),
                pl.BlockSpec((8, n), lambda i, w: (0, 0)),
            ],
            out_specs=(
                pl.BlockSpec((CAP, d), lambda i, w: (0, 0)),
                pl.BlockSpec((CAP, 128), lambda i, w: (0, 0)),
            ),
        ),
        compiler_params=pltpu.CompilerParams(vmem_limit_bytes=24 << 20),
        cost_estimate=pl.CostEstimate(flops=2 * CAP * n * d, bytes_accessed=2 * n * d, transcendentals=0),
        name="gather_rows",
    )(where, tokens, info)


def gate_up_body(n_weights, *refs):
    weights, rows = refs[:n_weights], refs[n_weights : n_weights + 6]
    own, other, x_all = refs[n_weights + 6 :]
    xo, xc, xa, xb, xac, xbc = rows
    x_all[0:128, :] = xo[...]
    x_all[128:256, :] = xc[...]
    x_all[256:320, :] = xb[...]
    x_all[320:384, :] = xa[...]
    x_all[384:448, :] = xbc[...]
    x_all[448:512, :] = xac[...]
    total = jnp.zeros((512, 384), F32)
    for ref, (start, size) in zip(weights, SPANS):
        total += jnp.dot(x_all[:, start : start + size], ref[0:size, :], preferred_element_type=F32)
    gate, up = total[:, :192], total[:, 192:]
    hidden = (gate * jax.nn.sigmoid(gate) * up).astype(BF16)
    own[...] = hidden[:256]
    other[...] = hidden[256:]


SPANS = []
for _i in range(3):
    SPANS += [(_i * 1024, 640), (_i * 1024 + 640, 384)]
SPANS += [(3072, 384), (3072 + 384, 256), (3072 + 640, 256), (3072 + 896, 128)]


def gate_up(weights, rows):
    half = jax.ShapeDtypeStruct((256, 192), BF16)
    return pl.pallas_call(
        lambda *refs: gate_up_body(len(weights), *refs),
        out_shape=(half, half),
        in_specs=[whole()] * (len(weights) + len(rows)),
        out_specs=(whole(), whole()),
        scratch_shapes=[VMEM((512, 4096), BF16)],
        compiler_params=pltpu.CompilerParams(vmem_limit_bytes=LIMIT),
        cost_estimate=pl.CostEstimate(flops=2 * 512 * 4096 * 384, bytes_accessed=8 << 20, transcendentals=512 * 192),
        name="gate_up",
    )(*weights, *rows)


def down_body(hidden, *refs):
    pieces, keep, send = refs[:-2], refs[-2], refs[-1]

    def dot(w):
        return lax.dot_general(hidden[...], w, (((1,), (1,)), ((), ())), preferred_element_type=F32)

    for r in range(NZ):
        at = slice(r * 128, r * 128 + 128)
        if r == 4:
            keep[:, at] = dot(pieces[4][...])
            send[:, at] = dot(pieces[8][...]).astype(BF16)
        else:
            both = dot(pieces[r][...])
            keep[:, at] = both[:, :128]
            send[:, at] = both[:, 128:].astype(BF16)


def down(hidden, pieces):
    return pl.pallas_call(
        down_body,
        out_shape=(jax.ShapeDtypeStruct((256, 1024), F32), jax.ShapeDtypeStruct((256, 1024), BF16)),
        in_specs=[whole()] * (1 + len(pieces)),
        out_specs=(whole(), whole()),
        compiler_params=pltpu.CompilerParams(vmem_limit_bytes=LIMIT),
        cost_estimate=pl.CostEstimate(flops=2 * 256 * 768 * 2048, bytes_accessed=5 << 20, transcendentals=0),
        name="down",
    )(hidden, *pieces)


def mix_body(where, mine, theirs, info, slot_route, out, slots):
    @pl.when(pl.program_id(0) == 0)
    def _():
        slot = lax.broadcasted_iota(I32, (CAP, 1), 0)
        scale = jnp.where(slot < where[2], slot_route[:, 0:1], 0.0)
        src = lax.broadcasted_iota(I32, (512, 512), 0)
        dst = lax.broadcasted_iota(I32, (512, 512), 1)
        moved = (src + where[1] * 64) & 511
        order = jnp.where(moved == dst, 1.0, 0.0).astype(BF16)
        for ref, column in ((mine, where[0]), (theirs, 1 - where[0])):
            scaled = (ref[...] * scale).astype(BF16)
            for y in range(2):
                part = jnp.concatenate(
                    [scaled[:, r * 128 + y * 64 : r * 128 + y * 64 + 64] for r in range(NZ)], axis=1
                )
                placed = jnp.dot(part, order, preferred_element_type=F32).astype(BF16)
                slots[:, pl.ds(pl.multiple_of(y * 1024 + column * 512, 512), 512)] = placed

    picked = table(info).astype(BF16)
    mixed = lax.dot_general(picked, slots[...], (((0,), (0,)), ((), ())), preferred_element_type=F32)
    out[...] = mixed.astype(BF16)


def mix(where, mine, theirs, info, slot_route):
    n, step = info.shape[1], 256
    return pl.pallas_call(
        mix_body,
        out_shape=jax.ShapeDtypeStruct((n, 2048), BF16),
        grid_spec=pltpu.PrefetchScalarGridSpec(
            num_scalar_prefetch=1,
            grid=(n // step,),
            in_specs=[
                pl.BlockSpec((CAP, 1024), lambda i, w: (0, 0)),
                pl.BlockSpec((CAP, 1024), lambda i, w: (0, 0)),
                pl.BlockSpec((8, step), lambda i, w: (0, i)),
                pl.BlockSpec((CAP, 128), lambda i, w: (0, 0)),
            ],
            out_specs=pl.BlockSpec((step, 2048), lambda i, w: (i, 0)),
            scratch_shapes=[VMEM((CAP, 2048), BF16)],
        ),
        compiler_params=pltpu.CompilerParams(vmem_limit_bytes=24 << 20),
        cost_estimate=pl.CostEstimate(flops=2 * n * CAP * 2048, bytes_accessed=6 << 20, transcendentals=0),
        name="mix",
    )(where, mine, theirs, info, slot_route)


def z_ring(u, cut):
    back, ahead, out = u, u, [u]
    for _ in range(3):
        back, ahead = Z(1)(back), Z(-1)(ahead)
        out += [back, ahead]
    return out, (Z(1)(back[:cut]), Z(-1)(ahead[cut:]))


def y_ring(u, cut):
    back, ahead = Y(1)(u), Y(-1)(u)
    return back, ahead, Y(1)(back[:cut]), Y(-1)(ahead[cut:])


def with_counts(units):
    return jnp.concatenate([u[:128] for u in units] + [u[128:] for u in units], axis=0)


def per_device(tokens, expert_ids, keep_mask, route_weight, gate_weight, up_weight, down_weight):
    y, xl, z, c, ha = (lax.axis_index(a) for a in ("y", "xl", "z", "c", "ha"))
    info, cnt = routing(expert_ids.T, keep_mask.T, route_weight.T)

    quarters = jnp.concatenate(
        [gate_weight.reshape(32, 4, 192).swapaxes(0, 1), up_weight.reshape(32, 4, 192).swapaxes(0, 1)], axis=2
    )
    counted = jnp.broadcast_to(cnt.astype(BF16)[None], (4, 8, 384))
    arrived = lax.all_to_all(
        jnp.concatenate([quarters, counted], axis=1), ("xl", "c"), split_axis=0, concat_axis=0, tiled=True
    )
    lane = lax.broadcasted_iota(I32, (8, 384), 1)
    tile = jnp.zeros((8, 384), BF16)
    for j in range(4):
        tile = jnp.where(lane == j, arrived[j, 32:40], tile)
    unit = jnp.concatenate([arrived[:, :32].reshape(128, 384), tile], axis=0)

    rows = lax.all_gather(down_weight, ("xl", "c"), axis=0, tiled=False)
    rows = lax.dynamic_slice_in_dim(rows, 2 * c, 2, axis=0).reshape(64, 768)
    d_back, d_ahead, d_far0, d_far1 = y_ring(rows, 32)
    turned = [rows, d_ahead, jnp.concatenate([d_far0, d_far1], axis=0), d_back]
    shift = lax.rem(2 * ha - y + NY, NY)
    ordered = []
    for j in range(4):
        pick = turned[j]
        for s in range(1, 4):
            pick = jnp.where(shift == s, turned[(j + s) % 4], pick)
        ordered.append(pick)
    d_near, d_last = z_ring(jnp.concatenate(ordered, axis=0), 128)
    pieces = [d_near[0], d_near[2], d_near[4], d_near[6], d_last[0], d_near[5], d_near[3], d_near[1], d_last[1]]

    g_near, g_last = z_ring(unit, 64)
    first = with_counts(g_near[:5])
    second = with_counts(g_near[5:] + [jnp.concatenate(g_last, axis=0)])
    f_back, f_ahead, f_far0, f_far1 = y_ring(first, 384)
    s_back, s_ahead, s_far0, s_far1 = y_ring(second, 256)

    slot_rows, slot_route = gather_rows(jnp.stack([y, z]), tokens, info)
    xa, xb = X(1)(slot_rows[64:]), X(-1)(slot_rows[:64])
    x_rows = [slot_rows, C(slot_rows), xa, xb, C(xa), C(xb)]
    weights = [first, second, f_back, s_back, f_ahead, s_ahead, f_far0, f_far1, s_far0, s_far1]
    h_own, h_other = gate_up(weights, x_rows)
    h_near = XL(h_other)
    swapped = C(
        jnp.concatenate(
            [jnp.concatenate([h_own[128:], h_own[:128]], 0), jnp.concatenate([h_near[128:], h_near[:128]], 0)], axis=1
        )
    )
    h_core, h_far = swapped[:, :192], swapped[:, 192:]
    c0, x0 = c == 0, xl == 0
    here = (jnp.where(c0, h_own, h_core), jnp.where(c0, h_core, h_own))
    there = (jnp.where(c0, h_near, h_far), jnp.where(c0, h_far, h_near))
    hidden = jnp.concatenate(
        [jnp.where(x0, a, b) for a, b in zip(here, there)] + [jnp.where(x0, b, a) for a, b in zip(here, there)], axis=1
    )
    keep, send = down(hidden, pieces)
    total = keep + HA(send).astype(F32)
    theirs = C(total[128:])

    counts = []
    for near, late in ((first[640:], second[384:]), (f_back[640:], s_back[384:]), (f_ahead[640:], s_ahead[384:]), (f_far1[256:], s_far1[128:])):
        counts += [near.reshape(5, 8, 384)[:, 0, :4], late.reshape(3, 8, 384)[:, 0, :4]]
    counts = jnp.concatenate(counts, axis=0).astype(I32)
    entry = lax.broadcasted_iota(I32, (32, 4), 0)
    quad = lax.broadcasted_iota(I32, (32, 4), 1)
    yi, zi = entry // 8, entry % 8
    ky = jnp.where(yi == 0, 0, jnp.where(yi == 1, 3, jnp.where(yi == 2, 1, 2)))
    kz = jnp.where(zi == 7, 4, jnp.where(zi % 2 == 0, zi // 2, 8 - (zi + 1) // 2))
    block = ((y + ky) % 4) * 32 + (quad // 2) * 16 + ((z + kz) % 8) * 2 + quad % 2
    me = y * 32 + xl * 16 + z * 2 + c
    earlier = jnp.sum(jnp.where(block < me, counts, 0))
    capacity = lax.axis_size(WA) * CAP // 2
    return mix(jnp.stack([c, z, capacity - earlier]), total[:128], theirs, info, slot_route)


def solution(mesh):
    finer = Mesh(mesh.devices.reshape(NY, 2, NZ, 2, mesh.shape["ha"]), ("y", "xl", "z", "c", "ha"))
    placed = (P(WA, None),) * 4 + (P(WA, "ha"),) * 3
    return jax.shard_map(per_device, mesh=finer, in_specs=placed, out_specs=P(WA, "ha"), check_vma=False)
```

time: 304 us -> 166 us (0.55)
  waiting for transfers between devices: 178 us -> 41.5 us
  starting transfers between devices: 0.01 us -> 66.4 us
  blocking collectives: 55 us -> 8.88 us
  matrix products: 25.6 us -> 0 us
  between operations: 24.2 us -> 1.12 us
  Pallas kernels: 0 us -> 17.1 us
  local copies, waits for them, and re-layouts: 11.5 us -> 21.2 us
    all_gather x1 -> x0, waiting for transfers between devices: 178 us -> none  [sent_together(): filled = lax.all_gather(both, axis, axis=dim, tiled=True)]
    ppermute x0 -> x37, starting transfers between devices: none -> 62.4 us  [the longest x28 40.5 us: ring(): return lambda a: lax.ppermute(a, axis, [(i, (i + k) % n) for i in range(n)])]
    ppermute x0 -> x37, waiting for transfers between devices: none -> 41.5 us  [the longest x28 25.6 us: ring(): return lambda a: lax.ppermute(a, axis, [(i, (i + k) % n) for i in range(n)])]
    all_to_all x1 -> x0, blocking collectives: 27.8 us -> none  [sent_and_summed(): lax.all_to_all(tiles, axis, split_axis=0, concat_axis=0, tiled=True)]
    unnamed x4 -> x0, blocking collectives: 27.2 us -> none
    dot_general x4 -> x0, matrix products: 25.6 us -> none  [the longest x1 8.52 us: per_device(): jnp.dot(combine_map, halves, precision=lax.Precision.HIGHEST, preferred_e...]
    pallas_call x0 -> x5, Pallas kernels: none -> 17.1 us  [the longest x1 5.25 us: gate_up(): pl.pallas_call(lambda *refs: gate_up_body(len(weights), *refs), out_shape...]
    all_gather x0 -> x1, blocking collectives: none -> 8.88 us  [per_device(): rows = lax.all_gather(down_weight, ('xl', 'c'), axis=0, tiled=False)]
  transfers between devices with their start and end apart: 1 -> 38, of which waited for: 1 -> 12; matrix products, arithmetic and copies ran while one was open for 7% -> 10% of each run, Pallas kernels for 0% -> 6%
where the time goes in v1:
time: 166 us; the launch traced here: 165 us
  starting transfers between devices  66.4 us (40%)
  waiting for transfers between devices  41.5 us (25%)
  local copies, waits for them, and re-layouts  21.2 us (13%)
  Pallas kernels  17.1 us (10%)
  other arithmetic  8.93 us (5%)
  blocking collectives  8.88 us (5%)
    ppermute x28, starting transfers between devices, ring(): return lambda a: lax.ppermute(a, axis, [(i, (i + k) % n) for i in range(n)])  40.5 us
    ppermute x28, waiting for transfers between devices, ring(): return lambda a: lax.ppermute(a, axis, [(i, (i + k) % n) for i in range(n)])  25.6 us
    ppermute x5, starting transfers between devices, C(): return lax.ppermute(a, 'c', [(0, 1), (1, 0)])  18.3 us
    unnamed x70, local copies, waits for them, and re-layouts  12.6 us
    ppermute x1, waiting for transfers between devices, HA(): return lax.ppermute(a, 'ha', [(0, 1), (1, 0)])  12.1 us
    all_gather x1, blocking collectives, per_device(): rows = lax.all_gather(down_weight, ('xl', 'c'), axis=0, tiled=False)  8.88 us
    pallas_call x1, Pallas kernels, gate_up(): pl.pallas_call(lambda *refs: gate_up_body(len(weights), *refs), out_shape...  5.25 us
    pallas_call x1, Pallas kernels, mix(): pl.pallas_call(mix_body, out_shape=jax.ShapeDtypeStruct((n, 2048), BF16),...  4.48 us
  transfers between devices with their start and end apart: 38, of which 12 were waited for; matrix products, arithmetic and copies ran while one was open for 10% of the time, Pallas kernels for 6%

profile of v1, /device:TPU:1, one launch (start us, length us, event | category | flops | bytes accessed | tf_op | source)
XLA Modules:
  0.0 165.1 jit_solution(18343683596716459835)
XLA Ops:
  0.0 8.9 %all-gather = bf16[128,768]{1,0:T(8,128)(2,1)S(1)} all-gather(bf16[32,768]{1,0:T(8,128)(2,1)} %param.13), channel_id=2, replica_groups=mesh['y'=4,'xl'=2,'z'=8,'c'=2,'ha'=2] {'xl','c'}, dimensions={0}, use_global_device_ids=true | all-gather | bytes 245760 | tf_op jit(solution)/shard_map/all_gather | solution.py:277
  16.7 4.0 %all-to-all-start = ((bf16[4,40,384]{2,1,0:T(8,128)(2,1)}), bf16[4,40,384]{2,1,0:T(8,128)(2,1)S(1)}, u32[]{:S(2)}, u32[]{:S(2)}) async-start(bf16[4,40,384]{2,1,0:T(8,128)(2,1)} %pad_maximum_fusion.2), calls=%async_computation | async-start | bytes 245760 | tf_op jit(solution)/shard_map/all_to_all | solution.py:268
  20.8 3.4 %copy-done = bf16[1024,4096]{1,0:T(8,128)(2,1)S(1)} copy-done((bf16[1024,4096]{1,0:T(8,128)(2,1)S(1)}, bf16[1024,4096]{1,0:T(8,128)(2,1)}, u32[]{:S(2)}) %copy-start) | copy-done | bytes 8388632
  24.9 3.5 %gather_rows.1 = (bf16[128,4096]{1,0:T(8,128)(2,1)S(1)}, f32[128,128]{1,0:T(8,128)S(1)}) custom-call(s32[2]{0:T(128)S(1)} %pad_add_fusion.1.where, bf16[1024,4096]{1,0:T(8,128)(2,1)S(1)} %copy-done, f32[8,1024]{1,0:T(8,128)S(1)} %copy-done.16), custom_call_target="tpu_custom_call" | custom-call | flops 1073741824 | bytes 8388608 | tf_op jit(solution)/shard_map/gather_rows/pallas_call | solution.py:108
  33.3 4.0 %collective-permute-start.1 = (bf16[136,384]{1,0:T(8,128)(2,1)S(1)}, bf16[136,384]{1,0:T(8,128)(2,1)S(1)}, u32[]{:S(2)}, u32[]{:S(2)}) collective-permute-start(bf16[136,384]{1,0:T(8,128)(2,1)S(1)} %pad_maximum_fusion.3), channel_id=1, source_target_pairs={{0,28},{4,0},{8,4},{12,8},{16,12},{20,16},{24,20},{28,24},{1,29},{... | collective-permute-start | bytes 313352 | tf_op jit(solution)/shard_map/ppermute | solution.py:22
  41.3 3.7 %collective-permute-start.27 = (bf16[256,768]{1,0:T(8,128)(2,1)S(1)}, bf16[256,768]{1,0:T(8,128)(2,1)S(1)}, u32[]{:S(2)}, u32[]{:S(2)}) collective-permute-start(bf16[256,768]{1,0:T(8,128)(2,1)S(1)} %pad_maximum_fusion.1.refs_0_), channel_id=1, source_target_pairs={{0,28},{4,0},{8,4},{12,8},{16,12},{20,16},{24,20},{28,24},{1,29},{... | collective-permute-start | bytes 1179656 | tf_op jit(solution)/shard_map/ppermute | solution.py:22
  45.0 2.7 %collective-permute-start.3 = (bf16[136,384]{1,0:T(8,128)(2,1)S(1)}, bf16[136,384]{1,0:T(8,128)(2,1)S(1)}, u32[]{:S(2)}, u32[]{:S(2)}) collective-permute-start(bf16[136,384]{1,0:T(8,128)(2,1)S(1)} %collective-permute-done.1), channel_id=1, source_target_pairs={{0,28},{4,0},{8,4},{12,8},{16,12},{20,16},{24,20},{28,24},{1,29},{... | collective-permute-start | bytes 313352 | tf_op jit(solution)/shard_map/ppermute | solution.py:22
  49.8 3.6 %collective-permute-done.3 = bf16[136,384]{1,0:T(8,128)(2,1)S(1)} collective-permute-done((bf16[136,384]{1,0:T(8,128)(2,1)S(1)}, bf16[136,384]{1,0:T(8,128)(2,1)S(1)}, u32[]{:S(2)}, u32[]{:S(2)}) %collective-permute-start.3) | collective-permute-done | bytes 104480 | tf_op jit(solution)/shard_map/ppermute | solution.py:22
  53.5 3.5 %collective-permute-start.5 = (bf16[136,384]{1,0:T(8,128)(2,1)S(1)}, bf16[136,384]{1,0:T(8,128)(2,1)S(1)}, u32[]{:S(2)}, u32[]{:S(2)}) collective-permute-start(bf16[136,384]{1,0:T(8,128)(2,1)S(1)} %collective-permute-done.3), channel_id=1, source_target_pairs={{0,28},{4,0},{8,4},{12,8},{16,12},{20,16},{24,20},{28,24},{1,29},{... | collective-permute-start | bytes 313352 | tf_op jit(solution)/shard_map/ppermute | solution.py:22
  58.7 3.1 %collective-permute-start.6 = (bf16[72,384]{1,0:T(8,128)(2,1)S(1)}, bf16[72,384]{1,0:T(8,128)(2,1)S(1)}, u32[]{:S(2)}, u32[]{:S(2)}) collective-permute-start(bf16[72,384]{1,0:T(8,128)(2,1)S(1)} %slice.228), channel_id=1, source_target_pairs={{0,28},{4,0},{8,4},{12,8},{16,12},{20,16},{24,20},{28,24},{1,29},{... | collective-permute-start | bytes 165896 | tf_op jit(solution)/shard_map/ppermute | solution.py:22
  62.0 4.1 %collective-permute-done.8 = bf16[64,384]{1,0:T(8,128)(2,1)S(1)} collective-permute-done((bf16[64,384]{1,0:T(8,128)(2,1)S(1)}, bf16[64,384]{1,0:T(8,128)(2,1)S(1)}, u32[]{:S(2)}, u32[]{:S(2)}) %collective-permute-start.8) | collective-permute-done | bytes 49184 | tf_op jit(solution)/shard_map/ppermute | solution.py:22
  66.7 2.7 %collective-permute-start.11 = (bf16[408,384]{1,0:T(8,128)(2,1)S(1)}, bf16[408,384]{1,0:T(8,128)(2,1)S(1)}, u32[]{:S(2)}, u32[]{:S(2)}) collective-permute-start(bf16[408,384]{1,0:T(8,128)(2,1)S(1)} %get-tuple-element.51.refs_1_), channel_id=1, source_target_pairs={{0,192},{64,0},{128,64},{192,128},{1,193},{65,1},{129,65},{193,129... | collective-permute-start | bytes 940040 | tf_op jit(solution)/shard_map/ppermute | solution.py:22
  69.4 2.7 %collective-permute-start.10 = (bf16[680,384]{1,0:T(8,128)(2,1)S(1)}, bf16[680,384]{1,0:T(8,128)(2,1)S(1)}, u32[]{:S(2)}, u32[]{:S(2)}) collective-permute-start(bf16[680,384]{1,0:T(8,128)(2,1)S(1)} %get-tuple-element.43.refs_0_), channel_id=1, source_target_pairs={{0,192},{64,0},{128,64},{192,128},{1,193},{65,1},{129,65},{193,129... | collective-permute-start | bytes 1566728 | tf_op jit(solution)/shard_map/ppermute | solution.py:22
  74.4 6.9 %collective-permute-start.16 = (bf16[128,4096]{1,0:T(8,128)(2,1)S(1)}, bf16[128,4096]{1,0:T(8,128)(2,1)}, u32[]{:S(2)}, u32[]{:S(2)}) collective-permute-start(bf16[128,4096]{1,0:T(8,128)(2,1)S(1)} %get-tuple-element.15.refs_10_), channel_id=1, source_target_pairs={{0,2},{2,0},{1,3},{3,1},{4,6},{6,4},{5,7},{7,5},{8,10},{10,8},{9,1... | collective-permute-start | bytes 3145736 | tf_op jit(solution)/shard_map/ppermute | solution.py:34
  87.0 5.1 %collective-permute-start.19 = (bf16[64,4096]{1,0:T(8,128)(2,1)}, bf16[64,4096]{1,0:T(8,128)(2,1)}, u32[]{:S(2)}, u32[]{:S(2)}) collective-permute-start(bf16[64,4096]{1,0:T(8,128)(2,1)} %copy-done.20), channel_id=1, source_target_pairs={{0,2},{2,0},{1,3},{3,1},{4,6},{6,4},{5,7},{7,5},{8,10},{10,8},{9,1... | collective-permute-start | bytes 1572872 | tf_op jit(solution)/shard_map/ppermute | solution.py:34
  98.6 2.8 %collective-permute-start.12 = (bf16[296,384]{1,0:T(8,128)(2,1)}, bf16[296,384]{1,0:T(8,128)(2,1)}, u32[]{:S(2)}, u32[]{:S(2)}) collective-permute-start(bf16[296,384]{1,0:T(8,128)(2,1)} %slice.246), channel_id=1, source_target_pairs={{0,192},{64,0},{128,64},{192,128},{1,193},{65,1},{129,65},{193,129... | collective-permute-start | bytes 681992 | tf_op jit(solution)/shard_map/ppermute | solution.py:22
  106.0 3.2 %collective-permute-start.29 = (bf16[256,768]{1,0:T(8,128)(2,1)}, bf16[256,768]{1,0:T(8,128)(2,1)S(1)}, u32[]{:S(2)}, u32[]{:S(2)}) collective-permute-start(bf16[256,768]{1,0:T(8,128)(2,1)} %copy-done.10), channel_id=1, source_target_pairs={{0,28},{4,0},{8,4},{12,8},{16,12},{20,16},{24,20},{28,24},{1,29},{... | collective-permute-start | bytes 1179656 | tf_op jit(solution)/shard_map/ppermute | solution.py:22
  109.1 3.4 %collective-permute-done.14.refs_6_ = bf16[384,384]{1,0:T(8,128)(2,1)} collective-permute-done((bf16[384,384]{1,0:T(8,128)(2,1)}, bf16[384,384]{1,0:T(8,128)(2,1)}, u32[]{:S(2)}, u32[]{:S(2)}) %collective-permute-start.14) | collective-permute-done | bytes 294944 | tf_op jit(solution)/shard_map/ppermute | solution.py:22
  115.4 5.3 %gate_up.1 = (bf16[256,192]{1,0:T(8,128)(2,1)S(1)}, bf16[256,192]{1,0:T(8,128)(2,1)S(1)}) custom-call(bf16[680,384]{1,0:T(8,128)(2,1)S(1)} %get-tuple-element.43.refs_0_, bf16[408,384]{1,0:T(8,128)(2,1)S(1)} %copy-done.5, bf16[680,384]{1,0:T(8,128)(2,1)S(1)} %collective-permute-done.7.refs_2_, bf16[408,384]{1,0:T(8,128)(2,1)S(1)} %collective-permute-done.9.refs_3_, ...), custom_call_target="tpu_custom_call" | custom-call | flops 1610612736 | bytes 8388608 | tf_op jit(solution)/shard_map/gate_up/pallas_call | solution.py:156
  120.8 3.8 %collective-permute-done.21 = bf16[256,192]{1,0:T(8,128)(2,1)S(1)} collective-permute-done((bf16[256,192]{1,0:T(8,128)(2,1)S(1)}, bf16[256,192]{1,0:T(8,128)(2,1)S(1)}, u32[]{:S(2)}, u32[]{:S(2)}) %collective-permute-start.21) | collective-permute-done | bytes 98336 | tf_op jit(solution)/shard_map/ppermute | solution.py:38
  124.7 2.8 %collective-permute-start.22 = (bf16[256,384]{1,0:T(8,128)(2,1)S(1)}, bf16[256,384]{1,0:T(8,128)(2,1)S(1)}, u32[]{:S(2)}, u32[]{:S(2)}) collective-permute-start(bf16[256,384]{1,0:T(8,128)(2,1)S(1)} %maximum_maximum_fusion), channel_id=1, source_target_pairs={{0,2},{2,0},{1,3},{3,1},{4,6},{6,4},{5,7},{7,5},{8,10},{10,8},{9,1... | collective-permute-start | bytes 589832 | tf_op jit(solution)/shard_map/ppermute | solution.py:34
  131.0 4.8 %collective-permute-done.33.refs_4_ = bf16[128,768]{1,0:T(8,128)(2,1)S(1)} collective-permute-done((bf16[128,768]{1,0:T(8,128)(2,1)S(1)}, bf16[128,768]{1,0:T(8,128)(2,1)S(1)}, u32[]{:S(2)}, u32[]{:S(2)}) %collective-permute-start.33) | collective-permute-done | bytes 196640 | tf_op jit(solution)/shard_map/ppermute | solution.py:22
  140.5 12.1 %collective-permute-done.35 = bf16[256,1024]{1,0:T(8,128)(2,1)S(1)} collective-permute-done((bf16[256,1024]{1,0:T(8,128)(2,1)S(1)}, bf16[256,1024]{1,0:T(8,128)(2,1)S(1)}, u32[]{:S(2)}, u32[]{:S(2)}) %collective-permute-start.35) | collective-permute-done | bytes 524320 | tf_op jit(solution)/shard_map/ppermute | solution.py:42
  160.6 4.5 %mix.1 = bf16[1024,2048]{1,0:T(8,128)(2,1)} custom-call(s32[3]{0:T(128)S(1)} %pad_add_fusion.where, f32[128,1024]{1,0:T(8,128)S(1)} %get-tuple-element.24.mine, f32[128,1024]{1,0:T(8,128)S(1)} %collective-permute-done.36.theirs, f32[8,1024]{1,0:T(8,128)S(1)} %copy-done.17, f32[128,128]{1,0:T(8,128)S(1)} %copy-done.19), custom_call_target="tpu_custom_call" | custom-call | flops 536870912 | bytes 6291456 | tf_op jit(solution)/shard_map/mix/pallas_call | solution.py:222
  (193 shorter events, 59.5 us)
Async XLA Ops:
  8.9 23.9 %collective-permute-start.23 = (bf16[64,768]{1,0:T(8,128)(2,1)S(1)}, bf16[64,768]{1,0:T(8,128)(2,1)S(1)}, u32[]{:S(2)}, u32[]{:S(2)}) collective-permute-start(bf16[64,768]{1,0:T(8,128)(2,1)S(1)} %bitcast.74), channel_id=1, source_target_pairs={{0,64},{64,128},{128,192},{192,0},{1,65},{65,129},{129,193},{193,1... | collective-permute-start | bytes 294920 | tf_op jit(solution)/shard_map/ppermute | solution.py:22
  9.0 24.3 %collective-permute-start.25 = (bf16[64,768]{1,0:T(8,128)(2,1)S(1)}, bf16[64,768]{1,0:T(8,128)(2,1)S(1)}, u32[]{:S(2)}, u32[]{:S(2)}) collective-permute-start(bf16[64,768]{1,0:T(8,128)(2,1)S(1)} %bitcast.75), channel_id=1, source_target_pairs={{0,192},{64,0},{128,64},{192,128},{1,193},{65,1},{129,65},{193,129... | collective-permute-start | bytes 294920 | tf_op jit(solution)/shard_map/ppermute | solution.py:22
  16.7 16.1 %all-to-all-start = ((bf16[4,40,384]{2,1,0:T(8,128)(2,1)}), bf16[4,40,384]{2,1,0:T(8,128)(2,1)S(1)}, u32[]{:S(2)}, u32[]{:S(2)}) async-start(bf16[4,40,384]{2,1,0:T(8,128)(2,1)} %pad_maximum_fusion.2), calls=%async_computation | async-start | bytes 245760 | tf_op jit(solution)/shard_map/all_to_all | solution.py:268
  30.0 36.7 %collective-permute-start.17 = (bf16[64,4096]{1,0:T(8,128)(2,1)}, bf16[64,4096]{1,0:T(8,128)(2,1)S(1)}, u32[]{:S(2)}, u32[]{:S(2)}) collective-permute-start(bf16[64,4096]{1,0:T(8,128)(2,1)} %get-tuple-element.26), channel_id=1, source_target_pairs={{0,32},{32,1},{1,33},{33,0},{2,34},{34,3},{3,35},{35,2},{4,36},{36... | collective-permute-start | bytes 1572872 | tf_op jit(solution)/shard_map/ppermute | solution.py:50
  31.4 38.0 %collective-permute-start.18 = (bf16[64,4096]{1,0:T(8,128)(2,1)S(1)}, bf16[64,4096]{1,0:T(8,128)(2,1)}, u32[]{:S(2)}, u32[]{:S(2)}) collective-permute-start(bf16[64,4096]{1,0:T(8,128)(2,1)S(1)} %get-tuple-element.25), channel_id=1, source_target_pairs={{0,33},{32,0},{1,32},{33,1},{2,35},{34,2},{3,34},{35,3},{4,37},{36... | collective-permute-start | bytes 1572872 | tf_op jit(solution)/shard_map/ppermute | solution.py:50
  32.9 12.1 %collective-permute-start = (bf16[136,384]{1,0:T(8,128)(2,1)S(1)}, bf16[136,384]{1,0:T(8,128)(2,1)S(1)}, u32[]{:S(2)}, u32[]{:S(2)}) collective-permute-start(bf16[136,384]{1,0:T(8,128)(2,1)S(1)} %pad_maximum_fusion.3), channel_id=1, source_target_pairs={{0,4},{4,8},{8,12},{12,16},{16,20},{20,24},{24,28},{28,0},{1,5},{5... | collective-permute-start | bytes 313352 | tf_op jit(solution)/shard_map/ppermute | solution.py:22
  33.3 11.8 %collective-permute-start.1 = (bf16[136,384]{1,0:T(8,128)(2,1)S(1)}, bf16[136,384]{1,0:T(8,128)(2,1)S(1)}, u32[]{:S(2)}, u32[]{:S(2)}) collective-permute-start(bf16[136,384]{1,0:T(8,128)(2,1)S(1)} %pad_maximum_fusion.3), channel_id=1, source_target_pairs={{0,28},{4,0},{8,4},{12,8},{16,12},{20,16},{24,20},{28,24},{1,29},{... | collective-permute-start | bytes 313352 | tf_op jit(solution)/shard_map/ppermute | solution.py:22
  41.3 28.2 %collective-permute-start.27 = (bf16[256,768]{1,0:T(8,128)(2,1)S(1)}, bf16[256,768]{1,0:T(8,128)(2,1)S(1)}, u32[]{:S(2)}, u32[]{:S(2)}) collective-permute-start(bf16[256,768]{1,0:T(8,128)(2,1)S(1)} %pad_maximum_fusion.1.refs_0_), channel_id=1, source_target_pairs={{0,28},{4,0},{8,4},{12,8},{16,12},{20,16},{24,20},{28,24},{1,29},{... | collective-permute-start | bytes 1179656 | tf_op jit(solution)/shard_map/ppermute | solution.py:22
  53.4 8.4 %collective-permute-start.4 = (bf16[136,384]{1,0:T(8,128)(2,1)S(1)}, bf16[136,384]{1,0:T(8,128)(2,1)S(1)}, u32[]{:S(2)}, u32[]{:S(2)}) collective-permute-start(bf16[136,384]{1,0:T(8,128)(2,1)S(1)} %collective-permute-done.2), channel_id=1, source_target_pairs={{0,4},{4,8},{8,12},{12,16},{16,20},{20,24},{24,28},{28,0},{1,5},{5... | collective-permute-start | bytes 313352 | tf_op jit(solution)/shard_map/ppermute | solution.py:22
  66.1 8.4 %collective-permute-start.30 = (bf16[256,768]{1,0:T(8,128)(2,1)S(1)}, bf16[256,768]{1,0:T(8,128)(2,1)S(1)}, u32[]{:S(2)}, u32[]{:S(2)}) collective-permute-start(bf16[256,768]{1,0:T(8,128)(2,1)S(1)} %pad_maximum_fusion.1.refs_0_), channel_id=1, source_target_pairs={{0,4},{4,8},{8,12},{12,16},{16,20},{20,24},{24,28},{28,0},{1,5},{5... | collective-permute-start | bytes 1179656 | tf_op jit(solution)/shard_map/ppermute | solution.py:22
  66.1 18.3 %collective-permute-start.7 = (bf16[680,384]{1,0:T(8,128)(2,1)S(1)}, bf16[680,384]{1,0:T(8,128)(2,1)S(1)}, u32[]{:S(2)}, u32[]{:S(2)}) collective-permute-start(bf16[680,384]{1,0:T(8,128)(2,1)S(1)} %get-tuple-element.43.refs_0_), channel_id=1, source_target_pairs={{0,64},{64,128},{128,192},{192,0},{1,65},{65,129},{129,193},{193,1... | collective-permute-start | bytes 1566728 | tf_op jit(solution)/shard_map/ppermute | solution.py:22
  66.7 14.6 %collective-permute-start.11 = (bf16[408,384]{1,0:T(8,128)(2,1)S(1)}, bf16[408,384]{1,0:T(8,128)(2,1)S(1)}, u32[]{:S(2)}, u32[]{:S(2)}) collective-permute-start(bf16[408,384]{1,0:T(8,128)(2,1)S(1)} %get-tuple-element.51.refs_1_), channel_id=1, source_target_pairs={{0,192},{64,0},{128,64},{192,128},{1,193},{65,1},{129,65},{193,129... | collective-permute-start | bytes 940040 | tf_op jit(solution)/shard_map/ppermute | solution.py:22
  69.4 13.8 %collective-permute-start.9 = (bf16[408,384]{1,0:T(8,128)(2,1)S(1)}, bf16[408,384]{1,0:T(8,128)(2,1)S(1)}, u32[]{:S(2)}, u32[]{:S(2)}) collective-permute-start(bf16[408,384]{1,0:T(8,128)(2,1)S(1)} %get-tuple-element.51.refs_1_), channel_id=1, source_target_pairs={{0,64},{64,128},{128,192},{192,0},{1,65},{65,129},{129,193},{193,1... | collective-permute-start | bytes 940040 | tf_op jit(solution)/shard_map/ppermute | solution.py:22
  69.4 17.6 %collective-permute-start.10 = (bf16[680,384]{1,0:T(8,128)(2,1)S(1)}, bf16[680,384]{1,0:T(8,128)(2,1)S(1)}, u32[]{:S(2)}, u32[]{:S(2)}) collective-permute-start(bf16[680,384]{1,0:T(8,128)(2,1)S(1)} %get-tuple-element.43.refs_0_), channel_id=1, source_target_pairs={{0,192},{64,0},{128,64},{192,128},{1,193},{65,1},{129,65},{193,129... | collective-permute-start | bytes 1566728 | tf_op jit(solution)/shard_map/ppermute | solution.py:22
  74.4 31.5 %collective-permute-start.16 = (bf16[128,4096]{1,0:T(8,128)(2,1)S(1)}, bf16[128,4096]{1,0:T(8,128)(2,1)}, u32[]{:S(2)}, u32[]{:S(2)}) collective-permute-start(bf16[128,4096]{1,0:T(8,128)(2,1)S(1)} %get-tuple-element.15.refs_10_), channel_id=1, source_target_pairs={{0,2},{2,0},{1,3},{3,1},{4,6},{6,4},{5,7},{7,5},{8,10},{10,8},{9,1... | collective-permute-start | bytes 3145736 | tf_op jit(solution)/shard_map/ppermute | solution.py:34
  81.3 13.2 %collective-permute-start.28 = (bf16[256,768]{1,0:T(8,128)(2,1)S(1)}, bf16[256,768]{1,0:T(8,128)(2,1)S(1)}, u32[]{:S(2)}, u32[]{:S(2)}) collective-permute-start(bf16[256,768]{1,0:T(8,128)(2,1)S(1)} %collective-permute-done.27.refs_1_), channel_id=1, source_target_pairs={{0,28},{4,0},{8,4},{12,8},{16,12},{20,16},{24,20},{28,24},{1,29},{... | collective-permute-start | bytes 1179656 | tf_op jit(solution)/shard_map/ppermute | solution.py:22
  83.2 14.6 %collective-permute-start.31 = (bf16[256,768]{1,0:T(8,128)(2,1)S(1)}, bf16[256,768]{1,0:T(8,128)(2,1)S(1)}, u32[]{:S(2)}, u32[]{:S(2)}) collective-permute-start(bf16[256,768]{1,0:T(8,128)(2,1)S(1)} %collective-permute-done.30.refs_7_), channel_id=1, source_target_pairs={{0,4},{4,8},{8,12},{12,16},{16,20},{20,24},{24,28},{28,0},{1,5},{5... | collective-permute-start | bytes 1179656 | tf_op jit(solution)/shard_map/ppermute | solution.py:22
  87.0 22.1 %collective-permute-start.19 = (bf16[64,4096]{1,0:T(8,128)(2,1)}, bf16[64,4096]{1,0:T(8,128)(2,1)}, u32[]{:S(2)}, u32[]{:S(2)}) collective-permute-start(bf16[64,4096]{1,0:T(8,128)(2,1)} %copy-done.20), channel_id=1, source_target_pairs={{0,2},{2,0},{1,3},{3,1},{4,6},{6,4},{5,7},{7,5},{8,10},{10,8},{9,1... | collective-permute-start | bytes 1572872 | tf_op jit(solution)/shard_map/ppermute | solution.py:34
  92.7 16.4 %collective-permute-start.20 = (bf16[64,4096]{1,0:T(8,128)(2,1)}, bf16[64,4096]{1,0:T(8,128)(2,1)}, u32[]{:S(2)}, u32[]{:S(2)}) collective-permute-start(bf16[64,4096]{1,0:T(8,128)(2,1)} %collective-permute-done.18.refs_13_), channel_id=1, source_target_pairs={{0,2},{2,0},{1,3},{3,1},{4,6},{6,4},{5,7},{7,5},{8,10},{10,8},{9,1... | collective-permute-start | bytes 1572872 | tf_op jit(solution)/shard_map/ppermute | solution.py:34
  98.6 10.6 %collective-permute-start.12 = (bf16[296,384]{1,0:T(8,128)(2,1)}, bf16[296,384]{1,0:T(8,128)(2,1)}, u32[]{:S(2)}, u32[]{:S(2)}) collective-permute-start(bf16[296,384]{1,0:T(8,128)(2,1)} %slice.246), channel_id=1, source_target_pairs={{0,192},{64,0},{128,64},{192,128},{1,193},{65,1},{129,65},{193,129... | collective-permute-start | bytes 681992 | tf_op jit(solution)/shard_map/ppermute | solution.py:22
  103.2 9.4 %collective-permute-start.14 = (bf16[384,384]{1,0:T(8,128)(2,1)}, bf16[384,384]{1,0:T(8,128)(2,1)}, u32[]{:S(2)}, u32[]{:S(2)}) collective-permute-start(bf16[384,384]{1,0:T(8,128)(2,1)} %slice.252), channel_id=1, source_target_pairs={{0,64},{64,128},{128,192},{192,0},{1,65},{65,129},{129,193},{193,1... | collective-permute-start | bytes 884744 | tf_op jit(solution)/shard_map/ppermute | solution.py:22
  106.0 22.3 %collective-permute-start.29 = (bf16[256,768]{1,0:T(8,128)(2,1)}, bf16[256,768]{1,0:T(8,128)(2,1)S(1)}, u32[]{:S(2)}, u32[]{:S(2)}) collective-permute-start(bf16[256,768]{1,0:T(8,128)(2,1)} %copy-done.10), channel_id=1, source_target_pairs={{0,28},{4,0},{8,4},{12,8},{16,12},{20,16},{24,20},{28,24},{1,29},{... | collective-permute-start | bytes 1179656 | tf_op jit(solution)/shard_map/ppermute | solution.py:22
  109.1 18.4 %collective-permute-start.32 = (bf16[256,768]{1,0:T(8,128)(2,1)}, bf16[256,768]{1,0:T(8,128)(2,1)S(1)}, u32[]{:S(2)}, u32[]{:S(2)}) collective-permute-start(bf16[256,768]{1,0:T(8,128)(2,1)} %copy-done.12), channel_id=1, source_target_pairs={{0,4},{4,8},{8,12},{12,16},{16,20},{20,24},{24,28},{28,0},{1,5},{5... | collective-permute-start | bytes 1179656 | tf_op jit(solution)/shard_map/ppermute | solution.py:22
  138.5 14.1 %collective-permute-start.35 = (bf16[256,1024]{1,0:T(8,128)(2,1)S(1)}, bf16[256,1024]{1,0:T(8,128)(2,1)S(1)}, u32[]{:S(2)}, u32[]{:S(2)}) collective-permute-start(bf16[256,1024]{1,0:T(8,128)(2,1)S(1)} %get-tuple-element.19), channel_id=1, source_target_pairs={{0,1},{1,0},{2,3},{3,2},{4,5},{5,4},{6,7},{7,6},{8,9},{9,8},{10,11... | collective-permute-start | bytes 1572872 | tf_op jit(solution)/shard_map/ppermute | solution.py:42
  (40 other events, 591.5 us)

commit v2 on v1

--- a/solution.py
+++ b/solution.py
@@ -11,7 +11,6 @@
 NY, NZ = 4, 8
 F32, BF16, I32 = jnp.float32, jnp.bfloat16, jnp.int32
 VMEM = pltpu.VMEM
-LIMIT = 50 << 20
 
 
 def whole(memory_space=VMEM):
@@ -50,7 +49,7 @@
     return lambda a: lax.ppermute(a, ("xl", "ha"), pairs)
 
 
-def route_body(ids, keep, rw, info, cnt):
+def prep_body(ids, keep, rw, gate, up, down_rows, info, packed):
     hit = (ids[...] == 0) & (keep[...] == 1)
     chosen = jnp.max(jnp.where(hit, 1.0, 0.0), axis=0, keepdims=True)
     route = jnp.sum(jnp.where(hit, rw[...], 0.0), axis=0, keepdims=True)
@@ -65,19 +64,25 @@
     info[2:3, :] = route
     info[3:8, :] = jnp.zeros((5, n), F32)
     total = jnp.sum(chosen, axis=1, keepdims=True)
-    cnt[...] = jnp.broadcast_to(total, cnt.shape)
-
-
-def routing(ids, keep, rw):
+    for q in range(4):
+        at = slice(q * 192, q * 192 + 192)
+        packed[q, 0:32, :] = jnp.concatenate([gate[:, at], up[:, at]], axis=1)
+        packed[q, 32:40, :] = jnp.broadcast_to(total, (8, 384)).astype(BF16)
+        packed[q, 40:72, :] = down_rows[:, :384]
+        packed[q, 72:104, :] = down_rows[:, 384:]
+
+
+def prep(ids, keep, rw, gate, up, down_rows):
     n = ids.shape[1]
     return pl.pallas_call(
-        route_body,
-        out_shape=(jax.ShapeDtypeStruct((8, n), F32), jax.ShapeDtypeStruct((8, 384), F32)),
-        in_specs=[whole()] * 3,
+        prep_body,
+        out_shape=(jax.ShapeDtypeStruct((8, n), F32), jax.ShapeDtypeStruct((4, 104, 384), BF16)),
+        in_specs=[whole()] * 6,
         out_specs=(whole(), whole()),
+        compiler_params=pltpu.CompilerParams(vmem_limit_bytes=12 << 20),
         cost_estimate=pl.CostEstimate(flops=2 * 16 * n * n, bytes_accessed=4 * 32 * n, transcendentals=0),
-        name="routing",
-    )(ids, keep, rw)
+        name="prep",
+    )(ids, keep, rw, gate, up, down_rows)
 
 
 def table(info):
@@ -159,37 +164,36 @@
         in_specs=[whole()] * (len(weights) + len(rows)),
         out_specs=(whole(), whole()),
         scratch_shapes=[VMEM((512, 4096), BF16)],
-        compiler_params=pltpu.CompilerParams(vmem_limit_bytes=LIMIT),
+        compiler_params=pltpu.CompilerParams(vmem_limit_bytes=20 << 20),
         cost_estimate=pl.CostEstimate(flops=2 * 512 * 4096 * 384, bytes_accessed=8 << 20, transcendentals=512 * 192),
         name="gate_up",
     )(*weights, *rows)
 
 
 def down_body(hidden, *refs):
-    pieces, keep, send = refs[:-2], refs[-2], refs[-1]
-
-    def dot(w):
-        return lax.dot_general(hidden[...], w, (((1,), (1,)), ((), ())), preferred_element_type=F32)
+    pieces, out = refs[:-1], refs[-1]
+
+    def dot(k, w):
+        return lax.dot_general(
+            hidden[:, k * 384 : k * 384 + 384], w, (((1,), (1,)), ((), ())), preferred_element_type=F32
+        )
 
     for r in range(NZ):
-        at = slice(r * 128, r * 128 + 128)
-        if r == 4:
-            keep[:, at] = dot(pieces[4][...])
-            send[:, at] = dot(pieces[8][...]).astype(BF16)
-        else:
-            both = dot(pieces[r][...])
-            keep[:, at] = both[:, :128]
-            send[:, at] = both[:, 128:].astype(BF16)
+        near, far = (pieces[4], pieces[8]) if r == 4 else (pieces[r], pieces[r])
+        base = 0 if r == 4 else 256
+        total = dot(0, near[0:128]) + dot(1, near[128:256])
+        total += dot(2, far[base : base + 128]) + dot(3, far[base + 128 : base + 256])
+        out[:, r * 128 : r * 128 + 128] = total
 
 
 def down(hidden, pieces):
     return pl.pallas_call(
         down_body,
-        out_shape=(jax.ShapeDtypeStruct((256, 1024), F32), jax.ShapeDtypeStruct((256, 1024), BF16)),
+        out_shape=jax.ShapeDtypeStruct((256, 1024), F32),
         in_specs=[whole()] * (1 + len(pieces)),
-        out_specs=(whole(), whole()),
-        compiler_params=pltpu.CompilerParams(vmem_limit_bytes=LIMIT),
-        cost_estimate=pl.CostEstimate(flops=2 * 256 * 768 * 2048, bytes_accessed=5 << 20, transcendentals=0),
+        out_specs=whole(),
+        compiler_params=pltpu.CompilerParams(vmem_limit_bytes=12 << 20),
+        cost_estimate=pl.CostEstimate(flops=2 * 256 * 1536 * 1024, bytes_accessed=5 << 20, transcendentals=0),
         name="down",
     )(hidden, *pieces)
 
@@ -240,43 +244,44 @@
     )(where, mine, theirs, info, slot_route)
 
 
-def z_ring(u, cut):
-    back, ahead, out = u, u, [u]
-    for _ in range(3):
-        back, ahead = Z(1)(back), Z(-1)(ahead)
-        out += [back, ahead]
-    return out, (Z(1)(back[:cut]), Z(-1)(ahead[cut:]))
-
-
-def y_ring(u, cut):
-    back, ahead = Y(1)(u), Y(-1)(u)
-    return back, ahead, Y(1)(back[:cut]), Y(-1)(ahead[cut:])
-
-
 def with_counts(units):
     return jnp.concatenate([u[:128] for u in units] + [u[128:] for u in units], axis=0)
 
 
+def together(*arrays):
+    return lax.optimization_barrier(arrays)
+
+
+def flipped(a):
+    return jnp.concatenate([a[128:], a[:128]], axis=0)
+
+
+def HIDDEN_FAR(a):
+    pairs = [(k, 3 - k) for k in range(4)]
+    return lax.ppermute(a, ("xl", "ha"), pairs)
+
+
 def per_device(tokens, expert_ids, keep_mask, route_weight, gate_weight, up_weight, down_weight):
     y, xl, z, c, ha = (lax.axis_index(a) for a in ("y", "xl", "z", "c", "ha"))
-    info, cnt = routing(expert_ids.T, keep_mask.T, route_weight.T)
-
-    quarters = jnp.concatenate(
-        [gate_weight.reshape(32, 4, 192).swapaxes(0, 1), up_weight.reshape(32, 4, 192).swapaxes(0, 1)], axis=2
-    )
-    counted = jnp.broadcast_to(cnt.astype(BF16)[None], (4, 8, 384))
-    arrived = lax.all_to_all(
-        jnp.concatenate([quarters, counted], axis=1), ("xl", "c"), split_axis=0, concat_axis=0, tiled=True
-    )
+    info, packed = prep(expert_ids.T, keep_mask.T, route_weight.T, gate_weight, up_weight, down_weight)
+    arrived = lax.all_to_all(packed, ("xl", "c"), split_axis=0, concat_axis=0, tiled=True)
+    slot_rows, slot_route = gather_rows(jnp.stack([y, z]), tokens, info)
+
     lane = lax.broadcasted_iota(I32, (8, 384), 1)
     tile = jnp.zeros((8, 384), BF16)
     for j in range(4):
         tile = jnp.where(lane == j, arrived[j, 32:40], tile)
     unit = jnp.concatenate([arrived[:, :32].reshape(128, 384), tile], axis=0)
-
-    rows = lax.all_gather(down_weight, ("xl", "c"), axis=0, tiled=False)
-    rows = lax.dynamic_slice_in_dim(rows, 2 * c, 2, axis=0).reshape(64, 768)
-    d_back, d_ahead, d_far0, d_far1 = y_ring(rows, 32)
+    picked = lax.dynamic_slice_in_dim(arrived, 2 * c, 2, axis=0)[:, 40:]
+    rows = jnp.concatenate([picked[0, :32], picked[1, :32], picked[0, 32:], picked[1, 32:]], axis=0)
+
+    b1, a1 = Z(1)(unit), Z(-1)(unit)
+    d_back, d_ahead = Y(1)(rows), Y(-1)(rows)
+    b1, a1, d_back, d_ahead = together(b1, a1, d_back, d_ahead)
+    b2, a2 = Z(1)(b1), Z(-1)(a1)
+    d_far = Y(1)(d_back[:64]), Y(-1)(d_ahead[64:])
+    b2, a2, d_far0, d_far1 = together(b2, a2, *d_far)
+
     turned = [rows, d_ahead, jnp.concatenate([d_far0, d_far1], axis=0), d_back]
     shift = lax.rem(2 * ha - y + NY, NY)
     ordered = []
@@ -285,39 +290,55 @@
         for s in range(1, 4):
             pick = jnp.where(shift == s, turned[(j + s) % 4], pick)
         ordered.append(pick)
-    d_near, d_last = z_ring(jnp.concatenate(ordered, axis=0), 128)
-    pieces = [d_near[0], d_near[2], d_near[4], d_near[6], d_last[0], d_near[5], d_near[3], d_near[1], d_last[1]]
-
-    g_near, g_last = z_ring(unit, 64)
-    first = with_counts(g_near[:5])
-    second = with_counts(g_near[5:] + [jnp.concatenate(g_last, axis=0)])
-    f_back, f_ahead, f_far0, f_far1 = y_ring(first, 384)
-    s_back, s_ahead, s_far0, s_far1 = y_ring(second, 256)
-
-    slot_rows, slot_route = gather_rows(jnp.stack([y, z]), tokens, info)
+
+    def halves(p, q):
+        return jnp.concatenate([p[:64], q[:64], p[64:], q[64:]], axis=0)
+
+    d_swap = HA(halves(ordered[2], ordered[3]))
+    b3, a3 = Z(1)(b2), Z(-1)(a2)
+    first = with_counts([unit, b1, a1, b2, a2])
+    f_back, f_ahead = Y(1)(first), Y(-1)(first)
+    b3, a3, d_swap = together(b3, a3, d_swap)
+
+    d0 = jnp.concatenate([halves(ordered[0], ordered[1]), d_swap], axis=0)
+    e0, e1 = Z(1)(b3[:64]), Z(-1)(a3[64:])
+    db1, da1 = Z(1)(d0), Z(-1)(d0)
+    e0, e1, f_back, f_ahead = together(e0, e1, f_back, f_ahead)
+    second = with_counts([b3, a3, jnp.concatenate([e0, e1], axis=0)])
+    f_far0, f_far1 = Y(1)(f_back[:384]), Y(-1)(f_ahead[384:])
+    s_back, s_ahead = Y(1)(second), Y(-1)(second)
+    s_back, s_ahead, db1, da1 = together(s_back, s_ahead, db1, da1)
+    s_far0, s_far1 = Y(1)(s_back[:256]), Y(-1)(s_ahead[256:])
+    db2, da2 = Z(1)(db1), Z(-1)(da1)
+
     xa, xb = X(1)(slot_rows[64:]), X(-1)(slot_rows[:64])
     x_rows = [slot_rows, C(slot_rows), xa, xb, C(xa), C(xb)]
     weights = [first, second, f_back, s_back, f_ahead, s_ahead, f_far0, f_far1, s_far0, s_far1]
     h_own, h_other = gate_up(weights, x_rows)
-    h_near = XL(h_other)
-    swapped = C(
-        jnp.concatenate(
-            [jnp.concatenate([h_own[128:], h_own[:128]], 0), jnp.concatenate([h_near[128:], h_near[:128]], 0)], axis=1
-        )
-    )
-    h_core, h_far = swapped[:, :192], swapped[:, 192:]
+    db3, da3 = Z(1)(db2), Z(-1)(da2)
+    h_near, h_ha, h_far = XL(h_other), HA(h_own), HIDDEN_FAR(h_other)
+    de0, de1 = Z(1)(db3[:256]), Z(-1)(da3[256:])
+    mine = (h_own, h_near, h_ha, h_far)
+    core = C(jnp.concatenate([flipped(h) for h in mine], axis=1))
+    theirs = [core[:, k * 192 : k * 192 + 192] for k in range(4)]
     c0, x0 = c == 0, xl == 0
-    here = (jnp.where(c0, h_own, h_core), jnp.where(c0, h_core, h_own))
-    there = (jnp.where(c0, h_near, h_far), jnp.where(c0, h_far, h_near))
-    hidden = jnp.concatenate(
-        [jnp.where(x0, a, b) for a, b in zip(here, there)] + [jnp.where(x0, b, a) for a, b in zip(here, there)], axis=1
-    )
-    keep, send = down(hidden, pieces)
-    total = keep + HA(send).astype(F32)
-    theirs = C(total[128:])
+    hidden = []
+    for k in (0, 2):
+        here = (jnp.where(c0, mine[k], theirs[k]), jnp.where(c0, theirs[k], mine[k]))
+        there = (jnp.where(c0, mine[k + 1], theirs[k + 1]), jnp.where(c0, theirs[k + 1], mine[k + 1]))
+        hidden += [jnp.where(x0, p, q) for p, q in zip(here, there)]
+        hidden += [jnp.where(x0, q, p) for p, q in zip(here, there)]
+    pieces = [d0, da1, da2, da3, de0, db3, db2, db1, de1]
+    total = down(jnp.concatenate(hidden, axis=1), pieces)
+    other = C(total[128:])
 
     counts = []
-    for near, late in ((first[640:], second[384:]), (f_back[640:], s_back[384:]), (f_ahead[640:], s_ahead[384:]), (f_far1[256:], s_far1[128:])):
+    for near, late in (
+        (first[640:], second[384:]),
+        (f_back[640:], s_back[384:]),
+        (f_ahead[640:], s_ahead[384:]),
+        (f_far1[256:], s_far1[128:]),
+    ):
         counts += [near.reshape(5, 8, 384)[:, 0, :4], late.reshape(3, 8, 384)[:, 0, :4]]
     counts = jnp.concatenate(counts, axis=0).astype(I32)
     entry = lax.broadcasted_iota(I32, (32, 4), 0)
@@ -329,7 +350,7 @@
     me = y * 32 + xl * 16 + z * 2 + c
     earlier = jnp.sum(jnp.where(block < me, counts, 0))
     capacity = lax.axis_size(WA) * CAP // 2
-    return mix(jnp.stack([c, z, capacity - earlier]), total[:128], theirs, info, slot_route)
+    return mix(jnp.stack([c, z, capacity - earlier]), total[:128], other, info, slot_route)
 
 
 def solution(mesh):

time: 166 us -> 155 us (0.934)
  blocking collectives: 8.88 us -> 0 us
  local copies, waits for them, and re-layouts: 21.2 us -> 27.9 us
  waiting for transfers between devices: 41.5 us -> 37.8 us
  starting transfers between devices: 66.4 us -> 62.9 us
  other arithmetic: 8.93 us -> 7.14 us
    ppermute x1 -> x2, waiting for transfers between devices: 12.1 us -> 2.68 us  [HA(): return lax.ppermute(a, 'ha', [(0, 1), (1, 0)])]
    all_gather x1 -> x0, blocking collectives: 8.88 us -> none  [per_device(): rows = lax.all_gather(down_weight, ('xl', 'c'), axis=0, tiled=False)]
    ppermute x2, waiting for transfers between devices: 0.01 us -> 7.85 us  [X(): return lambda a: lax.ppermute(a, ('xl', 'ha'), pairs)]
    ppermute x28, starting transfers between devices: 40.5 us -> 34.8 us  [ring(): return lambda a: lax.ppermute(a, axis, [(i, (i + k) % n) for i in range(n)])]
    ppermute x5, starting transfers between devices: 18.3 us -> 13 us  [C(): return lax.ppermute(a, 'c', [(0, 1), (1, 0)])]
    unnamed x70 -> x50, local copies, waits for them, and re-layouts: 12.6 us -> 17 us
    ppermute x1 -> x2, starting transfers between devices: 0.84 us -> 4.81 us  [HA(): return lax.ppermute(a, 'ha', [(0, 1), (1, 0)])]
    ppermute x1, waiting for transfers between devices: 3.79 us -> 0.01 us  [XL(): return lax.ppermute(a, 'xl', [(0, 1), (1, 0)])]
  transfers between devices with their start and end apart: 38 -> 40, of which waited for: 12 -> 11; matrix products, arithmetic and copies ran while one was open for 10% -> 15% of each run, Pallas kernels for 6% -> 5%
where the time goes in v2:
time: 155 us; the launch traced here: 154 us
  starting transfers between devices  62.9 us (41%)
  waiting for transfers between devices  37.8 us (24%)
  local copies, waits for them, and re-layouts  27.9 us (18%)
  Pallas kernels  16.9 us (11%)
  other arithmetic  7.14 us (5%)
    ppermute x28, starting transfers between devices, ring(): return lambda a: lax.ppermute(a, axis, [(i, (i + k) % n) for i in range(n)])  34.8 us
    ppermute x28, waiting for transfers between devices, ring(): return lambda a: lax.ppermute(a, axis, [(i, (i + k) % n) for i in range(n)])  26.1 us
    unnamed x50, local copies, waits for them, and re-layouts  17 us
    ppermute x5, starting transfers between devices, C(): return lax.ppermute(a, 'c', [(0, 1), (1, 0)])  13 us
    ppermute x2, waiting for transfers between devices, X(): return lambda a: lax.ppermute(a, ('xl', 'ha'), pairs)  7.85 us
    all_to_all x1, starting transfers between devices, per_device(): lax.all_to_all(packed, ('xl', 'c'), split_axis=0, concat_axis=0, tiled=True)  6.66 us
    ppermute x2, starting transfers between devices, HA(): return lax.ppermute(a, 'ha', [(0, 1), (1, 0)])  4.81 us
    pallas_call x1, Pallas kernels, gate_up(): pl.pallas_call(lambda *refs: gate_up_body(len(weights), *refs), out_shape...  4.62 us
  transfers between devices with their start and end apart: 40, of which 11 were waited for; matrix products, arithmetic and copies ran while one was open for 15% of the time, Pallas kernels for 5%

profile of v2, /device:TPU:1, one launch (start us, length us, event | category | flops | bytes accessed | tf_op | source)
XLA Modules:
  0.0 153.6 jit_solution(12459285591219047614)
XLA Ops:
  5.6 6.7 %all-to-all-start = ((bf16[4,104,384]{2,1,0:T(8,128)(2,1)}), bf16[4,104,384]{2,1,0:T(8,128)(2,1)S(1)}, u32[]{:S(2)}, u32[]{:S(2)}) async-start(bf16[4,104,384]{2,1,0:T(8,128)(2,1)} %get-tuple-element.30), calls=%async_computation | async-start | bytes 638976 | tf_op jit(solution)/shard_map/all_to_all | solution.py:267
  12.4 3.4 %copy-done = bf16[1024,4096]{1,0:T(8,128)(2,1)S(1)} copy-done((bf16[1024,4096]{1,0:T(8,128)(2,1)S(1)}, bf16[1024,4096]{1,0:T(8,128)(2,1)}, u32[]{:S(2)}) %copy-start) | copy-done | bytes 8388632
  15.8 3.6 %gather_rows.1 = (bf16[128,4096]{1,0:T(8,128)(2,1)S(1)}, f32[128,128]{1,0:T(8,128)S(1)}) custom-call(s32[2]{0:T(128)S(1)} %pad_add_fusion.1.where, bf16[1024,4096]{1,0:T(8,128)(2,1)S(1)} %copy-done, f32[8,1024]{1,0:T(8,128)S(1)} %get-tuple-element.48.info), custom_call_target="tpu_custom_call" | custom-call | flops 1073741824 | bytes 8388608 | tf_op jit(solution)/shard_map/gather_rows/pallas_call | solution.py:113
  25.2 3.9 %collective-permute-start.1 = (bf16[136,384]{1,0:T(8,128)(2,1)S(1)}, bf16[136,384]{1,0:T(8,128)(2,1)S(1)}, u32[]{:S(2)}, u32[]{:S(2)}) collective-permute-start(bf16[136,384]{1,0:T(8,128)(2,1)S(1)} %pad_maximum_fusion.1), channel_id=1, source_target_pairs={{0,28},{4,0},{8,4},{12,8},{16,12},{20,16},{24,20},{28,24},{1,29},{... | collective-permute-start | bytes 313352 | tf_op jit(solution)/shard_map/ppermute | solution.py:21
  32.1 2.3 %collective-permute-done.2 = bf16[128,384]{1,0:T(8,128)(2,1)S(1)} collective-permute-done((bf16[128,384]{1,0:T(8,128)(2,1)S(1)}, bf16[128,384]{1,0:T(8,128)(2,1)S(1)}, u32[]{:S(2)}, u32[]{:S(2)}) %collective-permute-start.2) | collective-permute-done | bytes 98336 | tf_op jit(solution)/shard_map/ppermute | solution.py:21
  34.5 2.7 %collective-permute-start.5 = (bf16[136,384]{1,0:T(8,128)(2,1)S(1)}, bf16[136,384]{1,0:T(8,128)(2,1)S(1)}, u32[]{:S(2)}, u32[]{:S(2)}) collective-permute-start(bf16[136,384]{1,0:T(8,128)(2,1)S(1)} %collective-permute-done.1), channel_id=1, source_target_pairs={{0,28},{4,0},{8,4},{12,8},{16,12},{20,16},{24,20},{28,24},{1,29},{... | collective-permute-start | bytes 313352 | tf_op jit(solution)/shard_map/ppermute | solution.py:21
  42.0 2.7 %collective-permute-start.9 = (bf16[136,384]{1,0:T(8,128)(2,1)S(1)}, bf16[136,384]{1,0:T(8,128)(2,1)S(1)}, u32[]{:S(2)}, u32[]{:S(2)}) collective-permute-start(bf16[136,384]{1,0:T(8,128)(2,1)S(1)} %collective-permute-done.5), channel_id=1, source_target_pairs={{0,28},{4,0},{8,4},{12,8},{16,12},{20,16},{24,20},{28,24},{1,29},{... | collective-permute-start | bytes 313352 | tf_op jit(solution)/shard_map/ppermute | solution.py:21
  44.9 2.7 %collective-permute-start.10 = (bf16[256,384]{1,0:T(8,128)(2,1)S(1)}, bf16[256,384]{1,0:T(8,128)(2,1)S(1)}, u32[]{:S(2)}, u32[]{:S(2)}) collective-permute-start(bf16[256,384]{1,0:T(8,128)(2,1)S(1)} %pad_maximum_fusion), channel_id=1, source_target_pairs={{0,1},{1,0},{2,3},{3,2},{4,5},{5,4},{6,7},{7,6},{8,9},{9,8},{10,11... | collective-permute-start | bytes 589832 | tf_op jit(solution)/shard_map/ppermute | solution.py:41
  53.0 2.7 %collective-permute-start.12 = (bf16[72,384]{1,0:T(8,128)(2,1)S(1)}, bf16[72,384]{1,0:T(8,128)(2,1)S(1)}, u32[]{:S(2)}, u32[]{:S(2)}) collective-permute-start(bf16[72,384]{1,0:T(8,128)(2,1)S(1)} %slice.245), channel_id=1, source_target_pairs={{0,28},{4,0},{8,4},{12,8},{16,12},{20,16},{24,20},{28,24},{1,29},{... | collective-permute-start | bytes 165896 | tf_op jit(solution)/shard_map/ppermute | solution.py:21
  57.6 5.7 %collective-permute-start.23 = (bf16[128,4096]{1,0:T(8,128)(2,1)S(1)}, bf16[128,4096]{1,0:T(8,128)(2,1)S(1)}, u32[]{:S(2)}, u32[]{:S(2)}) collective-permute-start(bf16[128,4096]{1,0:T(8,128)(2,1)S(1)} %get-tuple-element.49.refs_10_), channel_id=1, source_target_pairs={{0,2},{2,0},{1,3},{3,1},{4,6},{6,4},{5,7},{7,5},{8,10},{10,8},{9,1... | collective-permute-start | bytes 3145736 | tf_op jit(solution)/shard_map/ppermute | solution.py:33
  64.1 2.7 %collective-permute-start.18 = (bf16[512,384]{1,0:T(8,128)(2,1)}, bf16[512,384]{1,0:T(8,128)(2,1)}, u32[]{:S(2)}, u32[]{:S(2)}) collective-permute-start(bf16[512,384]{1,0:T(8,128)(2,1)} %constant_dynamic-update-slice_fusion.16.refs_0_), channel_id=1, source_target_pairs={{0,28},{4,0},{8,4},{12,8},{16,12},{20,16},{24,20},{28,24},{1,29},{... | collective-permute-start | bytes 1179656 | tf_op jit(solution)/shard_map/ppermute | solution.py:21
  69.2 7.9 %collective-permute-done.25.refs_13_ = bf16[64,4096]{1,0:T(8,128)(2,1)S(1)} collective-permute-done((bf16[64,4096]{1,0:T(8,128)(2,1)}, bf16[64,4096]{1,0:T(8,128)(2,1)S(1)}, u32[]{:S(2)}, u32[]{:S(2)}) %collective-permute-start.25) | collective-permute-done | bytes 524320 | tf_op jit(solution)/shard_map/ppermute | solution.py:49
  77.8 2.7 %collective-permute-start.16 = (bf16[408,384]{1,0:T(8,128)(2,1)}, bf16[408,384]{1,0:T(8,128)(2,1)}, u32[]{:S(2)}, u32[]{:S(2)}) collective-permute-start(bf16[408,384]{1,0:T(8,128)(2,1)} %get-tuple-element.100.refs_1_), channel_id=1, source_target_pairs={{0,192},{64,0},{128,64},{192,128},{1,193},{65,1},{129,65},{193,129... | collective-permute-start | bytes 940040 | tf_op jit(solution)/shard_map/ppermute | solution.py:21
  84.1 3.2 %collective-permute-done.15.refs_3_ = bf16[408,384]{1,0:T(8,128)(2,1)S(1)} collective-permute-done((bf16[408,384]{1,0:T(8,128)(2,1)}, bf16[408,384]{1,0:T(8,128)(2,1)S(1)}, u32[]{:S(2)}, u32[]{:S(2)}) %collective-permute-start.15) | collective-permute-done | bytes 313376 | tf_op jit(solution)/shard_map/ppermute | solution.py:21
  96.5 4.2 %collective-permute-done.22.refs_8_ = bf16[256,384]{1,0:T(8,128)(2,1)} collective-permute-done((bf16[256,384]{1,0:T(8,128)(2,1)}, bf16[256,384]{1,0:T(8,128)(2,1)}, u32[]{:S(2)}, u32[]{:S(2)}) %collective-permute-start.22) | collective-permute-done | bytes 196640 | tf_op jit(solution)/shard_map/ppermute | solution.py:21
  102.7 4.6 %gate_up.1 = (bf16[256,192]{1,0:T(8,128)(2,1)S(1)}, bf16[256,192]{1,0:T(8,128)(2,1)S(1)}) custom-call(bf16[680,384]{1,0:T(8,128)(2,1)S(1)} %copy-done.2, bf16[408,384]{1,0:T(8,128)(2,1)} %get-tuple-element.100.refs_1_, bf16[680,384]{1,0:T(8,128)(2,1)S(1)} %collective-permute-done.13.refs_2_, bf16[408,384]{1,0:T(8,128)(2,1)S(1)} %collective-permute-done.15.refs_3_, ...), custom_call_target="tpu_custom_call" | custom-call | flops 1610612736 | bytes 8388608 | tf_op jit(solution)/shard_map/gate_up/pallas_call | solution.py:161
  109.2 2.1 %collective-permute-start.29 = (bf16[256,192]{1,0:T(8,128)(2,1)S(1)}, bf16[256,192]{1,0:T(8,128)(2,1)S(1)}, u32[]{:S(2)}, u32[]{:S(2)}) collective-permute-start(bf16[256,192]{1,0:T(8,128)(2,1)S(1)} %get-tuple-element.50), channel_id=1, source_target_pairs={{0,1},{1,0},{2,3},{3,2},{4,5},{5,4},{6,7},{7,6},{8,9},{9,8},{10,11... | collective-permute-start | bytes 294920 | tf_op jit(solution)/shard_map/ppermute | solution.py:41
  112.5 2.7 %collective-permute-done.29 = bf16[256,192]{1,0:T(8,128)(2,1)S(1)} collective-permute-done((bf16[256,192]{1,0:T(8,128)(2,1)S(1)}, bf16[256,192]{1,0:T(8,128)(2,1)S(1)}, u32[]{:S(2)}, u32[]{:S(2)}) %collective-permute-start.29) | collective-permute-done | bytes 98336 | tf_op jit(solution)/shard_map/ppermute | solution.py:41
  115.4 3.6 %collective-permute-start.31 = (bf16[256,768]{1,0:T(8,128)(2,1)S(1)}, bf16[256,768]{1,0:T(8,128)(2,1)S(1)}, u32[]{:S(2)}, u32[]{:S(2)}) collective-permute-start(bf16[256,768]{1,0:T(8,128)(2,1)S(1)} %maximum_maximum_fusion), channel_id=1, source_target_pairs={{0,2},{2,0},{1,3},{3,1},{4,6},{6,4},{5,7},{7,5},{8,10},{10,8},{9,1... | collective-permute-start | bytes 1179656 | tf_op jit(solution)/shard_map/ppermute | solution.py:33
  122.4 9.7 %collective-permute-done.35.refs_5_ = bf16[512,384]{1,0:T(8,128)(2,1)S(1)} collective-permute-done((bf16[512,384]{1,0:T(8,128)(2,1)}, bf16[512,384]{1,0:T(8,128)(2,1)S(1)}, u32[]{:S(2)}, u32[]{:S(2)}) %collective-permute-start.35) | collective-permute-done | bytes 393248 | tf_op jit(solution)/shard_map/ppermute | solution.py:21
  133.5 2.7 %collective-permute-start.37 = (bf16[256,384]{1,0:T(8,128)(2,1)}, bf16[256,384]{1,0:T(8,128)(2,1)S(1)}, u32[]{:S(2)}, u32[]{:S(2)}) collective-permute-start(bf16[256,384]{1,0:T(8,128)(2,1)} %slice.327), channel_id=1, source_target_pairs={{0,28},{4,0},{8,4},{12,8},{16,12},{20,16},{24,20},{28,24},{1,29},{... | collective-permute-start | bytes 589832 | tf_op jit(solution)/shard_map/ppermute | solution.py:21
  136.9 3.0 %collective-permute-done.36.refs_4_ = bf16[256,384]{1,0:T(8,128)(2,1)S(1)} collective-permute-done((bf16[256,384]{1,0:T(8,128)(2,1)}, bf16[256,384]{1,0:T(8,128)(2,1)S(1)}, u32[]{:S(2)}, u32[]{:S(2)}) %collective-permute-start.36) | collective-permute-done | bytes 196640 | tf_op jit(solution)/shard_map/ppermute | solution.py:21
  139.8 3.3 %down.1 = f32[256,1024]{1,0:T(8,128)S(1)} custom-call(bf16[256,1536]{1,0:T(8,128)(2,1)S(1)} %concatenate.67.hidden, bf16[512,384]{1,0:T(8,128)(2,1)} %constant_dynamic-update-slice_fusion.16.refs_0_, bf16[512,384]{1,0:T(8,128)(2,1)} %collective-permute-done.18.refs_1_, bf16[512,384]{1,0:T(8,128)(2,1)} %collective-permute-done.32.refs_2_, ...), custom_call_target="tpu_custom_call" | custom-call | flops 805306368 | bytes 5242880 | tf_op jit(solution)/shard_map/down/pallas_call | solution.py:190
  149.2 4.5 %mix.1 = bf16[1024,2048]{1,0:T(8,128)(2,1)} custom-call(s32[3]{0:T(128)S(1)} %pad_add_fusion.where, f32[128,1024]{1,0:T(8,128)S(1)} %get-tuple-element.58.mine, f32[128,1024]{1,0:T(8,128)S(1)} %collective-permute-done.38.theirs, f32[8,1024]{1,0:T(8,128)S(1)} %get-tuple-element.48.info, f32[128,128]{1,0:T(8,128)S(1)} %copy-done.7), custom_call_target="tpu_custom_call" | custom-call | flops 536870912 | bytes 6291456 | tf_op jit(solution)/shard_map/mix/pallas_call | solution.py:226
  (177 shorter events, 59.5 us)
Async XLA Ops:
  5.6 19.4 %all-to-all-start = ((bf16[4,104,384]{2,1,0:T(8,128)(2,1)}), bf16[4,104,384]{2,1,0:T(8,128)(2,1)S(1)}, u32[]{:S(2)}, u32[]{:S(2)}) async-start(bf16[4,104,384]{2,1,0:T(8,128)(2,1)} %get-tuple-element.30), calls=%async_computation | async-start | bytes 638976 | tf_op jit(solution)/shard_map/all_to_all | solution.py:267
  20.8 36.8 %collective-permute-start.24 = (bf16[64,4096]{1,0:T(8,128)(2,1)S(1)}, bf16[64,4096]{1,0:T(8,128)(2,1)}, u32[]{:S(2)}, u32[]{:S(2)}) collective-permute-start(bf16[64,4096]{1,0:T(8,128)(2,1)S(1)} %get-tuple-element.60), channel_id=1, source_target_pairs={{0,32},{32,1},{1,33},{33,0},{2,34},{34,3},{3,35},{35,2},{4,36},{36... | collective-permute-start | bytes 1572872 | tf_op jit(solution)/shard_map/ppermute | solution.py:49
  25.1 9.3 %collective-permute-start = (bf16[136,384]{1,0:T(8,128)(2,1)S(1)}, bf16[136,384]{1,0:T(8,128)(2,1)S(1)}, u32[]{:S(2)}, u32[]{:S(2)}) collective-permute-start(bf16[136,384]{1,0:T(8,128)(2,1)S(1)} %pad_maximum_fusion.1), channel_id=1, source_target_pairs={{0,4},{4,8},{8,12},{12,16},{16,20},{20,24},{24,28},{28,0},{1,5},{5... | collective-permute-start | bytes 313352 | tf_op jit(solution)/shard_map/ppermute | solution.py:21
  25.2 9.2 %collective-permute-start.1 = (bf16[136,384]{1,0:T(8,128)(2,1)S(1)}, bf16[136,384]{1,0:T(8,128)(2,1)S(1)}, u32[]{:S(2)}, u32[]{:S(2)}) collective-permute-start(bf16[136,384]{1,0:T(8,128)(2,1)S(1)} %pad_maximum_fusion.1), channel_id=1, source_target_pairs={{0,28},{4,0},{8,4},{12,8},{16,12},{20,16},{24,20},{28,24},{1,29},{... | collective-permute-start | bytes 313352 | tf_op jit(solution)/shard_map/ppermute | solution.py:21
  41.9 9.3 %collective-permute-start.8 = (bf16[136,384]{1,0:T(8,128)(2,1)S(1)}, bf16[136,384]{1,0:T(8,128)(2,1)S(1)}, u32[]{:S(2)}, u32[]{:S(2)}) collective-permute-start(bf16[136,384]{1,0:T(8,128)(2,1)S(1)} %collective-permute-done.4), channel_id=1, source_target_pairs={{0,4},{4,8},{8,12},{12,16},{16,20},{20,24},{24,28},{28,0},{1,5},{5... | collective-permute-start | bytes 313352 | tf_op jit(solution)/shard_map/ppermute | solution.py:21
  42.0 10.8 %collective-permute-start.9 = (bf16[136,384]{1,0:T(8,128)(2,1)S(1)}, bf16[136,384]{1,0:T(8,128)(2,1)S(1)}, u32[]{:S(2)}, u32[]{:S(2)}) collective-permute-start(bf16[136,384]{1,0:T(8,128)(2,1)S(1)} %collective-permute-done.5), channel_id=1, source_target_pairs={{0,28},{4,0},{8,4},{12,8},{16,12},{20,16},{24,20},{28,24},{1,29},{... | collective-permute-start | bytes 313352 | tf_op jit(solution)/shard_map/ppermute | solution.py:21
  44.9 8.0 %collective-permute-start.10 = (bf16[256,384]{1,0:T(8,128)(2,1)S(1)}, bf16[256,384]{1,0:T(8,128)(2,1)S(1)}, u32[]{:S(2)}, u32[]{:S(2)}) collective-permute-start(bf16[256,384]{1,0:T(8,128)(2,1)S(1)} %pad_maximum_fusion), channel_id=1, source_target_pairs={{0,1},{1,0},{2,3},{3,2},{4,5},{5,4},{6,7},{7,6},{8,9},{9,8},{10,11... | collective-permute-start | bytes 589832 | tf_op jit(solution)/shard_map/ppermute | solution.py:41
  47.6 16.5 %collective-permute-start.13 = (bf16[680,384]{1,0:T(8,128)(2,1)S(1)}, bf16[680,384]{1,0:T(8,128)(2,1)S(1)}, u32[]{:S(2)}, u32[]{:S(2)}) collective-permute-start(bf16[680,384]{1,0:T(8,128)(2,1)S(1)} %get-tuple-element.88.refs_0_), channel_id=1, source_target_pairs={{0,64},{64,128},{128,192},{192,0},{1,65},{65,129},{129,193},{193,1... | collective-permute-start | bytes 1566728 | tf_op jit(solution)/shard_map/ppermute | solution.py:21
  51.2 12.9 %collective-permute-start.14 = (bf16[680,384]{1,0:T(8,128)(2,1)S(1)}, bf16[680,384]{1,0:T(8,128)(2,1)S(1)}, u32[]{:S(2)}, u32[]{:S(2)}) collective-permute-start(bf16[680,384]{1,0:T(8,128)(2,1)S(1)} %get-tuple-element.88.refs_0_), channel_id=1, source_target_pairs={{0,192},{64,0},{128,64},{192,128},{1,193},{65,1},{129,65},{193,129... | collective-permute-start | bytes 1566728 | tf_op jit(solution)/shard_map/ppermute | solution.py:21
  52.9 10.5 %collective-permute-start.11 = (bf16[64,384]{1,0:T(8,128)(2,1)S(1)}, bf16[64,384]{1,0:T(8,128)(2,1)S(1)}, u32[]{:S(2)}, u32[]{:S(2)}) collective-permute-start(bf16[64,384]{1,0:T(8,128)(2,1)S(1)} %slice.244), channel_id=1, source_target_pairs={{0,4},{4,8},{8,12},{12,16},{16,20},{20,24},{24,28},{28,0},{1,5},{5... | collective-permute-start | bytes 147464 | tf_op jit(solution)/shard_map/ppermute | solution.py:21
  53.0 10.7 %collective-permute-start.12 = (bf16[72,384]{1,0:T(8,128)(2,1)S(1)}, bf16[72,384]{1,0:T(8,128)(2,1)S(1)}, u32[]{:S(2)}, u32[]{:S(2)}) collective-permute-start(bf16[72,384]{1,0:T(8,128)(2,1)S(1)} %slice.245), channel_id=1, source_target_pairs={{0,28},{4,0},{8,4},{12,8},{16,12},{20,16},{24,20},{28,24},{1,29},{... | collective-permute-start | bytes 165896 | tf_op jit(solution)/shard_map/ppermute | solution.py:21
  57.6 33.7 %collective-permute-start.23 = (bf16[128,4096]{1,0:T(8,128)(2,1)S(1)}, bf16[128,4096]{1,0:T(8,128)(2,1)S(1)}, u32[]{:S(2)}, u32[]{:S(2)}) collective-permute-start(bf16[128,4096]{1,0:T(8,128)(2,1)S(1)} %get-tuple-element.49.refs_10_), channel_id=1, source_target_pairs={{0,2},{2,0},{1,3},{3,1},{4,6},{6,4},{5,7},{7,5},{8,10},{10,8},{9,1... | collective-permute-start | bytes 3145736 | tf_op jit(solution)/shard_map/ppermute | solution.py:33
  63.3 13.7 %collective-permute-start.25 = (bf16[64,4096]{1,0:T(8,128)(2,1)}, bf16[64,4096]{1,0:T(8,128)(2,1)S(1)}, u32[]{:S(2)}, u32[]{:S(2)}) collective-permute-start(bf16[64,4096]{1,0:T(8,128)(2,1)} %get-tuple-element.59), channel_id=1, source_target_pairs={{0,33},{32,0},{1,32},{33,1},{2,35},{34,2},{3,34},{35,3},{4,37},{36... | collective-permute-start | bytes 1572872 | tf_op jit(solution)/shard_map/ppermute | solution.py:49
  63.7 29.2 %collective-permute-start.26 = (bf16[64,4096]{1,0:T(8,128)(2,1)}, bf16[64,4096]{1,0:T(8,128)(2,1)}, u32[]{:S(2)}, u32[]{:S(2)}) collective-permute-start(bf16[64,4096]{1,0:T(8,128)(2,1)} %collective-permute-done.24.refs_12_), channel_id=1, source_target_pairs={{0,2},{2,0},{1,3},{3,1},{4,6},{6,4},{5,7},{7,5},{8,10},{10,8},{9,1... | collective-permute-start | bytes 1572872 | tf_op jit(solution)/shard_map/ppermute | solution.py:33
  64.1 13.8 %collective-permute-start.17 = (bf16[512,384]{1,0:T(8,128)(2,1)}, bf16[512,384]{1,0:T(8,128)(2,1)}, u32[]{:S(2)}, u32[]{:S(2)}) collective-permute-start(bf16[512,384]{1,0:T(8,128)(2,1)} %constant_dynamic-update-slice_fusion.16.refs_0_), channel_id=1, source_target_pairs={{0,4},{4,8},{8,12},{12,16},{16,20},{20,24},{24,28},{28,0},{1,5},{5... | collective-permute-start | bytes 1179656 | tf_op jit(solution)/shard_map/ppermute | solution.py:21
  64.1 18.6 %collective-permute-start.18 = (bf16[512,384]{1,0:T(8,128)(2,1)}, bf16[512,384]{1,0:T(8,128)(2,1)}, u32[]{:S(2)}, u32[]{:S(2)}) collective-permute-start(bf16[512,384]{1,0:T(8,128)(2,1)} %constant_dynamic-update-slice_fusion.16.refs_0_), channel_id=1, source_target_pairs={{0,28},{4,0},{8,4},{12,8},{16,12},{20,16},{24,20},{28,24},{1,29},{... | collective-permute-start | bytes 1179656 | tf_op jit(solution)/shard_map/ppermute | solution.py:21
  77.8 9.5 %collective-permute-start.15 = (bf16[408,384]{1,0:T(8,128)(2,1)}, bf16[408,384]{1,0:T(8,128)(2,1)S(1)}, u32[]{:S(2)}, u32[]{:S(2)}) collective-permute-start(bf16[408,384]{1,0:T(8,128)(2,1)} %get-tuple-element.100.refs_1_), channel_id=1, source_target_pairs={{0,64},{64,128},{128,192},{192,0},{1,65},{65,129},{129,193},{193,1... | collective-permute-start | bytes 940040 | tf_op jit(solution)/shard_map/ppermute | solution.py:21
  77.8 9.9 %collective-permute-start.16 = (bf16[408,384]{1,0:T(8,128)(2,1)}, bf16[408,384]{1,0:T(8,128)(2,1)}, u32[]{:S(2)}, u32[]{:S(2)}) collective-permute-start(bf16[408,384]{1,0:T(8,128)(2,1)} %get-tuple-element.100.refs_1_), channel_id=1, source_target_pairs={{0,192},{64,0},{128,64},{192,128},{1,193},{65,1},{129,65},{193,129... | collective-permute-start | bytes 940040 | tf_op jit(solution)/shard_map/ppermute | solution.py:21
  82.7 10.3 %collective-permute-start.27 = (bf16[64,4096]{1,0:T(8,128)(2,1)}, bf16[64,4096]{1,0:T(8,128)(2,1)}, u32[]{:S(2)}, u32[]{:S(2)}) collective-permute-start(bf16[64,4096]{1,0:T(8,128)(2,1)} %copy-done.3), channel_id=1, source_target_pairs={{0,2},{2,0},{1,3},{3,1},{4,6},{6,4},{5,7},{7,5},{8,10},{10,8},{9,1... | collective-permute-start | bytes 1572872 | tf_op jit(solution)/shard_map/ppermute | solution.py:33
  87.7 8.2 %collective-permute-start.21 = (bf16[384,384]{1,0:T(8,128)(2,1)}, bf16[384,384]{1,0:T(8,128)(2,1)}, u32[]{:S(2)}, u32[]{:S(2)}) collective-permute-start(bf16[384,384]{1,0:T(8,128)(2,1)} %slice.273), channel_id=1, source_target_pairs={{0,64},{64,128},{128,192},{192,0},{1,65},{65,129},{129,193},{193,1... | collective-permute-start | bytes 884744 | tf_op jit(solution)/shard_map/ppermute | solution.py:21
  93.0 26.9 %collective-permute-start.32 = (bf16[512,384]{1,0:T(8,128)(2,1)}, bf16[512,384]{1,0:T(8,128)(2,1)}, u32[]{:S(2)}, u32[]{:S(2)}) collective-permute-start(bf16[512,384]{1,0:T(8,128)(2,1)} %collective-permute-done.18.refs_1_), channel_id=1, source_target_pairs={{0,28},{4,0},{8,4},{12,8},{16,12},{20,16},{24,20},{28,24},{1,29},{... | collective-permute-start | bytes 1179656 | tf_op jit(solution)/shard_map/ppermute | solution.py:21
  93.1 26.9 %collective-permute-start.34 = (bf16[512,384]{1,0:T(8,128)(2,1)}, bf16[512,384]{1,0:T(8,128)(2,1)}, u32[]{:S(2)}, u32[]{:S(2)}) collective-permute-start(bf16[512,384]{1,0:T(8,128)(2,1)} %collective-permute-done.17.refs_7_), channel_id=1, source_target_pairs={{0,4},{4,8},{8,12},{12,16},{16,20},{20,24},{24,28},{28,0},{1,5},{5... | collective-permute-start | bytes 1179656 | tf_op jit(solution)/shard_map/ppermute | solution.py:21
  119.9 12.9 %collective-permute-start.33 = (bf16[512,384]{1,0:T(8,128)(2,1)}, bf16[512,384]{1,0:T(8,128)(2,1)S(1)}, u32[]{:S(2)}, u32[]{:S(2)}) collective-permute-start(bf16[512,384]{1,0:T(8,128)(2,1)} %collective-permute-done.32.refs_2_), channel_id=1, source_target_pairs={{0,28},{4,0},{8,4},{12,8},{16,12},{20,16},{24,20},{28,24},{1,29},{... | collective-permute-start | bytes 1179656 | tf_op jit(solution)/shard_map/ppermute | solution.py:21
  119.9 12.2 %collective-permute-start.35 = (bf16[512,384]{1,0:T(8,128)(2,1)}, bf16[512,384]{1,0:T(8,128)(2,1)S(1)}, u32[]{:S(2)}, u32[]{:S(2)}) collective-permute-start(bf16[512,384]{1,0:T(8,128)(2,1)} %collective-permute-done.34.refs_6_), channel_id=1, source_target_pairs={{0,4},{4,8},{8,12},{12,16},{16,20},{20,24},{24,28},{28,0},{1,5},{5... | collective-permute-start | bytes 1179656 | tf_op jit(solution)/shard_map/ppermute | solution.py:21
  (30 other events, 179.0 us)

commit v3 on v2

v3 whole, which is shorter than its diff:
```python
import jax
import jax.numpy as jnp
from jax import lax
from jax.experimental import pallas as pl
from jax.experimental.pallas import tpu as pltpu
from jax.sharding import Mesh
from jax.sharding import PartitionSpec as P

CAP = 128
WA = ("y", "xl", "z", "c")
NY, NZ = 4, 8
F32, BF16, I32 = jnp.float32, jnp.bfloat16, jnp.int32
VMEM = pltpu.VMEM


def whole(memory_space=VMEM):
    return pl.BlockSpec(memory_space=memory_space)


def ring(axis, n, k):
    return lambda a: lax.ppermute(a, axis, [(i, (i + k) % n) for i in range(n)])


def Z(k):
    return ring("z", NZ, k)


def Y(k):
    return ring("y", NY, k)


def C(a):
    return lax.ppermute(a, "c", [(0, 1), (1, 0)])


def XL(a):
    return lax.ppermute(a, "xl", [(0, 1), (1, 0)])


def HA(a):
    return lax.ppermute(a, "ha", [(0, 1), (1, 0)])


def across_x(a):
    def at(x, c):
        return (x % 2) * 4 + c * 2 + x // 2

    pairs = [(at(x, c), at((x + 1 - 2 * c) % 4, c)) for x in range(4) for c in range(2)]
    return lax.ppermute(a, ("xl", "c", "ha"), pairs)


def prep_body(*refs):
    far, (info, packed), near, arrive = refs[:6], refs[6:8], refs[8:14], refs[14]
    copies = [pltpu.make_async_copy(f, n, arrive.at[i]) for i, (f, n) in enumerate(zip(far, near))]
    for copy in copies:
        copy.start()
    for copy in copies:
        copy.wait()
    ids, keep, rw, gate, up, down_rows = near
    hit = (ids[...] == 0) & (keep[...] == 1)
    chosen = jnp.max(jnp.where(hit, 1.0, 0.0), axis=0, keepdims=True)
    route = jnp.sum(jnp.where(hit, rw[...], 0.0), axis=0, keepdims=True)
    n = chosen.shape[1]
    row = lax.broadcasted_iota(I32, (n, n), 0)
    col = lax.broadcasted_iota(I32, (n, n), 1)
    before = jnp.where(row < col, 1.0, 0.0).astype(BF16)
    ones = jnp.broadcast_to(chosen, (16, n)).astype(BF16)
    position = jnp.dot(ones, before, preferred_element_type=F32)[:1]
    info[0:1, :] = position
    info[1:2, :] = chosen
    info[2:3, :] = route
    info[3:8, :] = jnp.zeros((5, n), F32)
    total = jnp.sum(chosen, axis=1, keepdims=True)
    for q in range(4):
        at = slice(q * 192, q * 192 + 192)
        packed[q, 0:32, :] = jnp.concatenate([gate[:, at], up[:, at]], axis=1)
        packed[q, 32:40, :] = jnp.broadcast_to(total, (8, 384)).astype(BF16)
        packed[q, 40:72, :] = down_rows[:, :384]
        packed[q, 72:104, :] = down_rows[:, 384:]


def prep(ids, keep, rw, gate, up, down_rows):
    n = ids.shape[1]
    return pl.pallas_call(
        prep_body,
        out_shape=(jax.ShapeDtypeStruct((8, n), F32), jax.ShapeDtypeStruct((4, 104, 384), BF16)),
        in_specs=[whole(pltpu.HBM)] * 6,
        out_specs=(whole(), whole()),
        scratch_shapes=[VMEM(a.shape, a.dtype) for a in (ids, keep, rw, gate, up, down_rows)]
        + [pltpu.SemaphoreType.DMA((6,))],
        compiler_params=pltpu.CompilerParams(vmem_limit_bytes=12 << 20),
        cost_estimate=pl.CostEstimate(flops=2 * 16 * n * n, bytes_accessed=4 * 32 * n, transcendentals=0),
        name="prep",
    )(ids, keep, rw, gate, up, down_rows)


def table(info):
    slot = lax.broadcasted_iota(I32, (CAP, info.shape[1]), 0).astype(F32)
    return (info[0:1, :] == slot) & (info[1:2, :] > 0.5)


def gather_body(where, tokens, info, out, slot_route, near, arrive):
    n, width = near.shape[1:]
    copies = [
        pltpu.make_async_copy(tokens.at[:, i * width : (i + 1) * width], near.at[i], arrive.at[i]) for i in range(NY)
    ]
    for copy in copies:
        copy.start()
    picked = table(info)
    got = jnp.sum(jnp.where(picked, info[2:3, :], 0.0), axis=1, keepdims=True)
    slot_route[...] = jnp.broadcast_to(got, slot_route.shape)
    one_hot = picked.astype(BF16)
    for block in range(NY):
        copies[block].wait()
        rows = jnp.dot(one_hot, near[block], preferred_element_type=F32).astype(BF16)
        ky = lax.rem(block - where[0] + NY, NY)
        yi = jnp.where(ky == 0, 0, jnp.where(ky == 3, 1, jnp.where(ky == 1, 2, 3)))
        for z in range(NZ):
            kz = lax.rem(z - where[1] + NZ, NZ)
            zi = jnp.where(kz == 0, 0, jnp.where(kz <= 3, 2 * kz, jnp.where(kz == 4, 7, 15 - 2 * kz)))
            piece = jnp.concatenate([rows[:, z * 64 : z * 64 + 64], rows[:, 512 + z * 64 : 576 + z * 64]], axis=1)
            out[:, pl.ds(pl.multiple_of((yi * NZ + zi) * 128, 128), 128)] = piece


def gather_rows(where, tokens, info):
    n, d = tokens.shape
    return pl.pallas_call(
        gather_body,
        out_shape=(jax.ShapeDtypeStruct((CAP, d), BF16), jax.ShapeDtypeStruct((CAP, 128), F32)),
        in_specs=[whole(pltpu.SMEM), whole(pltpu.HBM), whole()],
        out_specs=(whole(), whole()),
        scratch_shapes=[VMEM((NY, n, d // NY), tokens.dtype), pltpu.SemaphoreType.DMA((NY,))],
        compiler_params=pltpu.CompilerParams(vmem_limit_bytes=16 << 20),
        cost_estimate=pl.CostEstimate(flops=2 * CAP * n * d, bytes_accessed=2 * n * d, transcendentals=0),
        name="gather_rows",
    )(where, tokens, info)


def near_body(first, second, f_back, s_back, f_ahead, s_ahead, xo, xc, xn, xnc, total, x_far, x_all):
    for i, ref in enumerate((xo, xc, xn, xnc)):
        x_all[i * 128 : i * 128 + 128, :] = ref[:, :3072]
        x_far[i * 128 : i * 128 + 128, :] = ref[:, 3072:]
    acc = jnp.zeros((512, 384), F32)
    for i, (f, s) in enumerate(((first, second), (f_back, s_back), (f_ahead, s_ahead))):
        acc += jnp.dot(x_all[:, i * 1024 : i * 1024 + 640], f[0:640, :], preferred_element_type=F32)
        acc += jnp.dot(x_all[:, i * 1024 + 640 : i * 1024 + 1024], s[0:384, :], preferred_element_type=F32)
    total[...] = acc


def gate_up_near(*arrays):
    return pl.pallas_call(
        near_body,
        out_shape=(jax.ShapeDtypeStruct((512, 384), F32), jax.ShapeDtypeStruct((512, 1024), BF16)),
        in_specs=[whole()] * len(arrays),
        out_specs=(whole(), whole()),
        scratch_shapes=[VMEM((512, 3072), BF16)],
        compiler_params=pltpu.CompilerParams(vmem_limit_bytes=16 << 20),
        cost_estimate=pl.CostEstimate(flops=2 * 512 * 3072 * 384, bytes_accessed=8 << 20, transcendentals=0),
        name="gate_up_near",
    )(*arrays)


def far_body(where, total, x_far, far0, far1, first, second, f_back, s_back, f_ahead, s_ahead, own, other, limit):
    acc = total[...]
    acc += jnp.dot(x_far[:, 0:384], far0[0:384, :], preferred_element_type=F32)
    acc += jnp.dot(x_far[:, 384:640], far1[0:256, :], preferred_element_type=F32)
    acc += jnp.dot(x_far[:, 640:768], far0[384:512, :], preferred_element_type=F32)
    acc += jnp.dot(x_far[:, 768:1024], far1[256:512, :], preferred_element_type=F32)
    gate, up = acc[:, :192], acc[:, 192:]
    hidden = (gate * jax.nn.sigmoid(gate) * up).astype(BF16)
    own[...] = hidden[:256]
    other[...] = hidden[256:]

    lane = lax.broadcasted_iota(I32, (8, 128), 1)
    quad = lax.shift_right_logical(lane, 1) * 16 + (lane & 1)
    earlier = jnp.zeros((8, 128), F32)
    groups = (
        (0, first[640:680, 0:128], second[384:408, 0:128]),
        (3, f_back[640:680, 0:128], s_back[384:408, 0:128]),
        (1, f_ahead[640:680, 0:128], s_ahead[384:408, 0:128]),
        (2, far1[512:552, 0:128], far1[552:576, 0:128]),
    )
    for ky, near, late in groups:
        tiles = jnp.concatenate([near.astype(F32), late.astype(F32)], axis=0)
        for zi, kz in enumerate((0, 7, 1, 6, 2, 5, 3, 4)):
            block = ((where[0] + ky) & 3) * 32 + ((where[1] + kz) & 7) * 2 + quad
            counted = (block < where[2]) & (lane < 4)
            earlier += jnp.where(counted, tiles[zi * 8 : zi * 8 + 8], 0.0)
    before = jnp.sum(earlier[0:1], axis=1, keepdims=True)
    limit[...] = jnp.broadcast_to(where[3].astype(F32) - before, limit.shape)


def gate_up_far(*arrays):
    half = jax.ShapeDtypeStruct((256, 192), BF16)
    return pl.pallas_call(
        far_body,
        out_shape=(half, half, jax.ShapeDtypeStruct((8, 128), F32)),
        in_specs=[whole(pltpu.SMEM)] + [whole()] * (len(arrays) - 1),
        out_specs=(whole(), whole(), whole()),
        compiler_params=pltpu.CompilerParams(vmem_limit_bytes=16 << 20),
        cost_estimate=pl.CostEstimate(flops=2 * 512 * 1024 * 384, bytes_accessed=4 << 20, transcendentals=512 * 192),
        name="gate_up_far",
    )(*arrays)


def down_body(hidden, *refs):
    pieces, out = refs[:-1], refs[-1]

    def dot(k, w):
        return lax.dot_general(
            hidden[:, k * 384 : k * 384 + 384], w, (((1,), (1,)), ((), ())), preferred_element_type=F32
        )

    for r in range(NZ):
        near, far = (pieces[4], pieces[8]) if r == 4 else (pieces[r], pieces[r])
        base = 0 if r == 4 else 256
        total = dot(0, near[0:128]) + dot(1, near[128:256])
        total += dot(2, far[base : base + 128]) + dot(3, far[base + 128 : base + 256])
        out[:, r * 128 : r * 128 + 128] = total


def down(hidden, pieces):
    return pl.pallas_call(
        down_body,
        out_shape=jax.ShapeDtypeStruct((256, 1024), F32),
        in_specs=[whole()] * (1 + len(pieces)),
        out_specs=whole(),
        compiler_params=pltpu.CompilerParams(vmem_limit_bytes=12 << 20),
        cost_estimate=pl.CostEstimate(flops=2 * 256 * 1536 * 1024, bytes_accessed=5 << 20, transcendentals=0),
        name="down",
    )(hidden, *pieces)


def mix_body(where, mine, theirs, info, slot_route, limit, out, slots):
    @pl.when(pl.program_id(0) == 0)
    def _():
        slot = lax.broadcasted_iota(I32, (CAP, 1), 0).astype(F32)
        scale = jnp.where(slot < limit[0:1, 0:1], slot_route[:, 0:1], 0.0)
        src = lax.broadcasted_iota(I32, (512, 512), 0)
        dst = lax.broadcasted_iota(I32, (512, 512), 1)
        moved = (src + where[1] * 64) & 511
        order = jnp.where(moved == dst, 1.0, 0.0).astype(BF16)
        for ref, column in ((mine, where[0]), (theirs, 1 - where[0])):
            scaled = (ref[...] * scale).astype(BF16)
            for y in range(2):
                part = jnp.concatenate(
                    [scaled[:, r * 128 + y * 64 : r * 128 + y * 64 + 64] for r in range(NZ)], axis=1
                )
                placed = jnp.dot(part, order, preferred_element_type=F32).astype(BF16)
                slots[:, pl.ds(pl.multiple_of(y * 1024 + column * 512, 512), 512)] = placed

    picked = table(info).astype(BF16)
    mixed = lax.dot_general(picked, slots[...], (((0,), (0,)), ((), ())), preferred_element_type=F32)
    out[...] = mixed.astype(BF16)


def mix(where, mine, theirs, info, slot_route, limit):
    n, step = info.shape[1], 256
    return pl.pallas_call(
        mix_body,
        out_shape=jax.ShapeDtypeStruct((n, 2048), BF16),
        grid_spec=pltpu.PrefetchScalarGridSpec(
            num_scalar_prefetch=1,
            grid=(n // step,),
            in_specs=[
                pl.BlockSpec((CAP, 1024), lambda i, w: (0, 0)),
                pl.BlockSpec((CAP, 1024), lambda i, w: (0, 0)),
                pl.BlockSpec((8, step), lambda i, w: (0, i)),
                pl.BlockSpec((CAP, 128), lambda i, w: (0, 0)),
                pl.BlockSpec((8, 128), lambda i, w: (0, 0)),
            ],
            out_specs=pl.BlockSpec((step, 2048), lambda i, w: (i, 0)),
            scratch_shapes=[VMEM((CAP, 2048), BF16)],
        ),
        compiler_params=pltpu.CompilerParams(vmem_limit_bytes=16 << 20),
        cost_estimate=pl.CostEstimate(flops=2 * n * CAP * 2048, bytes_accessed=6 << 20, transcendentals=0),
        name="mix",
    )(where, mine, theirs, info, slot_route, limit)


def with_counts(units):
    return jnp.concatenate([u[:128] for u in units] + [u[128:] for u in units], axis=0)


def together(*arrays):
    return lax.optimization_barrier(arrays)


def flipped(a):
    return jnp.concatenate([a[128:], a[:128]], axis=0)


def HIDDEN_FAR(a):
    pairs = [(k, 3 - k) for k in range(4)]
    return lax.ppermute(a, ("xl", "ha"), pairs)


def per_device(tokens, expert_ids, keep_mask, route_weight, gate_weight, up_weight, down_weight):
    y, xl, z, c, ha = (lax.axis_index(a) for a in ("y", "xl", "z", "c", "ha"))
    sources = (expert_ids.T, keep_mask.T, route_weight.T, gate_weight, up_weight, down_weight)
    info, packed = prep(*(pltpu.with_memory_space_constraint(a, pltpu.HBM) for a in sources))
    arrived = lax.all_to_all(packed, ("xl", "c"), split_axis=0, concat_axis=0, tiled=True)
    slot_rows, slot_route = gather_rows(
        jnp.stack([y, z]), pltpu.with_memory_space_constraint(tokens, pltpu.HBM), info
    )

    lane = lax.broadcasted_iota(I32, (8, 384), 1)
    tile = jnp.zeros((8, 384), BF16)
    for j in range(4):
        tile = jnp.where(lane == j, arrived[j, 32:40], tile)
    unit = jnp.concatenate([arrived[:, :32].reshape(128, 384), tile], axis=0)
    picked = lax.dynamic_slice_in_dim(arrived, 2 * c, 2, axis=0)[:, 40:]
    rows = jnp.concatenate([picked[0, :32], picked[1, :32], picked[0, 32:], picked[1, 32:]], axis=0)

    neighbour_rows = across_x(slot_rows)
    b1, a1 = Z(1)(unit), Z(-1)(unit)
    d_back, d_ahead = Y(1)(rows), Y(-1)(rows)
    b1, a1, d_back, d_ahead = together(b1, a1, d_back, d_ahead)
    b2, a2 = Z(1)(b1), Z(-1)(a1)
    d_far = Y(1)(d_back[:64]), Y(-1)(d_ahead[64:])
    b2, a2, d_far0, d_far1, neighbour_rows = together(b2, a2, *d_far, neighbour_rows)

    turned = [rows, d_ahead, jnp.concatenate([d_far0, d_far1], axis=0), d_back]
    shift = lax.rem(2 * ha - y + NY, NY)
    ordered = []
    for j in range(4):
        pick = turned[j]
        for s in range(1, 4):
            pick = jnp.where(shift == s, turned[(j + s) % 4], pick)
        ordered.append(pick)

    def halves(p, q):
        return jnp.concatenate([p[:64], q[:64], p[64:], q[64:]], axis=0)

    d_swap = HA(halves(ordered[2], ordered[3]))
    b3, a3 = Z(1)(b2), Z(-1)(a2)
    first = with_counts([unit, b1, a1, b2, a2])
    f_back, f_ahead = Y(1)(first), Y(-1)(first)
    b3, a3, d_swap = together(b3, a3, d_swap)

    d0 = jnp.concatenate([halves(ordered[0], ordered[1]), d_swap], axis=0)
    e = Z(1)(b3)
    db1, da1 = Z(1)(d0), Z(-1)(d0)
    e, f_back, f_ahead = together(e, f_back, f_ahead)
    second = with_counts([b3, a3, e])
    s_back, s_ahead = Y(1)(second), Y(-1)(second)
    x_rows = [slot_rows, C(slot_rows), neighbour_rows, C(neighbour_rows)]
    s_back, s_ahead, db1, da1 = together(s_back, s_ahead, db1, da1)
    far0 = Y(1)(jnp.concatenate([f_back[:384], s_back[:128]], axis=0))
    far1 = Y(-1)(jnp.concatenate([f_ahead[384:640], s_ahead[128:384], f_ahead[640:], s_ahead[384:]], axis=0))
    db2, da2 = Z(1)(db1), Z(-1)(da1)
    near = (first, second, f_back, s_back, f_ahead, s_ahead)
    partial, x_far = gate_up_near(*near, *x_rows)
    partial, x_far, far0, far1, db2, da2 = together(partial, x_far, far0, far1, db2, da2)

    db3, da3 = Z(1)(db2), Z(-1)(da2)
    me = y * 32 + xl * 16 + z * 2 + c
    capacity = lax.axis_size(WA) * CAP // 2
    h_own, h_other, limit = gate_up_far(jnp.stack([y, z, me, capacity]), partial, x_far, far0, far1, *near)
    h_near, h_ha, h_far = XL(h_other), HA(h_own), HIDDEN_FAR(h_other)
    de0, de1 = Z(1)(db3[:256]), Z(-1)(da3[256:])
    mine = (h_own, h_near, h_ha, h_far)
    core = C(jnp.concatenate([flipped(h) for h in mine], axis=1))
    theirs = [core[:, k * 192 : k * 192 + 192] for k in range(4)]
    c0, x0 = c == 0, xl == 0
    hidden = []
    for k in (0, 2):
        here = (jnp.where(c0, mine[k], theirs[k]), jnp.where(c0, theirs[k], mine[k]))
        there = (jnp.where(c0, mine[k + 1], theirs[k + 1]), jnp.where(c0, theirs[k + 1], mine[k + 1]))
        hidden += [jnp.where(x0, p, q) for p, q in zip(here, there)]
        hidden += [jnp.where(x0, q, p) for p, q in zip(here, there)]
    pieces = [d0, da1, da2, da3, de0, db3, db2, db1, de1]
    total = down(jnp.concatenate(hidden, axis=1), pieces)
    other = C(total[128:])

    return mix(jnp.stack([c, z]), total[:128], other, info, slot_route, limit)


def solution(mesh):
    finer = Mesh(mesh.devices.reshape(NY, 2, NZ, 2, mesh.shape["ha"]), ("y", "xl", "z", "c", "ha"))
    placed = (P(WA, None),) * 4 + (P(WA, "ha"),) * 3
    return jax.shard_map(per_device, mesh=finer, in_specs=placed, out_specs=P(WA, "ha"), check_vma=False)
```

time: 155 us -> 126 us (0.81)
  local copies, waits for them, and re-layouts: 27.9 us -> 6.11 us
  waiting for transfers between devices: 37.8 us -> 29.6 us
  Pallas kernels: 16.9 us -> 21.1 us
  other arithmetic: 7.14 us -> 3.27 us
  starting transfers between devices: 62.9 us -> 65.6 us
    unnamed x50 -> x26, local copies, waits for them, and re-layouts: 17 us -> 3.06 us
    ppermute x2 -> x1, waiting for transfers between devices: 7.85 us -> 0.01 us  [across_x(): return lax.ppermute(a, ('xl', 'c', 'ha'), pairs)]
    ppermute x5 -> x4, starting transfers between devices: 13 us -> 20.8 us  [C(): return lax.ppermute(a, 'c', [(0, 1), (1, 0)])]
    slice x15 -> x6, local copies, waits for them, and re-layouts: 4.67 us -> 0.09 us  [the longest x2 0.04 us: per_device(): far0 = Y(1)(jnp.concatenate([f_back[:384], s_back[:128]], axis=0))]
    ppermute x28 -> x25, starting transfers between devices: 34.8 us -> 30.7 us  [ring(): return lambda a: lax.ppermute(a, axis, [(i, (i + k) % n) for i in range(n)])]
    reshape x6 -> x0, local copies, waits for them, and re-layouts: 2.22 us -> none  [the longest x3 1.45 us: per_device(): late.reshape(3, 8, 384)[:, 0, :4]]
    pallas_call x1, Pallas kernels: 3.56 us -> 5.61 us  [gather_rows(): pl.pallas_call(gather_body, out_shape=(jax.ShapeDtypeStruct((CAP, d), BF1...]
    concatenate x0 -> x2, other arithmetic: none -> 1.61 us  [the longest x1 0.81 us: per_device(): jnp.concatenate([f_ahead[384:640], s_ahead[128:384], f_ahead[640:], s_ahe...]
  transfers between devices with their start and end apart: 40 -> 35, of which waited for: 11 -> 13; matrix products, arithmetic and copies ran while one was open for 15% -> 5% of each run, Pallas kernels for 5% -> 8%
where the time goes in v3:
time: 126 us
  starting transfers between devices  65.6 us (52%)
  waiting for transfers between devices  29.6 us (23%)
  Pallas kernels  21.1 us (17%)
  local copies, waits for them, and re-layouts  6.11 us (5%)
  other arithmetic  3.27 us (3%)
    ppermute x25, starting transfers between devices, ring(): return lambda a: lax.ppermute(a, axis, [(i, (i + k) % n) for i in range(n)])  30.7 us
    ppermute x25, waiting for transfers between devices, ring(): return lambda a: lax.ppermute(a, axis, [(i, (i + k) % n) for i in range(n)])  27 us
    ppermute x4, starting transfers between devices, C(): return lax.ppermute(a, 'c', [(0, 1), (1, 0)])  20.8 us
    all_to_all x1, starting transfers between devices, per_device(): lax.all_to_all(packed, ('xl', 'c'), split_axis=0, concat_axis=0, tiled=True)  6.67 us
    pallas_call x1, Pallas kernels, gather_rows(): pl.pallas_call(gather_body, out_shape=(jax.ShapeDtypeStruct((CAP, d), BF1...  5.61 us
    pallas_call x1, Pallas kernels, mix(): pl.pallas_call(mix_body, out_shape=jax.ShapeDtypeStruct((n, 2048), BF16),...  4.49 us
    ppermute x2, starting transfers between devices, HA(): return lax.ppermute(a, 'ha', [(0, 1), (1, 0)])  4.45 us
    pallas_call x1, Pallas kernels, gate_up_near(): pl.pallas_call(near_body, out_shape=(jax.ShapeDtypeStruct((512, 384), F32...  3.94 us
  transfers between devices with their start and end apart: 35, of which 13 were waited for; matrix products, arithmetic and copies ran while one was open for 5% of the time, Pallas kernels for 8%

profile of v3, /device:TPU:1, one launch (start us, length us, event | category | flops | bytes accessed | tf_op | source)
XLA Modules:
  0.0 126.1 jit_solution(4936377977530567562)
XLA Ops:
  1.9 6.7 %all-to-all-start = ((bf16[4,104,384]{2,1,0:T(8,128)(2,1)}), bf16[4,104,384]{2,1,0:T(8,128)(2,1)S(1)}, u32[]{:S(2)}, u32[]{:S(2)}) async-start(bf16[4,104,384]{2,1,0:T(8,128)(2,1)} %get-tuple-element.39), calls=%async_computation | async-start | bytes 638976 | tf_op jit(solution)/shard_map/all_to_all | solution.py:302
  8.7 5.6 %gather_rows.1 = (bf16[128,4096]{1,0:T(8,128)(2,1)}, f32[128,128]{1,0:T(8,128)S(1)}) custom-call(s32[2]{0:T(128)S(1)} %pad_add_fusion.2.where, bf16[1024,4096]{1,0:T(8,128)(2,1)} %tokens.1, f32[8,1024]{1,0:T(8,128)S(1)} %get-tuple-element.44.info), custom_call_target="tpu_custom_call" | custom-call | flops 1073741824 | bytes 8388608 | tf_op jit(solution)/shard_map/gather_rows/pallas_call | solution.py:127
  17.9 4.0 %collective-permute-start.1 = (bf16[136,384]{1,0:T(8,128)(2,1)S(1)}, bf16[136,384]{1,0:T(8,128)(2,1)S(1)}, u32[]{:S(2)}, u32[]{:S(2)}) collective-permute-start(bf16[136,384]{1,0:T(8,128)(2,1)S(1)} %pad_maximum_fusion.3), channel_id=1, source_target_pairs={{0,28},{4,0},{8,4},{12,8},{16,12},{20,16},{24,20},{28,24},{1,29},{... | collective-permute-start | bytes 313352 | tf_op jit(solution)/shard_map/ppermute | solution.py:21
  24.9 3.1 %collective-permute-done.2 = bf16[128,384]{1,0:T(8,128)(2,1)S(1)} collective-permute-done((bf16[128,384]{1,0:T(8,128)(2,1)S(1)}, bf16[128,384]{1,0:T(8,128)(2,1)S(1)}, u32[]{:S(2)}, u32[]{:S(2)}) %collective-permute-start.2) | collective-permute-done | bytes 98336 | tf_op jit(solution)/shard_map/ppermute | solution.py:21
  28.2 2.7 %collective-permute-start.5 = (bf16[136,384]{1,0:T(8,128)(2,1)S(1)}, bf16[136,384]{1,0:T(8,128)(2,1)S(1)}, u32[]{:S(2)}, u32[]{:S(2)}) collective-permute-start(bf16[136,384]{1,0:T(8,128)(2,1)S(1)} %collective-permute-done.1), channel_id=1, source_target_pairs={{0,28},{4,0},{8,4},{12,8},{16,12},{20,16},{24,20},{28,24},{1,29},{... | collective-permute-start | bytes 313352 | tf_op jit(solution)/shard_map/ppermute | solution.py:21
  35.1 2.0 %collective-permute-start.19 = (bf16[128,4096]{1,0:T(8,128)(2,1)}, bf16[128,4096]{1,0:T(8,128)(2,1)S(1)}, u32[]{:S(2)}, u32[]{:S(2)}) collective-permute-start(bf16[128,4096]{1,0:T(8,128)(2,1)} %get-tuple-element.45.xo), channel_id=1, source_target_pairs={{0,2},{2,0},{1,3},{3,1},{4,6},{6,4},{5,7},{7,5},{8,10},{10,8},{9,1... | collective-permute-start | bytes 3145736 | tf_op jit(solution)/shard_map/ppermute | solution.py:33
  37.5 2.7 %collective-permute-start.10 = (bf16[136,384]{1,0:T(8,128)(2,1)S(1)}, bf16[136,384]{1,0:T(8,128)(2,1)S(1)}, u32[]{:S(2)}, u32[]{:S(2)}) collective-permute-start(bf16[136,384]{1,0:T(8,128)(2,1)S(1)} %collective-permute-done.5), channel_id=1, source_target_pairs={{0,28},{4,0},{8,4},{12,8},{16,12},{20,16},{24,20},{28,24},{1,29},{... | collective-permute-start | bytes 313352 | tf_op jit(solution)/shard_map/ppermute | solution.py:21
  40.4 2.1 %collective-permute-start.11 = (bf16[256,384]{1,0:T(8,128)(2,1)S(1)}, bf16[256,384]{1,0:T(8,128)(2,1)S(1)}, u32[]{:S(2)}, u32[]{:S(2)}) collective-permute-start(bf16[256,384]{1,0:T(8,128)(2,1)S(1)} %pad_maximum_fusion.2), channel_id=1, source_target_pairs={{0,1},{1,0},{2,3},{3,2},{4,5},{5,4},{6,7},{7,6},{8,9},{9,8},{10,11... | collective-permute-start | bytes 589832 | tf_op jit(solution)/shard_map/ppermute | solution.py:41
  42.8 2.5 %collective-permute-start.14 = (bf16[680,384]{1,0:T(8,128)(2,1)S(1)}, bf16[680,384]{1,0:T(8,128)(2,1)S(1)}, u32[]{:S(2)}, u32[]{:S(2)}) collective-permute-start(bf16[680,384]{1,0:T(8,128)(2,1)S(1)} %constant_dynamic-update-slice_fusion.first), channel_id=1, source_target_pairs={{0,192},{64,0},{128,64},{192,128},{1,193},{65,1},{129,65},{193,129... | collective-permute-start | bytes 1566728 | tf_op jit(solution)/shard_map/ppermute | solution.py:21
  47.7 5.0 %collective-permute-done.12 = bf16[136,384]{1,0:T(8,128)(2,1)S(1)} collective-permute-done((bf16[136,384]{1,0:T(8,128)(2,1)S(1)}, bf16[136,384]{1,0:T(8,128)(2,1)S(1)}, u32[]{:S(2)}, u32[]{:S(2)}) %collective-permute-start.12) | collective-permute-done | bytes 104480 | tf_op jit(solution)/shard_map/ppermute | solution.py:21
  52.7 3.1 %collective-permute-done.13.f_back = bf16[680,384]{1,0:T(8,128)(2,1)S(1)} collective-permute-done((bf16[680,384]{1,0:T(8,128)(2,1)S(1)}, bf16[680,384]{1,0:T(8,128)(2,1)S(1)}, u32[]{:S(2)}, u32[]{:S(2)}) %collective-permute-start.13) | collective-permute-done | bytes 522272 | tf_op jit(solution)/shard_map/ppermute | solution.py:21
  56.3 5.6 %collective-permute-done.17.refs_7_ = bf16[512,384]{1,0:T(8,128)(2,1)} collective-permute-done((bf16[512,384]{1,0:T(8,128)(2,1)S(1)}, bf16[512,384]{1,0:T(8,128)(2,1)}, u32[]{:S(2)}, u32[]{:S(2)}) %collective-permute-start.17) | collective-permute-done | bytes 393248 | tf_op jit(solution)/shard_map/ppermute | solution.py:21
  62.0 2.4 %collective-permute-done.18.refs_1_ = bf16[512,384]{1,0:T(8,128)(2,1)} collective-permute-done((bf16[512,384]{1,0:T(8,128)(2,1)S(1)}, bf16[512,384]{1,0:T(8,128)(2,1)}, u32[]{:S(2)}, u32[]{:S(2)}) %collective-permute-start.18) | collective-permute-done | bytes 393248 | tf_op jit(solution)/shard_map/ppermute | solution.py:21
  64.4 3.3 %collective-permute-done.16.s_ahead = bf16[408,384]{1,0:T(8,128)(2,1)S(1)} collective-permute-done((bf16[408,384]{1,0:T(8,128)(2,1)S(1)}, bf16[408,384]{1,0:T(8,128)(2,1)S(1)}, u32[]{:S(2)}, u32[]{:S(2)}) %collective-permute-start.16) | collective-permute-done | bytes 313376 | tf_op jit(solution)/shard_map/ppermute | solution.py:21
  71.8 2.7 %collective-permute-start.24 = (bf16[512,384]{1,0:T(8,128)(2,1)}, bf16[512,384]{1,0:T(8,128)(2,1)}, u32[]{:S(2)}, u32[]{:S(2)}) collective-permute-start(bf16[512,384]{1,0:T(8,128)(2,1)} %collective-permute-done.18.refs_1_), channel_id=1, source_target_pairs={{0,28},{4,0},{8,4},{12,8},{16,12},{20,16},{24,20},{28,24},{1,29},{... | collective-permute-start | bytes 1179656 | tf_op jit(solution)/shard_map/ppermute | solution.py:21
  75.8 3.9 %gate_up_near.1 = (f32[512,384]{1,0:T(8,128)S(1)}, bf16[512,1024]{1,0:T(8,128)(2,1)S(1)}) custom-call(bf16[680,384]{1,0:T(8,128)(2,1)S(1)} %constant_dynamic-update-slice_fusion.first, bf16[408,384]{1,0:T(8,128)(2,1)S(1)} %constant_dynamic-update-slice_fusion.8.second, bf16[680,384]{1,0:T(8,128)(2,1)S(1)} %collective-permute-done.13.f_back, ...), custom_call_target="tpu_custom_call" | custom-call | flops 1207959552 | bytes 8388608 | tf_op jit(solution)/shard_map/gate_up_near/pallas_call | solution.py:151
  83.4 2.4 %collective-permute-start.26 = (bf16[256,192]{1,0:T(8,128)(2,1)S(1)}, bf16[256,192]{1,0:T(8,128)(2,1)S(1)}, u32[]{:S(2)}, u32[]{:S(2)}) collective-permute-start(bf16[256,192]{1,0:T(8,128)(2,1)S(1)} %get-tuple-element.67), channel_id=1, source_target_pairs={{0,1},{1,0},{2,3},{3,2},{4,5},{5,4},{6,7},{7,6},{8,9},{9,8},{10,11... | collective-permute-start | bytes 294920 | tf_op jit(solution)/shard_map/ppermute | solution.py:41
  85.8 3.2 %collective-permute-start.29 = (bf16[512,384]{1,0:T(8,128)(2,1)}, bf16[512,384]{1,0:T(8,128)(2,1)S(1)}, u32[]{:S(2)}, u32[]{:S(2)}) collective-permute-start(bf16[512,384]{1,0:T(8,128)(2,1)} %collective-permute-done.24.refs_2_), channel_id=1, source_target_pairs={{0,28},{4,0},{8,4},{12,8},{16,12},{20,16},{24,20},{28,24},{1,29},{... | collective-permute-start | bytes 1179656 | tf_op jit(solution)/shard_map/ppermute | solution.py:21
  89.8 8.2 %collective-permute-start.28 = (bf16[256,768]{1,0:T(8,128)(2,1)S(1)}, bf16[256,768]{1,0:T(8,128)(2,1)S(1)}, u32[]{:S(2)}, u32[]{:S(2)}) collective-permute-start(bf16[256,768]{1,0:T(8,128)(2,1)S(1)} %maximum_maximum_fusion), channel_id=1, source_target_pairs={{0,2},{2,0},{1,3},{3,1},{4,6},{6,4},{5,7},{7,5},{8,10},{10,8},{9,1... | collective-permute-start | bytes 1179656 | tf_op jit(solution)/shard_map/ppermute | solution.py:33
  99.4 3.4 %collective-permute-start.32 = (bf16[256,384]{1,0:T(8,128)(2,1)}, bf16[256,384]{1,0:T(8,128)(2,1)S(1)}, u32[]{:S(2)}, u32[]{:S(2)}) collective-permute-start(bf16[256,384]{1,0:T(8,128)(2,1)} %slice.249), channel_id=1, source_target_pairs={{0,28},{4,0},{8,4},{12,8},{16,12},{20,16},{24,20},{28,24},{1,29},{... | collective-permute-start | bytes 589832 | tf_op jit(solution)/shard_map/ppermute | solution.py:21
  105.2 2.7 %collective-permute-done.31.refs_4_ = bf16[256,384]{1,0:T(8,128)(2,1)S(1)} collective-permute-done((bf16[256,384]{1,0:T(8,128)(2,1)}, bf16[256,384]{1,0:T(8,128)(2,1)S(1)}, u32[]{:S(2)}, u32[]{:S(2)}) %collective-permute-start.31) | collective-permute-done | bytes 196640 | tf_op jit(solution)/shard_map/ppermute | solution.py:21
  107.9 3.2 %down.1 = f32[256,1024]{1,0:T(8,128)S(1)} custom-call(bf16[256,1536]{1,0:T(8,128)(2,1)S(1)} %concatenate.59.hidden, bf16[512,384]{1,0:T(8,128)(2,1)S(1)} %constant_dynamic-update-slice_fusion.11.refs_0_, bf16[512,384]{1,0:T(8,128)(2,1)} %collective-permute-done.18.refs_1_, bf16[512,384]{1,0:T(8,128)(2,1)} %collective-permute-done.24.refs_2_, ...), custom_call_target="tpu_custom_call" | custom-call | flops 805306368 | bytes 5242880 | tf_op jit(solution)/shard_map/down/pallas_call | solution.py:223
  111.2 8.8 %collective-permute-start.33 = (f32[128,1024]{1,0:T(8,128)S(1)}, f32[128,1024]{1,0:T(8,128)S(1)}, u32[]{:S(2)}, u32[]{:S(2)}) collective-permute-start(f32[128,1024]{1,0:T(8,128)S(1)} %get-tuple-element.73), channel_id=1, source_target_pairs={{0,2},{2,0},{1,3},{3,1},{4,6},{6,4},{5,7},{7,5},{8,10},{10,8},{9,1... | collective-permute-start | bytes 1572872 | tf_op jit(solution)/shard_map/ppermute | solution.py:33
  121.6 4.5 %mix.1 = bf16[1024,2048]{1,0:T(8,128)(2,1)} custom-call(s32[2]{0:T(128)S(1)} %pad_add_fusion.where, f32[128,1024]{1,0:T(8,128)S(1)} %get-tuple-element.74.mine, f32[128,1024]{1,0:T(8,128)S(1)} %collective-permute-done.33.theirs, f32[8,1024]{1,0:T(8,128)S(1)} %get-tuple-element.44.info, f32[128,128]{1,0:T(8,128)S(1)} %copy-done.3, ...), custom_call_target="tpu_custom_call" | custom-call | flops 536870912 | bytes 6291456 | tf_op jit(solution)/shard_map/mix/pallas_call | solution.py:259
  (119 shorter events, 31.8 us)
Async XLA Ops:
  1.9 14.2 %all-to-all-start = ((bf16[4,104,384]{2,1,0:T(8,128)(2,1)}), bf16[4,104,384]{2,1,0:T(8,128)(2,1)S(1)}, u32[]{:S(2)}, u32[]{:S(2)}) async-start(bf16[4,104,384]{2,1,0:T(8,128)(2,1)} %get-tuple-element.39), calls=%async_computation | async-start | bytes 638976 | tf_op jit(solution)/shard_map/all_to_all | solution.py:302
  14.9 22.2 %collective-permute-start.8 = (bf16[128,4096]{1,0:T(8,128)(2,1)}, bf16[128,4096]{1,0:T(8,128)(2,1)}, u32[]{:S(2)}, u32[]{:S(2)}) collective-permute-start(bf16[128,4096]{1,0:T(8,128)(2,1)} %get-tuple-element.45.xo), channel_id=1, source_target_pairs={{0,32},{2,35},{32,1},{34,2},{1,33},{3,34},{33,0},{35,3},{4,36},{6,... | collective-permute-start | bytes 3145736 | tf_op jit(solution)/shard_map/ppermute | solution.py:49
  16.2 12.0 %collective-permute-start = (bf16[136,384]{1,0:T(8,128)(2,1)S(1)}, bf16[136,384]{1,0:T(8,128)(2,1)S(1)}, u32[]{:S(2)}, u32[]{:S(2)}) collective-permute-start(bf16[136,384]{1,0:T(8,128)(2,1)S(1)} %pad_maximum_fusion.3), channel_id=1, source_target_pairs={{0,4},{4,8},{8,12},{12,16},{16,20},{20,24},{24,28},{28,0},{1,5},{5... | collective-permute-start | bytes 313352 | tf_op jit(solution)/shard_map/ppermute | solution.py:21
  17.9 10.3 %collective-permute-start.1 = (bf16[136,384]{1,0:T(8,128)(2,1)S(1)}, bf16[136,384]{1,0:T(8,128)(2,1)S(1)}, u32[]{:S(2)}, u32[]{:S(2)}) collective-permute-start(bf16[136,384]{1,0:T(8,128)(2,1)S(1)} %pad_maximum_fusion.3), channel_id=1, source_target_pairs={{0,28},{4,0},{8,4},{12,8},{16,12},{20,16},{24,20},{28,24},{1,29},{... | collective-permute-start | bytes 313352 | tf_op jit(solution)/shard_map/ppermute | solution.py:21
  28.2 8.9 %collective-permute-start.4 = (bf16[136,384]{1,0:T(8,128)(2,1)S(1)}, bf16[136,384]{1,0:T(8,128)(2,1)S(1)}, u32[]{:S(2)}, u32[]{:S(2)}) collective-permute-start(bf16[136,384]{1,0:T(8,128)(2,1)S(1)} %collective-permute-done), channel_id=1, source_target_pairs={{0,4},{4,8},{8,12},{12,16},{16,20},{20,24},{24,28},{28,0},{1,5},{5... | collective-permute-start | bytes 313352 | tf_op jit(solution)/shard_map/ppermute | solution.py:21
  28.2 8.9 %collective-permute-start.5 = (bf16[136,384]{1,0:T(8,128)(2,1)S(1)}, bf16[136,384]{1,0:T(8,128)(2,1)S(1)}, u32[]{:S(2)}, u32[]{:S(2)}) collective-permute-start(bf16[136,384]{1,0:T(8,128)(2,1)S(1)} %collective-permute-done.1), channel_id=1, source_target_pairs={{0,28},{4,0},{8,4},{12,8},{16,12},{20,16},{24,20},{28,24},{1,29},{... | collective-permute-start | bytes 313352 | tf_op jit(solution)/shard_map/ppermute | solution.py:21
  35.1 35.7 %collective-permute-start.19 = (bf16[128,4096]{1,0:T(8,128)(2,1)}, bf16[128,4096]{1,0:T(8,128)(2,1)S(1)}, u32[]{:S(2)}, u32[]{:S(2)}) collective-permute-start(bf16[128,4096]{1,0:T(8,128)(2,1)} %get-tuple-element.45.xo), channel_id=1, source_target_pairs={{0,2},{2,0},{1,3},{3,1},{4,6},{6,4},{5,7},{7,5},{8,10},{10,8},{9,1... | collective-permute-start | bytes 3145736 | tf_op jit(solution)/shard_map/ppermute | solution.py:33
  37.5 7.8 %collective-permute-start.10 = (bf16[136,384]{1,0:T(8,128)(2,1)S(1)}, bf16[136,384]{1,0:T(8,128)(2,1)S(1)}, u32[]{:S(2)}, u32[]{:S(2)}) collective-permute-start(bf16[136,384]{1,0:T(8,128)(2,1)S(1)} %collective-permute-done.5), channel_id=1, source_target_pairs={{0,28},{4,0},{8,4},{12,8},{16,12},{20,16},{24,20},{28,24},{1,29},{... | collective-permute-start | bytes 313352 | tf_op jit(solution)/shard_map/ppermute | solution.py:21
  42.4 13.4 %collective-permute-start.13 = (bf16[680,384]{1,0:T(8,128)(2,1)S(1)}, bf16[680,384]{1,0:T(8,128)(2,1)S(1)}, u32[]{:S(2)}, u32[]{:S(2)}) collective-permute-start(bf16[680,384]{1,0:T(8,128)(2,1)S(1)} %constant_dynamic-update-slice_fusion.first), channel_id=1, source_target_pairs={{0,64},{64,128},{128,192},{192,0},{1,65},{65,129},{129,193},{193,1... | collective-permute-start | bytes 1566728 | tf_op jit(solution)/shard_map/ppermute | solution.py:21
  42.8 13.3 %collective-permute-start.14 = (bf16[680,384]{1,0:T(8,128)(2,1)S(1)}, bf16[680,384]{1,0:T(8,128)(2,1)S(1)}, u32[]{:S(2)}, u32[]{:S(2)}) collective-permute-start(bf16[680,384]{1,0:T(8,128)(2,1)S(1)} %constant_dynamic-update-slice_fusion.first), channel_id=1, source_target_pairs={{0,192},{64,0},{128,64},{192,128},{1,193},{65,1},{129,65},{193,129... | collective-permute-start | bytes 1566728 | tf_op jit(solution)/shard_map/ppermute | solution.py:21
  45.2 29.3 %collective-permute-start.20 = (bf16[128,4096]{1,0:T(8,128)(2,1)}, bf16[128,4096]{1,0:T(8,128)(2,1)}, u32[]{:S(2)}, u32[]{:S(2)}) collective-permute-start(bf16[128,4096]{1,0:T(8,128)(2,1)} %collective-permute-done.8.xn), channel_id=1, source_target_pairs={{0,2},{2,0},{1,3},{3,1},{4,6},{6,4},{5,7},{7,5},{8,10},{10,8},{9,1... | collective-permute-start | bytes 3145736 | tf_op jit(solution)/shard_map/ppermute | solution.py:33
  52.7 9.2 %collective-permute-start.17 = (bf16[512,384]{1,0:T(8,128)(2,1)S(1)}, bf16[512,384]{1,0:T(8,128)(2,1)}, u32[]{:S(2)}, u32[]{:S(2)}) collective-permute-start(bf16[512,384]{1,0:T(8,128)(2,1)S(1)} %constant_dynamic-update-slice_fusion.11.refs_0_), channel_id=1, source_target_pairs={{0,4},{4,8},{8,12},{12,16},{16,20},{20,24},{24,28},{28,0},{1,5},{5... | collective-permute-start | bytes 1179656 | tf_op jit(solution)/shard_map/ppermute | solution.py:21
  55.8 8.6 %collective-permute-start.18 = (bf16[512,384]{1,0:T(8,128)(2,1)S(1)}, bf16[512,384]{1,0:T(8,128)(2,1)}, u32[]{:S(2)}, u32[]{:S(2)}) collective-permute-start(bf16[512,384]{1,0:T(8,128)(2,1)S(1)} %constant_dynamic-update-slice_fusion.11.refs_0_), channel_id=1, source_target_pairs={{0,28},{4,0},{8,4},{12,8},{16,12},{20,16},{24,20},{28,24},{1,29},{... | collective-permute-start | bytes 1179656 | tf_op jit(solution)/shard_map/ppermute | solution.py:21
  56.2 8.2 %collective-permute-start.15 = (bf16[408,384]{1,0:T(8,128)(2,1)S(1)}, bf16[408,384]{1,0:T(8,128)(2,1)S(1)}, u32[]{:S(2)}, u32[]{:S(2)}) collective-permute-start(bf16[408,384]{1,0:T(8,128)(2,1)S(1)} %constant_dynamic-update-slice_fusion.8.second), channel_id=1, source_target_pairs={{0,64},{64,128},{128,192},{192,0},{1,65},{65,129},{129,193},{193,1... | collective-permute-start | bytes 940040 | tf_op jit(solution)/shard_map/ppermute | solution.py:21
  68.5 11.2 %collective-permute-start.22 = (bf16[576,384]{1,0:T(8,128)(2,1)}, bf16[576,384]{1,0:T(8,128)(2,1)S(1)}, u32[]{:S(2)}, u32[]{:S(2)}) collective-permute-start(bf16[576,384]{1,0:T(8,128)(2,1)} %pad_maximum_fusion), channel_id=1, source_target_pairs={{0,192},{64,0},{128,64},{192,128},{1,193},{65,1},{129,65},{193,129... | collective-permute-start | bytes 1327112 | tf_op jit(solution)/shard_map/ppermute | solution.py:21
  70.6 9.2 %collective-permute-start.21 = (bf16[512,384]{1,0:T(8,128)(2,1)}, bf16[512,384]{1,0:T(8,128)(2,1)}, u32[]{:S(2)}, u32[]{:S(2)}) collective-permute-start(bf16[512,384]{1,0:T(8,128)(2,1)} %pad_maximum_fusion.1), channel_id=1, source_target_pairs={{0,64},{64,128},{128,192},{192,0},{1,65},{65,129},{129,193},{193,1... | collective-permute-start | bytes 1179656 | tf_op jit(solution)/shard_map/ppermute | solution.py:21
  70.8 8.9 %collective-permute-start.23 = (bf16[512,384]{1,0:T(8,128)(2,1)}, bf16[512,384]{1,0:T(8,128)(2,1)}, u32[]{:S(2)}, u32[]{:S(2)}) collective-permute-start(bf16[512,384]{1,0:T(8,128)(2,1)} %collective-permute-done.17.refs_7_), channel_id=1, source_target_pairs={{0,4},{4,8},{8,12},{12,16},{16,20},{20,24},{24,28},{28,0},{1,5},{5... | collective-permute-start | bytes 1179656 | tf_op jit(solution)/shard_map/ppermute | solution.py:21
  71.8 8.0 %collective-permute-start.24 = (bf16[512,384]{1,0:T(8,128)(2,1)}, bf16[512,384]{1,0:T(8,128)(2,1)}, u32[]{:S(2)}, u32[]{:S(2)}) collective-permute-start(bf16[512,384]{1,0:T(8,128)(2,1)} %collective-permute-done.18.refs_1_), channel_id=1, source_target_pairs={{0,28},{4,0},{8,4},{12,8},{16,12},{20,16},{24,20},{28,24},{1,29},{... | collective-permute-start | bytes 1179656 | tf_op jit(solution)/shard_map/ppermute | solution.py:21
  85.8 12.9 %collective-permute-start.29 = (bf16[512,384]{1,0:T(8,128)(2,1)}, bf16[512,384]{1,0:T(8,128)(2,1)S(1)}, u32[]{:S(2)}, u32[]{:S(2)}) collective-permute-start(bf16[512,384]{1,0:T(8,128)(2,1)} %collective-permute-done.24.refs_2_), channel_id=1, source_target_pairs={{0,28},{4,0},{8,4},{12,8},{16,12},{20,16},{24,20},{28,24},{1,29},{... | collective-permute-start | bytes 1179656 | tf_op jit(solution)/shard_map/ppermute | solution.py:21
  89.1 8.9 %collective-permute-start.30 = (bf16[512,384]{1,0:T(8,128)(2,1)}, bf16[512,384]{1,0:T(8,128)(2,1)S(1)}, u32[]{:S(2)}, u32[]{:S(2)}) collective-permute-start(bf16[512,384]{1,0:T(8,128)(2,1)} %collective-permute-done.23.refs_6_), channel_id=1, source_target_pairs={{0,4},{4,8},{8,12},{12,16},{16,20},{20,24},{24,28},{28,0},{1,5},{5... | collective-permute-start | bytes 1179656 | tf_op jit(solution)/shard_map/ppermute | solution.py:21
  89.8 13.0 %collective-permute-start.28 = (bf16[256,768]{1,0:T(8,128)(2,1)S(1)}, bf16[256,768]{1,0:T(8,128)(2,1)S(1)}, u32[]{:S(2)}, u32[]{:S(2)}) collective-permute-start(bf16[256,768]{1,0:T(8,128)(2,1)S(1)} %maximum_maximum_fusion), channel_id=1, source_target_pairs={{0,2},{2,0},{1,3},{3,1},{4,6},{6,4},{5,7},{7,5},{8,10},{10,8},{9,1... | collective-permute-start | bytes 1179656 | tf_op jit(solution)/shard_map/ppermute | solution.py:33
  98.7 9.1 %collective-permute-start.31 = (bf16[256,384]{1,0:T(8,128)(2,1)}, bf16[256,384]{1,0:T(8,128)(2,1)S(1)}, u32[]{:S(2)}, u32[]{:S(2)}) collective-permute-start(bf16[256,384]{1,0:T(8,128)(2,1)} %slice.248), channel_id=1, source_target_pairs={{0,4},{4,8},{8,12},{12,16},{16,20},{20,24},{24,28},{28,0},{1,5},{5... | collective-permute-start | bytes 589832 | tf_op jit(solution)/shard_map/ppermute | solution.py:21
  99.4 8.4 %collective-permute-start.32 = (bf16[256,384]{1,0:T(8,128)(2,1)}, bf16[256,384]{1,0:T(8,128)(2,1)S(1)}, u32[]{:S(2)}, u32[]{:S(2)}) collective-permute-start(bf16[256,384]{1,0:T(8,128)(2,1)} %slice.249), channel_id=1, source_target_pairs={{0,28},{4,0},{8,4},{12,8},{16,12},{20,16},{24,20},{28,24},{1,29},{... | collective-permute-start | bytes 589832 | tf_op jit(solution)/shard_map/ppermute | solution.py:21
  111.2 10.4 %collective-permute-start.33 = (f32[128,1024]{1,0:T(8,128)S(1)}, f32[128,1024]{1,0:T(8,128)S(1)}, u32[]{:S(2)}, u32[]{:S(2)}) collective-permute-start(f32[128,1024]{1,0:T(8,128)S(1)} %get-tuple-element.73), channel_id=1, source_target_pairs={{0,2},{2,0},{1,3},{3,1},{4,6},{6,4},{5,7},{7,5},{8,10},{10,8},{9,1... | collective-permute-start | bytes 1572872 | tf_op jit(solution)/shard_map/ppermute | solution.py:33
  (15 other events, 107.2 us)

commit v4 on v3

--- a/solution.py
+++ b/solution.py
@@ -203,32 +203,50 @@
     )(*arrays)
 
 
-def down_body(hidden, *refs):
-    pieces, out = refs[:-1], refs[-1]
+def down_body(where, own, near, ha, far, core, *refs):
+    pieces, (out, hidden) = refs[:-2], refs[-2:]
+
+    for xl in range(2):
+        for c in range(2):
+
+            @pl.when((where[0] == xl) & (where[1] == c))
+            def _():
+                for k, ref in enumerate((own, near, ha, far)):
+                    pair = xl if k % 2 == 0 else 1 - xl
+                    base = (k // 2) * 768 + pair * 384
+                    hidden[:, base + c * 192 : base + c * 192 + 192] = ref[...]
+                    got = core[:, k * 192 : k * 192 + 192]
+                    hidden[:, base + (1 - c) * 192 : base + (1 - c) * 192 + 192] = jnp.concatenate(
+                        [got[128:], got[:128]], axis=0
+                    )
 
     def dot(k, w):
         return lax.dot_general(
             hidden[:, k * 384 : k * 384 + 384], w, (((1,), (1,)), ((), ())), preferred_element_type=F32
         )
 
+    blocks = []
     for r in range(NZ):
-        near, far = (pieces[4], pieces[8]) if r == 4 else (pieces[r], pieces[r])
+        front, rear = (pieces[4], pieces[8]) if r == 4 else (pieces[r], pieces[r])
         base = 0 if r == 4 else 256
-        total = dot(0, near[0:128]) + dot(1, near[128:256])
-        total += dot(2, far[base : base + 128]) + dot(3, far[base + 128 : base + 256])
-        out[:, r * 128 : r * 128 + 128] = total
-
-
-def down(hidden, pieces):
+        total = dot(0, front[0:128]) + dot(1, front[128:256])
+        blocks.append(total + dot(2, rear[base : base + 128]) + dot(3, rear[base + 128 : base + 256]))
+    for y in range(2):
+        part = jnp.concatenate([b[:, y * 64 : y * 64 + 64] for b in blocks], axis=1)
+        out[:, y * 512 : y * 512 + 512] = pltpu.roll(part, where[2] * 64, 1)
+
+
+def down(where, hidden, pieces):
     return pl.pallas_call(
         down_body,
         out_shape=jax.ShapeDtypeStruct((256, 1024), F32),
-        in_specs=[whole()] * (1 + len(pieces)),
+        in_specs=[whole(pltpu.SMEM)] + [whole()] * (len(hidden) + len(pieces)),
         out_specs=whole(),
+        scratch_shapes=[VMEM((256, 1536), BF16)],
         compiler_params=pltpu.CompilerParams(vmem_limit_bytes=12 << 20),
         cost_estimate=pl.CostEstimate(flops=2 * 256 * 1536 * 1024, bytes_accessed=5 << 20, transcendentals=0),
         name="down",
-    )(hidden, *pieces)
+    )(where, *hidden, *pieces)
 
 
 def mix_body(where, mine, theirs, info, slot_route, limit, out, slots):
@@ -236,18 +254,11 @@
     def _():
         slot = lax.broadcasted_iota(I32, (CAP, 1), 0).astype(F32)
         scale = jnp.where(slot < limit[0:1, 0:1], slot_route[:, 0:1], 0.0)
-        src = lax.broadcasted_iota(I32, (512, 512), 0)
-        dst = lax.broadcasted_iota(I32, (512, 512), 1)
-        moved = (src + where[1] * 64) & 511
-        order = jnp.where(moved == dst, 1.0, 0.0).astype(BF16)
         for ref, column in ((mine, where[0]), (theirs, 1 - where[0])):
             scaled = (ref[...] * scale).astype(BF16)
             for y in range(2):
-                part = jnp.concatenate(
-                    [scaled[:, r * 128 + y * 64 : r * 128 + y * 64 + 64] for r in range(NZ)], axis=1
-                )
-                placed = jnp.dot(part, order, preferred_element_type=F32).astype(BF16)
-                slots[:, pl.ds(pl.multiple_of(y * 1024 + column * 512, 512), 512)] = placed
+                at = pl.multiple_of(y * 1024 + column * 512, 512)
+                slots[:, pl.ds(at, 512)] = scaled[:, y * 512 : y * 512 + 512]
 
     picked = table(info).astype(BF16)
     mixed = lax.dot_general(picked, slots[...], (((0,), (0,)), ((), ())), preferred_element_type=F32)
@@ -286,10 +297,6 @@
     return lax.optimization_barrier(arrays)
 
 
-def flipped(a):
-    return jnp.concatenate([a[128:], a[:128]], axis=0)
-
-
 def HIDDEN_FAR(a):
     pairs = [(k, 3 - k) for k in range(4)]
     return lax.ppermute(a, ("xl", "ha"), pairs)
@@ -315,10 +322,10 @@
     neighbour_rows = across_x(slot_rows)
     b1, a1 = Z(1)(unit), Z(-1)(unit)
     d_back, d_ahead = Y(1)(rows), Y(-1)(rows)
-    b1, a1, d_back, d_ahead = together(b1, a1, d_back, d_ahead)
     b2, a2 = Z(1)(b1), Z(-1)(a1)
     d_far = Y(1)(d_back[:64]), Y(-1)(d_ahead[64:])
-    b2, a2, d_far0, d_far1, neighbour_rows = together(b2, a2, *d_far, neighbour_rows)
+    d_far0, d_far1 = d_far
+    b2, a2, neighbour_rows = together(b2, a2, neighbour_rows)
 
     turned = [rows, d_ahead, jnp.concatenate([d_far0, d_far1], axis=0), d_back]
     shift = lax.rem(2 * ha - y + NY, NY)
@@ -341,39 +348,31 @@
     d0 = jnp.concatenate([halves(ordered[0], ordered[1]), d_swap], axis=0)
     e = Z(1)(b3)
     db1, da1 = Z(1)(d0), Z(-1)(d0)
-    e, f_back, f_ahead = together(e, f_back, f_ahead)
+    e, f_back, f_ahead, db1, da1 = together(e, f_back, f_ahead, db1, da1)
+
     second = with_counts([b3, a3, e])
     s_back, s_ahead = Y(1)(second), Y(-1)(second)
-    x_rows = [slot_rows, C(slot_rows), neighbour_rows, C(neighbour_rows)]
-    s_back, s_ahead, db1, da1 = together(s_back, s_ahead, db1, da1)
+    db2, da2 = Z(1)(db1), Z(-1)(da1)
+    core_rows, far_rows = C(slot_rows), C(neighbour_rows)
+    s_back, s_ahead, db2, da2, core_rows, far_rows = together(s_back, s_ahead, db2, da2, core_rows, far_rows)
+
     far0 = Y(1)(jnp.concatenate([f_back[:384], s_back[:128]], axis=0))
     far1 = Y(-1)(jnp.concatenate([f_ahead[384:640], s_ahead[128:384], f_ahead[640:], s_ahead[384:]], axis=0))
-    db2, da2 = Z(1)(db1), Z(-1)(da1)
+    db3, da3 = Z(1)(db2), Z(-1)(da2)
     near = (first, second, f_back, s_back, f_ahead, s_ahead)
-    partial, x_far = gate_up_near(*near, *x_rows)
-    partial, x_far, far0, far1, db2, da2 = together(partial, x_far, far0, far1, db2, da2)
-
-    db3, da3 = Z(1)(db2), Z(-1)(da2)
+    partial, x_far = gate_up_near(*near, slot_rows, core_rows, neighbour_rows, far_rows)
+    partial, x_far, far0, far1, db3, da3 = together(partial, x_far, far0, far1, db3, da3)
+
     me = y * 32 + xl * 16 + z * 2 + c
     capacity = lax.axis_size(WA) * CAP // 2
     h_own, h_other, limit = gate_up_far(jnp.stack([y, z, me, capacity]), partial, x_far, far0, far1, *near)
     h_near, h_ha, h_far = XL(h_other), HA(h_own), HIDDEN_FAR(h_other)
     de0, de1 = Z(1)(db3[:256]), Z(-1)(da3[256:])
-    mine = (h_own, h_near, h_ha, h_far)
-    core = C(jnp.concatenate([flipped(h) for h in mine], axis=1))
-    theirs = [core[:, k * 192 : k * 192 + 192] for k in range(4)]
-    c0, x0 = c == 0, xl == 0
-    hidden = []
-    for k in (0, 2):
-        here = (jnp.where(c0, mine[k], theirs[k]), jnp.where(c0, theirs[k], mine[k]))
-        there = (jnp.where(c0, mine[k + 1], theirs[k + 1]), jnp.where(c0, theirs[k + 1], mine[k + 1]))
-        hidden += [jnp.where(x0, p, q) for p, q in zip(here, there)]
-        hidden += [jnp.where(x0, q, p) for p, q in zip(here, there)]
+    core = C(jnp.concatenate([h_own, h_near, h_ha, h_far], axis=1))
     pieces = [d0, da1, da2, da3, de0, db3, db2, db1, de1]
-    total = down(jnp.concatenate(hidden, axis=1), pieces)
+    total = down(jnp.stack([xl, c, z]), (h_own, h_near, h_ha, h_far, core), pieces)
     other = C(total[128:])
-
-    return mix(jnp.stack([c, z]), total[:128], other, info, slot_route, limit)
+    return mix(jnp.stack([c]), total[:128], other, info, slot_route, limit)
 
 
 def solution(mesh):

time: 126 us -> 120 us (0.952)
  starting transfers between devices: 65.6 us -> 58.1 us
  local copies, waits for them, and re-layouts: 6.11 us -> 12.8 us
  Pallas kernels: 21.1 us -> 17.6 us
  waiting for transfers between devices: 29.6 us -> 27.7 us
    ppermute x4, starting transfers between devices: 20.8 us -> 9.01 us  [C(): return lax.ppermute(a, 'c', [(0, 1), (1, 0)])]
    unnamed x26 -> x45, local copies, waits for them, and re-layouts: 3.06 us -> 10.5 us
    ppermute x25, starting transfers between devices: 30.7 us -> 37.1 us  [ring(): return lambda a: lax.ppermute(a, axis, [(i, (i + k) % n) for i in range(n)])]
    ppermute x25, waiting for transfers between devices: 27 us -> 23.2 us  [ring(): return lambda a: lax.ppermute(a, axis, [(i, (i + k) % n) for i in range(n)])]
    ppermute x2, starting transfers between devices: 4.45 us -> 1.36 us  [HA(): return lax.ppermute(a, 'ha', [(0, 1), (1, 0)])]
    ppermute x1, starting transfers between devices: 0.64 us -> 2.58 us  [HIDDEN_FAR(): return lax.ppermute(a, ('xl', 'ha'), pairs)]
    pallas_call x1, Pallas kernels: 3.94 us -> 2.04 us  [gate_up_near(): pl.pallas_call(near_body, out_shape=(jax.ShapeDtypeStruct((512, 384), F32...]
    ppermute x1, waiting for transfers between devices: 0.01 us -> 1.35 us  [HIDDEN_FAR(): return lax.ppermute(a, ('xl', 'ha'), pairs)]
  transfers between devices with their start and end apart: 35 -> 35, of which waited for: 13 -> 10; matrix products, arithmetic and copies ran while one was open for 5% -> 3% of each run, Pallas kernels for 8% -> 6%
where the time goes in v4:
time: 120 us; the launch traced here: 119 us
  starting transfers between devices  58.1 us (48%)
  waiting for transfers between devices  27.7 us (23%)
  Pallas kernels  17.6 us (15%)
  local copies, waits for them, and re-layouts  12.8 us (11%)
  other arithmetic  2.25 us (2%)
    ppermute x25, starting transfers between devices, ring(): return lambda a: lax.ppermute(a, axis, [(i, (i + k) % n) for i in range(n)])  37.1 us
    ppermute x25, waiting for transfers between devices, ring(): return lambda a: lax.ppermute(a, axis, [(i, (i + k) % n) for i in range(n)])  23.2 us
    unnamed x45, local copies, waits for them, and re-layouts  10.5 us
    ppermute x4, starting transfers between devices, C(): return lax.ppermute(a, 'c', [(0, 1), (1, 0)])  9.01 us
    all_to_all x1, starting transfers between devices, per_device(): lax.all_to_all(packed, ('xl', 'c'), split_axis=0, concat_axis=0, tiled=True)  6.67 us
    pallas_call x1, Pallas kernels, gather_rows(): pl.pallas_call(gather_body, out_shape=(jax.ShapeDtypeStruct((CAP, d), BF1...  4.64 us
    pallas_call x1, Pallas kernels, down(): pl.pallas_call(down_body, out_shape=jax.ShapeDtypeStruct((256, 1024), F32...  3.62 us
    pallas_call x1, Pallas kernels, mix(): pl.pallas_call(mix_body, out_shape=jax.ShapeDtypeStruct((n, 2048), BF16),...  3.5 us
  transfers between devices with their start and end apart: 35, of which 10 were waited for; matrix products, arithmetic and copies ran while one was open for 3% of the time, Pallas kernels for 6%

profile of v4, /device:TPU:1, one launch (start us, length us, event | category | flops | bytes accessed | tf_op | source)
XLA Modules:
  0.0 118.9 jit_solution(14801701738491001400)
XLA Ops:
  0.0 1.9 %prep.1 = (f32[8,1024]{1,0:T(8,128)S(1)}, bf16[4,104,384]{2,1,0:T(8,128)(2,1)}) custom-call(s32[8,1024]{1,0:T(8,128)} %bitcast.49, s32[8,1024]{1,0:T(8,128)} %bitcast.50, f32[8,1024]{1,0:T(8,128)} %bitcast.51, bf16[32,768]{1,0:T(8,128)(2,1)} %refs_3_.1, bf16[32,768]{1,0:T(8,128)(2,1)} %refs_4_.1, bf16[32,768]{1,0:T(8,128)(2,1)} %refs_5_.1), custom_call_target="tpu_custom_call" | custom-call | flops 33554432 | bytes 131072 | tf_op jit(solution)/shard_map/prep/pallas_call | solution.py:84
  1.9 6.7 %all-to-all-start = ((bf16[4,104,384]{2,1,0:T(8,128)(2,1)}), bf16[4,104,384]{2,1,0:T(8,128)(2,1)S(1)}, u32[]{:S(2)}, u32[]{:S(2)}) async-start(bf16[4,104,384]{2,1,0:T(8,128)(2,1)} %get-tuple-element.37), calls=%async_computation | async-start | bytes 638976 | tf_op jit(solution)/shard_map/all_to_all | solution.py:309
  8.7 4.6 %gather_rows.1 = (bf16[128,4096]{1,0:T(8,128)(2,1)S(1)}, f32[128,128]{1,0:T(8,128)S(1)}) custom-call(s32[2]{0:T(128)S(1)} %pad_add_fusion.2.where, bf16[1024,4096]{1,0:T(8,128)(2,1)} %tokens.1, f32[8,1024]{1,0:T(8,128)S(1)} %get-tuple-element.38.info), custom_call_target="tpu_custom_call" | custom-call | flops 1073741824 | bytes 8388608 | tf_op jit(solution)/shard_map/gather_rows/pallas_call | solution.py:127
  16.4 4.0 %collective-permute-start.1 = (bf16[136,384]{1,0:T(8,128)(2,1)S(1)}, bf16[136,384]{1,0:T(8,128)(2,1)S(1)}, u32[]{:S(2)}, u32[]{:S(2)}) collective-permute-start(bf16[136,384]{1,0:T(8,128)(2,1)S(1)} %pad_maximum_fusion.4), channel_id=1, source_target_pairs={{0,28},{4,0},{8,4},{12,8},{16,12},{20,16},{24,20},{28,24},{1,29},{... | collective-permute-start | bytes 313352 | tf_op jit(solution)/shard_map/ppermute | solution.py:21
  23.4 3.0 %collective-permute-done.8 = bf16[128,384]{1,0:T(8,128)(2,1)S(1)} collective-permute-done((bf16[128,384]{1,0:T(8,128)(2,1)S(1)}, bf16[128,384]{1,0:T(8,128)(2,1)S(1)}, u32[]{:S(2)}, u32[]{:S(2)}) %collective-permute-start.8) | collective-permute-done | bytes 98336 | tf_op jit(solution)/shard_map/ppermute | solution.py:21
  26.6 2.8 %collective-permute-start.10 = (bf16[64,384]{1,0:T(8,128)(2,1)S(1)}, bf16[64,384]{1,0:T(8,128)(2,1)S(1)}, u32[]{:S(2)}, u32[]{:S(2)}) collective-permute-start(bf16[64,384]{1,0:T(8,128)(2,1)S(1)} %slice.187), channel_id=1, source_target_pairs={{0,192},{64,0},{128,64},{192,128},{1,193},{65,1},{129,65},{193,129... | collective-permute-start | bytes 147464 | tf_op jit(solution)/shard_map/ppermute | solution.py:21
  29.4 2.7 %collective-permute-start.3 = (bf16[136,384]{1,0:T(8,128)(2,1)S(1)}, bf16[136,384]{1,0:T(8,128)(2,1)S(1)}, u32[]{:S(2)}, u32[]{:S(2)}) collective-permute-start(bf16[136,384]{1,0:T(8,128)(2,1)S(1)} %collective-permute-done.1), channel_id=1, source_target_pairs={{0,28},{4,0},{8,4},{12,8},{16,12},{20,16},{24,20},{28,24},{1,29},{... | collective-permute-start | bytes 313352 | tf_op jit(solution)/shard_map/ppermute | solution.py:21
  34.6 2.7 %collective-permute-start.6 = (bf16[136,384]{1,0:T(8,128)(2,1)S(1)}, bf16[136,384]{1,0:T(8,128)(2,1)S(1)}, u32[]{:S(2)}, u32[]{:S(2)}) collective-permute-start(bf16[136,384]{1,0:T(8,128)(2,1)S(1)} %collective-permute-done.3), channel_id=1, source_target_pairs={{0,28},{4,0},{8,4},{12,8},{16,12},{20,16},{24,20},{28,24},{1,29},{... | collective-permute-start | bytes 313352 | tf_op jit(solution)/shard_map/ppermute | solution.py:21
  37.7 2.7 %collective-permute-start.14 = (bf16[680,384]{1,0:T(8,128)(2,1)S(1)}, bf16[680,384]{1,0:T(8,128)(2,1)S(1)}, u32[]{:S(2)}, u32[]{:S(2)}) collective-permute-start(bf16[680,384]{1,0:T(8,128)(2,1)S(1)} %constant_dynamic-update-slice_fusion.first), channel_id=1, source_target_pairs={{0,192},{64,0},{128,64},{192,128},{1,193},{65,1},{129,65},{193,129... | collective-permute-start | bytes 1566728 | tf_op jit(solution)/shard_map/ppermute | solution.py:21
  43.2 8.7 %collective-permute-done.12 = bf16[136,384]{1,0:T(8,128)(2,1)S(1)} collective-permute-done((bf16[136,384]{1,0:T(8,128)(2,1)S(1)}, bf16[136,384]{1,0:T(8,128)(2,1)S(1)}, u32[]{:S(2)}, u32[]{:S(2)}) %collective-permute-start.12) | collective-permute-done | bytes 104480 | tf_op jit(solution)/shard_map/ppermute | solution.py:21
  51.9 3.5 %collective-permute-start.21 = (bf16[128,4096]{1,0:T(8,128)(2,1)S(1)}, bf16[128,4096]{1,0:T(8,128)(2,1)S(1)}, u32[]{:S(2)}, u32[]{:S(2)}) collective-permute-start(bf16[128,4096]{1,0:T(8,128)(2,1)S(1)} %get-tuple-element.39.xo), channel_id=1, source_target_pairs={{0,2},{2,0},{1,3},{3,1},{4,6},{6,4},{5,7},{7,5},{8,10},{10,8},{9,1... | collective-permute-start | bytes 3145736 | tf_op jit(solution)/shard_map/ppermute | solution.py:33
  56.5 2.7 %collective-permute-start.20 = (bf16[512,384]{1,0:T(8,128)(2,1)S(1)}, bf16[512,384]{1,0:T(8,128)(2,1)}, u32[]{:S(2)}, u32[]{:S(2)}) collective-permute-start(bf16[512,384]{1,0:T(8,128)(2,1)S(1)} %collective-permute-done.16.refs_1_), channel_id=1, source_target_pairs={{0,28},{4,0},{8,4},{12,8},{16,12},{20,16},{24,20},{28,24},{1,29},{... | collective-permute-start | bytes 1179656 | tf_op jit(solution)/shard_map/ppermute | solution.py:21
  61.0 2.6 %collective-permute-start.18 = (bf16[408,384]{1,0:T(8,128)(2,1)S(1)}, bf16[408,384]{1,0:T(8,128)(2,1)S(1)}, u32[]{:S(2)}, u32[]{:S(2)}) collective-permute-start(bf16[408,384]{1,0:T(8,128)(2,1)S(1)} %constant_dynamic-update-slice_fusion.9.second), channel_id=1, source_target_pairs={{0,192},{64,0},{128,64},{192,128},{1,193},{65,1},{129,65},{193,129... | collective-permute-start | bytes 940040 | tf_op jit(solution)/shard_map/ppermute | solution.py:21
  63.7 5.3 %collective-permute-done.17.s_back = bf16[408,384]{1,0:T(8,128)(2,1)S(1)} collective-permute-done((bf16[408,384]{1,0:T(8,128)(2,1)S(1)}, bf16[408,384]{1,0:T(8,128)(2,1)S(1)}, u32[]{:S(2)}, u32[]{:S(2)}) %collective-permute-start.17) | collective-permute-done | bytes 313376 | tf_op jit(solution)/shard_map/ppermute | solution.py:21
  71.0 3.4 %collective-permute-start.24 = (bf16[576,384]{1,0:T(8,128)(2,1)}, bf16[576,384]{1,0:T(8,128)(2,1)S(1)}, u32[]{:S(2)}, u32[]{:S(2)}) collective-permute-start(bf16[576,384]{1,0:T(8,128)(2,1)} %pad_maximum_fusion), channel_id=1, source_target_pairs={{0,192},{64,0},{128,64},{192,128},{1,193},{65,1},{129,65},{193,129... | collective-permute-start | bytes 1327112 | tf_op jit(solution)/shard_map/ppermute | solution.py:21
  75.1 2.7 %collective-permute-start.26 = (bf16[512,384]{1,0:T(8,128)(2,1)}, bf16[512,384]{1,0:T(8,128)(2,1)}, u32[]{:S(2)}, u32[]{:S(2)}) collective-permute-start(bf16[512,384]{1,0:T(8,128)(2,1)} %collective-permute-done.20.refs_2_), channel_id=1, source_target_pairs={{0,28},{4,0},{8,4},{12,8},{16,12},{20,16},{24,20},{28,24},{1,29},{... | collective-permute-start | bytes 1179656 | tf_op jit(solution)/shard_map/ppermute | solution.py:21
  82.8 2.0 %gate_up_near.1 = (f32[512,384]{1,0:T(8,128)S(1)}, bf16[512,1024]{1,0:T(8,128)(2,1)S(1)}) custom-call(bf16[680,384]{1,0:T(8,128)(2,1)S(1)} %constant_dynamic-update-slice_fusion.first, bf16[408,384]{1,0:T(8,128)(2,1)S(1)} %constant_dynamic-update-slice_fusion.9.second, bf16[680,384]{1,0:T(8,128)(2,1)S(1)} %collective-permute-done.13.f_back, ...), custom_call_target="tpu_custom_call" | custom-call | flops 1207959552 | bytes 8388608 | tf_op jit(solution)/shard_map/gate_up_near/pallas_call | solution.py:151
  84.9 1.9 %gate_up_far.1 = (bf16[256,192]{1,0:T(8,128)(2,1)S(1)}, bf16[256,192]{1,0:T(8,128)(2,1)S(1)}, f32[8,128]{1,0:T(8,128)S(1)}) custom-call(s32[4]{0:T(128)S(1)} %pad_add_fusion.1.where, f32[512,384]{1,0:T(8,128)S(1)} %get-tuple-element.59.total, bf16[512,1024]{1,0:T(8,128)(2,1)S(1)} %get-tuple-element.60.x_far, bf16[512,384]{1,0:T(8,128)(2,1)} %collective-permute-done.23.far0, ...), custom_call_target="tpu_custom_call" | custom-call | flops 402653184 | bytes 4194304 | tf_op jit(solution)/shard_map/gate_up_far/pallas_call | solution.py:195
  88.1 2.6 %collective-permute-start.29 = (bf16[256,192]{1,0:T(8,128)(2,1)S(1)}, bf16[256,192]{1,0:T(8,128)(2,1)S(1)}, u32[]{:S(2)}, u32[]{:S(2)}) collective-permute-start(bf16[256,192]{1,0:T(8,128)(2,1)S(1)} %get-tuple-element.64), channel_id=1, source_target_pairs={{0,33},{1,32},{32,1},{33,0},{2,35},{3,34},{34,3},{35,2},{4,37},{5,... | collective-permute-start | bytes 294920 | tf_op jit(solution)/shard_map/ppermute | solution.py:302
  93.8 4.6 %collective-permute-start.30 = (bf16[256,768]{1,0:T(8,128)(2,1)S(1)}, bf16[256,768]{1,0:T(8,128)(2,1)S(1)}, u32[]{:S(2)}, u32[]{:S(2)}) collective-permute-start(bf16[256,768]{1,0:T(8,128)(2,1)S(1)} %pad_maximum_fusion.2), channel_id=1, source_target_pairs={{0,2},{2,0},{1,3},{3,1},{4,6},{6,4},{5,7},{7,5},{8,10},{10,8},{9,1... | collective-permute-start | bytes 1179656 | tf_op jit(solution)/shard_map/ppermute | solution.py:33
  100.4 2.7 %collective-permute-start.32 = (bf16[256,384]{1,0:T(8,128)(2,1)S(1)}, bf16[256,384]{1,0:T(8,128)(2,1)S(1)}, u32[]{:S(2)}, u32[]{:S(2)}) collective-permute-start(bf16[256,384]{1,0:T(8,128)(2,1)S(1)} %slice.174), channel_id=1, source_target_pairs={{0,28},{4,0},{8,4},{12,8},{16,12},{20,16},{24,20},{28,24},{1,29},{... | collective-permute-start | bytes 589832 | tf_op jit(solution)/shard_map/ppermute | solution.py:21
  103.2 4.0 %collective-permute-done.31.refs_4_ = bf16[256,384]{1,0:T(8,128)(2,1)S(1)} collective-permute-done((bf16[256,384]{1,0:T(8,128)(2,1)S(1)}, bf16[256,384]{1,0:T(8,128)(2,1)S(1)}, u32[]{:S(2)}, u32[]{:S(2)}) %collective-permute-start.31) | collective-permute-done | bytes 196640 | tf_op jit(solution)/shard_map/ppermute | solution.py:21
  109.3 3.6 %down.1 = f32[256,1024]{1,0:T(8,128)S(1)} custom-call(s32[3]{0:T(128)S(1)} %pad_add_fusion.where, bf16[256,192]{1,0:T(8,128)(2,1)S(1)} %get-tuple-element.63.own, bf16[256,192]{1,0:T(8,128)(2,1)S(1)} %collective-permute-done.27.near, bf16[256,192]{1,0:T(8,128)(2,1)S(1)} %collective-permute-done.28.ha, bf16[256,192]{1,0:T(8,128)(2,1)S(1)} %collective-permute-done.29.far, ...), custom_call_target="tpu_custom_call" | custom-call | flops 805306368 | bytes 5242880 | tf_op jit(solution)/shard_map/down/pallas_call | solution.py:240
  115.4 3.5 %mix.1 = bf16[1024,2048]{1,0:T(8,128)(2,1)} custom-call(s32[1]{0:T(128)} %bitcast.where, f32[128,1024]{1,0:T(8,128)S(1)} %get-tuple-element.70.mine, f32[128,1024]{1,0:T(8,128)S(1)} %collective-permute-done.33.theirs, f32[8,1024]{1,0:T(8,128)S(1)} %get-tuple-element.38.info, f32[128,128]{1,0:T(8,128)S(1)} %get-tuple-element.67.slot_route, ...), custom_call_target="tpu_custom_call" | custom-call | flops 536870912 | bytes 6291456 | tf_op jit(solution)/shard_map/mix/pallas_call | solution.py:270
  (131 shorter events, 33.4 us)
Async XLA Ops:
  1.9 12.7 %all-to-all-start = ((bf16[4,104,384]{2,1,0:T(8,128)(2,1)}), bf16[4,104,384]{2,1,0:T(8,128)(2,1)S(1)}, u32[]{:S(2)}, u32[]{:S(2)}) async-start(bf16[4,104,384]{2,1,0:T(8,128)(2,1)} %get-tuple-element.37), calls=%async_computation | async-start | bytes 638976 | tf_op jit(solution)/shard_map/all_to_all | solution.py:309
  13.3 21.1 %collective-permute-start.4 = (bf16[128,4096]{1,0:T(8,128)(2,1)S(1)}, bf16[128,4096]{1,0:T(8,128)(2,1)S(1)}, u32[]{:S(2)}, u32[]{:S(2)}) collective-permute-start(bf16[128,4096]{1,0:T(8,128)(2,1)S(1)} %get-tuple-element.39.xo), channel_id=1, source_target_pairs={{0,32},{2,35},{32,1},{34,2},{1,33},{3,34},{33,0},{35,3},{4,36},{6,... | collective-permute-start | bytes 3145736 | tf_op jit(solution)/shard_map/ppermute | solution.py:49
  14.7 14.7 %collective-permute-start = (bf16[136,384]{1,0:T(8,128)(2,1)S(1)}, bf16[136,384]{1,0:T(8,128)(2,1)S(1)}, u32[]{:S(2)}, u32[]{:S(2)}) collective-permute-start(bf16[136,384]{1,0:T(8,128)(2,1)S(1)} %pad_maximum_fusion.4), channel_id=1, source_target_pairs={{0,4},{4,8},{8,12},{12,16},{16,20},{20,24},{24,28},{28,0},{1,5},{5... | collective-permute-start | bytes 313352 | tf_op jit(solution)/shard_map/ppermute | solution.py:21
  16.4 13.0 %collective-permute-start.1 = (bf16[136,384]{1,0:T(8,128)(2,1)S(1)}, bf16[136,384]{1,0:T(8,128)(2,1)S(1)}, u32[]{:S(2)}, u32[]{:S(2)}) collective-permute-start(bf16[136,384]{1,0:T(8,128)(2,1)S(1)} %pad_maximum_fusion.4), channel_id=1, source_target_pairs={{0,28},{4,0},{8,4},{12,8},{16,12},{20,16},{24,20},{28,24},{1,29},{... | collective-permute-start | bytes 313352 | tf_op jit(solution)/shard_map/ppermute | solution.py:21
  20.5 5.9 %collective-permute-start.8 = (bf16[128,384]{1,0:T(8,128)(2,1)S(1)}, bf16[128,384]{1,0:T(8,128)(2,1)S(1)}, u32[]{:S(2)}, u32[]{:S(2)}) collective-permute-start(bf16[128,384]{1,0:T(8,128)(2,1)S(1)} %pad_maximum_fusion.5), channel_id=1, source_target_pairs={{0,64},{64,128},{128,192},{192,0},{1,65},{65,129},{129,193},{193,1... | collective-permute-start | bytes 294920 | tf_op jit(solution)/shard_map/ppermute | solution.py:21
  32.5 7.8 %collective-permute-start.11 = (bf16[256,384]{1,0:T(8,128)(2,1)S(1)}, bf16[256,384]{1,0:T(8,128)(2,1)S(1)}, u32[]{:S(2)}, u32[]{:S(2)}) collective-permute-start(bf16[256,384]{1,0:T(8,128)(2,1)S(1)} %pad_maximum_fusion.3), channel_id=1, source_target_pairs={{0,1},{1,0},{2,3},{3,2},{4,5},{5,4},{6,7},{7,6},{8,9},{9,8},{10,11... | collective-permute-start | bytes 589832 | tf_op jit(solution)/shard_map/ppermute | solution.py:41
  37.4 18.2 %collective-permute-start.13 = (bf16[680,384]{1,0:T(8,128)(2,1)S(1)}, bf16[680,384]{1,0:T(8,128)(2,1)S(1)}, u32[]{:S(2)}, u32[]{:S(2)}) collective-permute-start(bf16[680,384]{1,0:T(8,128)(2,1)S(1)} %constant_dynamic-update-slice_fusion.first), channel_id=1, source_target_pairs={{0,64},{64,128},{128,192},{192,0},{1,65},{65,129},{129,193},{193,1... | collective-permute-start | bytes 1566728 | tf_op jit(solution)/shard_map/ppermute | solution.py:21
  37.7 17.9 %collective-permute-start.14 = (bf16[680,384]{1,0:T(8,128)(2,1)S(1)}, bf16[680,384]{1,0:T(8,128)(2,1)S(1)}, u32[]{:S(2)}, u32[]{:S(2)}) collective-permute-start(bf16[680,384]{1,0:T(8,128)(2,1)S(1)} %constant_dynamic-update-slice_fusion.first), channel_id=1, source_target_pairs={{0,192},{64,0},{128,64},{192,128},{1,193},{65,1},{129,65},{193,129... | collective-permute-start | bytes 1566728 | tf_op jit(solution)/shard_map/ppermute | solution.py:21
  40.4 15.1 %collective-permute-start.15 = (bf16[512,384]{1,0:T(8,128)(2,1)S(1)}, bf16[512,384]{1,0:T(8,128)(2,1)S(1)}, u32[]{:S(2)}, u32[]{:S(2)}) collective-permute-start(bf16[512,384]{1,0:T(8,128)(2,1)S(1)} %constant_dynamic-update-slice_fusion.8.refs_0_), channel_id=1, source_target_pairs={{0,4},{4,8},{8,12},{12,16},{16,20},{20,24},{24,28},{28,0},{1,5},{5... | collective-permute-start | bytes 1179656 | tf_op jit(solution)/shard_map/ppermute | solution.py:21
  41.3 14.3 %collective-permute-start.16 = (bf16[512,384]{1,0:T(8,128)(2,1)S(1)}, bf16[512,384]{1,0:T(8,128)(2,1)S(1)}, u32[]{:S(2)}, u32[]{:S(2)}) collective-permute-start(bf16[512,384]{1,0:T(8,128)(2,1)S(1)} %constant_dynamic-update-slice_fusion.8.refs_0_), channel_id=1, source_target_pairs={{0,28},{4,0},{8,4},{12,8},{16,12},{20,16},{24,20},{28,24},{1,29},{... | collective-permute-start | bytes 1179656 | tf_op jit(solution)/shard_map/ppermute | solution.py:21
  43.2 8.8 %collective-permute-start.12 = (bf16[136,384]{1,0:T(8,128)(2,1)S(1)}, bf16[136,384]{1,0:T(8,128)(2,1)S(1)}, u32[]{:S(2)}, u32[]{:S(2)}) collective-permute-start(bf16[136,384]{1,0:T(8,128)(2,1)S(1)} %collective-permute-done.5), channel_id=1, source_target_pairs={{0,4},{4,8},{8,12},{12,16},{16,20},{20,24},{24,28},{28,0},{1,5},{5... | collective-permute-start | bytes 313352 | tf_op jit(solution)/shard_map/ppermute | solution.py:21
  51.9 8.1 %collective-permute-start.21 = (bf16[128,4096]{1,0:T(8,128)(2,1)S(1)}, bf16[128,4096]{1,0:T(8,128)(2,1)S(1)}, u32[]{:S(2)}, u32[]{:S(2)}) collective-permute-start(bf16[128,4096]{1,0:T(8,128)(2,1)S(1)} %get-tuple-element.39.xo), channel_id=1, source_target_pairs={{0,2},{2,0},{1,3},{3,1},{4,6},{6,4},{5,7},{7,5},{8,10},{10,8},{9,1... | collective-permute-start | bytes 3145736 | tf_op jit(solution)/shard_map/ppermute | solution.py:33
  55.5 13.6 %collective-permute-start.22 = (bf16[128,4096]{1,0:T(8,128)(2,1)}, bf16[128,4096]{1,0:T(8,128)(2,1)S(1)}, u32[]{:S(2)}, u32[]{:S(2)}) collective-permute-start(bf16[128,4096]{1,0:T(8,128)(2,1)} %copy-done.2), channel_id=1, source_target_pairs={{0,2},{2,0},{1,3},{3,1},{4,6},{6,4},{5,7},{7,5},{8,10},{10,8},{9,1... | collective-permute-start | bytes 3145736 | tf_op jit(solution)/shard_map/ppermute | solution.py:33
  55.6 13.5 %collective-permute-start.19 = (bf16[512,384]{1,0:T(8,128)(2,1)S(1)}, bf16[512,384]{1,0:T(8,128)(2,1)}, u32[]{:S(2)}, u32[]{:S(2)}) collective-permute-start(bf16[512,384]{1,0:T(8,128)(2,1)S(1)} %collective-permute-done.15.refs_7_), channel_id=1, source_target_pairs={{0,4},{4,8},{8,12},{12,16},{16,20},{20,24},{24,28},{28,0},{1,5},{5... | collective-permute-start | bytes 1179656 | tf_op jit(solution)/shard_map/ppermute | solution.py:21
  56.5 12.6 %collective-permute-start.20 = (bf16[512,384]{1,0:T(8,128)(2,1)S(1)}, bf16[512,384]{1,0:T(8,128)(2,1)}, u32[]{:S(2)}, u32[]{:S(2)}) collective-permute-start(bf16[512,384]{1,0:T(8,128)(2,1)S(1)} %collective-permute-done.16.refs_1_), channel_id=1, source_target_pairs={{0,28},{4,0},{8,4},{12,8},{16,12},{20,16},{24,20},{28,24},{1,29},{... | collective-permute-start | bytes 1179656 | tf_op jit(solution)/shard_map/ppermute | solution.py:21
  59.9 9.1 %collective-permute-start.17 = (bf16[408,384]{1,0:T(8,128)(2,1)S(1)}, bf16[408,384]{1,0:T(8,128)(2,1)S(1)}, u32[]{:S(2)}, u32[]{:S(2)}) collective-permute-start(bf16[408,384]{1,0:T(8,128)(2,1)S(1)} %constant_dynamic-update-slice_fusion.9.second), channel_id=1, source_target_pairs={{0,64},{64,128},{128,192},{192,0},{1,65},{65,129},{129,193},{193,1... | collective-permute-start | bytes 940040 | tf_op jit(solution)/shard_map/ppermute | solution.py:21
  61.0 8.1 %collective-permute-start.18 = (bf16[408,384]{1,0:T(8,128)(2,1)S(1)}, bf16[408,384]{1,0:T(8,128)(2,1)S(1)}, u32[]{:S(2)}, u32[]{:S(2)}) collective-permute-start(bf16[408,384]{1,0:T(8,128)(2,1)S(1)} %constant_dynamic-update-slice_fusion.9.second), channel_id=1, source_target_pairs={{0,192},{64,0},{128,64},{192,128},{1,193},{65,1},{129,65},{193,129... | collective-permute-start | bytes 940040 | tf_op jit(solution)/shard_map/ppermute | solution.py:21
  71.0 13.9 %collective-permute-start.24 = (bf16[576,384]{1,0:T(8,128)(2,1)}, bf16[576,384]{1,0:T(8,128)(2,1)S(1)}, u32[]{:S(2)}, u32[]{:S(2)}) collective-permute-start(bf16[576,384]{1,0:T(8,128)(2,1)} %pad_maximum_fusion), channel_id=1, source_target_pairs={{0,192},{64,0},{128,64},{192,128},{1,193},{65,1},{129,65},{193,129... | collective-permute-start | bytes 1327112 | tf_op jit(solution)/shard_map/ppermute | solution.py:21
  75.1 9.7 %collective-permute-start.23 = (bf16[512,384]{1,0:T(8,128)(2,1)}, bf16[512,384]{1,0:T(8,128)(2,1)}, u32[]{:S(2)}, u32[]{:S(2)}) collective-permute-start(bf16[512,384]{1,0:T(8,128)(2,1)} %pad_maximum_fusion.1), channel_id=1, source_target_pairs={{0,64},{64,128},{128,192},{192,0},{1,65},{65,129},{129,193},{193,1... | collective-permute-start | bytes 1179656 | tf_op jit(solution)/shard_map/ppermute | solution.py:21
  75.1 9.7 %collective-permute-start.25 = (bf16[512,384]{1,0:T(8,128)(2,1)}, bf16[512,384]{1,0:T(8,128)(2,1)}, u32[]{:S(2)}, u32[]{:S(2)}) collective-permute-start(bf16[512,384]{1,0:T(8,128)(2,1)} %collective-permute-done.19.refs_6_), channel_id=1, source_target_pairs={{0,4},{4,8},{8,12},{12,16},{16,20},{20,24},{24,28},{28,0},{1,5},{5... | collective-permute-start | bytes 1179656 | tf_op jit(solution)/shard_map/ppermute | solution.py:21
  75.1 9.7 %collective-permute-start.26 = (bf16[512,384]{1,0:T(8,128)(2,1)}, bf16[512,384]{1,0:T(8,128)(2,1)}, u32[]{:S(2)}, u32[]{:S(2)}) collective-permute-start(bf16[512,384]{1,0:T(8,128)(2,1)} %collective-permute-done.20.refs_2_), channel_id=1, source_target_pairs={{0,28},{4,0},{8,4},{12,8},{16,12},{20,16},{24,20},{28,24},{1,29},{... | collective-permute-start | bytes 1179656 | tf_op jit(solution)/shard_map/ppermute | solution.py:21
  93.8 13.5 %collective-permute-start.30 = (bf16[256,768]{1,0:T(8,128)(2,1)S(1)}, bf16[256,768]{1,0:T(8,128)(2,1)S(1)}, u32[]{:S(2)}, u32[]{:S(2)}) collective-permute-start(bf16[256,768]{1,0:T(8,128)(2,1)S(1)} %pad_maximum_fusion.2), channel_id=1, source_target_pairs={{0,2},{2,0},{1,3},{3,1},{4,6},{6,4},{5,7},{7,5},{8,10},{10,8},{9,1... | collective-permute-start | bytes 1179656 | tf_op jit(solution)/shard_map/ppermute | solution.py:33
  99.3 7.8 %collective-permute-start.31 = (bf16[256,384]{1,0:T(8,128)(2,1)S(1)}, bf16[256,384]{1,0:T(8,128)(2,1)S(1)}, u32[]{:S(2)}, u32[]{:S(2)}) collective-permute-start(bf16[256,384]{1,0:T(8,128)(2,1)S(1)} %slice.173), channel_id=1, source_target_pairs={{0,4},{4,8},{8,12},{12,16},{16,20},{20,24},{24,28},{28,0},{1,5},{5... | collective-permute-start | bytes 589832 | tf_op jit(solution)/shard_map/ppermute | solution.py:21
  100.4 7.0 %collective-permute-start.32 = (bf16[256,384]{1,0:T(8,128)(2,1)S(1)}, bf16[256,384]{1,0:T(8,128)(2,1)S(1)}, u32[]{:S(2)}, u32[]{:S(2)}) collective-permute-start(bf16[256,384]{1,0:T(8,128)(2,1)S(1)} %slice.174), channel_id=1, source_target_pairs={{0,28},{4,0},{8,4},{12,8},{16,12},{20,16},{24,20},{28,24},{1,29},{... | collective-permute-start | bytes 589832 | tf_op jit(solution)/shard_map/ppermute | solution.py:21
  (25 other events, 168.5 us)

commit v5 on v4

--- a/solution.py
+++ b/solution.py
@@ -136,36 +136,47 @@
     )(where, tokens, info)
 
 
-def near_body(first, second, f_back, s_back, f_ahead, s_ahead, xo, xc, xn, xnc, total, x_far, x_all):
+def near_body(first, second, last, f_back, f_ahead, g_back, g_ahead, xo, xc, xn, xnc, total, x_far, x_all):
     for i, ref in enumerate((xo, xc, xn, xnc)):
-        x_all[i * 128 : i * 128 + 128, :] = ref[:, :3072]
-        x_far[i * 128 : i * 128 + 128, :] = ref[:, 3072:]
+        at = slice(i * 128, i * 128 + 128)
+        x_all[at, :] = ref[:, :3712]
+        x_far[at, 0:128] = ref[:, 1920:2048]
+        x_far[at, 128:256] = ref[:, 2944:3072]
+        x_far[at, 256:640] = ref[:, 3712:]
     acc = jnp.zeros((512, 384), F32)
-    for i, (f, s) in enumerate(((first, second), (f_back, s_back), (f_ahead, s_ahead))):
-        acc += jnp.dot(x_all[:, i * 1024 : i * 1024 + 640], f[0:640, :], preferred_element_type=F32)
-        acc += jnp.dot(x_all[:, i * 1024 + 640 : i * 1024 + 1024], s[0:384, :], preferred_element_type=F32)
+    for start, ref, row, size in (
+        (0, first, 0, 640),
+        (640, second, 0, 256),
+        (896, last, 0, 128),
+        (1024, f_back, 0, 640),
+        (1664, g_back, 0, 256),
+        (2048, f_ahead, 0, 640),
+        (2688, g_ahead, 0, 256),
+        (3072, g_back, 256, 384),
+        (3456, g_ahead, 256, 256),
+    ):
+        acc += jnp.dot(x_all[:, start : start + size], ref[row : row + size, :], preferred_element_type=F32)
     total[...] = acc
 
 
 def gate_up_near(*arrays):
     return pl.pallas_call(
         near_body,
-        out_shape=(jax.ShapeDtypeStruct((512, 384), F32), jax.ShapeDtypeStruct((512, 1024), BF16)),
+        out_shape=(jax.ShapeDtypeStruct((512, 384), F32), jax.ShapeDtypeStruct((512, 640), BF16)),
         in_specs=[whole()] * len(arrays),
         out_specs=(whole(), whole()),
-        scratch_shapes=[VMEM((512, 3072), BF16)],
+        scratch_shapes=[VMEM((512, 3712), BF16)],
         compiler_params=pltpu.CompilerParams(vmem_limit_bytes=16 << 20),
-        cost_estimate=pl.CostEstimate(flops=2 * 512 * 3072 * 384, bytes_accessed=8 << 20, transcendentals=0),
+        cost_estimate=pl.CostEstimate(flops=2 * 512 * 3456 * 384, bytes_accessed=8 << 20, transcendentals=0),
         name="gate_up_near",
     )(*arrays)
 
 
-def far_body(where, total, x_far, far0, far1, first, second, f_back, s_back, f_ahead, s_ahead, own, other, limit):
+def far_body(where, total, x_far, k_back, k_ahead, k_far, *refs):
+    (first, second, last, f_back, f_ahead, g_back, g_ahead), (own, other, limit) = refs[:7], refs[7:]
     acc = total[...]
-    acc += jnp.dot(x_far[:, 0:384], far0[0:384, :], preferred_element_type=F32)
-    acc += jnp.dot(x_far[:, 384:640], far1[0:256, :], preferred_element_type=F32)
-    acc += jnp.dot(x_far[:, 640:768], far0[384:512, :], preferred_element_type=F32)
-    acc += jnp.dot(x_far[:, 768:1024], far1[256:512, :], preferred_element_type=F32)
+    for start, ref, row in ((0, k_back, 0), (128, k_ahead, 0), (256, k_back, 128), (384, k_ahead, 128), (512, k_far, 0)):
+        acc += jnp.dot(x_far[:, start : start + 128], ref[row : row + 128, :], preferred_element_type=F32)
     gate, up = acc[:, :192], acc[:, 192:]
     hidden = (gate * jax.nn.sigmoid(gate) * up).astype(BF16)
     own[...] = hidden[:256]
@@ -175,19 +186,19 @@
     quad = lax.shift_right_logical(lane, 1) * 16 + (lane & 1)
     earlier = jnp.zeros((8, 128), F32)
     groups = (
-        (0, first[640:680, 0:128], second[384:408, 0:128]),
-        (3, f_back[640:680, 0:128], s_back[384:408, 0:128]),
-        (1, f_ahead[640:680, 0:128], s_ahead[384:408, 0:128]),
-        (2, far1[512:552, 0:128], far1[552:576, 0:128]),
+        (0, first[640:680, 0:128], second[256:272, 0:128], last[128:136, 0:128]),
+        (3, f_back[640:680, 0:128], g_back[640:656, 0:128], k_back[256:264, 0:128]),
+        (1, f_ahead[640:680, 0:128], g_ahead[512:528, 0:128], k_ahead[256:264, 0:128]),
+        (2, g_ahead[528:568, 0:128], k_ahead[264:280, 0:128], k_far[128:136, 0:128]),
     )
-    for ky, near, late in groups:
-        tiles = jnp.concatenate([near.astype(F32), late.astype(F32)], axis=0)
+    for ky, *parts in groups:
+        tiles = jnp.concatenate([part.astype(F32) for part in parts], axis=0)
         for zi, kz in enumerate((0, 7, 1, 6, 2, 5, 3, 4)):
             block = ((where[0] + ky) & 3) * 32 + ((where[1] + kz) & 7) * 2 + quad
-            counted = (block < where[2]) & (lane < 4)
+            counted = (block < where[4]) & (lane < 4)
             earlier += jnp.where(counted, tiles[zi * 8 : zi * 8 + 8], 0.0)
     before = jnp.sum(earlier[0:1], axis=1, keepdims=True)
-    limit[...] = jnp.broadcast_to(where[3].astype(F32) - before, limit.shape)
+    limit[...] = jnp.broadcast_to(where[5].astype(F32) - before, limit.shape)
 
 
 def gate_up_far(*arrays):
@@ -198,7 +209,7 @@
         in_specs=[whole(pltpu.SMEM)] + [whole()] * (len(arrays) - 1),
         out_specs=(whole(), whole(), whole()),
         compiler_params=pltpu.CompilerParams(vmem_limit_bytes=16 << 20),
-        cost_estimate=pl.CostEstimate(flops=2 * 512 * 1024 * 384, bytes_accessed=4 << 20, transcendentals=512 * 192),
+        cost_estimate=pl.CostEstimate(flops=2 * 512 * 640 * 384, bytes_accessed=3 << 20, transcendentals=512 * 192),
         name="gate_up_far",
     )(*arrays)
 
@@ -209,7 +220,7 @@
     for xl in range(2):
         for c in range(2):
 
-            @pl.when((where[0] == xl) & (where[1] == c))
+            @pl.when((where[2] == xl) & (where[3] == c))
             def _():
                 for k, ref in enumerate((own, near, ha, far)):
                     pair = xl if k % 2 == 0 else 1 - xl
@@ -233,7 +244,7 @@
         blocks.append(total + dot(2, rear[base : base + 128]) + dot(3, rear[base + 128 : base + 256]))
     for y in range(2):
         part = jnp.concatenate([b[:, y * 64 : y * 64 + 64] for b in blocks], axis=1)
-        out[:, y * 512 : y * 512 + 512] = pltpu.roll(part, where[2] * 64, 1)
+        out[:, y * 512 : y * 512 + 512] = pltpu.roll(part, where[1] * 64, 1)
 
 
 def down(where, hidden, pieces):
@@ -254,7 +265,7 @@
     def _():
         slot = lax.broadcasted_iota(I32, (CAP, 1), 0).astype(F32)
         scale = jnp.where(slot < limit[0:1, 0:1], slot_route[:, 0:1], 0.0)
-        for ref, column in ((mine, where[0]), (theirs, 1 - where[0])):
+        for ref, column in ((mine, where[3]), (theirs, 1 - where[3])):
             scaled = (ref[...] * scale).astype(BF16)
             for y in range(2):
                 at = pl.multiple_of(y * 1024 + column * 512, 512)
@@ -304,12 +315,13 @@
 
 def per_device(tokens, expert_ids, keep_mask, route_weight, gate_weight, up_weight, down_weight):
     y, xl, z, c, ha = (lax.axis_index(a) for a in ("y", "xl", "z", "c", "ha"))
+    me = y * 32 + xl * 16 + z * 2 + c
+    shift = lax.rem(2 * ha - y + NY, NY)
+    where = jnp.stack([y, z, xl, c, me, lax.axis_size(WA) * CAP // 2])
     sources = (expert_ids.T, keep_mask.T, route_weight.T, gate_weight, up_weight, down_weight)
     info, packed = prep(*(pltpu.with_memory_space_constraint(a, pltpu.HBM) for a in sources))
     arrived = lax.all_to_all(packed, ("xl", "c"), split_axis=0, concat_axis=0, tiled=True)
-    slot_rows, slot_route = gather_rows(
-        jnp.stack([y, z]), pltpu.with_memory_space_constraint(tokens, pltpu.HBM), info
-    )
+    slot_rows, slot_route = gather_rows(where, pltpu.with_memory_space_constraint(tokens, pltpu.HBM), info)
 
     lane = lax.broadcasted_iota(I32, (8, 384), 1)
     tile = jnp.zeros((8, 384), BF16)
@@ -319,16 +331,13 @@
     picked = lax.dynamic_slice_in_dim(arrived, 2 * c, 2, axis=0)[:, 40:]
     rows = jnp.concatenate([picked[0, :32], picked[1, :32], picked[0, 32:], picked[1, 32:]], axis=0)
 
+    b1, a1 = Z(1)(unit), Z(-1)(unit)
+    d_back, d_ahead, d_far = Y(1)(rows), Y(-1)(rows), Y(2)(rows)
+    b1, a1, slot_rows = together(b1, a1, slot_rows)
+    b2, a2 = Z(1)(b1), Z(-1)(a1)
     neighbour_rows = across_x(slot_rows)
-    b1, a1 = Z(1)(unit), Z(-1)(unit)
-    d_back, d_ahead = Y(1)(rows), Y(-1)(rows)
-    b2, a2 = Z(1)(b1), Z(-1)(a1)
-    d_far = Y(1)(d_back[:64]), Y(-1)(d_ahead[64:])
-    d_far0, d_far1 = d_far
-    b2, a2, neighbour_rows = together(b2, a2, neighbour_rows)
-
-    turned = [rows, d_ahead, jnp.concatenate([d_far0, d_far1], axis=0), d_back]
-    shift = lax.rem(2 * ha - y + NY, NY)
+
+    turned = [rows, d_ahead, d_far, d_back]
     ordered = []
     for j in range(4):
         pick = turned[j]
@@ -340,39 +349,39 @@
         return jnp.concatenate([p[:64], q[:64], p[64:], q[64:]], axis=0)
 
     d_swap = HA(halves(ordered[2], ordered[3]))
-    b3, a3 = Z(1)(b2), Z(-1)(a2)
+    b2, a2, d_swap = together(b2, a2, d_swap)
+
+    d0 = jnp.concatenate([halves(ordered[0], ordered[1]), d_swap], axis=0)
+    up1, dn1 = Z(1)(jnp.concatenate([d0, b2], axis=0)), Z(-1)(jnp.concatenate([d0, a2], axis=0))
     first = with_counts([unit, b1, a1, b2, a2])
     f_back, f_ahead = Y(1)(first), Y(-1)(first)
-    b3, a3, d_swap = together(b3, a3, d_swap)
-
-    d0 = jnp.concatenate([halves(ordered[0], ordered[1]), d_swap], axis=0)
-    e = Z(1)(b3)
-    db1, da1 = Z(1)(d0), Z(-1)(d0)
-    e, f_back, f_ahead, db1, da1 = together(e, f_back, f_ahead, db1, da1)
-
-    second = with_counts([b3, a3, e])
-    s_back, s_ahead = Y(1)(second), Y(-1)(second)
-    db2, da2 = Z(1)(db1), Z(-1)(da1)
+    up1, dn1, f_back, f_ahead, neighbour_rows = together(up1, dn1, f_back, f_ahead, neighbour_rows)
+
+    up2, dn2 = Z(1)(up1), Z(-1)(dn1[:512])
+    second = with_counts([up1[512:], dn1[512:]])
+    g_back = Y(1)(jnp.concatenate([second[:256], f_back[:384], second[256:]], axis=0))
+    g_ahead = Y(-1)(jnp.concatenate([second[:256], f_ahead[384:640], second[256:], f_ahead[640:]], axis=0))
     core_rows, far_rows = C(slot_rows), C(neighbour_rows)
-    s_back, s_ahead, db2, da2, core_rows, far_rows = together(s_back, s_ahead, db2, da2, core_rows, far_rows)
-
-    far0 = Y(1)(jnp.concatenate([f_back[:384], s_back[:128]], axis=0))
-    far1 = Y(-1)(jnp.concatenate([f_ahead[384:640], s_ahead[128:384], f_ahead[640:], s_ahead[384:]], axis=0))
-    db3, da3 = Z(1)(db2), Z(-1)(da2)
-    near = (first, second, f_back, s_back, f_ahead, s_ahead)
+    up2, dn2, g_back, g_ahead, core_rows, far_rows = together(up2, dn2, g_back, g_ahead, core_rows, far_rows)
+
+    last = up2[512:]
+    up3, dn3 = Z(1)(up2[:512]), Z(-1)(dn2)
+    k_back = Y(1)(jnp.concatenate([last[:128], g_back[:128], last[128:]], axis=0))
+    k_ahead = Y(-1)(jnp.concatenate([last[:128], g_ahead[128:256], last[128:], g_ahead[512:528]], axis=0))
+    k_far = Y(2)(last)
+    near = (first, second, last, f_back, f_ahead, g_back, g_ahead)
     partial, x_far = gate_up_near(*near, slot_rows, core_rows, neighbour_rows, far_rows)
-    partial, x_far, far0, far1, db3, da3 = together(partial, x_far, far0, far1, db3, da3)
-
-    me = y * 32 + xl * 16 + z * 2 + c
-    capacity = lax.axis_size(WA) * CAP // 2
-    h_own, h_other, limit = gate_up_far(jnp.stack([y, z, me, capacity]), partial, x_far, far0, far1, *near)
+    k_back, k_ahead, k_far, up3, dn3, partial, x_far = together(k_back, k_ahead, k_far, up3, dn3, partial, x_far)
+
+    de0, de1 = Z(1)(up3[:256]), Z(-1)(dn3[256:])
+    h_own, h_other, limit = gate_up_far(where, partial, x_far, k_back, k_ahead, k_far, *near)
     h_near, h_ha, h_far = XL(h_other), HA(h_own), HIDDEN_FAR(h_other)
-    de0, de1 = Z(1)(db3[:256]), Z(-1)(da3[256:])
+    h_near, h_ha, h_far, de0, de1 = together(h_near, h_ha, h_far, de0, de1)
     core = C(jnp.concatenate([h_own, h_near, h_ha, h_far], axis=1))
-    pieces = [d0, da1, da2, da3, de0, db3, db2, db1, de1]
-    total = down(jnp.stack([xl, c, z]), (h_own, h_near, h_ha, h_far, core), pieces)
+    pieces = [d0, dn1, dn2, dn3, de0, up3, up2, up1, de1]
+    total = down(where, (h_own, h_near, h_ha, h_far, core), pieces)
     other = C(total[128:])
-    return mix(jnp.stack([c]), total[:128], other, info, slot_route, limit)
+    return mix(where, total[:128], other, info, slot_route, limit)
 
 
 def solution(mesh):

time: 120 us -> 108 us (0.900)
  local copies, waits for them, and re-layouts: 12.8 us -> 0.92 us
  starting transfers between devices: 58.1 us -> 60.4 us
  other arithmetic: 2.25 us -> 0.49 us
    unnamed x45 -> x15, local copies, waits for them, and re-layouts: 10.5 us -> 0.32 us
    ppermute x4, starting transfers between devices: 9.01 us -> 14 us  [C(): return lax.ppermute(a, 'c', [(0, 1), (1, 0)])]
    ppermute x25 -> x22, starting transfers between devices: 37.1 us -> 32.2 us  [ring(): return lambda a: lax.ppermute(a, axis, [(i, (i + k) % n) for i in range(n)])]
    ppermute x2, starting transfers between devices: 1.36 us -> 4.82 us  [HA(): return lax.ppermute(a, 'ha', [(0, 1), (1, 0)])]
    ppermute x25 -> x22, waiting for transfers between devices: 23.2 us -> 20.8 us  [ring(): return lambda a: lax.ppermute(a, axis, [(i, (i + k) % n) for i in range(n)])]
    slice x10 -> x14, local copies, waits for them, and re-layouts: 2 us -> 0.26 us  [the longest x2 0.07 us: with_counts(): u[:128]]
    concatenate x2 -> x3, other arithmetic: 1.6 us -> 0.07 us  [the longest x1 0.02 us: per_device(): jnp.concatenate([last[:128], g_ahead[128:256], last[128:], g_ahead[512:52...]
    ppermute x4, waiting for transfers between devices: 1.54 us -> 3.01 us  [C(): return lax.ppermute(a, 'c', [(0, 1), (1, 0)])]
  transfers between devices with their start and end apart: 35 -> 32, of which waited for: 10 -> 12; matrix products, arithmetic and copies ran while one was open for 3% -> 1% of each run, Pallas kernels for 6% -> 8%
where the time goes in v5:
time: 108 us
  starting transfers between devices  60.4 us (56%)
  waiting for transfers between devices  28.2 us (26%)
  Pallas kernels  17.1 us (16%)
    ppermute x22, starting transfers between devices, ring(): return lambda a: lax.ppermute(a, axis, [(i, (i + k) % n) for i in range(n)])  32.2 us
    ppermute x22, waiting for transfers between devices, ring(): return lambda a: lax.ppermute(a, axis, [(i, (i + k) % n) for i in range(n)])  20.8 us
    ppermute x4, starting transfers between devices, C(): return lax.ppermute(a, 'c', [(0, 1), (1, 0)])  14 us
    all_to_all x1, starting transfers between devices, per_device(): lax.all_to_all(packed, ('xl', 'c'), split_axis=0, concat_axis=0, tiled=True)  6.67 us
    ppermute x2, starting transfers between devices, HA(): return lax.ppermute(a, 'ha', [(0, 1), (1, 0)])  4.82 us
    pallas_call x1, Pallas kernels, gather_rows(): pl.pallas_call(gather_body, out_shape=(jax.ShapeDtypeStruct((CAP, d), BF1...  4.64 us
    pallas_call x1, Pallas kernels, mix(): pl.pallas_call(mix_body, out_shape=jax.ShapeDtypeStruct((n, 2048), BF16),...  4.07 us
    ppermute x4, waiting for transfers between devices, C(): return lax.ppermute(a, 'c', [(0, 1), (1, 0)])  3.01 us
  transfers between devices with their start and end apart: 32, of which 12 were waited for; matrix products, arithmetic and copies ran while one was open for 1% of the time, Pallas kernels for 8%

profile of v5, /device:TPU:1, one launch (start us, length us, event | category | flops | bytes accessed | tf_op | source)
XLA Modules:
  0.0 107.6 jit_solution(6055712066029288825)
XLA Ops:
  0.0 1.9 %prep.1 = (f32[8,1024]{1,0:T(8,128)S(1)}, bf16[4,104,384]{2,1,0:T(8,128)(2,1)}) custom-call(s32[8,1024]{1,0:T(8,128)} %bitcast.49, s32[8,1024]{1,0:T(8,128)} %bitcast.50, f32[8,1024]{1,0:T(8,128)} %bitcast.51, bf16[32,768]{1,0:T(8,128)(2,1)} %refs_3_.1, bf16[32,768]{1,0:T(8,128)(2,1)} %refs_4_.1, bf16[32,768]{1,0:T(8,128)(2,1)} %refs_5_.1), custom_call_target="tpu_custom_call" | custom-call | flops 33554432 | bytes 131072 | tf_op jit(solution)/shard_map/prep/pallas_call | solution.py:84
  1.9 6.7 %all-to-all-start = ((bf16[4,104,384]{2,1,0:T(8,128)(2,1)}), bf16[4,104,384]{2,1,0:T(8,128)(2,1)S(1)}, u32[]{:S(2)}, u32[]{:S(2)}) async-start(bf16[4,104,384]{2,1,0:T(8,128)(2,1)} %get-tuple-element.43), calls=%async_computation | async-start | bytes 638976 | tf_op jit(solution)/shard_map/all_to_all | solution.py:323
  8.7 4.6 %gather_rows.1 = (bf16[128,4096]{1,0:T(8,128)(2,1)S(1)}, f32[128,128]{1,0:T(8,128)S(1)}) custom-call(s32[6]{0:T(128)S(1)} %stack.23.where, bf16[1024,4096]{1,0:T(8,128)(2,1)} %tokens.1, f32[8,1024]{1,0:T(8,128)S(1)} %get-tuple-element.44.info), custom_call_target="tpu_custom_call" | custom-call | flops 1073741824 | bytes 8388608 | tf_op jit(solution)/shard_map/gather_rows/pallas_call | solution.py:127
  14.5 2.2 %collective-permute-start.1 = (bf16[128,384]{1,0:T(8,128)(2,1)S(1)}, bf16[128,384]{1,0:T(8,128)(2,1)S(1)}, u32[]{:S(2)}, u32[]{:S(2)}) collective-permute-start(bf16[128,384]{1,0:T(8,128)(2,1)S(1)} %pad_maximum_fusion.6), channel_id=1, source_target_pairs={{0,128},{64,192},{128,0},{192,64},{1,129},{65,193},{129,1},{193,65... | collective-permute-start | bytes 294920 | tf_op jit(solution)/shard_map/ppermute | solution.py:21
  19.5 4.0 %collective-permute-start.4 = (bf16[136,384]{1,0:T(8,128)(2,1)S(1)}, bf16[136,384]{1,0:T(8,128)(2,1)S(1)}, u32[]{:S(2)}, u32[]{:S(2)}) collective-permute-start(bf16[136,384]{1,0:T(8,128)(2,1)S(1)} %pad_maximum_fusion.5), channel_id=1, source_target_pairs={{0,28},{4,0},{8,4},{12,8},{16,12},{20,16},{24,20},{28,24},{1,29},{... | collective-permute-start | bytes 313352 | tf_op jit(solution)/shard_map/ppermute | solution.py:21
  23.9 2.8 %collective-permute-start.7 = (bf16[256,384]{1,0:T(8,128)(2,1)S(1)}, bf16[256,384]{1,0:T(8,128)(2,1)S(1)}, u32[]{:S(2)}, u32[]{:S(2)}) collective-permute-start(bf16[256,384]{1,0:T(8,128)(2,1)S(1)} %pad_maximum_fusion.4), channel_id=1, source_target_pairs={{0,1},{1,0},{2,3},{3,2},{4,5},{5,4},{6,7},{7,6},{8,9},{9,8},{10,11... | collective-permute-start | bytes 589832 | tf_op jit(solution)/shard_map/ppermute | solution.py:41
  26.9 2.7 %collective-permute-start.6 = (bf16[136,384]{1,0:T(8,128)(2,1)S(1)}, bf16[136,384]{1,0:T(8,128)(2,1)S(1)}, u32[]{:S(2)}, u32[]{:S(2)}) collective-permute-start(bf16[136,384]{1,0:T(8,128)(2,1)S(1)} %collective-permute-done.4), channel_id=1, source_target_pairs={{0,28},{4,0},{8,4},{12,8},{16,12},{20,16},{24,20},{28,24},{1,29},{... | collective-permute-start | bytes 313352 | tf_op jit(solution)/shard_map/ppermute | solution.py:21
  32.6 2.2 %collective-permute-start.11 = (bf16[680,384]{1,0:T(8,128)(2,1)S(1)}, bf16[680,384]{1,0:T(8,128)(2,1)S(1)}, u32[]{:S(2)}, u32[]{:S(2)}) collective-permute-start(bf16[680,384]{1,0:T(8,128)(2,1)S(1)} %constant_dynamic-update-slice_fusion.12.first.refs_0_), channel_id=1, source_target_pairs={{0,192},{64,0},{128,64},{192,128},{1,193},{65,1},{129,65},{193,129... | collective-permute-start | bytes 1566728 | tf_op jit(solution)/shard_map/ppermute | solution.py:21
  34.9 2.8 %collective-permute-start.9 = (bf16[648,384]{1,0:T(8,128)(2,1)S(1)}, bf16[648,384]{1,0:T(8,128)(2,1)S(1)}, u32[]{:S(2)}, u32[]{:S(2)}) collective-permute-start(bf16[648,384]{1,0:T(8,128)(2,1)S(1)} %constant_dynamic-update-slice_fusion.6), channel_id=1, source_target_pairs={{0,28},{4,0},{8,4},{12,8},{16,12},{20,16},{24,20},{28,24},{1,29},{... | collective-permute-start | bytes 1493000 | tf_op jit(solution)/shard_map/ppermute | solution.py:21
  38.0 6.5 %collective-permute-done.9.refs_1_ = bf16[648,384]{1,0:T(8,128)(2,1)S(1)} collective-permute-done((bf16[648,384]{1,0:T(8,128)(2,1)S(1)}, bf16[648,384]{1,0:T(8,128)(2,1)S(1)}, u32[]{:S(2)}, u32[]{:S(2)}) %collective-permute-start.9) | collective-permute-done | bytes 497696 | tf_op jit(solution)/shard_map/ppermute | solution.py:21
  44.5 4.8 %collective-permute-start.17 = (bf16[128,4096]{1,0:T(8,128)(2,1)S(1)}, bf16[128,4096]{1,0:T(8,128)(2,1)S(1)}, u32[]{:S(2)}, u32[]{:S(2)}) collective-permute-start(bf16[128,4096]{1,0:T(8,128)(2,1)S(1)} %get-tuple-element.51.xo), channel_id=1, source_target_pairs={{0,2},{2,0},{1,3},{3,1},{4,6},{6,4},{5,7},{7,5},{8,10},{10,8},{9,1... | collective-permute-start | bytes 3145736 | tf_op jit(solution)/shard_map/ppermute | solution.py:33
  49.8 3.5 %collective-permute-start.18 = (bf16[128,4096]{1,0:T(8,128)(2,1)S(1)}, bf16[128,4096]{1,0:T(8,128)(2,1)S(1)}, u32[]{:S(2)}, u32[]{:S(2)}) collective-permute-start(bf16[128,4096]{1,0:T(8,128)(2,1)S(1)} %collective-permute-done.12.xn), channel_id=1, source_target_pairs={{0,2},{2,0},{1,3},{3,1},{4,6},{6,4},{5,7},{7,5},{8,10},{10,8},{9,1... | collective-permute-start | bytes 3145736 | tf_op jit(solution)/shard_map/ppermute | solution.py:33
  53.5 2.7 %collective-permute-start.16 = (bf16[568,384]{1,0:T(8,128)(2,1)S(1)}, bf16[568,384]{1,0:T(8,128)(2,1)S(1)}, u32[]{:S(2)}, u32[]{:S(2)}) collective-permute-start(bf16[568,384]{1,0:T(8,128)(2,1)S(1)} %constant_dynamic-update-slice_fusion.22), channel_id=1, source_target_pairs={{0,192},{64,0},{128,64},{192,128},{1,193},{65,1},{129,65},{193,129... | collective-permute-start | bytes 1308680 | tf_op jit(solution)/shard_map/ppermute | solution.py:21
  56.2 2.9 %collective-permute-start.14 = (bf16[512,384]{1,0:T(8,128)(2,1)S(1)}, bf16[512,384]{1,0:T(8,128)(2,1)S(1)}, u32[]{:S(2)}, u32[]{:S(2)}) collective-permute-start(bf16[512,384]{1,0:T(8,128)(2,1)S(1)} %slice.178), channel_id=1, source_target_pairs={{0,28},{4,0},{8,4},{12,8},{16,12},{20,16},{24,20},{28,24},{1,29},{... | collective-permute-start | bytes 1179656 | tf_op jit(solution)/shard_map/ppermute | solution.py:21
  59.1 7.9 %collective-permute-done.14.refs_2_ = bf16[512,384]{1,0:T(8,128)(2,1)S(1)} collective-permute-done((bf16[512,384]{1,0:T(8,128)(2,1)S(1)}, bf16[512,384]{1,0:T(8,128)(2,1)S(1)}, u32[]{:S(2)}, u32[]{:S(2)}) %collective-permute-start.14) | collective-permute-done | bytes 393248 | tf_op jit(solution)/shard_map/ppermute | solution.py:21
  68.0 2.9 %collective-permute-start.23 = (bf16[512,384]{1,0:T(8,128)(2,1)S(1)}, bf16[512,384]{1,0:T(8,128)(2,1)S(1)}, u32[]{:S(2)}, u32[]{:S(2)}) collective-permute-start(bf16[512,384]{1,0:T(8,128)(2,1)S(1)} %collective-permute-done.14.refs_2_), channel_id=1, source_target_pairs={{0,28},{4,0},{8,4},{12,8},{16,12},{20,16},{24,20},{28,24},{1,29},{... | collective-permute-start | bytes 1179656 | tf_op jit(solution)/shard_map/ppermute | solution.py:21
  73.4 2.3 %gate_up_near.1 = (f32[512,384]{1,0:T(8,128)S(1)}, bf16[512,640]{1,0:T(8,128)(2,1)S(1)}) custom-call(bf16[680,384]{1,0:T(8,128)(2,1)S(1)} %constant_dynamic-update-slice_fusion.12.first.refs_0_, bf16[272,384]{1,0:T(8,128)(2,1)S(1)} %pad_maximum_fusion.2.second.refs_1_, bf16[136,384]{1,0:T(8,128)(2,1)S(1)} %slice.191.last.refs_2_, ...), custom_call_target="tpu_custom_call" | custom-call | flops 1358954496 | bytes 8388608 | tf_op jit(solution)/shard_map/gate_up_near/pallas_call | solution.py:163
  75.7 3.2 %collective-permute-done.21.k_far = bf16[136,384]{1,0:T(8,128)(2,1)S(1)} collective-permute-done((bf16[136,384]{1,0:T(8,128)(2,1)S(1)}, bf16[136,384]{1,0:T(8,128)(2,1)S(1)}, u32[]{:S(2)}, u32[]{:S(2)}) %collective-permute-start.21) | collective-permute-done | bytes 104480 | tf_op jit(solution)/shard_map/ppermute | solution.py:21
  80.7 2.3 %collective-permute-start.28 = (bf16[256,384]{1,0:T(8,128)(2,1)S(1)}, bf16[256,384]{1,0:T(8,128)(2,1)S(1)}, u32[]{:S(2)}, u32[]{:S(2)}) collective-permute-start(bf16[256,384]{1,0:T(8,128)(2,1)S(1)} %slice.194), channel_id=1, source_target_pairs={{0,28},{4,0},{8,4},{12,8},{16,12},{20,16},{24,20},{28,24},{1,29},{... | collective-permute-start | bytes 589832 | tf_op jit(solution)/shard_map/ppermute | solution.py:21
  84.5 2.0 %collective-permute-start.25 = (bf16[256,192]{1,0:T(8,128)(2,1)S(1)}, bf16[256,192]{1,0:T(8,128)(2,1)S(1)}, u32[]{:S(2)}, u32[]{:S(2)}) collective-permute-start(bf16[256,192]{1,0:T(8,128)(2,1)S(1)} %get-tuple-element.70.own), channel_id=1, source_target_pairs={{0,1},{1,0},{2,3},{3,2},{4,5},{5,4},{6,7},{7,6},{8,9},{9,8},{10,11... | collective-permute-start | bytes 294920 | tf_op jit(solution)/shard_map/ppermute | solution.py:41
  86.5 1.8 %collective-permute-start.26 = (bf16[256,192]{1,0:T(8,128)(2,1)S(1)}, bf16[256,192]{1,0:T(8,128)(2,1)S(1)}, u32[]{:S(2)}, u32[]{:S(2)}) collective-permute-start(bf16[256,192]{1,0:T(8,128)(2,1)S(1)} %get-tuple-element.71), channel_id=1, source_target_pairs={{0,33},{1,32},{32,1},{33,0},{2,35},{3,34},{34,3},{35,2},{4,37},{5,... | collective-permute-start | bytes 294920 | tf_op jit(solution)/shard_map/ppermute | solution.py:313
  91.8 5.4 %collective-permute-start.29 = (bf16[256,768]{1,0:T(8,128)(2,1)S(1)}, bf16[256,768]{1,0:T(8,128)(2,1)S(1)}, u32[]{:S(2)}, u32[]{:S(2)}) collective-permute-start(bf16[256,768]{1,0:T(8,128)(2,1)S(1)} %pad_maximum_fusion), channel_id=1, source_target_pairs={{0,2},{2,0},{1,3},{3,1},{4,6},{6,4},{5,7},{7,5},{8,10},{10,8},{9,1... | collective-permute-start | bytes 1179656 | tf_op jit(solution)/shard_map/ppermute | solution.py:33
  98.6 2.9 %down.1 = f32[256,1024]{1,0:T(8,128)S(1)} custom-call(s32[6]{0:T(128)S(1)} %stack.23.where, bf16[256,192]{1,0:T(8,128)(2,1)S(1)} %get-tuple-element.70.own, bf16[256,192]{1,0:T(8,128)(2,1)S(1)} %collective-permute-done.24.near, bf16[256,192]{1,0:T(8,128)(2,1)S(1)} %collective-permute-done.25.ha, bf16[256,192]{1,0:T(8,128)(2,1)S(1)} %collective-permute-done.26.far, ...), custom_call_target="tpu_custom_call" | custom-call | flops 805306368 | bytes 5242880 | tf_op jit(solution)/shard_map/down/pallas_call | solution.py:251
  103.5 4.1 %mix.1 = bf16[1024,2048]{1,0:T(8,128)(2,1)} custom-call(s32[6]{0:T(128)S(1)} %stack.23.where, f32[128,1024]{1,0:T(8,128)S(1)} %get-tuple-element.82.mine, f32[128,1024]{1,0:T(8,128)S(1)} %collective-permute-done.30.theirs, f32[8,1024]{1,0:T(8,128)S(1)} %get-tuple-element.44.info, f32[128,128]{1,0:T(8,128)S(1)} %get-tuple-element.79.slot_route, ...), custom_call_target="tpu_custom_call" | custom-call | flops 536870912 | bytes 6291456 | tf_op jit(solution)/shard_map/mix/pallas_call | solution.py:281
  (98 shorter events, 22.1 us)
Async XLA Ops:
  1.9 12.5 %all-to-all-start = ((bf16[4,104,384]{2,1,0:T(8,128)(2,1)}), bf16[4,104,384]{2,1,0:T(8,128)(2,1)S(1)}, u32[]{:S(2)}, u32[]{:S(2)}) async-start(bf16[4,104,384]{2,1,0:T(8,128)(2,1)} %get-tuple-element.43), calls=%async_computation | async-start | bytes 638976 | tf_op jit(solution)/shard_map/all_to_all | solution.py:323
  14.4 9.1 %collective-permute-start = (bf16[128,384]{1,0:T(8,128)(2,1)S(1)}, bf16[128,384]{1,0:T(8,128)(2,1)S(1)}, u32[]{:S(2)}, u32[]{:S(2)}) collective-permute-start(bf16[128,384]{1,0:T(8,128)(2,1)S(1)} %pad_maximum_fusion.6), channel_id=1, source_target_pairs={{0,64},{64,128},{128,192},{192,0},{1,65},{65,129},{129,193},{193,1... | collective-permute-start | bytes 294920 | tf_op jit(solution)/shard_map/ppermute | solution.py:21
  14.5 9.1 %collective-permute-start.1 = (bf16[128,384]{1,0:T(8,128)(2,1)S(1)}, bf16[128,384]{1,0:T(8,128)(2,1)S(1)}, u32[]{:S(2)}, u32[]{:S(2)}) collective-permute-start(bf16[128,384]{1,0:T(8,128)(2,1)S(1)} %pad_maximum_fusion.6), channel_id=1, source_target_pairs={{0,128},{64,192},{128,0},{192,64},{1,129},{65,193},{129,1},{193,65... | collective-permute-start | bytes 294920 | tf_op jit(solution)/shard_map/ppermute | solution.py:21
  16.7 6.9 %collective-permute-start.2 = (bf16[128,384]{1,0:T(8,128)(2,1)S(1)}, bf16[128,384]{1,0:T(8,128)(2,1)S(1)}, u32[]{:S(2)}, u32[]{:S(2)}) collective-permute-start(bf16[128,384]{1,0:T(8,128)(2,1)S(1)} %pad_maximum_fusion.6), channel_id=1, source_target_pairs={{0,192},{64,0},{128,64},{192,128},{1,193},{65,1},{129,65},{193,129... | collective-permute-start | bytes 294920 | tf_op jit(solution)/shard_map/ppermute | solution.py:21
  17.8 8.9 %collective-permute-start.3 = (bf16[136,384]{1,0:T(8,128)(2,1)S(1)}, bf16[136,384]{1,0:T(8,128)(2,1)S(1)}, u32[]{:S(2)}, u32[]{:S(2)}) collective-permute-start(bf16[136,384]{1,0:T(8,128)(2,1)S(1)} %pad_maximum_fusion.5), channel_id=1, source_target_pairs={{0,4},{4,8},{8,12},{12,16},{16,20},{20,24},{24,28},{28,0},{1,5},{5... | collective-permute-start | bytes 313352 | tf_op jit(solution)/shard_map/ppermute | solution.py:21
  19.5 7.2 %collective-permute-start.4 = (bf16[136,384]{1,0:T(8,128)(2,1)S(1)}, bf16[136,384]{1,0:T(8,128)(2,1)S(1)}, u32[]{:S(2)}, u32[]{:S(2)}) collective-permute-start(bf16[136,384]{1,0:T(8,128)(2,1)S(1)} %pad_maximum_fusion.5), channel_id=1, source_target_pairs={{0,28},{4,0},{8,4},{12,8},{16,12},{20,16},{24,20},{28,24},{1,29},{... | collective-permute-start | bytes 313352 | tf_op jit(solution)/shard_map/ppermute | solution.py:21
  23.9 8.0 %collective-permute-start.7 = (bf16[256,384]{1,0:T(8,128)(2,1)S(1)}, bf16[256,384]{1,0:T(8,128)(2,1)S(1)}, u32[]{:S(2)}, u32[]{:S(2)}) collective-permute-start(bf16[256,384]{1,0:T(8,128)(2,1)S(1)} %pad_maximum_fusion.4), channel_id=1, source_target_pairs={{0,1},{1,0},{2,3},{3,2},{4,5},{5,4},{6,7},{7,6},{8,9},{9,8},{10,11... | collective-permute-start | bytes 589832 | tf_op jit(solution)/shard_map/ppermute | solution.py:41
  29.6 19.7 %collective-permute-start.12 = (bf16[128,4096]{1,0:T(8,128)(2,1)S(1)}, bf16[128,4096]{1,0:T(8,128)(2,1)S(1)}, u32[]{:S(2)}, u32[]{:S(2)}) collective-permute-start(bf16[128,4096]{1,0:T(8,128)(2,1)S(1)} %get-tuple-element.51.xo), channel_id=1, source_target_pairs={{0,32},{2,35},{32,1},{34,2},{1,33},{3,34},{33,0},{35,3},{4,36},{6,... | collective-permute-start | bytes 3145736 | tf_op jit(solution)/shard_map/ppermute | solution.py:49
  32.0 17.3 %collective-permute-start.10 = (bf16[680,384]{1,0:T(8,128)(2,1)S(1)}, bf16[680,384]{1,0:T(8,128)(2,1)S(1)}, u32[]{:S(2)}, u32[]{:S(2)}) collective-permute-start(bf16[680,384]{1,0:T(8,128)(2,1)S(1)} %constant_dynamic-update-slice_fusion.12.first.refs_0_), channel_id=1, source_target_pairs={{0,64},{64,128},{128,192},{192,0},{1,65},{65,129},{129,193},{193,1... | collective-permute-start | bytes 1566728 | tf_op jit(solution)/shard_map/ppermute | solution.py:21
  32.6 16.7 %collective-permute-start.11 = (bf16[680,384]{1,0:T(8,128)(2,1)S(1)}, bf16[680,384]{1,0:T(8,128)(2,1)S(1)}, u32[]{:S(2)}, u32[]{:S(2)}) collective-permute-start(bf16[680,384]{1,0:T(8,128)(2,1)S(1)} %constant_dynamic-update-slice_fusion.12.first.refs_0_), channel_id=1, source_target_pairs={{0,192},{64,0},{128,64},{192,128},{1,193},{65,1},{129,65},{193,129... | collective-permute-start | bytes 1566728 | tf_op jit(solution)/shard_map/ppermute | solution.py:21
  34.9 9.6 %collective-permute-start.9 = (bf16[648,384]{1,0:T(8,128)(2,1)S(1)}, bf16[648,384]{1,0:T(8,128)(2,1)S(1)}, u32[]{:S(2)}, u32[]{:S(2)}) collective-permute-start(bf16[648,384]{1,0:T(8,128)(2,1)S(1)} %constant_dynamic-update-slice_fusion.6), channel_id=1, source_target_pairs={{0,28},{4,0},{8,4},{12,8},{16,12},{20,16},{24,20},{28,24},{1,29},{... | collective-permute-start | bytes 1493000 | tf_op jit(solution)/shard_map/ppermute | solution.py:21
  37.8 11.6 %collective-permute-start.8 = (bf16[648,384]{1,0:T(8,128)(2,1)S(1)}, bf16[648,384]{1,0:T(8,128)(2,1)S(1)}, u32[]{:S(2)}, u32[]{:S(2)}) collective-permute-start(bf16[648,384]{1,0:T(8,128)(2,1)S(1)} %constant_dynamic-update-slice_fusion), channel_id=1, source_target_pairs={{0,4},{4,8},{8,12},{12,16},{16,20},{20,24},{24,28},{28,0},{1,5},{5... | collective-permute-start | bytes 1493000 | tf_op jit(solution)/shard_map/ppermute | solution.py:21
  44.5 11.7 %collective-permute-start.17 = (bf16[128,4096]{1,0:T(8,128)(2,1)S(1)}, bf16[128,4096]{1,0:T(8,128)(2,1)S(1)}, u32[]{:S(2)}, u32[]{:S(2)}) collective-permute-start(bf16[128,4096]{1,0:T(8,128)(2,1)S(1)} %get-tuple-element.51.xo), channel_id=1, source_target_pairs={{0,2},{2,0},{1,3},{3,1},{4,6},{6,4},{5,7},{7,5},{8,10},{10,8},{9,1... | collective-permute-start | bytes 3145736 | tf_op jit(solution)/shard_map/ppermute | solution.py:33
  49.4 17.7 %collective-permute-start.13 = (bf16[648,384]{1,0:T(8,128)(2,1)S(1)}, bf16[648,384]{1,0:T(8,128)(2,1)S(1)}, u32[]{:S(2)}, u32[]{:S(2)}) collective-permute-start(bf16[648,384]{1,0:T(8,128)(2,1)S(1)} %collective-permute-done.8.refs_7_), channel_id=1, source_target_pairs={{0,4},{4,8},{8,12},{12,16},{16,20},{20,24},{24,28},{28,0},{1,5},{5... | collective-permute-start | bytes 1493000 | tf_op jit(solution)/shard_map/ppermute | solution.py:21
  49.8 18.0 %collective-permute-start.18 = (bf16[128,4096]{1,0:T(8,128)(2,1)S(1)}, bf16[128,4096]{1,0:T(8,128)(2,1)S(1)}, u32[]{:S(2)}, u32[]{:S(2)}) collective-permute-start(bf16[128,4096]{1,0:T(8,128)(2,1)S(1)} %collective-permute-done.12.xn), channel_id=1, source_target_pairs={{0,2},{2,0},{1,3},{3,1},{4,6},{6,4},{5,7},{7,5},{8,10},{10,8},{9,1... | collective-permute-start | bytes 3145736 | tf_op jit(solution)/shard_map/ppermute | solution.py:33
  53.4 14.4 %collective-permute-start.15 = (bf16[656,384]{1,0:T(8,128)(2,1)S(1)}, bf16[656,384]{1,0:T(8,128)(2,1)S(1)}, u32[]{:S(2)}, u32[]{:S(2)}) collective-permute-start(bf16[656,384]{1,0:T(8,128)(2,1)S(1)} %get-tuple-element.93), channel_id=1, source_target_pairs={{0,64},{64,128},{128,192},{192,0},{1,65},{65,129},{129,193},{193,1... | collective-permute-start | bytes 1511432 | tf_op jit(solution)/shard_map/ppermute | solution.py:21
  53.5 13.6 %collective-permute-start.16 = (bf16[568,384]{1,0:T(8,128)(2,1)S(1)}, bf16[568,384]{1,0:T(8,128)(2,1)S(1)}, u32[]{:S(2)}, u32[]{:S(2)}) collective-permute-start(bf16[568,384]{1,0:T(8,128)(2,1)S(1)} %constant_dynamic-update-slice_fusion.22), channel_id=1, source_target_pairs={{0,192},{64,0},{128,64},{192,128},{1,193},{65,1},{129,65},{193,129... | collective-permute-start | bytes 1308680 | tf_op jit(solution)/shard_map/ppermute | solution.py:21
  56.2 10.8 %collective-permute-start.14 = (bf16[512,384]{1,0:T(8,128)(2,1)S(1)}, bf16[512,384]{1,0:T(8,128)(2,1)S(1)}, u32[]{:S(2)}, u32[]{:S(2)}) collective-permute-start(bf16[512,384]{1,0:T(8,128)(2,1)S(1)} %slice.178), channel_id=1, source_target_pairs={{0,28},{4,0},{8,4},{12,8},{16,12},{20,16},{24,20},{28,24},{1,29},{... | collective-permute-start | bytes 1179656 | tf_op jit(solution)/shard_map/ppermute | solution.py:21
  67.9 12.0 %collective-permute-start.22 = (bf16[512,384]{1,0:T(8,128)(2,1)S(1)}, bf16[512,384]{1,0:T(8,128)(2,1)S(1)}, u32[]{:S(2)}, u32[]{:S(2)}) collective-permute-start(bf16[512,384]{1,0:T(8,128)(2,1)S(1)} %slice.192), channel_id=1, source_target_pairs={{0,4},{4,8},{8,12},{12,16},{16,20},{20,24},{24,28},{28,0},{1,5},{5... | collective-permute-start | bytes 1179656 | tf_op jit(solution)/shard_map/ppermute | solution.py:21
  68.0 11.9 %collective-permute-start.23 = (bf16[512,384]{1,0:T(8,128)(2,1)S(1)}, bf16[512,384]{1,0:T(8,128)(2,1)S(1)}, u32[]{:S(2)}, u32[]{:S(2)}) collective-permute-start(bf16[512,384]{1,0:T(8,128)(2,1)S(1)} %collective-permute-done.14.refs_2_), channel_id=1, source_target_pairs={{0,28},{4,0},{8,4},{12,8},{16,12},{20,16},{24,20},{28,24},{1,29},{... | collective-permute-start | bytes 1179656 | tf_op jit(solution)/shard_map/ppermute | solution.py:21
  70.9 8.9 %collective-permute-start.20 = (bf16[280,384]{1,0:T(8,128)(2,1)S(1)}, bf16[280,384]{1,0:T(8,128)(2,1)S(1)}, u32[]{:S(2)}, u32[]{:S(2)}) collective-permute-start(bf16[280,384]{1,0:T(8,128)(2,1)S(1)} %pad_maximum_fusion.1), channel_id=1, source_target_pairs={{0,192},{64,0},{128,64},{192,128},{1,193},{65,1},{129,65},{193,129... | collective-permute-start | bytes 645128 | tf_op jit(solution)/shard_map/ppermute | solution.py:21
  72.0 7.8 %collective-permute-start.19 = (bf16[264,384]{1,0:T(8,128)(2,1)S(1)}, bf16[264,384]{1,0:T(8,128)(2,1)S(1)}, u32[]{:S(2)}, u32[]{:S(2)}) collective-permute-start(bf16[264,384]{1,0:T(8,128)(2,1)S(1)} %pad_maximum_fusion.3), channel_id=1, source_target_pairs={{0,64},{64,128},{128,192},{192,0},{1,65},{65,129},{129,193},{193,1... | collective-permute-start | bytes 608264 | tf_op jit(solution)/shard_map/ppermute | solution.py:21
  79.9 11.8 %collective-permute-start.27 = (bf16[256,384]{1,0:T(8,128)(2,1)S(1)}, bf16[256,384]{1,0:T(8,128)(2,1)S(1)}, u32[]{:S(2)}, u32[]{:S(2)}) collective-permute-start(bf16[256,384]{1,0:T(8,128)(2,1)S(1)} %slice.193), channel_id=1, source_target_pairs={{0,4},{4,8},{8,12},{12,16},{16,20},{20,24},{24,28},{28,0},{1,5},{5... | collective-permute-start | bytes 589832 | tf_op jit(solution)/shard_map/ppermute | solution.py:21
  80.7 11.0 %collective-permute-start.28 = (bf16[256,384]{1,0:T(8,128)(2,1)S(1)}, bf16[256,384]{1,0:T(8,128)(2,1)S(1)}, u32[]{:S(2)}, u32[]{:S(2)}) collective-permute-start(bf16[256,384]{1,0:T(8,128)(2,1)S(1)} %slice.194), channel_id=1, source_target_pairs={{0,28},{4,0},{8,4},{12,8},{16,12},{20,16},{24,20},{28,24},{1,29},{... | collective-permute-start | bytes 589832 | tf_op jit(solution)/shard_map/ppermute | solution.py:21
  (8 other events, 40.2 us)

commit v6 on v5

--- a/solution.py
+++ b/solution.py
@@ -50,7 +50,7 @@
 
 
 def prep_body(*refs):
-    far, (info, packed), near, arrive = refs[:6], refs[6:8], refs[8:14], refs[14]
+    where, far, (info, packed), near, arrive = refs[0], refs[1:7], refs[7:9], refs[9:15], refs[15]
     copies = [pltpu.make_async_copy(f, n, arrive.at[i]) for i, (f, n) in enumerate(zip(far, near))]
     for copy in copies:
         copy.start()
@@ -73,25 +73,27 @@
     total = jnp.sum(chosen, axis=1, keepdims=True)
     for q in range(4):
         at = slice(q * 192, q * 192 + 192)
-        packed[q, 0:32, :] = jnp.concatenate([gate[:, at], up[:, at]], axis=1)
-        packed[q, 32:40, :] = jnp.broadcast_to(total, (8, 384)).astype(BF16)
-        packed[q, 40:72, :] = down_rows[:, :384]
-        packed[q, 72:104, :] = down_rows[:, 384:]
-
-
-def prep(ids, keep, rw, gate, up, down_rows):
+        to = where[2] * 2 + where[3]
+        to = q + to - 2 * (q & to)
+        packed[to, 0:32, :] = jnp.concatenate([gate[:, at], up[:, at]], axis=1)
+        packed[to, 32:40, :] = jnp.broadcast_to(total, (8, 384)).astype(BF16)
+        packed[to, 40:72, :] = down_rows[:, :384]
+        packed[to, 72:104, :] = down_rows[:, 384:]
+
+
+def prep(where, ids, keep, rw, gate, up, down_rows):
     n = ids.shape[1]
     return pl.pallas_call(
         prep_body,
         out_shape=(jax.ShapeDtypeStruct((8, n), F32), jax.ShapeDtypeStruct((4, 104, 384), BF16)),
-        in_specs=[whole(pltpu.HBM)] * 6,
+        in_specs=[whole(pltpu.SMEM)] + [whole(pltpu.HBM)] * 6,
         out_specs=(whole(), whole()),
         scratch_shapes=[VMEM(a.shape, a.dtype) for a in (ids, keep, rw, gate, up, down_rows)]
         + [pltpu.SemaphoreType.DMA((6,))],
         compiler_params=pltpu.CompilerParams(vmem_limit_bytes=12 << 20),
         cost_estimate=pl.CostEstimate(flops=2 * 16 * n * n, bytes_accessed=4 * 32 * n, transcendentals=0),
         name="prep",
-    )(ids, keep, rw, gate, up, down_rows)
+    )(where, ids, keep, rw, gate, up, down_rows)
 
 
 def table(info):
@@ -319,8 +321,11 @@
     shift = lax.rem(2 * ha - y + NY, NY)
     where = jnp.stack([y, z, xl, c, me, lax.axis_size(WA) * CAP // 2])
     sources = (expert_ids.T, keep_mask.T, route_weight.T, gate_weight, up_weight, down_weight)
-    info, packed = prep(*(pltpu.with_memory_space_constraint(a, pltpu.HBM) for a in sources))
-    arrived = lax.all_to_all(packed, ("xl", "c"), split_axis=0, concat_axis=0, tiled=True)
+    info, packed = prep(where, *(pltpu.with_memory_space_constraint(a, pltpu.HBM) for a in sources))
+    both = [(k, 3 - k) for k in range(4)]
+    tiles = [packed[0], C(packed[1]), XL(packed[2]), lax.ppermute(packed[3], ("xl", "c"), both)]
+    tiles = [jnp.where(c == 0, tiles[k], tiles[k ^ 1]) for k in range(4)]
+    arrived = jnp.stack([jnp.where(xl == 0, tiles[k], tiles[k ^ 2]) for k in range(4)])
     slot_rows, slot_route = gather_rows(where, pltpu.with_memory_space_constraint(tokens, pltpu.HBM), info)
 
     lane = lax.broadcasted_iota(I32, (8, 384), 1)
@@ -349,29 +354,33 @@
         return jnp.concatenate([p[:64], q[:64], p[64:], q[64:]], axis=0)
 
     d_swap = HA(halves(ordered[2], ordered[3]))
-    b2, a2, d_swap = together(b2, a2, d_swap)
+    core_rows = C(slot_rows)
+    b2, a2, d_swap, core_rows = together(b2, a2, d_swap, core_rows)
 
     d0 = jnp.concatenate([halves(ordered[0], ordered[1]), d_swap], axis=0)
     up1, dn1 = Z(1)(jnp.concatenate([d0, b2], axis=0)), Z(-1)(jnp.concatenate([d0, a2], axis=0))
     first = with_counts([unit, b1, a1, b2, a2])
     f_back, f_ahead = Y(1)(first), Y(-1)(first)
-    up1, dn1, f_back, f_ahead, neighbour_rows = together(up1, dn1, f_back, f_ahead, neighbour_rows)
-
-    up2, dn2 = Z(1)(up1), Z(-1)(dn1[:512])
+    up1, dn1 = together(up1, dn1)
+    f_back, f_ahead, neighbour_rows = together(f_back, f_ahead, neighbour_rows)
+
+    up2, dn2 = Z(1)(up1[:576]), Z(-1)(jnp.concatenate([dn1[:512], dn1[576:]], axis=0))
     second = with_counts([up1[512:], dn1[512:]])
     g_back = Y(1)(jnp.concatenate([second[:256], f_back[:384], second[256:]], axis=0))
     g_ahead = Y(-1)(jnp.concatenate([second[:256], f_ahead[384:640], second[256:], f_ahead[640:]], axis=0))
-    core_rows, far_rows = C(slot_rows), C(neighbour_rows)
-    up2, dn2, g_back, g_ahead, core_rows, far_rows = together(up2, dn2, g_back, g_ahead, core_rows, far_rows)
-
-    last = up2[512:]
-    up3, dn3 = Z(1)(up2[:512]), Z(-1)(dn2)
+    far_rows = C(neighbour_rows)
+    up2, dn2 = together(up2, dn2)
+    g_back, g_ahead, far_rows = together(g_back, g_ahead, far_rows)
+
+    last = jnp.concatenate([up2[512:], dn2[512:]], axis=0)
+    up3, dn3 = Z(1)(up2[:512]), Z(-1)(dn2[:512])
     k_back = Y(1)(jnp.concatenate([last[:128], g_back[:128], last[128:]], axis=0))
     k_ahead = Y(-1)(jnp.concatenate([last[:128], g_ahead[128:256], last[128:], g_ahead[512:528]], axis=0))
     k_far = Y(2)(last)
     near = (first, second, last, f_back, f_ahead, g_back, g_ahead)
     partial, x_far = gate_up_near(*near, slot_rows, core_rows, neighbour_rows, far_rows)
-    k_back, k_ahead, k_far, up3, dn3, partial, x_far = together(k_back, k_ahead, k_far, up3, dn3, partial, x_far)
+    k_back, k_ahead, k_far, partial, x_far = together(k_back, k_ahead, k_far, partial, x_far)
+    up3, dn3 = together(up3, dn3)
 
     de0, de1 = Z(1)(up3[:256]), Z(-1)(dn3[256:])
     h_own, h_other, limit = gate_up_far(where, partial, x_far, k_back, k_ahead, k_far, *near)

time: 108 us -> 105 us (0.972)
  starting transfers between devices: 60.4 us -> 52.5 us
  waiting for transfers between devices: 28.2 us -> 32.7 us
    all_to_all x1 -> x0, starting transfers between devices: 6.67 us -> none  [per_device(): lax.all_to_all(packed, ('xl', 'c'), split_axis=0, concat_axis=0, tiled=True)]
    ppermute x22, waiting for transfers between devices: 20.8 us -> 25.6 us  [ring(): return lambda a: lax.ppermute(a, axis, [(i, (i + k) % n) for i in range(n)])]
    ppermute x22, starting transfers between devices: 32.2 us -> 30 us  [ring(): return lambda a: lax.ppermute(a, axis, [(i, (i + k) % n) for i in range(n)])]
    ppermute x0 -> x1, starting transfers between devices: none -> 1.73 us  [per_device(): lax.ppermute(packed[3], ('xl', 'c'), both)]
    ppermute x2, starting transfers between devices: 4.82 us -> 3.16 us  [HA(): return lax.ppermute(a, 'ha', [(0, 1), (1, 0)])]
    ppermute x2, waiting for transfers between devices: 1.74 us -> 3.14 us  [HA(): return lax.ppermute(a, 'ha', [(0, 1), (1, 0)])]
    ppermute x1 -> x2, starting transfers between devices: 0.19 us -> 1.37 us  [XL(): return lax.ppermute(a, 'xl', [(0, 1), (1, 0)])]
    ppermute x4 -> x5, starting transfers between devices: 14 us -> 13 us  [C(): return lax.ppermute(a, 'c', [(0, 1), (1, 0)])]
  transfers between devices with their start and end apart: 32 -> 34, of which waited for: 12 -> 13; matrix products, arithmetic and copies ran while one was open for 1% -> 1% of each run, Pallas kernels for 8% -> 8%
where the time goes in v6:
time: 105 us; the launch traced here: 104 us
  starting transfers between devices  52.5 us (50%)
  waiting for transfers between devices  32.7 us (31%)
  Pallas kernels  17 us (16%)
    ppermute x22, starting transfers between devices, ring(): return lambda a: lax.ppermute(a, axis, [(i, (i + k) % n) for i in range(n)])  30 us
    ppermute x22, waiting for transfers between devices, ring(): return lambda a: lax.ppermute(a, axis, [(i, (i + k) % n) for i in range(n)])  25.6 us
    ppermute x5, starting transfers between devices, C(): return lax.ppermute(a, 'c', [(0, 1), (1, 0)])  13 us
    pallas_call x1, Pallas kernels, gather_rows(): pl.pallas_call(gather_body, out_shape=(jax.ShapeDtypeStruct((CAP, d), BF1...  4.65 us
    pallas_call x1, Pallas kernels, mix(): pl.pallas_call(mix_body, out_shape=jax.ShapeDtypeStruct((n, 2048), BF16),...  4.07 us
    ppermute x2, starting transfers between devices, HA(): return lax.ppermute(a, 'ha', [(0, 1), (1, 0)])  3.16 us
    ppermute x2, waiting for transfers between devices, HA(): return lax.ppermute(a, 'ha', [(0, 1), (1, 0)])  3.14 us
    ppermute x5, waiting for transfers between devices, C(): return lax.ppermute(a, 'c', [(0, 1), (1, 0)])  3.01 us
  transfers between devices with their start and end apart: 34, of which 13 were waited for; matrix products, arithmetic and copies ran while one was open for 1% of the time, Pallas kernels for 8%

profile of v6, /device:TPU:1, one launch (start us, length us, event | category | flops | bytes accessed | tf_op | source)
XLA Modules:
  0.0 104.4 jit_solution(18368002734288678569)
XLA Ops:
  0.1 1.8 %prep.1 = (f32[8,1024]{1,0:T(8,128)S(1)}, bf16[4,104,384]{2,1,0:T(8,128)(2,1)S(1)}) custom-call(s32[6]{0:T(128)S(1)} %stack.38.refs_0_.where, s32[8,1024]{1,0:T(8,128)} %bitcast.66, s32[8,1024]{1,0:T(8,128)} %bitcast.67, f32[8,1024]{1,0:T(8,128)} %bitcast.68, bf16[32,768]{1,0:T(8,128)(2,1)} %refs_4_.1, bf16[32,768]{1,0:T(8,128)(2,1)} %refs_5_.1, ...), custom_call_target="tpu_custom_call" | custom-call | flops 33554432 | bytes 131072 | tf_op jit(solution)/shard_map/prep/pallas_call | solution.py:86
  1.9 3.3 %collective-permute-start = (bf16[104,384]{1,0:T(8,128)(2,1)S(1)}, bf16[104,384]{1,0:T(8,128)(2,1)S(1)}, u32[]{:S(2)}, u32[]{:S(2)}) collective-permute-start(bf16[104,384]{1,0:T(8,128)(2,1)S(1)} %get-tuple-element.106), channel_id=1, source_target_pairs={{0,2},{2,0},{1,3},{3,1},{4,6},{6,4},{5,7},{7,5},{8,10},{10,8},{9,1... | collective-permute-start | bytes 239624 | tf_op jit(solution)/shard_map/ppermute | solution.py:33
  7.0 4.6 %gather_rows.1 = (bf16[128,4096]{1,0:T(8,128)(2,1)S(1)}, f32[128,128]{1,0:T(8,128)S(1)}) custom-call(s32[6]{0:T(128)S(1)} %stack.38.refs_0_.where, bf16[1024,4096]{1,0:T(8,128)(2,1)} %tokens.1, f32[8,1024]{1,0:T(8,128)S(1)} %get-tuple-element.44.info), custom_call_target="tpu_custom_call" | custom-call | flops 1073741824 | bytes 8388608 | tf_op jit(solution)/shard_map/gather_rows/pallas_call | solution.py:129
  12.0 3.9 %collective-permute-start.7 = (bf16[136,384]{1,0:T(8,128)(2,1)S(1)}, bf16[136,384]{1,0:T(8,128)(2,1)S(1)}, u32[]{:S(2)}, u32[]{:S(2)}) collective-permute-start(bf16[136,384]{1,0:T(8,128)(2,1)S(1)} %pad_maximum_fusion.8), channel_id=1, source_target_pairs={{0,28},{4,0},{8,4},{12,8},{16,12},{20,16},{24,20},{28,24},{1,29},{... | collective-permute-start | bytes 313352 | tf_op jit(solution)/shard_map/ppermute | solution.py:21
  17.3 2.6 %collective-permute-start.4 = (bf16[128,384]{1,0:T(8,128)(2,1)S(1)}, bf16[128,384]{1,0:T(8,128)(2,1)S(1)}, u32[]{:S(2)}, u32[]{:S(2)}) collective-permute-start(bf16[128,384]{1,0:T(8,128)(2,1)S(1)} %pad_maximum_fusion.9), channel_id=1, source_target_pairs={{0,128},{64,192},{128,0},{192,64},{1,129},{65,193},{129,1},{193,65... | collective-permute-start | bytes 294920 | tf_op jit(solution)/shard_map/ppermute | solution.py:21
  21.3 3.2 %collective-permute-done.4 = bf16[128,384]{1,0:T(8,128)(2,1)S(1)} collective-permute-done((bf16[128,384]{1,0:T(8,128)(2,1)S(1)}, bf16[128,384]{1,0:T(8,128)(2,1)S(1)}, u32[]{:S(2)}, u32[]{:S(2)}) %collective-permute-start.4) | collective-permute-done | bytes 98336 | tf_op jit(solution)/shard_map/ppermute | solution.py:21
  26.2 2.8 %collective-permute-start.10 = (bf16[256,384]{1,0:T(8,128)(2,1)S(1)}, bf16[256,384]{1,0:T(8,128)(2,1)S(1)}, u32[]{:S(2)}, u32[]{:S(2)}) collective-permute-start(bf16[256,384]{1,0:T(8,128)(2,1)S(1)} %pad_maximum_fusion.6), channel_id=1, source_target_pairs={{0,1},{1,0},{2,3},{3,2},{4,5},{5,4},{6,7},{7,6},{8,9},{9,8},{10,11... | collective-permute-start | bytes 589832 | tf_op jit(solution)/shard_map/ppermute | solution.py:41
  30.0 2.7 %collective-permute-start.9 = (bf16[136,384]{1,0:T(8,128)(2,1)S(1)}, bf16[136,384]{1,0:T(8,128)(2,1)S(1)}, u32[]{:S(2)}, u32[]{:S(2)}) collective-permute-start(bf16[136,384]{1,0:T(8,128)(2,1)S(1)} %collective-permute-done.7), channel_id=1, source_target_pairs={{0,28},{4,0},{8,4},{12,8},{16,12},{20,16},{24,20},{28,24},{1,29},{... | collective-permute-start | bytes 313352 | tf_op jit(solution)/shard_map/ppermute | solution.py:21
  32.7 3.0 %collective-permute-done.8 = bf16[136,384]{1,0:T(8,128)(2,1)S(1)} collective-permute-done((bf16[136,384]{1,0:T(8,128)(2,1)S(1)}, bf16[136,384]{1,0:T(8,128)(2,1)S(1)}, u32[]{:S(2)}, u32[]{:S(2)}) %collective-permute-start.8) | collective-permute-done | bytes 104480 | tf_op jit(solution)/shard_map/ppermute | solution.py:21
  36.0 2.6 %collective-permute-start.13 = (bf16[648,384]{1,0:T(8,128)(2,1)S(1)}, bf16[648,384]{1,0:T(8,128)(2,1)S(1)}, u32[]{:S(2)}, u32[]{:S(2)}) collective-permute-start(bf16[648,384]{1,0:T(8,128)(2,1)S(1)} %constant_dynamic-update-slice_fusion.6), channel_id=1, source_target_pairs={{0,28},{4,0},{8,4},{12,8},{16,12},{20,16},{24,20},{28,24},{1,29},{... | collective-permute-start | bytes 1493000 | tf_op jit(solution)/shard_map/ppermute | solution.py:21
  41.4 6.9 %collective-permute-done.13.refs_1_ = bf16[648,384]{1,0:T(8,128)(2,1)S(1)} collective-permute-done((bf16[648,384]{1,0:T(8,128)(2,1)S(1)}, bf16[648,384]{1,0:T(8,128)(2,1)S(1)}, u32[]{:S(2)}, u32[]{:S(2)}) %collective-permute-start.13) | collective-permute-done | bytes 497696 | tf_op jit(solution)/shard_map/ppermute | solution.py:21
  48.3 2.9 %collective-permute-done.12.refs_7_ = bf16[648,384]{1,0:T(8,128)(2,1)S(1)} collective-permute-done((bf16[648,384]{1,0:T(8,128)(2,1)S(1)}, bf16[648,384]{1,0:T(8,128)(2,1)S(1)}, u32[]{:S(2)}, u32[]{:S(2)}) %collective-permute-start.12) | collective-permute-done | bytes 497696 | tf_op jit(solution)/shard_map/ppermute | solution.py:21
  53.1 3.0 %collective-permute-start.21 = (bf16[128,4096]{1,0:T(8,128)(2,1)S(1)}, bf16[128,4096]{1,0:T(8,128)(2,1)S(1)}, u32[]{:S(2)}, u32[]{:S(2)}) collective-permute-start(bf16[128,4096]{1,0:T(8,128)(2,1)S(1)} %collective-permute-done.18.xn), channel_id=1, source_target_pairs={{0,2},{2,0},{1,3},{3,1},{4,6},{6,4},{5,7},{7,5},{8,10},{10,8},{9,1... | collective-permute-start | bytes 3145736 | tf_op jit(solution)/shard_map/ppermute | solution.py:33
  59.0 3.4 %collective-permute-done.14.refs_6_ = bf16[576,384]{1,0:T(8,128)(2,1)S(1)} collective-permute-done((bf16[576,384]{1,0:T(8,128)(2,1)S(1)}, bf16[576,384]{1,0:T(8,128)(2,1)S(1)}, u32[]{:S(2)}, u32[]{:S(2)}) %collective-permute-start.14) | collective-permute-done | bytes 442400 | tf_op jit(solution)/shard_map/ppermute | solution.py:21
  62.6 2.7 %collective-permute-start.29 = (bf16[512,384]{1,0:T(8,128)(2,1)S(1)}, bf16[512,384]{1,0:T(8,128)(2,1)S(1)}, u32[]{:S(2)}, u32[]{:S(2)}) collective-permute-start(bf16[512,384]{1,0:T(8,128)(2,1)S(1)} %slice.223), channel_id=1, source_target_pairs={{0,28},{4,0},{8,4},{12,8},{16,12},{20,16},{24,20},{28,24},{1,29},{... | collective-permute-start | bytes 1179656 | tf_op jit(solution)/shard_map/ppermute | solution.py:21
  65.3 3.3 %collective-permute-done.20.g_ahead.refs_6_ = bf16[568,384]{1,0:T(8,128)(2,1)S(1)} collective-permute-done((bf16[568,384]{1,0:T(8,128)(2,1)S(1)}, bf16[568,384]{1,0:T(8,128)(2,1)S(1)}, u32[]{:S(2)}, u32[]{:S(2)}) %collective-permute-start.20) | collective-permute-done | bytes 436256 | tf_op jit(solution)/shard_map/ppermute | solution.py:21
  68.6 2.0 %collective-permute-done.19.g_back.refs_5_ = bf16[656,384]{1,0:T(8,128)(2,1)S(1)} collective-permute-done((bf16[656,384]{1,0:T(8,128)(2,1)S(1)}, bf16[656,384]{1,0:T(8,128)(2,1)S(1)}, u32[]{:S(2)}, u32[]{:S(2)}) %collective-permute-start.19) | collective-permute-done | bytes 503840 | tf_op jit(solution)/shard_map/ppermute | solution.py:21
  73.7 3.0 %collective-permute-start.31 = (bf16[256,384]{1,0:T(8,128)(2,1)S(1)}, bf16[256,384]{1,0:T(8,128)(2,1)S(1)}, u32[]{:S(2)}, u32[]{:S(2)}) collective-permute-start(bf16[256,384]{1,0:T(8,128)(2,1)S(1)} %slice.225), channel_id=1, source_target_pairs={{0,28},{4,0},{8,4},{12,8},{16,12},{20,16},{24,20},{28,24},{1,29},{... | collective-permute-start | bytes 589832 | tf_op jit(solution)/shard_map/ppermute | solution.py:21
  76.6 2.2 %gate_up_near.1 = (f32[512,384]{1,0:T(8,128)S(1)}, bf16[512,640]{1,0:T(8,128)(2,1)S(1)}) custom-call(bf16[680,384]{1,0:T(8,128)(2,1)S(1)} %constant_dynamic-update-slice_fusion.12.first.refs_0_, bf16[272,384]{1,0:T(8,128)(2,1)S(1)} %pad_maximum_fusion.4.second.refs_1_, bf16[136,384]{1,0:T(8,128)(2,1)S(1)} %pad_maximum_fusion.7.last.refs_2_, ...), custom_call_target="tpu_custom_call" | custom-call | flops 1358954496 | bytes 8388608 | tf_op jit(solution)/shard_map/gate_up_near/pallas_call | solution.py:165
  82.4 2.2 %collective-permute-start.27 = (bf16[256,192]{1,0:T(8,128)(2,1)S(1)}, bf16[256,192]{1,0:T(8,128)(2,1)S(1)}, u32[]{:S(2)}, u32[]{:S(2)}) collective-permute-start(bf16[256,192]{1,0:T(8,128)(2,1)S(1)} %get-tuple-element.71), channel_id=1, source_target_pairs={{0,33},{1,32},{32,1},{33,0},{2,35},{3,34},{34,3},{35,2},{4,37},{5,... | collective-permute-start | bytes 294920 | tf_op jit(solution)/shard_map/ppermute | solution.py:315
  84.7 3.1 %collective-permute-done.26.ha = bf16[256,192]{1,0:T(8,128)(2,1)S(1)} collective-permute-done((bf16[256,192]{1,0:T(8,128)(2,1)S(1)}, bf16[256,192]{1,0:T(8,128)(2,1)S(1)}, u32[]{:S(2)}, u32[]{:S(2)}) %collective-permute-start.26) | collective-permute-done | bytes 98336 | tf_op jit(solution)/shard_map/ppermute | solution.py:41
  89.0 5.0 %collective-permute-start.32 = (bf16[256,768]{1,0:T(8,128)(2,1)S(1)}, bf16[256,768]{1,0:T(8,128)(2,1)S(1)}, u32[]{:S(2)}, u32[]{:S(2)}) collective-permute-start(bf16[256,768]{1,0:T(8,128)(2,1)S(1)} %pad_maximum_fusion.1), channel_id=1, source_target_pairs={{0,2},{2,0},{1,3},{3,1},{4,6},{6,4},{5,7},{7,5},{8,10},{10,8},{9,1... | collective-permute-start | bytes 1179656 | tf_op jit(solution)/shard_map/ppermute | solution.py:33
  95.4 2.9 %down.1 = f32[256,1024]{1,0:T(8,128)S(1)} custom-call(s32[6]{0:T(128)S(1)} %stack.38.refs_0_.where, bf16[256,192]{1,0:T(8,128)(2,1)S(1)} %get-tuple-element.70.own, bf16[256,192]{1,0:T(8,128)(2,1)S(1)} %collective-permute-done.25.near, bf16[256,192]{1,0:T(8,128)(2,1)S(1)} %collective-permute-done.26.ha, bf16[256,192]{1,0:T(8,128)(2,1)S(1)} %collective-permute-done.27.far, ...), custom_call_target="tpu_custom_call" | custom-call | flops 805306368 | bytes 5242880 | tf_op jit(solution)/shard_map/down/pallas_call | solution.py:253
  100.3 4.1 %mix.1 = bf16[1024,2048]{1,0:T(8,128)(2,1)} custom-call(s32[6]{0:T(128)S(1)} %stack.38.refs_0_.where, f32[128,1024]{1,0:T(8,128)S(1)} %get-tuple-element.82.mine, f32[128,1024]{1,0:T(8,128)S(1)} %collective-permute-done.33.theirs, f32[8,1024]{1,0:T(8,128)S(1)} %get-tuple-element.44.info, f32[128,128]{1,0:T(8,128)S(1)} %get-tuple-element.79.slot_route, ...), custom_call_target="tpu_custom_call" | custom-call | flops 536870912 | bytes 6291456 | tf_op jit(solution)/shard_map/mix/pallas_call | solution.py:283
  (111 shorter events, 26.5 us)
Async XLA Ops:
  1.9 9.7 %collective-permute-start = (bf16[104,384]{1,0:T(8,128)(2,1)S(1)}, bf16[104,384]{1,0:T(8,128)(2,1)S(1)}, u32[]{:S(2)}, u32[]{:S(2)}) collective-permute-start(bf16[104,384]{1,0:T(8,128)(2,1)S(1)} %get-tuple-element.106), channel_id=1, source_target_pairs={{0,2},{2,0},{1,3},{3,1},{4,6},{6,4},{5,7},{7,5},{8,10},{10,8},{9,1... | collective-permute-start | bytes 239624 | tf_op jit(solution)/shard_map/ppermute | solution.py:33
  5.3 6.4 %collective-permute-start.2 = (bf16[104,384]{1,0:T(8,128)(2,1)S(1)}, bf16[104,384]{1,0:T(8,128)(2,1)S(1)}, u32[]{:S(2)}, u32[]{:S(2)}) collective-permute-start(bf16[104,384]{1,0:T(8,128)(2,1)S(1)} %get-tuple-element.107), channel_id=1, source_target_pairs={{0,34},{2,32},{32,2},{34,0},{1,35},{3,33},{33,3},{35,1},{4,38},{6,... | collective-permute-start | bytes 239624 | tf_op jit(solution)/shard_map/ppermute | solution.py:326
  11.9 12.8 %collective-permute-start.6 = (bf16[136,384]{1,0:T(8,128)(2,1)S(1)}, bf16[136,384]{1,0:T(8,128)(2,1)S(1)}, u32[]{:S(2)}, u32[]{:S(2)}) collective-permute-start(bf16[136,384]{1,0:T(8,128)(2,1)S(1)} %pad_maximum_fusion.8), channel_id=1, source_target_pairs={{0,4},{4,8},{8,12},{12,16},{16,20},{20,24},{24,28},{28,0},{1,5},{5... | collective-permute-start | bytes 313352 | tf_op jit(solution)/shard_map/ppermute | solution.py:21
  12.0 12.7 %collective-permute-start.7 = (bf16[136,384]{1,0:T(8,128)(2,1)S(1)}, bf16[136,384]{1,0:T(8,128)(2,1)S(1)}, u32[]{:S(2)}, u32[]{:S(2)}) collective-permute-start(bf16[136,384]{1,0:T(8,128)(2,1)S(1)} %pad_maximum_fusion.8), channel_id=1, source_target_pairs={{0,28},{4,0},{8,4},{12,8},{16,12},{20,16},{24,20},{28,24},{1,29},{... | collective-permute-start | bytes 313352 | tf_op jit(solution)/shard_map/ppermute | solution.py:21
  17.3 7.2 %collective-permute-start.4 = (bf16[128,384]{1,0:T(8,128)(2,1)S(1)}, bf16[128,384]{1,0:T(8,128)(2,1)S(1)}, u32[]{:S(2)}, u32[]{:S(2)}) collective-permute-start(bf16[128,384]{1,0:T(8,128)(2,1)S(1)} %pad_maximum_fusion.9), channel_id=1, source_target_pairs={{0,128},{64,192},{128,0},{192,64},{1,129},{65,193},{129,1},{193,65... | collective-permute-start | bytes 294920 | tf_op jit(solution)/shard_map/ppermute | solution.py:21
  24.7 11.0 %collective-permute-start.11 = (bf16[128,4096]{1,0:T(8,128)(2,1)S(1)}, bf16[128,4096]{1,0:T(8,128)(2,1)S(1)}, u32[]{:S(2)}, u32[]{:S(2)}) collective-permute-start(bf16[128,4096]{1,0:T(8,128)(2,1)S(1)} %get-tuple-element.48.xo), channel_id=1, source_target_pairs={{0,2},{2,0},{1,3},{3,1},{4,6},{6,4},{5,7},{7,5},{8,10},{10,8},{9,1... | collective-permute-start | bytes 3145736 | tf_op jit(solution)/shard_map/ppermute | solution.py:33
  26.2 9.6 %collective-permute-start.10 = (bf16[256,384]{1,0:T(8,128)(2,1)S(1)}, bf16[256,384]{1,0:T(8,128)(2,1)S(1)}, u32[]{:S(2)}, u32[]{:S(2)}) collective-permute-start(bf16[256,384]{1,0:T(8,128)(2,1)S(1)} %pad_maximum_fusion.6), channel_id=1, source_target_pairs={{0,1},{1,0},{2,3},{3,2},{4,5},{5,4},{6,7},{7,6},{8,9},{9,8},{10,11... | collective-permute-start | bytes 589832 | tf_op jit(solution)/shard_map/ppermute | solution.py:41
  29.0 24.1 %collective-permute-start.18 = (bf16[128,4096]{1,0:T(8,128)(2,1)S(1)}, bf16[128,4096]{1,0:T(8,128)(2,1)S(1)}, u32[]{:S(2)}, u32[]{:S(2)}) collective-permute-start(bf16[128,4096]{1,0:T(8,128)(2,1)S(1)} %get-tuple-element.48.xo), channel_id=1, source_target_pairs={{0,32},{2,35},{32,1},{34,2},{1,33},{3,34},{33,0},{35,3},{4,36},{6,... | collective-permute-start | bytes 3145736 | tf_op jit(solution)/shard_map/ppermute | solution.py:49
  36.0 12.3 %collective-permute-start.13 = (bf16[648,384]{1,0:T(8,128)(2,1)S(1)}, bf16[648,384]{1,0:T(8,128)(2,1)S(1)}, u32[]{:S(2)}, u32[]{:S(2)}) collective-permute-start(bf16[648,384]{1,0:T(8,128)(2,1)S(1)} %constant_dynamic-update-slice_fusion.6), channel_id=1, source_target_pairs={{0,28},{4,0},{8,4},{12,8},{16,12},{20,16},{24,20},{28,24},{1,29},{... | collective-permute-start | bytes 1493000 | tf_op jit(solution)/shard_map/ppermute | solution.py:21
  38.6 12.6 %collective-permute-start.12 = (bf16[648,384]{1,0:T(8,128)(2,1)S(1)}, bf16[648,384]{1,0:T(8,128)(2,1)S(1)}, u32[]{:S(2)}, u32[]{:S(2)}) collective-permute-start(bf16[648,384]{1,0:T(8,128)(2,1)S(1)} %constant_dynamic-update-slice_fusion), channel_id=1, source_target_pairs={{0,4},{4,8},{8,12},{12,16},{16,20},{20,24},{24,28},{28,0},{1,5},{5... | collective-permute-start | bytes 1493000 | tf_op jit(solution)/shard_map/ppermute | solution.py:21
  38.6 14.5 %collective-permute-start.16 = (bf16[680,384]{1,0:T(8,128)(2,1)S(1)}, bf16[680,384]{1,0:T(8,128)(2,1)S(1)}, u32[]{:S(2)}, u32[]{:S(2)}) collective-permute-start(bf16[680,384]{1,0:T(8,128)(2,1)S(1)} %constant_dynamic-update-slice_fusion.12.first.refs_0_), channel_id=1, source_target_pairs={{0,64},{64,128},{128,192},{192,0},{1,65},{65,129},{129,193},{193,1... | collective-permute-start | bytes 1566728 | tf_op jit(solution)/shard_map/ppermute | solution.py:21
  39.7 13.5 %collective-permute-start.17 = (bf16[680,384]{1,0:T(8,128)(2,1)S(1)}, bf16[680,384]{1,0:T(8,128)(2,1)S(1)}, u32[]{:S(2)}, u32[]{:S(2)}) collective-permute-start(bf16[680,384]{1,0:T(8,128)(2,1)S(1)} %constant_dynamic-update-slice_fusion.12.first.refs_0_), channel_id=1, source_target_pairs={{0,192},{64,0},{128,64},{192,128},{1,193},{65,1},{129,65},{193,129... | collective-permute-start | bytes 1566728 | tf_op jit(solution)/shard_map/ppermute | solution.py:21
  51.4 11.0 %collective-permute-start.15 = (bf16[584,384]{1,0:T(8,128)(2,1)S(1)}, bf16[584,384]{1,0:T(8,128)(2,1)S(1)}, u32[]{:S(2)}, u32[]{:S(2)}) collective-permute-start(bf16[584,384]{1,0:T(8,128)(2,1)S(1)} %pad_maximum_fusion), channel_id=1, source_target_pairs={{0,28},{4,0},{8,4},{12,8},{16,12},{20,16},{24,20},{28,24},{1,29},{... | collective-permute-start | bytes 1345544 | tf_op jit(solution)/shard_map/ppermute | solution.py:21
  51.8 10.6 %collective-permute-start.14 = (bf16[576,384]{1,0:T(8,128)(2,1)S(1)}, bf16[576,384]{1,0:T(8,128)(2,1)S(1)}, u32[]{:S(2)}, u32[]{:S(2)}) collective-permute-start(bf16[576,384]{1,0:T(8,128)(2,1)S(1)} %slice.197), channel_id=1, source_target_pairs={{0,4},{4,8},{8,12},{12,16},{16,20},{20,24},{24,28},{28,0},{1,5},{5... | collective-permute-start | bytes 1327112 | tf_op jit(solution)/shard_map/ppermute | solution.py:21
  53.1 17.5 %collective-permute-start.21 = (bf16[128,4096]{1,0:T(8,128)(2,1)S(1)}, bf16[128,4096]{1,0:T(8,128)(2,1)S(1)}, u32[]{:S(2)}, u32[]{:S(2)}) collective-permute-start(bf16[128,4096]{1,0:T(8,128)(2,1)S(1)} %collective-permute-done.18.xn), channel_id=1, source_target_pairs={{0,2},{2,0},{1,3},{3,1},{4,6},{6,4},{5,7},{7,5},{8,10},{10,8},{9,1... | collective-permute-start | bytes 3145736 | tf_op jit(solution)/shard_map/ppermute | solution.py:33
  56.2 14.4 %collective-permute-start.19 = (bf16[656,384]{1,0:T(8,128)(2,1)S(1)}, bf16[656,384]{1,0:T(8,128)(2,1)S(1)}, u32[]{:S(2)}, u32[]{:S(2)}) collective-permute-start(bf16[656,384]{1,0:T(8,128)(2,1)S(1)} %get-tuple-element.97), channel_id=1, source_target_pairs={{0,64},{64,128},{128,192},{192,0},{1,65},{65,129},{129,193},{193,1... | collective-permute-start | bytes 1511432 | tf_op jit(solution)/shard_map/ppermute | solution.py:21
  57.3 11.3 %collective-permute-start.20 = (bf16[568,384]{1,0:T(8,128)(2,1)S(1)}, bf16[568,384]{1,0:T(8,128)(2,1)S(1)}, u32[]{:S(2)}, u32[]{:S(2)}) collective-permute-start(bf16[568,384]{1,0:T(8,128)(2,1)S(1)} %constant_dynamic-update-slice_fusion.22), channel_id=1, source_target_pairs={{0,192},{64,0},{128,64},{192,128},{1,193},{65,1},{129,65},{193,129... | collective-permute-start | bytes 1308680 | tf_op jit(solution)/shard_map/ppermute | solution.py:21
  62.5 11.0 %collective-permute-start.28 = (bf16[512,384]{1,0:T(8,128)(2,1)S(1)}, bf16[512,384]{1,0:T(8,128)(2,1)S(1)}, u32[]{:S(2)}, u32[]{:S(2)}) collective-permute-start(bf16[512,384]{1,0:T(8,128)(2,1)S(1)} %slice.222), channel_id=1, source_target_pairs={{0,4},{4,8},{8,12},{12,16},{16,20},{20,24},{24,28},{28,0},{1,5},{5... | collective-permute-start | bytes 1179656 | tf_op jit(solution)/shard_map/ppermute | solution.py:21
  62.6 10.9 %collective-permute-start.29 = (bf16[512,384]{1,0:T(8,128)(2,1)S(1)}, bf16[512,384]{1,0:T(8,128)(2,1)S(1)}, u32[]{:S(2)}, u32[]{:S(2)}) collective-permute-start(bf16[512,384]{1,0:T(8,128)(2,1)S(1)} %slice.223), channel_id=1, source_target_pairs={{0,28},{4,0},{8,4},{12,8},{16,12},{20,16},{24,20},{28,24},{1,29},{... | collective-permute-start | bytes 1179656 | tf_op jit(solution)/shard_map/ppermute | solution.py:21
  70.7 8.7 %collective-permute-start.23 = (bf16[280,384]{1,0:T(8,128)(2,1)S(1)}, bf16[280,384]{1,0:T(8,128)(2,1)S(1)}, u32[]{:S(2)}, u32[]{:S(2)}) collective-permute-start(bf16[280,384]{1,0:T(8,128)(2,1)S(1)} %pad_maximum_fusion.3), channel_id=1, source_target_pairs={{0,192},{64,0},{128,64},{192,128},{1,193},{65,1},{129,65},{193,129... | collective-permute-start | bytes 645128 | tf_op jit(solution)/shard_map/ppermute | solution.py:21
  71.7 7.6 %collective-permute-start.22 = (bf16[264,384]{1,0:T(8,128)(2,1)S(1)}, bf16[264,384]{1,0:T(8,128)(2,1)S(1)}, u32[]{:S(2)}, u32[]{:S(2)}) collective-permute-start(bf16[264,384]{1,0:T(8,128)(2,1)S(1)} %pad_maximum_fusion.5), channel_id=1, source_target_pairs={{0,64},{64,128},{128,192},{192,0},{1,65},{65,129},{129,193},{193,1... | collective-permute-start | bytes 608264 | tf_op jit(solution)/shard_map/ppermute | solution.py:21
  72.4 7.0 %collective-permute-start.24 = (bf16[136,384]{1,0:T(8,128)(2,1)S(1)}, bf16[136,384]{1,0:T(8,128)(2,1)S(1)}, u32[]{:S(2)}, u32[]{:S(2)}) collective-permute-start(bf16[136,384]{1,0:T(8,128)(2,1)S(1)} %pad_maximum_fusion.7.last.refs_2_), channel_id=1, source_target_pairs={{0,128},{64,192},{128,0},{192,64},{1,129},{65,193},{129,1},{193,65... | collective-permute-start | bytes 313352 | tf_op jit(solution)/shard_map/ppermute | solution.py:21
  73.6 11.1 %collective-permute-start.30 = (bf16[256,384]{1,0:T(8,128)(2,1)S(1)}, bf16[256,384]{1,0:T(8,128)(2,1)S(1)}, u32[]{:S(2)}, u32[]{:S(2)}) collective-permute-start(bf16[256,384]{1,0:T(8,128)(2,1)S(1)} %slice.224), channel_id=1, source_target_pairs={{0,4},{4,8},{8,12},{12,16},{16,20},{20,24},{24,28},{28,0},{1,5},{5... | collective-permute-start | bytes 589832 | tf_op jit(solution)/shard_map/ppermute | solution.py:21
  73.7 11.0 %collective-permute-start.31 = (bf16[256,384]{1,0:T(8,128)(2,1)S(1)}, bf16[256,384]{1,0:T(8,128)(2,1)S(1)}, u32[]{:S(2)}, u32[]{:S(2)}) collective-permute-start(bf16[256,384]{1,0:T(8,128)(2,1)S(1)} %slice.225), channel_id=1, source_target_pairs={{0,28},{4,0},{8,4},{12,8},{16,12},{20,16},{24,20},{28,24},{1,29},{... | collective-permute-start | bytes 589832 | tf_op jit(solution)/shard_map/ppermute | solution.py:21
  (10 other events, 52.3 us)

commit v7 on v6

--- a/solution.py
+++ b/solution.py
@@ -338,7 +338,7 @@
 
     b1, a1 = Z(1)(unit), Z(-1)(unit)
     d_back, d_ahead, d_far = Y(1)(rows), Y(-1)(rows), Y(2)(rows)
-    b1, a1, slot_rows = together(b1, a1, slot_rows)
+    b1, a1, slot_rows, d_back, d_ahead, d_far = together(b1, a1, slot_rows, d_back, d_ahead, d_far)
     b2, a2 = Z(1)(b1), Z(-1)(a1)
     neighbour_rows = across_x(slot_rows)
 

time: 105 us -> 112 us (1.067)
  starting transfers between devices: 52.5 us -> 64.2 us
  waiting for transfers between devices: 32.7 us -> 28.5 us
    ppermute x5, starting transfers between devices: 13 us -> 25.4 us  [C(): return lax.ppermute(a, 'c', [(0, 1), (1, 0)])]
    ppermute x22, waiting for transfers between devices: 25.6 us -> 20.1 us  [ring(): return lambda a: lax.ppermute(a, axis, [(i, (i + k) % n) for i in range(n)])]
    ppermute x2, starting transfers between devices: 3.16 us -> 1.08 us  [HA(): return lax.ppermute(a, 'ha', [(0, 1), (1, 0)])]
    ppermute x1, starting transfers between devices: 0.94 us -> 2.47 us  [across_x(): return lax.ppermute(a, ('xl', 'c', 'ha'), pairs)]
    ppermute x2, waiting for transfers between devices: 3.14 us -> 4.66 us  [HA(): return lax.ppermute(a, 'ha', [(0, 1), (1, 0)])]
    ppermute x2, starting transfers between devices: 1.37 us -> 0.1 us  [XL(): return lax.ppermute(a, 'xl', [(0, 1), (1, 0)])]
    ppermute x1, starting transfers between devices: 2.24 us -> 3.38 us  [HIDDEN_FAR(): return lax.ppermute(a, ('xl', 'ha'), pairs)]
  transfers between devices with their start and end apart: 34 -> 34, of which waited for: 13 -> 13; matrix products, arithmetic and copies ran while one was open for 1% -> 1% of each run, Pallas kernels for 8% -> 7%
where the time goes in v7:
time: 112 us
  starting transfers between devices  64.2 us (57%)
  waiting for transfers between devices  28.5 us (25%)
  Pallas kernels  17 us (15%)
    ppermute x22, starting transfers between devices, ring(): return lambda a: lax.ppermute(a, axis, [(i, (i + k) % n) for i in range(n)])  30.1 us
    ppermute x5, starting transfers between devices, C(): return lax.ppermute(a, 'c', [(0, 1), (1, 0)])  25.4 us
    ppermute x22, waiting for transfers between devices, ring(): return lambda a: lax.ppermute(a, axis, [(i, (i + k) % n) for i in range(n)])  20.1 us
    ppermute x2, waiting for transfers between devices, HA(): return lax.ppermute(a, 'ha', [(0, 1), (1, 0)])  4.66 us
    pallas_call x1, Pallas kernels, gather_rows(): pl.pallas_call(gather_body, out_shape=(jax.ShapeDtypeStruct((CAP, d), BF1...  4.64 us
    pallas_call x1, Pallas kernels, mix(): pl.pallas_call(mix_body, out_shape=jax.ShapeDtypeStruct((n, 2048), BF16),...  4.07 us
    ppermute x1, starting transfers between devices, HIDDEN_FAR(): return lax.ppermute(a, ('xl', 'ha'), pairs)  3.38 us
    ppermute x5, waiting for transfers between devices, C(): return lax.ppermute(a, 'c', [(0, 1), (1, 0)])  3.02 us
  transfers between devices with their start and end apart: 34, of which 13 were waited for; matrix products, arithmetic and copies ran while one was open for 1% of the time, Pallas kernels for 7%

profile of v7, /device:TPU:1, one launch (start us, length us, event | category | flops | bytes accessed | tf_op | source)
XLA Modules:
  0.0 112.0 jit_solution(206479799339803667)
XLA Ops:
  1.9 3.3 %collective-permute-start = (bf16[104,384]{1,0:T(8,128)(2,1)S(1)}, bf16[104,384]{1,0:T(8,128)(2,1)S(1)}, u32[]{:S(2)}, u32[]{:S(2)}) collective-permute-start(bf16[104,384]{1,0:T(8,128)(2,1)S(1)} %get-tuple-element.112), channel_id=1, source_target_pairs={{0,2},{2,0},{1,3},{3,1},{4,6},{6,4},{5,7},{7,5},{8,10},{10,8},{9,1... | collective-permute-start | bytes 239624 | tf_op jit(solution)/shard_map/ppermute | solution.py:33
  7.0 4.6 %gather_rows.1 = (bf16[128,4096]{1,0:T(8,128)(2,1)S(1)}, f32[128,128]{1,0:T(8,128)S(1)}) custom-call(s32[6]{0:T(128)S(1)} %stack.38.refs_0_.where, bf16[1024,4096]{1,0:T(8,128)(2,1)} %tokens.1, f32[8,1024]{1,0:T(8,128)S(1)} %get-tuple-element.47.info), custom_call_target="tpu_custom_call" | custom-call | flops 1073741824 | bytes 8388608 | tf_op jit(solution)/shard_map/gather_rows/pallas_call | solution.py:129
  12.0 2.7 %collective-permute-start.6 = (bf16[128,384]{1,0:T(8,128)(2,1)S(1)}, bf16[128,384]{1,0:T(8,128)(2,1)S(1)}, u32[]{:S(2)}, u32[]{:S(2)}) collective-permute-start(bf16[128,384]{1,0:T(8,128)(2,1)S(1)} %pad_maximum_fusion.9), channel_id=1, source_target_pairs={{0,192},{64,0},{128,64},{192,128},{1,193},{65,1},{129,65},{193,129... | collective-permute-start | bytes 294920 | tf_op jit(solution)/shard_map/ppermute | solution.py:21
  16.4 4.0 %collective-permute-start.4 = (bf16[136,384]{1,0:T(8,128)(2,1)S(1)}, bf16[136,384]{1,0:T(8,128)(2,1)S(1)}, u32[]{:S(2)}, u32[]{:S(2)}) collective-permute-start(bf16[136,384]{1,0:T(8,128)(2,1)S(1)} %pad_maximum_fusion.8), channel_id=1, source_target_pairs={{0,28},{4,0},{8,4},{12,8},{16,12},{20,16},{24,20},{28,24},{1,29},{... | collective-permute-start | bytes 313352 | tf_op jit(solution)/shard_map/ppermute | solution.py:21
  24.3 2.5 %collective-permute-start.18 = (bf16[128,4096]{1,0:T(8,128)(2,1)S(1)}, bf16[128,4096]{1,0:T(8,128)(2,1)S(1)}, u32[]{:S(2)}, u32[]{:S(2)}) collective-permute-start(bf16[128,4096]{1,0:T(8,128)(2,1)S(1)} %get-tuple-element.54.xo), channel_id=1, source_target_pairs={{0,32},{2,35},{32,1},{34,2},{1,33},{3,34},{33,0},{35,3},{4,36},{6,... | collective-permute-start | bytes 3145736 | tf_op jit(solution)/shard_map/ppermute | solution.py:49
  27.6 3.0 %collective-permute-start.9 = (bf16[136,384]{1,0:T(8,128)(2,1)S(1)}, bf16[136,384]{1,0:T(8,128)(2,1)S(1)}, u32[]{:S(2)}, u32[]{:S(2)}) collective-permute-start(bf16[136,384]{1,0:T(8,128)(2,1)S(1)} %collective-permute-done.4), channel_id=1, source_target_pairs={{0,28},{4,0},{8,4},{12,8},{16,12},{20,16},{24,20},{28,24},{1,29},{... | collective-permute-start | bytes 313352 | tf_op jit(solution)/shard_map/ppermute | solution.py:21
  30.8 2.2 %collective-permute-done.8 = bf16[136,384]{1,0:T(8,128)(2,1)S(1)} collective-permute-done((bf16[136,384]{1,0:T(8,128)(2,1)S(1)}, bf16[136,384]{1,0:T(8,128)(2,1)S(1)}, u32[]{:S(2)}, u32[]{:S(2)}) %collective-permute-start.8) | collective-permute-done | bytes 104480 | tf_op jit(solution)/shard_map/ppermute | solution.py:21
  33.0 2.3 %collective-permute-done.10 = bf16[256,384]{1,0:T(8,128)(2,1)S(1)} collective-permute-done((bf16[256,384]{1,0:T(8,128)(2,1)S(1)}, bf16[256,384]{1,0:T(8,128)(2,1)S(1)}, u32[]{:S(2)}, u32[]{:S(2)}) %collective-permute-start.10) | collective-permute-done | bytes 196640 | tf_op jit(solution)/shard_map/ppermute | solution.py:41
  35.5 3.3 %collective-permute-start.13 = (bf16[648,384]{1,0:T(8,128)(2,1)S(1)}, bf16[648,384]{1,0:T(8,128)(2,1)S(1)}, u32[]{:S(2)}, u32[]{:S(2)}) collective-permute-start(bf16[648,384]{1,0:T(8,128)(2,1)S(1)} %constant_dynamic-update-slice_fusion.6), channel_id=1, source_target_pairs={{0,28},{4,0},{8,4},{12,8},{16,12},{20,16},{24,20},{28,24},{1,29},{... | collective-permute-start | bytes 1493000 | tf_op jit(solution)/shard_map/ppermute | solution.py:21
  39.3 2.3 %collective-permute-start.17 = (bf16[680,384]{1,0:T(8,128)(2,1)S(1)}, bf16[680,384]{1,0:T(8,128)(2,1)S(1)}, u32[]{:S(2)}, u32[]{:S(2)}) collective-permute-start(bf16[680,384]{1,0:T(8,128)(2,1)S(1)} %constant_dynamic-update-slice_fusion.12.first.refs_0_), channel_id=1, source_target_pairs={{0,192},{64,0},{128,64},{192,128},{1,193},{65,1},{129,65},{193,129... | collective-permute-start | bytes 1566728 | tf_op jit(solution)/shard_map/ppermute | solution.py:21
  41.6 3.1 %collective-permute-done.13.refs_1_ = bf16[648,384]{1,0:T(8,128)(2,1)S(1)} collective-permute-done((bf16[648,384]{1,0:T(8,128)(2,1)S(1)}, bf16[648,384]{1,0:T(8,128)(2,1)S(1)}, u32[]{:S(2)}, u32[]{:S(2)}) %collective-permute-start.13) | collective-permute-done | bytes 497696 | tf_op jit(solution)/shard_map/ppermute | solution.py:21
  44.7 3.1 %collective-permute-done.12.refs_7_ = bf16[648,384]{1,0:T(8,128)(2,1)S(1)} collective-permute-done((bf16[648,384]{1,0:T(8,128)(2,1)S(1)}, bf16[648,384]{1,0:T(8,128)(2,1)S(1)}, u32[]{:S(2)}, u32[]{:S(2)}) %collective-permute-start.12) | collective-permute-done | bytes 497696 | tf_op jit(solution)/shard_map/ppermute | solution.py:21
  49.7 15.6 %collective-permute-start.21 = (bf16[128,4096]{1,0:T(8,128)(2,1)S(1)}, bf16[128,4096]{1,0:T(8,128)(2,1)S(1)}, u32[]{:S(2)}, u32[]{:S(2)}) collective-permute-start(bf16[128,4096]{1,0:T(8,128)(2,1)S(1)} %collective-permute-done.18.xn), channel_id=1, source_target_pairs={{0,2},{2,0},{1,3},{3,1},{4,6},{6,4},{5,7},{7,5},{8,10},{10,8},{9,1... | collective-permute-start | bytes 3145736 | tf_op jit(solution)/shard_map/ppermute | solution.py:33
  65.9 2.3 %collective-permute-start.20 = (bf16[568,384]{1,0:T(8,128)(2,1)S(1)}, bf16[568,384]{1,0:T(8,128)(2,1)S(1)}, u32[]{:S(2)}, u32[]{:S(2)}) collective-permute-start(bf16[568,384]{1,0:T(8,128)(2,1)S(1)} %constant_dynamic-update-slice_fusion.22), channel_id=1, source_target_pairs={{0,192},{64,0},{128,64},{192,128},{1,193},{65,1},{129,65},{193,129... | collective-permute-start | bytes 1308680 | tf_op jit(solution)/shard_map/ppermute | solution.py:21
  68.5 2.7 %collective-permute-start.29 = (bf16[512,384]{1,0:T(8,128)(2,1)S(1)}, bf16[512,384]{1,0:T(8,128)(2,1)S(1)}, u32[]{:S(2)}, u32[]{:S(2)}) collective-permute-start(bf16[512,384]{1,0:T(8,128)(2,1)S(1)} %slice.223), channel_id=1, source_target_pairs={{0,28},{4,0},{8,4},{12,8},{16,12},{20,16},{24,20},{28,24},{1,29},{... | collective-permute-start | bytes 1179656 | tf_op jit(solution)/shard_map/ppermute | solution.py:21
  71.2 6.2 %collective-permute-done.20.g_ahead.refs_6_ = bf16[568,384]{1,0:T(8,128)(2,1)S(1)} collective-permute-done((bf16[568,384]{1,0:T(8,128)(2,1)S(1)}, bf16[568,384]{1,0:T(8,128)(2,1)S(1)}, u32[]{:S(2)}, u32[]{:S(2)}) %collective-permute-start.20) | collective-permute-done | bytes 436256 | tf_op jit(solution)/shard_map/ppermute | solution.py:21
  77.3 2.5 %collective-permute-done.19.g_back.refs_5_ = bf16[656,384]{1,0:T(8,128)(2,1)S(1)} collective-permute-done((bf16[656,384]{1,0:T(8,128)(2,1)S(1)}, bf16[656,384]{1,0:T(8,128)(2,1)S(1)}, u32[]{:S(2)}, u32[]{:S(2)}) %collective-permute-start.19) | collective-permute-done | bytes 503840 | tf_op jit(solution)/shard_map/ppermute | solution.py:21
  82.5 3.0 %collective-permute-start.31 = (bf16[256,384]{1,0:T(8,128)(2,1)S(1)}, bf16[256,384]{1,0:T(8,128)(2,1)S(1)}, u32[]{:S(2)}, u32[]{:S(2)}) collective-permute-start(bf16[256,384]{1,0:T(8,128)(2,1)S(1)} %slice.225), channel_id=1, source_target_pairs={{0,28},{4,0},{8,4},{12,8},{16,12},{20,16},{24,20},{28,24},{1,29},{... | collective-permute-start | bytes 589832 | tf_op jit(solution)/shard_map/ppermute | solution.py:21
  85.4 2.2 %gate_up_near.1 = (f32[512,384]{1,0:T(8,128)S(1)}, bf16[512,640]{1,0:T(8,128)(2,1)S(1)}) custom-call(bf16[680,384]{1,0:T(8,128)(2,1)S(1)} %constant_dynamic-update-slice_fusion.12.first.refs_0_, bf16[272,384]{1,0:T(8,128)(2,1)S(1)} %pad_maximum_fusion.4.second.refs_1_, bf16[136,384]{1,0:T(8,128)(2,1)S(1)} %pad_maximum_fusion.7.last.refs_2_, ...), custom_call_target="tpu_custom_call" | custom-call | flops 1358954496 | bytes 8388608 | tf_op jit(solution)/shard_map/gate_up_near/pallas_call | solution.py:165
  90.7 3.4 %collective-permute-start.27 = (bf16[256,192]{1,0:T(8,128)(2,1)S(1)}, bf16[256,192]{1,0:T(8,128)(2,1)S(1)}, u32[]{:S(2)}, u32[]{:S(2)}) collective-permute-start(bf16[256,192]{1,0:T(8,128)(2,1)S(1)} %get-tuple-element.77), channel_id=1, source_target_pairs={{0,33},{1,32},{32,1},{33,0},{2,35},{3,34},{34,3},{35,2},{4,37},{5,... | collective-permute-start | bytes 294920 | tf_op jit(solution)/shard_map/ppermute | solution.py:315
  94.1 2.4 %collective-permute-done.26.ha = bf16[256,192]{1,0:T(8,128)(2,1)S(1)} collective-permute-done((bf16[256,192]{1,0:T(8,128)(2,1)S(1)}, bf16[256,192]{1,0:T(8,128)(2,1)S(1)}, u32[]{:S(2)}, u32[]{:S(2)}) %collective-permute-start.26) | collective-permute-done | bytes 98336 | tf_op jit(solution)/shard_map/ppermute | solution.py:41
  97.3 4.2 %collective-permute-start.32 = (bf16[256,768]{1,0:T(8,128)(2,1)S(1)}, bf16[256,768]{1,0:T(8,128)(2,1)S(1)}, u32[]{:S(2)}, u32[]{:S(2)}) collective-permute-start(bf16[256,768]{1,0:T(8,128)(2,1)S(1)} %pad_maximum_fusion.1), channel_id=1, source_target_pairs={{0,2},{2,0},{1,3},{3,1},{4,6},{6,4},{5,7},{7,5},{8,10},{10,8},{9,1... | collective-permute-start | bytes 1179656 | tf_op jit(solution)/shard_map/ppermute | solution.py:33
  102.9 2.9 %down.1 = f32[256,1024]{1,0:T(8,128)S(1)} custom-call(s32[6]{0:T(128)S(1)} %stack.38.refs_0_.where, bf16[256,192]{1,0:T(8,128)(2,1)S(1)} %get-tuple-element.76.own, bf16[256,192]{1,0:T(8,128)(2,1)S(1)} %collective-permute-done.25.near, bf16[256,192]{1,0:T(8,128)(2,1)S(1)} %collective-permute-done.26.ha, bf16[256,192]{1,0:T(8,128)(2,1)S(1)} %collective-permute-done.27.far, ...), custom_call_target="tpu_custom_call" | custom-call | flops 805306368 | bytes 5242880 | tf_op jit(solution)/shard_map/down/pallas_call | solution.py:253
  107.9 4.1 %mix.1 = bf16[1024,2048]{1,0:T(8,128)(2,1)} custom-call(s32[6]{0:T(128)S(1)} %stack.38.refs_0_.where, f32[128,1024]{1,0:T(8,128)S(1)} %get-tuple-element.88.mine, f32[128,1024]{1,0:T(8,128)S(1)} %collective-permute-done.33.theirs, f32[8,1024]{1,0:T(8,128)S(1)} %get-tuple-element.47.info, f32[128,128]{1,0:T(8,128)S(1)} %get-tuple-element.85.slot_route, ...), custom_call_target="tpu_custom_call" | custom-call | flops 536870912 | bytes 6291456 | tf_op jit(solution)/shard_map/mix/pallas_call | solution.py:283
  (112 shorter events, 23.6 us)
Async XLA Ops:
  1.9 9.7 %collective-permute-start = (bf16[104,384]{1,0:T(8,128)(2,1)S(1)}, bf16[104,384]{1,0:T(8,128)(2,1)S(1)}, u32[]{:S(2)}, u32[]{:S(2)}) collective-permute-start(bf16[104,384]{1,0:T(8,128)(2,1)S(1)} %get-tuple-element.112), channel_id=1, source_target_pairs={{0,2},{2,0},{1,3},{3,1},{4,6},{6,4},{5,7},{7,5},{8,10},{10,8},{9,1... | collective-permute-start | bytes 239624 | tf_op jit(solution)/shard_map/ppermute | solution.py:33
  11.9 8.5 %collective-permute-start.5 = (bf16[128,384]{1,0:T(8,128)(2,1)S(1)}, bf16[128,384]{1,0:T(8,128)(2,1)S(1)}, u32[]{:S(2)}, u32[]{:S(2)}) collective-permute-start(bf16[128,384]{1,0:T(8,128)(2,1)S(1)} %pad_maximum_fusion.9), channel_id=1, source_target_pairs={{0,64},{64,128},{128,192},{192,0},{1,65},{65,129},{129,193},{193,1... | collective-permute-start | bytes 294920 | tf_op jit(solution)/shard_map/ppermute | solution.py:21
  12.0 8.5 %collective-permute-start.6 = (bf16[128,384]{1,0:T(8,128)(2,1)S(1)}, bf16[128,384]{1,0:T(8,128)(2,1)S(1)}, u32[]{:S(2)}, u32[]{:S(2)}) collective-permute-start(bf16[128,384]{1,0:T(8,128)(2,1)S(1)} %pad_maximum_fusion.9), channel_id=1, source_target_pairs={{0,192},{64,0},{128,64},{192,128},{1,193},{65,1},{129,65},{193,129... | collective-permute-start | bytes 294920 | tf_op jit(solution)/shard_map/ppermute | solution.py:21
  14.7 7.7 %collective-permute-start.3 = (bf16[136,384]{1,0:T(8,128)(2,1)S(1)}, bf16[136,384]{1,0:T(8,128)(2,1)S(1)}, u32[]{:S(2)}, u32[]{:S(2)}) collective-permute-start(bf16[136,384]{1,0:T(8,128)(2,1)S(1)} %pad_maximum_fusion.8), channel_id=1, source_target_pairs={{0,4},{4,8},{8,12},{12,16},{16,20},{20,24},{24,28},{28,0},{1,5},{5... | collective-permute-start | bytes 313352 | tf_op jit(solution)/shard_map/ppermute | solution.py:21
  22.4 12.9 %collective-permute-start.11 = (bf16[128,4096]{1,0:T(8,128)(2,1)S(1)}, bf16[128,4096]{1,0:T(8,128)(2,1)S(1)}, u32[]{:S(2)}, u32[]{:S(2)}) collective-permute-start(bf16[128,4096]{1,0:T(8,128)(2,1)S(1)} %get-tuple-element.54.xo), channel_id=1, source_target_pairs={{0,2},{2,0},{1,3},{3,1},{4,6},{6,4},{5,7},{7,5},{8,10},{10,8},{9,1... | collective-permute-start | bytes 3145736 | tf_op jit(solution)/shard_map/ppermute | solution.py:33
  24.3 25.4 %collective-permute-start.18 = (bf16[128,4096]{1,0:T(8,128)(2,1)S(1)}, bf16[128,4096]{1,0:T(8,128)(2,1)S(1)}, u32[]{:S(2)}, u32[]{:S(2)}) collective-permute-start(bf16[128,4096]{1,0:T(8,128)(2,1)S(1)} %get-tuple-element.54.xo), channel_id=1, source_target_pairs={{0,32},{2,35},{32,1},{34,2},{1,33},{3,34},{33,0},{35,3},{4,36},{6,... | collective-permute-start | bytes 3145736 | tf_op jit(solution)/shard_map/ppermute | solution.py:49
  27.0 8.3 %collective-permute-start.10 = (bf16[256,384]{1,0:T(8,128)(2,1)S(1)}, bf16[256,384]{1,0:T(8,128)(2,1)S(1)}, u32[]{:S(2)}, u32[]{:S(2)}) collective-permute-start(bf16[256,384]{1,0:T(8,128)(2,1)S(1)} %pad_maximum_fusion.6), channel_id=1, source_target_pairs={{0,1},{1,0},{2,3},{3,2},{4,5},{5,4},{6,7},{7,6},{8,9},{9,8},{10,11... | collective-permute-start | bytes 589832 | tf_op jit(solution)/shard_map/ppermute | solution.py:41
  35.5 9.1 %collective-permute-start.13 = (bf16[648,384]{1,0:T(8,128)(2,1)S(1)}, bf16[648,384]{1,0:T(8,128)(2,1)S(1)}, u32[]{:S(2)}, u32[]{:S(2)}) collective-permute-start(bf16[648,384]{1,0:T(8,128)(2,1)S(1)} %constant_dynamic-update-slice_fusion.6), channel_id=1, source_target_pairs={{0,28},{4,0},{8,4},{12,8},{16,12},{20,16},{24,20},{28,24},{1,29},{... | collective-permute-start | bytes 1493000 | tf_op jit(solution)/shard_map/ppermute | solution.py:21
  38.8 9.0 %collective-permute-start.12 = (bf16[648,384]{1,0:T(8,128)(2,1)S(1)}, bf16[648,384]{1,0:T(8,128)(2,1)S(1)}, u32[]{:S(2)}, u32[]{:S(2)}) collective-permute-start(bf16[648,384]{1,0:T(8,128)(2,1)S(1)} %constant_dynamic-update-slice_fusion), channel_id=1, source_target_pairs={{0,4},{4,8},{8,12},{12,16},{16,20},{20,24},{24,28},{28,0},{1,5},{5... | collective-permute-start | bytes 1493000 | tf_op jit(solution)/shard_map/ppermute | solution.py:21
  38.8 10.8 %collective-permute-start.16 = (bf16[680,384]{1,0:T(8,128)(2,1)S(1)}, bf16[680,384]{1,0:T(8,128)(2,1)S(1)}, u32[]{:S(2)}, u32[]{:S(2)}) collective-permute-start(bf16[680,384]{1,0:T(8,128)(2,1)S(1)} %constant_dynamic-update-slice_fusion.12.first.refs_0_), channel_id=1, source_target_pairs={{0,64},{64,128},{128,192},{192,0},{1,65},{65,129},{129,193},{193,1... | collective-permute-start | bytes 1566728 | tf_op jit(solution)/shard_map/ppermute | solution.py:21
  39.3 10.3 %collective-permute-start.17 = (bf16[680,384]{1,0:T(8,128)(2,1)S(1)}, bf16[680,384]{1,0:T(8,128)(2,1)S(1)}, u32[]{:S(2)}, u32[]{:S(2)}) collective-permute-start(bf16[680,384]{1,0:T(8,128)(2,1)S(1)} %constant_dynamic-update-slice_fusion.12.first.refs_0_), channel_id=1, source_target_pairs={{0,192},{64,0},{128,64},{192,128},{1,193},{65,1},{129,65},{193,129... | collective-permute-start | bytes 1566728 | tf_op jit(solution)/shard_map/ppermute | solution.py:21
  47.9 20.3 %collective-permute-start.15 = (bf16[584,384]{1,0:T(8,128)(2,1)S(1)}, bf16[584,384]{1,0:T(8,128)(2,1)S(1)}, u32[]{:S(2)}, u32[]{:S(2)}) collective-permute-start(bf16[584,384]{1,0:T(8,128)(2,1)S(1)} %pad_maximum_fusion), channel_id=1, source_target_pairs={{0,28},{4,0},{8,4},{12,8},{16,12},{20,16},{24,20},{28,24},{1,29},{... | collective-permute-start | bytes 1345544 | tf_op jit(solution)/shard_map/ppermute | solution.py:21
  48.3 19.9 %collective-permute-start.14 = (bf16[576,384]{1,0:T(8,128)(2,1)S(1)}, bf16[576,384]{1,0:T(8,128)(2,1)S(1)}, u32[]{:S(2)}, u32[]{:S(2)}) collective-permute-start(bf16[576,384]{1,0:T(8,128)(2,1)S(1)} %slice.197), channel_id=1, source_target_pairs={{0,4},{4,8},{8,12},{12,16},{16,20},{20,24},{24,28},{28,0},{1,5},{5... | collective-permute-start | bytes 1327112 | tf_op jit(solution)/shard_map/ppermute | solution.py:21
  49.7 30.2 %collective-permute-start.21 = (bf16[128,4096]{1,0:T(8,128)(2,1)S(1)}, bf16[128,4096]{1,0:T(8,128)(2,1)S(1)}, u32[]{:S(2)}, u32[]{:S(2)}) collective-permute-start(bf16[128,4096]{1,0:T(8,128)(2,1)S(1)} %collective-permute-done.18.xn), channel_id=1, source_target_pairs={{0,2},{2,0},{1,3},{3,1},{4,6},{6,4},{5,7},{7,5},{8,10},{10,8},{9,1... | collective-permute-start | bytes 3145736 | tf_op jit(solution)/shard_map/ppermute | solution.py:33
  65.4 14.4 %collective-permute-start.19 = (bf16[656,384]{1,0:T(8,128)(2,1)S(1)}, bf16[656,384]{1,0:T(8,128)(2,1)S(1)}, u32[]{:S(2)}, u32[]{:S(2)}) collective-permute-start(bf16[656,384]{1,0:T(8,128)(2,1)S(1)} %get-tuple-element.103), channel_id=1, source_target_pairs={{0,64},{64,128},{128,192},{192,0},{1,65},{65,129},{129,193},{193,1... | collective-permute-start | bytes 1511432 | tf_op jit(solution)/shard_map/ppermute | solution.py:21
  65.9 11.4 %collective-permute-start.20 = (bf16[568,384]{1,0:T(8,128)(2,1)S(1)}, bf16[568,384]{1,0:T(8,128)(2,1)S(1)}, u32[]{:S(2)}, u32[]{:S(2)}) collective-permute-start(bf16[568,384]{1,0:T(8,128)(2,1)S(1)} %constant_dynamic-update-slice_fusion.22), channel_id=1, source_target_pairs={{0,192},{64,0},{128,64},{192,128},{1,193},{65,1},{129,65},{193,129... | collective-permute-start | bytes 1308680 | tf_op jit(solution)/shard_map/ppermute | solution.py:21
  68.4 13.9 %collective-permute-start.28 = (bf16[512,384]{1,0:T(8,128)(2,1)S(1)}, bf16[512,384]{1,0:T(8,128)(2,1)S(1)}, u32[]{:S(2)}, u32[]{:S(2)}) collective-permute-start(bf16[512,384]{1,0:T(8,128)(2,1)S(1)} %slice.222), channel_id=1, source_target_pairs={{0,4},{4,8},{8,12},{12,16},{16,20},{20,24},{24,28},{28,0},{1,5},{5... | collective-permute-start | bytes 1179656 | tf_op jit(solution)/shard_map/ppermute | solution.py:21
  68.5 13.9 %collective-permute-start.29 = (bf16[512,384]{1,0:T(8,128)(2,1)S(1)}, bf16[512,384]{1,0:T(8,128)(2,1)S(1)}, u32[]{:S(2)}, u32[]{:S(2)}) collective-permute-start(bf16[512,384]{1,0:T(8,128)(2,1)S(1)} %slice.223), channel_id=1, source_target_pairs={{0,28},{4,0},{8,4},{12,8},{16,12},{20,16},{24,20},{28,24},{1,29},{... | collective-permute-start | bytes 1179656 | tf_op jit(solution)/shard_map/ppermute | solution.py:21
  79.9 8.9 %collective-permute-start.23 = (bf16[280,384]{1,0:T(8,128)(2,1)S(1)}, bf16[280,384]{1,0:T(8,128)(2,1)S(1)}, u32[]{:S(2)}, u32[]{:S(2)}) collective-permute-start(bf16[280,384]{1,0:T(8,128)(2,1)S(1)} %pad_maximum_fusion.3), channel_id=1, source_target_pairs={{0,192},{64,0},{128,64},{192,128},{1,193},{65,1},{129,65},{193,129... | collective-permute-start | bytes 645128 | tf_op jit(solution)/shard_map/ppermute | solution.py:21
  80.9 7.8 %collective-permute-start.22 = (bf16[264,384]{1,0:T(8,128)(2,1)S(1)}, bf16[264,384]{1,0:T(8,128)(2,1)S(1)}, u32[]{:S(2)}, u32[]{:S(2)}) collective-permute-start(bf16[264,384]{1,0:T(8,128)(2,1)S(1)} %pad_maximum_fusion.5), channel_id=1, source_target_pairs={{0,64},{64,128},{128,192},{192,0},{1,65},{65,129},{129,193},{193,1... | collective-permute-start | bytes 608264 | tf_op jit(solution)/shard_map/ppermute | solution.py:21
  81.6 6.5 %collective-permute-start.24 = (bf16[136,384]{1,0:T(8,128)(2,1)S(1)}, bf16[136,384]{1,0:T(8,128)(2,1)S(1)}, u32[]{:S(2)}, u32[]{:S(2)}) collective-permute-start(bf16[136,384]{1,0:T(8,128)(2,1)S(1)} %pad_maximum_fusion.7.last.refs_2_), channel_id=1, source_target_pairs={{0,128},{64,192},{128,0},{192,64},{1,129},{65,193},{129,1},{193,65... | collective-permute-start | bytes 313352 | tf_op jit(solution)/shard_map/ppermute | solution.py:21
  82.3 11.8 %collective-permute-start.30 = (bf16[256,384]{1,0:T(8,128)(2,1)S(1)}, bf16[256,384]{1,0:T(8,128)(2,1)S(1)}, u32[]{:S(2)}, u32[]{:S(2)}) collective-permute-start(bf16[256,384]{1,0:T(8,128)(2,1)S(1)} %slice.224), channel_id=1, source_target_pairs={{0,4},{4,8},{8,12},{12,16},{16,20},{20,24},{24,28},{28,0},{1,5},{5... | collective-permute-start | bytes 589832 | tf_op jit(solution)/shard_map/ppermute | solution.py:21
  82.5 11.6 %collective-permute-start.31 = (bf16[256,384]{1,0:T(8,128)(2,1)S(1)}, bf16[256,384]{1,0:T(8,128)(2,1)S(1)}, u32[]{:S(2)}, u32[]{:S(2)}) collective-permute-start(bf16[256,384]{1,0:T(8,128)(2,1)S(1)} %slice.225), channel_id=1, source_target_pairs={{0,28},{4,0},{8,4},{12,8},{16,12},{20,16},{24,20},{28,24},{1,29},{... | collective-permute-start | bytes 589832 | tf_op jit(solution)/shard_map/ppermute | solution.py:21
  90.7 6.5 %collective-permute-start.27 = (bf16[256,192]{1,0:T(8,128)(2,1)S(1)}, bf16[256,192]{1,0:T(8,128)(2,1)S(1)}, u32[]{:S(2)}, u32[]{:S(2)}) collective-permute-start(bf16[256,192]{1,0:T(8,128)(2,1)S(1)} %get-tuple-element.77), channel_id=1, source_target_pairs={{0,33},{1,32},{32,1},{33,0},{2,35},{3,34},{34,3},{35,2},{4,37},{5,... | collective-permute-start | bytes 294920 | tf_op jit(solution)/shard_map/ppermute | solution.py:315
  (10 other events, 53.3 us)

commit v8 on v7

--- a/solution.py
+++ b/solution.py
@@ -338,9 +338,8 @@
 
     b1, a1 = Z(1)(unit), Z(-1)(unit)
     d_back, d_ahead, d_far = Y(1)(rows), Y(-1)(rows), Y(2)(rows)
-    b1, a1, slot_rows, d_back, d_ahead, d_far = together(b1, a1, slot_rows, d_back, d_ahead, d_far)
+    b1, a1, d_back, d_ahead, d_far = together(b1, a1, d_back, d_ahead, d_far)
     b2, a2 = Z(1)(b1), Z(-1)(a1)
-    neighbour_rows = across_x(slot_rows)
 
     turned = [rows, d_ahead, d_far, d_back]
     ordered = []
@@ -355,7 +354,8 @@
 
     d_swap = HA(halves(ordered[2], ordered[3]))
     core_rows = C(slot_rows)
-    b2, a2, d_swap, core_rows = together(b2, a2, d_swap, core_rows)
+    b2, a2, d_swap, core_rows, slot_rows = together(b2, a2, d_swap, core_rows, slot_rows)
+    neighbour_rows = across_x(slot_rows)
 
     d0 = jnp.concatenate([halves(ordered[0], ordered[1]), d_swap], axis=0)
     up1, dn1 = Z(1)(jnp.concatenate([d0, b2], axis=0)), Z(-1)(jnp.concatenate([d0, a2], axis=0))

time: 112 us -> 99.4 us (0.89)
  starting transfers between devices: 64.2 us -> 53.2 us
  waiting for transfers between devices: 28.5 us -> 26.6 us
    ppermute x5, starting transfers between devices: 25.4 us -> 13.3 us  [C(): return lax.ppermute(a, 'c', [(0, 1), (1, 0)])]
    ppermute x2, starting transfers between devices: 1.08 us -> 5.84 us  [HA(): return lax.ppermute(a, 'ha', [(0, 1), (1, 0)])]
    ppermute x1, starting transfers between devices: 3.38 us -> 0.1 us  [HIDDEN_FAR(): return lax.ppermute(a, ('xl', 'ha'), pairs)]
    ppermute x22, waiting for transfers between devices: 20.1 us -> 18.1 us  [ring(): return lambda a: lax.ppermute(a, axis, [(i, (i + k) % n) for i in range(n)])]
    ppermute x1, starting transfers between devices: 2.47 us -> 0.69 us  [across_x(): return lax.ppermute(a, ('xl', 'c', 'ha'), pairs)]
  transfers between devices with their start and end apart: 34 -> 34, of which waited for: 13 -> 12; matrix products, arithmetic and copies ran while one was open for 1% -> 1% of each run, Pallas kernels for 7% -> 8%
where the time goes in v8:
time: 99.4 us; the launch traced here: 99 us
  starting transfers between devices  53.2 us (54%)
  waiting for transfers between devices  26.6 us (27%)
  Pallas kernels  17 us (17%)
  local copies, waits for them, and re-layouts  1.06 us (1%)
    ppermute x22, starting transfers between devices, ring(): return lambda a: lax.ppermute(a, axis, [(i, (i + k) % n) for i in range(n)])  30.7 us
    ppermute x22, waiting for transfers between devices, ring(): return lambda a: lax.ppermute(a, axis, [(i, (i + k) % n) for i in range(n)])  18.1 us
    ppermute x5, starting transfers between devices, C(): return lax.ppermute(a, 'c', [(0, 1), (1, 0)])  13.3 us
    ppermute x2, starting transfers between devices, HA(): return lax.ppermute(a, 'ha', [(0, 1), (1, 0)])  5.84 us
    pallas_call x1, Pallas kernels, gather_rows(): pl.pallas_call(gather_body, out_shape=(jax.ShapeDtypeStruct((CAP, d), BF1...  4.64 us
    pallas_call x1, Pallas kernels, mix(): pl.pallas_call(mix_body, out_shape=jax.ShapeDtypeStruct((n, 2048), BF16),...  4.07 us
    ppermute x2, waiting for transfers between devices, HA(): return lax.ppermute(a, 'ha', [(0, 1), (1, 0)])  3.93 us
    ppermute x5, waiting for transfers between devices, C(): return lax.ppermute(a, 'c', [(0, 1), (1, 0)])  3.01 us
  transfers between devices with their start and end apart: 34, of which 12 were waited for; matrix products, arithmetic and copies ran while one was open for 1% of the time, Pallas kernels for 8%

profile of v8, /device:TPU:1, one launch (start us, length us, event | category | flops | bytes accessed | tf_op | source)
XLA Modules:
  0.0 99.0 jit_solution(13345187856530149986)
XLA Ops:
  0.1 1.8 %prep.1 = (f32[8,1024]{1,0:T(8,128)S(1)}, bf16[4,104,384]{2,1,0:T(8,128)(2,1)S(1)}) custom-call(s32[6]{0:T(128)S(1)} %stack.38.refs_0_.where, s32[8,1024]{1,0:T(8,128)} %bitcast.66, s32[8,1024]{1,0:T(8,128)} %bitcast.67, f32[8,1024]{1,0:T(8,128)} %bitcast.68, bf16[32,768]{1,0:T(8,128)(2,1)} %refs_4_.1, bf16[32,768]{1,0:T(8,128)(2,1)} %refs_5_.1, ...), custom_call_target="tpu_custom_call" | custom-call | flops 33554432 | bytes 131072 | tf_op jit(solution)/shard_map/prep/pallas_call | solution.py:86
  1.9 3.3 %collective-permute-start = (bf16[104,384]{1,0:T(8,128)(2,1)S(1)}, bf16[104,384]{1,0:T(8,128)(2,1)S(1)}, u32[]{:S(2)}, u32[]{:S(2)}) collective-permute-start(bf16[104,384]{1,0:T(8,128)(2,1)S(1)} %get-tuple-element.112), channel_id=1, source_target_pairs={{0,2},{2,0},{1,3},{3,1},{4,6},{6,4},{5,7},{7,5},{8,10},{10,8},{9,1... | collective-permute-start | bytes 239624 | tf_op jit(solution)/shard_map/ppermute | solution.py:33
  7.0 4.6 %gather_rows.1 = (bf16[128,4096]{1,0:T(8,128)(2,1)S(1)}, f32[128,128]{1,0:T(8,128)S(1)}) custom-call(s32[6]{0:T(128)S(1)} %stack.38.refs_0_.where, bf16[1024,4096]{1,0:T(8,128)(2,1)} %tokens.1, f32[8,1024]{1,0:T(8,128)S(1)} %get-tuple-element.52.info), custom_call_target="tpu_custom_call" | custom-call | flops 1073741824 | bytes 8388608 | tf_op jit(solution)/shard_map/gather_rows/pallas_call | solution.py:129
  12.0 2.7 %collective-permute-start.6 = (bf16[128,384]{1,0:T(8,128)(2,1)S(1)}, bf16[128,384]{1,0:T(8,128)(2,1)S(1)}, u32[]{:S(2)}, u32[]{:S(2)}) collective-permute-start(bf16[128,384]{1,0:T(8,128)(2,1)S(1)} %pad_maximum_fusion.9), channel_id=1, source_target_pairs={{0,192},{64,0},{128,64},{192,128},{1,193},{65,1},{129,65},{193,129... | collective-permute-start | bytes 294920 | tf_op jit(solution)/shard_map/ppermute | solution.py:21
  16.4 4.0 %collective-permute-start.4 = (bf16[136,384]{1,0:T(8,128)(2,1)S(1)}, bf16[136,384]{1,0:T(8,128)(2,1)S(1)}, u32[]{:S(2)}, u32[]{:S(2)}) collective-permute-start(bf16[136,384]{1,0:T(8,128)(2,1)S(1)} %pad_maximum_fusion.8), channel_id=1, source_target_pairs={{0,28},{4,0},{8,4},{12,8},{16,12},{20,16},{24,20},{28,24},{1,29},{... | collective-permute-start | bytes 313352 | tf_op jit(solution)/shard_map/ppermute | solution.py:21
  22.6 2.8 %collective-permute-start.10 = (bf16[256,384]{1,0:T(8,128)(2,1)S(1)}, bf16[256,384]{1,0:T(8,128)(2,1)S(1)}, u32[]{:S(2)}, u32[]{:S(2)}) collective-permute-start(bf16[256,384]{1,0:T(8,128)(2,1)S(1)} %pad_maximum_fusion.6), channel_id=1, source_target_pairs={{0,1},{1,0},{2,3},{3,2},{4,5},{5,4},{6,7},{7,6},{8,9},{9,8},{10,11... | collective-permute-start | bytes 589832 | tf_op jit(solution)/shard_map/ppermute | solution.py:41
  25.5 2.8 %collective-permute-start.9 = (bf16[136,384]{1,0:T(8,128)(2,1)S(1)}, bf16[136,384]{1,0:T(8,128)(2,1)S(1)}, u32[]{:S(2)}, u32[]{:S(2)}) collective-permute-start(bf16[136,384]{1,0:T(8,128)(2,1)S(1)} %collective-permute-done.4), channel_id=1, source_target_pairs={{0,28},{4,0},{8,4},{12,8},{16,12},{20,16},{24,20},{28,24},{1,29},{... | collective-permute-start | bytes 313352 | tf_op jit(solution)/shard_map/ppermute | solution.py:21
  28.4 2.2 %collective-permute-done.8 = bf16[136,384]{1,0:T(8,128)(2,1)S(1)} collective-permute-done((bf16[136,384]{1,0:T(8,128)(2,1)S(1)}, bf16[136,384]{1,0:T(8,128)(2,1)S(1)}, u32[]{:S(2)}, u32[]{:S(2)}) %collective-permute-start.8) | collective-permute-done | bytes 104480 | tf_op jit(solution)/shard_map/ppermute | solution.py:21
  31.6 2.8 %collective-permute-start.13 = (bf16[648,384]{1,0:T(8,128)(2,1)S(1)}, bf16[648,384]{1,0:T(8,128)(2,1)S(1)}, u32[]{:S(2)}, u32[]{:S(2)}) collective-permute-start(bf16[648,384]{1,0:T(8,128)(2,1)S(1)} %constant_dynamic-update-slice_fusion.6), channel_id=1, source_target_pairs={{0,28},{4,0},{8,4},{12,8},{16,12},{20,16},{24,20},{28,24},{1,29},{... | collective-permute-start | bytes 1493000 | tf_op jit(solution)/shard_map/ppermute | solution.py:21
  35.0 2.2 %collective-permute-start.17 = (bf16[680,384]{1,0:T(8,128)(2,1)S(1)}, bf16[680,384]{1,0:T(8,128)(2,1)S(1)}, u32[]{:S(2)}, u32[]{:S(2)}) collective-permute-start(bf16[680,384]{1,0:T(8,128)(2,1)S(1)} %constant_dynamic-update-slice_fusion.12.first.refs_0_), channel_id=1, source_target_pairs={{0,192},{64,0},{128,64},{192,128},{1,193},{65,1},{129,65},{193,129... | collective-permute-start | bytes 1566728 | tf_op jit(solution)/shard_map/ppermute | solution.py:21
  37.1 5.1 %collective-permute-done.13.refs_1_ = bf16[648,384]{1,0:T(8,128)(2,1)S(1)} collective-permute-done((bf16[648,384]{1,0:T(8,128)(2,1)S(1)}, bf16[648,384]{1,0:T(8,128)(2,1)S(1)}, u32[]{:S(2)}, u32[]{:S(2)}) %collective-permute-start.13) | collective-permute-done | bytes 497696 | tf_op jit(solution)/shard_map/ppermute | solution.py:21
  42.2 2.7 %collective-permute-done.12.refs_7_ = bf16[648,384]{1,0:T(8,128)(2,1)S(1)} collective-permute-done((bf16[648,384]{1,0:T(8,128)(2,1)S(1)}, bf16[648,384]{1,0:T(8,128)(2,1)S(1)}, u32[]{:S(2)}, u32[]{:S(2)}) %collective-permute-start.12) | collective-permute-done | bytes 497696 | tf_op jit(solution)/shard_map/ppermute | solution.py:21
  46.9 5.0 %collective-permute-start.21 = (bf16[128,4096]{1,0:T(8,128)(2,1)S(1)}, bf16[128,4096]{1,0:T(8,128)(2,1)S(1)}, u32[]{:S(2)}, u32[]{:S(2)}) collective-permute-start(bf16[128,4096]{1,0:T(8,128)(2,1)S(1)} %collective-permute-done.18.xn), channel_id=1, source_target_pairs={{0,2},{2,0},{1,3},{3,1},{4,6},{6,4},{5,7},{7,5},{8,10},{10,8},{9,1... | collective-permute-start | bytes 3145736 | tf_op jit(solution)/shard_map/ppermute | solution.py:33
  52.6 2.2 %collective-permute-start.20 = (bf16[568,384]{1,0:T(8,128)(2,1)S(1)}, bf16[568,384]{1,0:T(8,128)(2,1)S(1)}, u32[]{:S(2)}, u32[]{:S(2)}) collective-permute-start(bf16[568,384]{1,0:T(8,128)(2,1)S(1)} %constant_dynamic-update-slice_fusion.22), channel_id=1, source_target_pairs={{0,192},{64,0},{128,64},{192,128},{1,193},{65,1},{129,65},{193,129... | collective-permute-start | bytes 1308680 | tf_op jit(solution)/shard_map/ppermute | solution.py:21
  55.7 1.9 %collective-permute-start.29 = (bf16[512,384]{1,0:T(8,128)(2,1)S(1)}, bf16[512,384]{1,0:T(8,128)(2,1)S(1)}, u32[]{:S(2)}, u32[]{:S(2)}) collective-permute-start(bf16[512,384]{1,0:T(8,128)(2,1)S(1)} %slice.223), channel_id=1, source_target_pairs={{0,28},{4,0},{8,4},{12,8},{16,12},{20,16},{24,20},{28,24},{1,29},{... | collective-permute-start | bytes 1179656 | tf_op jit(solution)/shard_map/ppermute | solution.py:21
  57.7 6.2 %collective-permute-done.20.g_ahead.refs_6_ = bf16[568,384]{1,0:T(8,128)(2,1)S(1)} collective-permute-done((bf16[568,384]{1,0:T(8,128)(2,1)S(1)}, bf16[568,384]{1,0:T(8,128)(2,1)S(1)}, u32[]{:S(2)}, u32[]{:S(2)}) %collective-permute-start.20) | collective-permute-done | bytes 436256 | tf_op jit(solution)/shard_map/ppermute | solution.py:21
  63.9 2.1 %collective-permute-start.24 = (bf16[136,384]{1,0:T(8,128)(2,1)S(1)}, bf16[136,384]{1,0:T(8,128)(2,1)S(1)}, u32[]{:S(2)}, u32[]{:S(2)}) collective-permute-start(bf16[136,384]{1,0:T(8,128)(2,1)S(1)} %pad_maximum_fusion.7.last.refs_2_), channel_id=1, source_target_pairs={{0,128},{64,192},{128,0},{192,64},{1,129},{65,193},{129,1},{193,65... | collective-permute-start | bytes 313352 | tf_op jit(solution)/shard_map/ppermute | solution.py:21
  69.1 2.2 %collective-permute-start.31 = (bf16[256,384]{1,0:T(8,128)(2,1)S(1)}, bf16[256,384]{1,0:T(8,128)(2,1)S(1)}, u32[]{:S(2)}, u32[]{:S(2)}) collective-permute-start(bf16[256,384]{1,0:T(8,128)(2,1)S(1)} %slice.225), channel_id=1, source_target_pairs={{0,28},{4,0},{8,4},{12,8},{16,12},{20,16},{24,20},{28,24},{1,29},{... | collective-permute-start | bytes 589832 | tf_op jit(solution)/shard_map/ppermute | solution.py:21
  71.3 2.2 %gate_up_near.1 = (f32[512,384]{1,0:T(8,128)S(1)}, bf16[512,640]{1,0:T(8,128)(2,1)S(1)}) custom-call(bf16[680,384]{1,0:T(8,128)(2,1)S(1)} %constant_dynamic-update-slice_fusion.12.first.refs_0_, bf16[272,384]{1,0:T(8,128)(2,1)S(1)} %pad_maximum_fusion.4.second.refs_1_, bf16[136,384]{1,0:T(8,128)(2,1)S(1)} %pad_maximum_fusion.7.last.refs_2_, ...), custom_call_target="tpu_custom_call" | custom-call | flops 1358954496 | bytes 8388608 | tf_op jit(solution)/shard_map/gate_up_near/pallas_call | solution.py:165
  76.6 3.0 %collective-permute-start.26 = (bf16[256,192]{1,0:T(8,128)(2,1)S(1)}, bf16[256,192]{1,0:T(8,128)(2,1)S(1)}, u32[]{:S(2)}, u32[]{:S(2)}) collective-permute-start(bf16[256,192]{1,0:T(8,128)(2,1)S(1)} %get-tuple-element.76.own), channel_id=1, source_target_pairs={{0,1},{1,0},{2,3},{3,2},{4,5},{5,4},{6,7},{7,6},{8,9},{9,8},{10,11... | collective-permute-start | bytes 294920 | tf_op jit(solution)/shard_map/ppermute | solution.py:41
  79.7 3.9 %collective-permute-done.26.ha = bf16[256,192]{1,0:T(8,128)(2,1)S(1)} collective-permute-done((bf16[256,192]{1,0:T(8,128)(2,1)S(1)}, bf16[256,192]{1,0:T(8,128)(2,1)S(1)}, u32[]{:S(2)}, u32[]{:S(2)}) %collective-permute-start.26) | collective-permute-done | bytes 98336 | tf_op jit(solution)/shard_map/ppermute | solution.py:41
  85.3 3.3 %collective-permute-start.32 = (bf16[256,768]{1,0:T(8,128)(2,1)S(1)}, bf16[256,768]{1,0:T(8,128)(2,1)S(1)}, u32[]{:S(2)}, u32[]{:S(2)}) collective-permute-start(bf16[256,768]{1,0:T(8,128)(2,1)S(1)} %pad_maximum_fusion.1), channel_id=1, source_target_pairs={{0,2},{2,0},{1,3},{3,1},{4,6},{6,4},{5,7},{7,5},{8,10},{10,8},{9,1... | collective-permute-start | bytes 1179656 | tf_op jit(solution)/shard_map/ppermute | solution.py:33
  90.0 2.9 %down.1 = f32[256,1024]{1,0:T(8,128)S(1)} custom-call(s32[6]{0:T(128)S(1)} %stack.38.refs_0_.where, bf16[256,192]{1,0:T(8,128)(2,1)S(1)} %get-tuple-element.76.own, bf16[256,192]{1,0:T(8,128)(2,1)S(1)} %collective-permute-done.25.near, bf16[256,192]{1,0:T(8,128)(2,1)S(1)} %collective-permute-done.26.ha, bf16[256,192]{1,0:T(8,128)(2,1)S(1)} %collective-permute-done.27.far, ...), custom_call_target="tpu_custom_call" | custom-call | flops 805306368 | bytes 5242880 | tf_op jit(solution)/shard_map/down/pallas_call | solution.py:253
  94.9 4.1 %mix.1 = bf16[1024,2048]{1,0:T(8,128)(2,1)} custom-call(s32[6]{0:T(128)S(1)} %stack.38.refs_0_.where, f32[128,1024]{1,0:T(8,128)S(1)} %get-tuple-element.88.mine, f32[128,1024]{1,0:T(8,128)S(1)} %collective-permute-done.33.theirs, f32[8,1024]{1,0:T(8,128)S(1)} %get-tuple-element.52.info, f32[128,128]{1,0:T(8,128)S(1)} %get-tuple-element.85.slot_route, ...), custom_call_target="tpu_custom_call" | custom-call | flops 536870912 | bytes 6291456 | tf_op jit(solution)/shard_map/mix/pallas_call | solution.py:283
  (112 shorter events, 22.4 us)
Async XLA Ops:
  1.9 9.7 %collective-permute-start = (bf16[104,384]{1,0:T(8,128)(2,1)S(1)}, bf16[104,384]{1,0:T(8,128)(2,1)S(1)}, u32[]{:S(2)}, u32[]{:S(2)}) collective-permute-start(bf16[104,384]{1,0:T(8,128)(2,1)S(1)} %get-tuple-element.112), channel_id=1, source_target_pairs={{0,2},{2,0},{1,3},{3,1},{4,6},{6,4},{5,7},{7,5},{8,10},{10,8},{9,1... | collective-permute-start | bytes 239624 | tf_op jit(solution)/shard_map/ppermute | solution.py:33
  11.9 8.5 %collective-permute-start.5 = (bf16[128,384]{1,0:T(8,128)(2,1)S(1)}, bf16[128,384]{1,0:T(8,128)(2,1)S(1)}, u32[]{:S(2)}, u32[]{:S(2)}) collective-permute-start(bf16[128,384]{1,0:T(8,128)(2,1)S(1)} %pad_maximum_fusion.9), channel_id=1, source_target_pairs={{0,64},{64,128},{128,192},{192,0},{1,65},{65,129},{129,193},{193,1... | collective-permute-start | bytes 294920 | tf_op jit(solution)/shard_map/ppermute | solution.py:21
  12.0 9.8 %collective-permute-start.6 = (bf16[128,384]{1,0:T(8,128)(2,1)S(1)}, bf16[128,384]{1,0:T(8,128)(2,1)S(1)}, u32[]{:S(2)}, u32[]{:S(2)}) collective-permute-start(bf16[128,384]{1,0:T(8,128)(2,1)S(1)} %pad_maximum_fusion.9), channel_id=1, source_target_pairs={{0,192},{64,0},{128,64},{192,128},{1,193},{65,1},{129,65},{193,129... | collective-permute-start | bytes 294920 | tf_op jit(solution)/shard_map/ppermute | solution.py:21
  14.6 7.2 %collective-permute-start.7 = (bf16[128,384]{1,0:T(8,128)(2,1)S(1)}, bf16[128,384]{1,0:T(8,128)(2,1)S(1)}, u32[]{:S(2)}, u32[]{:S(2)}) collective-permute-start(bf16[128,384]{1,0:T(8,128)(2,1)S(1)} %pad_maximum_fusion.9), channel_id=1, source_target_pairs={{0,128},{64,192},{128,0},{192,64},{1,129},{65,193},{129,1},{193,65... | collective-permute-start | bytes 294920 | tf_op jit(solution)/shard_map/ppermute | solution.py:21
  14.7 7.7 %collective-permute-start.3 = (bf16[136,384]{1,0:T(8,128)(2,1)S(1)}, bf16[136,384]{1,0:T(8,128)(2,1)S(1)}, u32[]{:S(2)}, u32[]{:S(2)}) collective-permute-start(bf16[136,384]{1,0:T(8,128)(2,1)S(1)} %pad_maximum_fusion.8), channel_id=1, source_target_pairs={{0,4},{4,8},{8,12},{12,16},{16,20},{20,24},{24,28},{28,0},{1,5},{5... | collective-permute-start | bytes 313352 | tf_op jit(solution)/shard_map/ppermute | solution.py:21
  20.4 10.2 %collective-permute-start.11 = (bf16[128,4096]{1,0:T(8,128)(2,1)S(1)}, bf16[128,4096]{1,0:T(8,128)(2,1)S(1)}, u32[]{:S(2)}, u32[]{:S(2)}) collective-permute-start(bf16[128,4096]{1,0:T(8,128)(2,1)S(1)} %get-tuple-element.61.xo), channel_id=1, source_target_pairs={{0,2},{2,0},{1,3},{3,1},{4,6},{6,4},{5,7},{7,5},{8,10},{10,8},{9,1... | collective-permute-start | bytes 3145736 | tf_op jit(solution)/shard_map/ppermute | solution.py:33
  22.6 8.0 %collective-permute-start.10 = (bf16[256,384]{1,0:T(8,128)(2,1)S(1)}, bf16[256,384]{1,0:T(8,128)(2,1)S(1)}, u32[]{:S(2)}, u32[]{:S(2)}) collective-permute-start(bf16[256,384]{1,0:T(8,128)(2,1)S(1)} %pad_maximum_fusion.6), channel_id=1, source_target_pairs={{0,1},{1,0},{2,3},{3,2},{4,5},{5,4},{6,7},{7,6},{8,9},{9,8},{10,11... | collective-permute-start | bytes 589832 | tf_op jit(solution)/shard_map/ppermute | solution.py:41
  30.9 16.0 %collective-permute-start.18 = (bf16[128,4096]{1,0:T(8,128)(2,1)S(1)}, bf16[128,4096]{1,0:T(8,128)(2,1)S(1)}, u32[]{:S(2)}, u32[]{:S(2)}) collective-permute-start(bf16[128,4096]{1,0:T(8,128)(2,1)S(1)} %get-tuple-element.61.xo), channel_id=1, source_target_pairs={{0,32},{2,35},{32,1},{34,2},{1,33},{3,34},{33,0},{35,3},{4,36},{6,... | collective-permute-start | bytes 3145736 | tf_op jit(solution)/shard_map/ppermute | solution.py:49
  31.6 10.7 %collective-permute-start.13 = (bf16[648,384]{1,0:T(8,128)(2,1)S(1)}, bf16[648,384]{1,0:T(8,128)(2,1)S(1)}, u32[]{:S(2)}, u32[]{:S(2)}) collective-permute-start(bf16[648,384]{1,0:T(8,128)(2,1)S(1)} %constant_dynamic-update-slice_fusion.6), channel_id=1, source_target_pairs={{0,28},{4,0},{8,4},{12,8},{16,12},{20,16},{24,20},{28,24},{1,29},{... | collective-permute-start | bytes 1493000 | tf_op jit(solution)/shard_map/ppermute | solution.py:21
  34.3 10.6 %collective-permute-start.12 = (bf16[648,384]{1,0:T(8,128)(2,1)S(1)}, bf16[648,384]{1,0:T(8,128)(2,1)S(1)}, u32[]{:S(2)}, u32[]{:S(2)}) collective-permute-start(bf16[648,384]{1,0:T(8,128)(2,1)S(1)} %constant_dynamic-update-slice_fusion), channel_id=1, source_target_pairs={{0,4},{4,8},{8,12},{12,16},{16,20},{20,24},{24,28},{28,0},{1,5},{5... | collective-permute-start | bytes 1493000 | tf_op jit(solution)/shard_map/ppermute | solution.py:21
  34.4 12.5 %collective-permute-start.16 = (bf16[680,384]{1,0:T(8,128)(2,1)S(1)}, bf16[680,384]{1,0:T(8,128)(2,1)S(1)}, u32[]{:S(2)}, u32[]{:S(2)}) collective-permute-start(bf16[680,384]{1,0:T(8,128)(2,1)S(1)} %constant_dynamic-update-slice_fusion.12.first.refs_0_), channel_id=1, source_target_pairs={{0,64},{64,128},{128,192},{192,0},{1,65},{65,129},{129,193},{193,1... | collective-permute-start | bytes 1566728 | tf_op jit(solution)/shard_map/ppermute | solution.py:21
  35.0 11.9 %collective-permute-start.17 = (bf16[680,384]{1,0:T(8,128)(2,1)S(1)}, bf16[680,384]{1,0:T(8,128)(2,1)S(1)}, u32[]{:S(2)}, u32[]{:S(2)}) collective-permute-start(bf16[680,384]{1,0:T(8,128)(2,1)S(1)} %constant_dynamic-update-slice_fusion.12.first.refs_0_), channel_id=1, source_target_pairs={{0,192},{64,0},{128,64},{192,128},{1,193},{65,1},{129,65},{193,129... | collective-permute-start | bytes 1566728 | tf_op jit(solution)/shard_map/ppermute | solution.py:21
  45.1 9.7 %collective-permute-start.15 = (bf16[584,384]{1,0:T(8,128)(2,1)S(1)}, bf16[584,384]{1,0:T(8,128)(2,1)S(1)}, u32[]{:S(2)}, u32[]{:S(2)}) collective-permute-start(bf16[584,384]{1,0:T(8,128)(2,1)S(1)} %pad_maximum_fusion), channel_id=1, source_target_pairs={{0,28},{4,0},{8,4},{12,8},{16,12},{20,16},{24,20},{28,24},{1,29},{... | collective-permute-start | bytes 1345544 | tf_op jit(solution)/shard_map/ppermute | solution.py:21
  45.5 9.2 %collective-permute-start.14 = (bf16[576,384]{1,0:T(8,128)(2,1)S(1)}, bf16[576,384]{1,0:T(8,128)(2,1)S(1)}, u32[]{:S(2)}, u32[]{:S(2)}) collective-permute-start(bf16[576,384]{1,0:T(8,128)(2,1)S(1)} %slice.197), channel_id=1, source_target_pairs={{0,4},{4,8},{8,12},{12,16},{16,20},{20,24},{24,28},{28,0},{1,5},{5... | collective-permute-start | bytes 1327112 | tf_op jit(solution)/shard_map/ppermute | solution.py:21
  46.9 19.5 %collective-permute-start.21 = (bf16[128,4096]{1,0:T(8,128)(2,1)S(1)}, bf16[128,4096]{1,0:T(8,128)(2,1)S(1)}, u32[]{:S(2)}, u32[]{:S(2)}) collective-permute-start(bf16[128,4096]{1,0:T(8,128)(2,1)S(1)} %collective-permute-done.18.xn), channel_id=1, source_target_pairs={{0,2},{2,0},{1,3},{3,1},{4,6},{6,4},{5,7},{7,5},{8,10},{10,8},{9,1... | collective-permute-start | bytes 3145736 | tf_op jit(solution)/shard_map/ppermute | solution.py:33
  52.0 14.4 %collective-permute-start.19 = (bf16[656,384]{1,0:T(8,128)(2,1)S(1)}, bf16[656,384]{1,0:T(8,128)(2,1)S(1)}, u32[]{:S(2)}, u32[]{:S(2)}) collective-permute-start(bf16[656,384]{1,0:T(8,128)(2,1)S(1)} %get-tuple-element.103), channel_id=1, source_target_pairs={{0,64},{64,128},{128,192},{192,0},{1,65},{65,129},{129,193},{193,1... | collective-permute-start | bytes 1511432 | tf_op jit(solution)/shard_map/ppermute | solution.py:21
  52.6 11.3 %collective-permute-start.20 = (bf16[568,384]{1,0:T(8,128)(2,1)S(1)}, bf16[568,384]{1,0:T(8,128)(2,1)S(1)}, u32[]{:S(2)}, u32[]{:S(2)}) collective-permute-start(bf16[568,384]{1,0:T(8,128)(2,1)S(1)} %constant_dynamic-update-slice_fusion.22), channel_id=1, source_target_pairs={{0,192},{64,0},{128,64},{192,128},{1,193},{65,1},{129,65},{193,129... | collective-permute-start | bytes 1308680 | tf_op jit(solution)/shard_map/ppermute | solution.py:21
  54.9 13.3 %collective-permute-start.28 = (bf16[512,384]{1,0:T(8,128)(2,1)S(1)}, bf16[512,384]{1,0:T(8,128)(2,1)S(1)}, u32[]{:S(2)}, u32[]{:S(2)}) collective-permute-start(bf16[512,384]{1,0:T(8,128)(2,1)S(1)} %slice.222), channel_id=1, source_target_pairs={{0,4},{4,8},{8,12},{12,16},{16,20},{20,24},{24,28},{28,0},{1,5},{5... | collective-permute-start | bytes 1179656 | tf_op jit(solution)/shard_map/ppermute | solution.py:21
  55.7 12.5 %collective-permute-start.29 = (bf16[512,384]{1,0:T(8,128)(2,1)S(1)}, bf16[512,384]{1,0:T(8,128)(2,1)S(1)}, u32[]{:S(2)}, u32[]{:S(2)}) collective-permute-start(bf16[512,384]{1,0:T(8,128)(2,1)S(1)} %slice.223), channel_id=1, source_target_pairs={{0,28},{4,0},{8,4},{12,8},{16,12},{20,16},{24,20},{28,24},{1,29},{... | collective-permute-start | bytes 1179656 | tf_op jit(solution)/shard_map/ppermute | solution.py:21
  63.9 9.6 %collective-permute-start.24 = (bf16[136,384]{1,0:T(8,128)(2,1)S(1)}, bf16[136,384]{1,0:T(8,128)(2,1)S(1)}, u32[]{:S(2)}, u32[]{:S(2)}) collective-permute-start(bf16[136,384]{1,0:T(8,128)(2,1)S(1)} %pad_maximum_fusion.7.last.refs_2_), channel_id=1, source_target_pairs={{0,128},{64,192},{128,0},{192,64},{1,129},{65,193},{129,1},{193,65... | collective-permute-start | bytes 313352 | tf_op jit(solution)/shard_map/ppermute | solution.py:21
  66.4 8.0 %collective-permute-start.23 = (bf16[280,384]{1,0:T(8,128)(2,1)S(1)}, bf16[280,384]{1,0:T(8,128)(2,1)S(1)}, u32[]{:S(2)}, u32[]{:S(2)}) collective-permute-start(bf16[280,384]{1,0:T(8,128)(2,1)S(1)} %pad_maximum_fusion.3), channel_id=1, source_target_pairs={{0,192},{64,0},{128,64},{192,128},{1,193},{65,1},{129,65},{193,129... | collective-permute-start | bytes 645128 | tf_op jit(solution)/shard_map/ppermute | solution.py:21
  68.2 11.5 %collective-permute-start.30 = (bf16[256,384]{1,0:T(8,128)(2,1)S(1)}, bf16[256,384]{1,0:T(8,128)(2,1)S(1)}, u32[]{:S(2)}, u32[]{:S(2)}) collective-permute-start(bf16[256,384]{1,0:T(8,128)(2,1)S(1)} %slice.224), channel_id=1, source_target_pairs={{0,4},{4,8},{8,12},{12,16},{16,20},{20,24},{24,28},{28,0},{1,5},{5... | collective-permute-start | bytes 589832 | tf_op jit(solution)/shard_map/ppermute | solution.py:21
  69.1 10.6 %collective-permute-start.31 = (bf16[256,384]{1,0:T(8,128)(2,1)S(1)}, bf16[256,384]{1,0:T(8,128)(2,1)S(1)}, u32[]{:S(2)}, u32[]{:S(2)}) collective-permute-start(bf16[256,384]{1,0:T(8,128)(2,1)S(1)} %slice.225), channel_id=1, source_target_pairs={{0,28},{4,0},{8,4},{12,8},{16,12},{20,16},{24,20},{28,24},{1,29},{... | collective-permute-start | bytes 589832 | tf_op jit(solution)/shard_map/ppermute | solution.py:21
  76.6 7.1 %collective-permute-start.26 = (bf16[256,192]{1,0:T(8,128)(2,1)S(1)}, bf16[256,192]{1,0:T(8,128)(2,1)S(1)}, u32[]{:S(2)}, u32[]{:S(2)}) collective-permute-start(bf16[256,192]{1,0:T(8,128)(2,1)S(1)} %get-tuple-element.76.own), channel_id=1, source_target_pairs={{0,1},{1,0},{2,3},{3,2},{4,5},{5,4},{6,7},{7,6},{8,9},{9,8},{10,11... | collective-permute-start | bytes 294920 | tf_op jit(solution)/shard_map/ppermute | solution.py:41
  (10 other events, 51.7 us)

commit v9 on v8

--- a/solution.py
+++ b/solution.py
@@ -1,3 +1,5 @@
+import functools
+
 import jax
 import jax.numpy as jnp
 from jax import lax
@@ -262,44 +264,42 @@
     )(where, *hidden, *pieces)
 
 
-def mix_body(where, mine, theirs, info, slot_route, limit, out, slots):
-    @pl.when(pl.program_id(0) == 0)
-    def _():
-        slot = lax.broadcasted_iota(I32, (CAP, 1), 0).astype(F32)
-        scale = jnp.where(slot < limit[0:1, 0:1], slot_route[:, 0:1], 0.0)
-        for ref, column in ((mine, where[3]), (theirs, 1 - where[3])):
-            scaled = (ref[...] * scale).astype(BF16)
-            for y in range(2):
-                at = pl.multiple_of(y * 1024 + column * 512, 512)
-                slots[:, pl.ds(at, 512)] = scaled[:, y * 512 : y * 512 + 512]
-
-    picked = table(info).astype(BF16)
-    mixed = lax.dot_general(picked, slots[...], (((0,), (0,)), ((), ())), preferred_element_type=F32)
-    out[...] = mixed.astype(BF16)
-
-
-def mix(where, mine, theirs, info, slot_route, limit):
-    n, step = info.shape[1], 256
-    return pl.pallas_call(
-        mix_body,
+def mix_body(theirs, where, rows, info, slot_route, limit, *refs):
+    out, done, sent = refs[-3:]
+    slot = lax.broadcasted_iota(I32, (CAP, 1), 0).astype(F32)
+    scale = jnp.where(slot < limit[0:1, 0:1], slot_route[:, 0:1], 0.0)
+    one_hot = table(info).astype(BF16)
+    column = 1 - where[3] if theirs else where[3]
+    n = one_hot.shape[1]
+    copies = []
+    for y in range(2):
+        scaled = (rows[0:CAP, y * 512 : y * 512 + 512] * scale).astype(BF16)
+        for t in range(0, n, 256):
+            mixed = lax.dot_general(
+                one_hot[:, t : t + 256], scaled, (((0,), (0,)), ((), ())), preferred_element_type=F32
+            )
+            done[y, t : t + 256, :] = mixed.astype(BF16)
+        at = pl.multiple_of(y * 1024 + column * 512, 512)
+        copies.append(pltpu.make_async_copy(done.at[y], out.at[:, pl.ds(at, 512)], sent.at[y]))
+        copies[-1].start()
+    for copy in copies:
+        copy.wait()
+
+
+def mix(where, rows, info, slot_route, limit, half=None):
+    n = info.shape[1]
+    extra = () if half is None else (half,)
+    return pl.pallas_call(
+        functools.partial(mix_body, half is not None),
         out_shape=jax.ShapeDtypeStruct((n, 2048), BF16),
-        grid_spec=pltpu.PrefetchScalarGridSpec(
-            num_scalar_prefetch=1,
-            grid=(n // step,),
-            in_specs=[
-                pl.BlockSpec((CAP, 1024), lambda i, w: (0, 0)),
-                pl.BlockSpec((CAP, 1024), lambda i, w: (0, 0)),
-                pl.BlockSpec((8, step), lambda i, w: (0, i)),
-                pl.BlockSpec((CAP, 128), lambda i, w: (0, 0)),
-                pl.BlockSpec((8, 128), lambda i, w: (0, 0)),
-            ],
-            out_specs=pl.BlockSpec((step, 2048), lambda i, w: (i, 0)),
-            scratch_shapes=[VMEM((CAP, 2048), BF16)],
-        ),
-        compiler_params=pltpu.CompilerParams(vmem_limit_bytes=16 << 20),
-        cost_estimate=pl.CostEstimate(flops=2 * n * CAP * 2048, bytes_accessed=6 << 20, transcendentals=0),
-        name="mix",
-    )(where, mine, theirs, info, slot_route, limit)
+        in_specs=[whole(pltpu.SMEM)] + [whole()] * 4 + [whole(pltpu.HBM)] * len(extra),
+        out_specs=whole(pltpu.HBM),
+        scratch_shapes=[VMEM((2, n, 512), BF16), pltpu.SemaphoreType.DMA((2,))],
+        input_output_aliases={} if half is None else {5: 0},
+        compiler_params=pltpu.CompilerParams(vmem_limit_bytes=12 << 20),
+        cost_estimate=pl.CostEstimate(flops=2 * n * CAP * 1024, bytes_accessed=3 << 20, transcendentals=0),
+        name="mix_own" if half is None else "mix_rest",
+    )(where, rows, info, slot_route, limit, *extra)
 
 
 def with_counts(units):
@@ -390,7 +390,8 @@
     pieces = [d0, dn1, dn2, dn3, de0, up3, up2, up1, de1]
     total = down(where, (h_own, h_near, h_ha, h_far, core), pieces)
     other = C(total[128:])
-    return mix(where, total[:128], other, info, slot_route, limit)
+    half = mix(where, total, info, slot_route, limit)
+    return mix(where, other, info, slot_route, limit, half)
 
 
 def solution(mesh):

time: 99.4 us -> 98.6 us (level)
  waiting for transfers between devices: 26.6 us -> 25 us
    ppermute x5, waiting for transfers between devices: 3.01 us -> 1.36 us  [C(): return lax.ppermute(a, 'c', [(0, 1), (1, 0)])]
    pallas_call x1 -> x2, Pallas kernels: 4.07 us -> 4.77 us  [mix(): pl.pallas_call(functools.partial(mix_body, half is not None), out_shape=j...]
  transfers between devices with their start and end apart: 34 -> 34, of which waited for: 12 -> 11; matrix products, arithmetic and copies ran while one was open for 1% -> 1% of each run, Pallas kernels for 8% -> 11%
where the time goes in v9:
time: 98.6 us; the launch traced here: 98.2 us
  starting transfers between devices  53.2 us (54%)
  waiting for transfers between devices  25 us (25%)
  Pallas kernels  17.7 us (18%)
  local copies, waits for them, and re-layouts  1 us (1%)
    ppermute x22, starting transfers between devices, ring(): return lambda a: lax.ppermute(a, axis, [(i, (i + k) % n) for i in range(n)])  30.7 us
    ppermute x22, waiting for transfers between devices, ring(): return lambda a: lax.ppermute(a, axis, [(i, (i + k) % n) for i in range(n)])  18.1 us
    ppermute x5, starting transfers between devices, C(): return lax.ppermute(a, 'c', [(0, 1), (1, 0)])  13.3 us
    ppermute x2, starting transfers between devices, HA(): return lax.ppermute(a, 'ha', [(0, 1), (1, 0)])  5.84 us
    pallas_call x2, Pallas kernels, mix(): pl.pallas_call(functools.partial(mix_body, half is not None), out_shape=j...  4.77 us
    pallas_call x1, Pallas kernels, gather_rows(): pl.pallas_call(gather_body, out_shape=(jax.ShapeDtypeStruct((CAP, d), BF1...  4.64 us
    ppermute x2, waiting for transfers between devices, HA(): return lax.ppermute(a, 'ha', [(0, 1), (1, 0)])  3.93 us
    pallas_call x1, Pallas kernels, down(): pl.pallas_call(down_body, out_shape=jax.ShapeDtypeStruct((256, 1024), F32...  2.86 us
  transfers between devices with their start and end apart: 34, of which 11 were waited for; matrix products, arithmetic and copies ran while one was open for 1% of the time, Pallas kernels for 11%

profile of v9, /device:TPU:1, one launch (start us, length us, event | category | flops | bytes accessed | tf_op | source)
XLA Modules:
  0.0 98.2 jit_solution(4298191131396826013)
XLA Ops:
  1.9 3.3 %collective-permute-start = (bf16[104,384]{1,0:T(8,128)(2,1)S(1)}, bf16[104,384]{1,0:T(8,128)(2,1)S(1)}, u32[]{:S(2)}, u32[]{:S(2)}) collective-permute-start(bf16[104,384]{1,0:T(8,128)(2,1)S(1)} %get-tuple-element.110), channel_id=1, source_target_pairs={{0,2},{2,0},{1,3},{3,1},{4,6},{6,4},{5,7},{7,5},{8,10},{10,8},{9,1... | collective-permute-start | bytes 239624 | tf_op jit(solution)/shard_map/ppermute | solution.py:35
  7.0 4.6 %gather_rows.1 = (bf16[128,4096]{1,0:T(8,128)(2,1)S(1)}, f32[128,128]{1,0:T(8,128)S(1)}) custom-call(s32[6]{0:T(128)S(1)} %stack.38.refs_0_.where, bf16[1024,4096]{1,0:T(8,128)(2,1)} %tokens.1, f32[8,1024]{1,0:T(8,128)S(1)} %get-tuple-element.52.info), custom_call_target="tpu_custom_call" | custom-call | flops 1073741824 | bytes 8388608 | tf_op jit(solution)/shard_map/gather_rows/pallas_call | solution.py:131
  12.0 2.7 %collective-permute-start.6 = (bf16[128,384]{1,0:T(8,128)(2,1)S(1)}, bf16[128,384]{1,0:T(8,128)(2,1)S(1)}, u32[]{:S(2)}, u32[]{:S(2)}) collective-permute-start(bf16[128,384]{1,0:T(8,128)(2,1)S(1)} %pad_maximum_fusion.9), channel_id=1, source_target_pairs={{0,192},{64,0},{128,64},{192,128},{1,193},{65,1},{129,65},{193,129... | collective-permute-start | bytes 294920 | tf_op jit(solution)/shard_map/ppermute | solution.py:23
  16.4 4.0 %collective-permute-start.4 = (bf16[136,384]{1,0:T(8,128)(2,1)S(1)}, bf16[136,384]{1,0:T(8,128)(2,1)S(1)}, u32[]{:S(2)}, u32[]{:S(2)}) collective-permute-start(bf16[136,384]{1,0:T(8,128)(2,1)S(1)} %pad_maximum_fusion.8), channel_id=1, source_target_pairs={{0,28},{4,0},{8,4},{12,8},{16,12},{20,16},{24,20},{28,24},{1,29},{... | collective-permute-start | bytes 313352 | tf_op jit(solution)/shard_map/ppermute | solution.py:23
  22.6 2.8 %collective-permute-start.10 = (bf16[256,384]{1,0:T(8,128)(2,1)S(1)}, bf16[256,384]{1,0:T(8,128)(2,1)S(1)}, u32[]{:S(2)}, u32[]{:S(2)}) collective-permute-start(bf16[256,384]{1,0:T(8,128)(2,1)S(1)} %pad_maximum_fusion.6), channel_id=1, source_target_pairs={{0,1},{1,0},{2,3},{3,2},{4,5},{5,4},{6,7},{7,6},{8,9},{9,8},{10,11... | collective-permute-start | bytes 589832 | tf_op jit(solution)/shard_map/ppermute | solution.py:43
  25.5 2.8 %collective-permute-start.9 = (bf16[136,384]{1,0:T(8,128)(2,1)S(1)}, bf16[136,384]{1,0:T(8,128)(2,1)S(1)}, u32[]{:S(2)}, u32[]{:S(2)}) collective-permute-start(bf16[136,384]{1,0:T(8,128)(2,1)S(1)} %collective-permute-done.4), channel_id=1, source_target_pairs={{0,28},{4,0},{8,4},{12,8},{16,12},{20,16},{24,20},{28,24},{1,29},{... | collective-permute-start | bytes 313352 | tf_op jit(solution)/shard_map/ppermute | solution.py:23
  28.4 2.2 %collective-permute-done.8 = bf16[136,384]{1,0:T(8,128)(2,1)S(1)} collective-permute-done((bf16[136,384]{1,0:T(8,128)(2,1)S(1)}, bf16[136,384]{1,0:T(8,128)(2,1)S(1)}, u32[]{:S(2)}, u32[]{:S(2)}) %collective-permute-start.8) | collective-permute-done | bytes 104480 | tf_op jit(solution)/shard_map/ppermute | solution.py:23
  31.6 2.8 %collective-permute-start.13 = (bf16[648,384]{1,0:T(8,128)(2,1)S(1)}, bf16[648,384]{1,0:T(8,128)(2,1)S(1)}, u32[]{:S(2)}, u32[]{:S(2)}) collective-permute-start(bf16[648,384]{1,0:T(8,128)(2,1)S(1)} %constant_dynamic-update-slice_fusion.6), channel_id=1, source_target_pairs={{0,28},{4,0},{8,4},{12,8},{16,12},{20,16},{24,20},{28,24},{1,29},{... | collective-permute-start | bytes 1493000 | tf_op jit(solution)/shard_map/ppermute | solution.py:23
  35.0 2.2 %collective-permute-start.17 = (bf16[680,384]{1,0:T(8,128)(2,1)S(1)}, bf16[680,384]{1,0:T(8,128)(2,1)S(1)}, u32[]{:S(2)}, u32[]{:S(2)}) collective-permute-start(bf16[680,384]{1,0:T(8,128)(2,1)S(1)} %constant_dynamic-update-slice_fusion.12.first.refs_0_), channel_id=1, source_target_pairs={{0,192},{64,0},{128,64},{192,128},{1,193},{65,1},{129,65},{193,129... | collective-permute-start | bytes 1566728 | tf_op jit(solution)/shard_map/ppermute | solution.py:23
  37.1 5.1 %collective-permute-done.13.refs_1_ = bf16[648,384]{1,0:T(8,128)(2,1)S(1)} collective-permute-done((bf16[648,384]{1,0:T(8,128)(2,1)S(1)}, bf16[648,384]{1,0:T(8,128)(2,1)S(1)}, u32[]{:S(2)}, u32[]{:S(2)}) %collective-permute-start.13) | collective-permute-done | bytes 497696 | tf_op jit(solution)/shard_map/ppermute | solution.py:23
  42.2 2.7 %collective-permute-done.12.refs_7_ = bf16[648,384]{1,0:T(8,128)(2,1)S(1)} collective-permute-done((bf16[648,384]{1,0:T(8,128)(2,1)S(1)}, bf16[648,384]{1,0:T(8,128)(2,1)S(1)}, u32[]{:S(2)}, u32[]{:S(2)}) %collective-permute-start.12) | collective-permute-done | bytes 497696 | tf_op jit(solution)/shard_map/ppermute | solution.py:23
  46.9 5.0 %collective-permute-start.21 = (bf16[128,4096]{1,0:T(8,128)(2,1)S(1)}, bf16[128,4096]{1,0:T(8,128)(2,1)S(1)}, u32[]{:S(2)}, u32[]{:S(2)}) collective-permute-start(bf16[128,4096]{1,0:T(8,128)(2,1)S(1)} %collective-permute-done.18.xn), channel_id=1, source_target_pairs={{0,2},{2,0},{1,3},{3,1},{4,6},{6,4},{5,7},{7,5},{8,10},{10,8},{9,1... | collective-permute-start | bytes 3145736 | tf_op jit(solution)/shard_map/ppermute | solution.py:35
  52.6 2.2 %collective-permute-start.20 = (bf16[568,384]{1,0:T(8,128)(2,1)S(1)}, bf16[568,384]{1,0:T(8,128)(2,1)S(1)}, u32[]{:S(2)}, u32[]{:S(2)}) collective-permute-start(bf16[568,384]{1,0:T(8,128)(2,1)S(1)} %constant_dynamic-update-slice_fusion.22), channel_id=1, source_target_pairs={{0,192},{64,0},{128,64},{192,128},{1,193},{65,1},{129,65},{193,129... | collective-permute-start | bytes 1308680 | tf_op jit(solution)/shard_map/ppermute | solution.py:23
  55.7 1.9 %collective-permute-start.29 = (bf16[512,384]{1,0:T(8,128)(2,1)S(1)}, bf16[512,384]{1,0:T(8,128)(2,1)S(1)}, u32[]{:S(2)}, u32[]{:S(2)}) collective-permute-start(bf16[512,384]{1,0:T(8,128)(2,1)S(1)} %slice.220), channel_id=1, source_target_pairs={{0,28},{4,0},{8,4},{12,8},{16,12},{20,16},{24,20},{28,24},{1,29},{... | collective-permute-start | bytes 1179656 | tf_op jit(solution)/shard_map/ppermute | solution.py:23
  57.7 6.2 %collective-permute-done.20.g_ahead.refs_6_ = bf16[568,384]{1,0:T(8,128)(2,1)S(1)} collective-permute-done((bf16[568,384]{1,0:T(8,128)(2,1)S(1)}, bf16[568,384]{1,0:T(8,128)(2,1)S(1)}, u32[]{:S(2)}, u32[]{:S(2)}) %collective-permute-start.20) | collective-permute-done | bytes 436256 | tf_op jit(solution)/shard_map/ppermute | solution.py:23
  63.9 2.1 %collective-permute-start.24 = (bf16[136,384]{1,0:T(8,128)(2,1)S(1)}, bf16[136,384]{1,0:T(8,128)(2,1)S(1)}, u32[]{:S(2)}, u32[]{:S(2)}) collective-permute-start(bf16[136,384]{1,0:T(8,128)(2,1)S(1)} %pad_maximum_fusion.7.last.refs_2_), channel_id=1, source_target_pairs={{0,128},{64,192},{128,0},{192,64},{1,129},{65,193},{129,1},{193,65... | collective-permute-start | bytes 313352 | tf_op jit(solution)/shard_map/ppermute | solution.py:23
  69.1 2.2 %collective-permute-start.31 = (bf16[256,384]{1,0:T(8,128)(2,1)S(1)}, bf16[256,384]{1,0:T(8,128)(2,1)S(1)}, u32[]{:S(2)}, u32[]{:S(2)}) collective-permute-start(bf16[256,384]{1,0:T(8,128)(2,1)S(1)} %slice.222), channel_id=1, source_target_pairs={{0,28},{4,0},{8,4},{12,8},{16,12},{20,16},{24,20},{28,24},{1,29},{... | collective-permute-start | bytes 589832 | tf_op jit(solution)/shard_map/ppermute | solution.py:23
  71.3 2.2 %gate_up_near.1 = (f32[512,384]{1,0:T(8,128)S(1)}, bf16[512,640]{1,0:T(8,128)(2,1)S(1)}) custom-call(bf16[680,384]{1,0:T(8,128)(2,1)S(1)} %constant_dynamic-update-slice_fusion.12.first.refs_0_, bf16[272,384]{1,0:T(8,128)(2,1)S(1)} %pad_maximum_fusion.4.second.refs_1_, bf16[136,384]{1,0:T(8,128)(2,1)S(1)} %pad_maximum_fusion.7.last.refs_2_, ...), custom_call_target="tpu_custom_call" | custom-call | flops 1358954496 | bytes 8388608 | tf_op jit(solution)/shard_map/gate_up_near/pallas_call | solution.py:167
  76.6 3.0 %collective-permute-start.26 = (bf16[256,192]{1,0:T(8,128)(2,1)S(1)}, bf16[256,192]{1,0:T(8,128)(2,1)S(1)}, u32[]{:S(2)}, u32[]{:S(2)}) collective-permute-start(bf16[256,192]{1,0:T(8,128)(2,1)S(1)} %get-tuple-element.76.own), channel_id=1, source_target_pairs={{0,1},{1,0},{2,3},{3,2},{4,5},{5,4},{6,7},{7,6},{8,9},{9,8},{10,11... | collective-permute-start | bytes 294920 | tf_op jit(solution)/shard_map/ppermute | solution.py:43
  79.7 3.9 %collective-permute-done.26.ha = bf16[256,192]{1,0:T(8,128)(2,1)S(1)} collective-permute-done((bf16[256,192]{1,0:T(8,128)(2,1)S(1)}, bf16[256,192]{1,0:T(8,128)(2,1)S(1)}, u32[]{:S(2)}, u32[]{:S(2)}) %collective-permute-start.26) | collective-permute-done | bytes 98336 | tf_op jit(solution)/shard_map/ppermute | solution.py:43
  85.3 3.3 %collective-permute-start.32 = (bf16[256,768]{1,0:T(8,128)(2,1)S(1)}, bf16[256,768]{1,0:T(8,128)(2,1)S(1)}, u32[]{:S(2)}, u32[]{:S(2)}) collective-permute-start(bf16[256,768]{1,0:T(8,128)(2,1)S(1)} %pad_maximum_fusion.1), channel_id=1, source_target_pairs={{0,2},{2,0},{1,3},{3,1},{4,6},{6,4},{5,7},{7,5},{8,10},{10,8},{9,1... | collective-permute-start | bytes 1179656 | tf_op jit(solution)/shard_map/ppermute | solution.py:35
  90.0 2.9 %down.1.rows = f32[256,1024]{1,0:T(8,128)S(1)} custom-call(s32[6]{0:T(128)S(1)} %stack.38.refs_0_.where, bf16[256,192]{1,0:T(8,128)(2,1)S(1)} %get-tuple-element.76.own, bf16[256,192]{1,0:T(8,128)(2,1)S(1)} %collective-permute-done.25.near, bf16[256,192]{1,0:T(8,128)(2,1)S(1)} %collective-permute-done.26.ha, ...), custom_call_target="tpu_custom_call" | custom-call | flops 805306368 | bytes 5242880 | tf_op jit(solution)/shard_map/down/pallas_call | solution.py:255
  93.2 2.4 %mix_own.1.refs_0_ = bf16[1024,2048]{1,0:T(8,128)(2,1)} custom-call(s32[6]{0:T(128)S(1)} %stack.38.refs_0_.where, f32[256,1024]{1,0:T(8,128)S(1)} %down.1.rows, f32[8,1024]{1,0:T(8,128)S(1)} %get-tuple-element.52.info, f32[128,128]{1,0:T(8,128)S(1)} %get-tuple-element.85.slot_route, f32[8,128]{1,0:T(8,128)S(1)} %get-tuple-element.86.limit), custom_call_target="tpu_custom_call" | custom-call | flops 268435456 | bytes 3145728 | tf_op jit(solution)/shard_map/mix_own/pallas_call | solution.py:292
  95.6 2.4 %mix_rest.1 = bf16[1024,2048]{1,0:T(8,128)(2,1)} custom-call(s32[6]{0:T(128)S(1)} %stack.38.refs_0_.where, f32[128,1024]{1,0:T(8,128)S(1)} %collective-permute-done.33.rows, f32[8,1024]{1,0:T(8,128)S(1)} %get-tuple-element.52.info, f32[128,128]{1,0:T(8,128)S(1)} %get-tuple-element.85.slot_route, ...), custom_call_target="tpu_custom_call", output_to_operand_aliasing={{}: (5, {})} | custom-call | flops 268435456 | bytes 3145728 | tf_op jit(solution)/shard_map/mix_rest/pallas_call | solution.py:292
  (113 shorter events, 22.5 us)
Async XLA Ops:
  1.9 9.7 %collective-permute-start = (bf16[104,384]{1,0:T(8,128)(2,1)S(1)}, bf16[104,384]{1,0:T(8,128)(2,1)S(1)}, u32[]{:S(2)}, u32[]{:S(2)}) collective-permute-start(bf16[104,384]{1,0:T(8,128)(2,1)S(1)} %get-tuple-element.110), channel_id=1, source_target_pairs={{0,2},{2,0},{1,3},{3,1},{4,6},{6,4},{5,7},{7,5},{8,10},{10,8},{9,1... | collective-permute-start | bytes 239624 | tf_op jit(solution)/shard_map/ppermute | solution.py:35
  11.9 8.5 %collective-permute-start.5 = (bf16[128,384]{1,0:T(8,128)(2,1)S(1)}, bf16[128,384]{1,0:T(8,128)(2,1)S(1)}, u32[]{:S(2)}, u32[]{:S(2)}) collective-permute-start(bf16[128,384]{1,0:T(8,128)(2,1)S(1)} %pad_maximum_fusion.9), channel_id=1, source_target_pairs={{0,64},{64,128},{128,192},{192,0},{1,65},{65,129},{129,193},{193,1... | collective-permute-start | bytes 294920 | tf_op jit(solution)/shard_map/ppermute | solution.py:23
  12.0 9.8 %collective-permute-start.6 = (bf16[128,384]{1,0:T(8,128)(2,1)S(1)}, bf16[128,384]{1,0:T(8,128)(2,1)S(1)}, u32[]{:S(2)}, u32[]{:S(2)}) collective-permute-start(bf16[128,384]{1,0:T(8,128)(2,1)S(1)} %pad_maximum_fusion.9), channel_id=1, source_target_pairs={{0,192},{64,0},{128,64},{192,128},{1,193},{65,1},{129,65},{193,129... | collective-permute-start | bytes 294920 | tf_op jit(solution)/shard_map/ppermute | solution.py:23
  14.6 7.2 %collective-permute-start.7 = (bf16[128,384]{1,0:T(8,128)(2,1)S(1)}, bf16[128,384]{1,0:T(8,128)(2,1)S(1)}, u32[]{:S(2)}, u32[]{:S(2)}) collective-permute-start(bf16[128,384]{1,0:T(8,128)(2,1)S(1)} %pad_maximum_fusion.9), channel_id=1, source_target_pairs={{0,128},{64,192},{128,0},{192,64},{1,129},{65,193},{129,1},{193,65... | collective-permute-start | bytes 294920 | tf_op jit(solution)/shard_map/ppermute | solution.py:23
  14.7 7.7 %collective-permute-start.3 = (bf16[136,384]{1,0:T(8,128)(2,1)S(1)}, bf16[136,384]{1,0:T(8,128)(2,1)S(1)}, u32[]{:S(2)}, u32[]{:S(2)}) collective-permute-start(bf16[136,384]{1,0:T(8,128)(2,1)S(1)} %pad_maximum_fusion.8), channel_id=1, source_target_pairs={{0,4},{4,8},{8,12},{12,16},{16,20},{20,24},{24,28},{28,0},{1,5},{5... | collective-permute-start | bytes 313352 | tf_op jit(solution)/shard_map/ppermute | solution.py:23
  20.4 10.2 %collective-permute-start.11 = (bf16[128,4096]{1,0:T(8,128)(2,1)S(1)}, bf16[128,4096]{1,0:T(8,128)(2,1)S(1)}, u32[]{:S(2)}, u32[]{:S(2)}) collective-permute-start(bf16[128,4096]{1,0:T(8,128)(2,1)S(1)} %get-tuple-element.61.xo), channel_id=1, source_target_pairs={{0,2},{2,0},{1,3},{3,1},{4,6},{6,4},{5,7},{7,5},{8,10},{10,8},{9,1... | collective-permute-start | bytes 3145736 | tf_op jit(solution)/shard_map/ppermute | solution.py:35
  22.6 8.0 %collective-permute-start.10 = (bf16[256,384]{1,0:T(8,128)(2,1)S(1)}, bf16[256,384]{1,0:T(8,128)(2,1)S(1)}, u32[]{:S(2)}, u32[]{:S(2)}) collective-permute-start(bf16[256,384]{1,0:T(8,128)(2,1)S(1)} %pad_maximum_fusion.6), channel_id=1, source_target_pairs={{0,1},{1,0},{2,3},{3,2},{4,5},{5,4},{6,7},{7,6},{8,9},{9,8},{10,11... | collective-permute-start | bytes 589832 | tf_op jit(solution)/shard_map/ppermute | solution.py:43
  30.9 16.0 %collective-permute-start.18 = (bf16[128,4096]{1,0:T(8,128)(2,1)S(1)}, bf16[128,4096]{1,0:T(8,128)(2,1)S(1)}, u32[]{:S(2)}, u32[]{:S(2)}) collective-permute-start(bf16[128,4096]{1,0:T(8,128)(2,1)S(1)} %get-tuple-element.61.xo), channel_id=1, source_target_pairs={{0,32},{2,35},{32,1},{34,2},{1,33},{3,34},{33,0},{35,3},{4,36},{6,... | collective-permute-start | bytes 3145736 | tf_op jit(solution)/shard_map/ppermute | solution.py:51
  31.6 10.7 %collective-permute-start.13 = (bf16[648,384]{1,0:T(8,128)(2,1)S(1)}, bf16[648,384]{1,0:T(8,128)(2,1)S(1)}, u32[]{:S(2)}, u32[]{:S(2)}) collective-permute-start(bf16[648,384]{1,0:T(8,128)(2,1)S(1)} %constant_dynamic-update-slice_fusion.6), channel_id=1, source_target_pairs={{0,28},{4,0},{8,4},{12,8},{16,12},{20,16},{24,20},{28,24},{1,29},{... | collective-permute-start | bytes 1493000 | tf_op jit(solution)/shard_map/ppermute | solution.py:23
  34.3 10.6 %collective-permute-start.12 = (bf16[648,384]{1,0:T(8,128)(2,1)S(1)}, bf16[648,384]{1,0:T(8,128)(2,1)S(1)}, u32[]{:S(2)}, u32[]{:S(2)}) collective-permute-start(bf16[648,384]{1,0:T(8,128)(2,1)S(1)} %constant_dynamic-update-slice_fusion), channel_id=1, source_target_pairs={{0,4},{4,8},{8,12},{12,16},{16,20},{20,24},{24,28},{28,0},{1,5},{5... | collective-permute-start | bytes 1493000 | tf_op jit(solution)/shard_map/ppermute | solution.py:23
  34.4 12.5 %collective-permute-start.16 = (bf16[680,384]{1,0:T(8,128)(2,1)S(1)}, bf16[680,384]{1,0:T(8,128)(2,1)S(1)}, u32[]{:S(2)}, u32[]{:S(2)}) collective-permute-start(bf16[680,384]{1,0:T(8,128)(2,1)S(1)} %constant_dynamic-update-slice_fusion.12.first.refs_0_), channel_id=1, source_target_pairs={{0,64},{64,128},{128,192},{192,0},{1,65},{65,129},{129,193},{193,1... | collective-permute-start | bytes 1566728 | tf_op jit(solution)/shard_map/ppermute | solution.py:23
  35.0 11.9 %collective-permute-start.17 = (bf16[680,384]{1,0:T(8,128)(2,1)S(1)}, bf16[680,384]{1,0:T(8,128)(2,1)S(1)}, u32[]{:S(2)}, u32[]{:S(2)}) collective-permute-start(bf16[680,384]{1,0:T(8,128)(2,1)S(1)} %constant_dynamic-update-slice_fusion.12.first.refs_0_), channel_id=1, source_target_pairs={{0,192},{64,0},{128,64},{192,128},{1,193},{65,1},{129,65},{193,129... | collective-permute-start | bytes 1566728 | tf_op jit(solution)/shard_map/ppermute | solution.py:23
  45.1 9.7 %collective-permute-start.15 = (bf16[584,384]{1,0:T(8,128)(2,1)S(1)}, bf16[584,384]{1,0:T(8,128)(2,1)S(1)}, u32[]{:S(2)}, u32[]{:S(2)}) collective-permute-start(bf16[584,384]{1,0:T(8,128)(2,1)S(1)} %pad_maximum_fusion), channel_id=1, source_target_pairs={{0,28},{4,0},{8,4},{12,8},{16,12},{20,16},{24,20},{28,24},{1,29},{... | collective-permute-start | bytes 1345544 | tf_op jit(solution)/shard_map/ppermute | solution.py:23
  45.5 9.2 %collective-permute-start.14 = (bf16[576,384]{1,0:T(8,128)(2,1)S(1)}, bf16[576,384]{1,0:T(8,128)(2,1)S(1)}, u32[]{:S(2)}, u32[]{:S(2)}) collective-permute-start(bf16[576,384]{1,0:T(8,128)(2,1)S(1)} %slice.194), channel_id=1, source_target_pairs={{0,4},{4,8},{8,12},{12,16},{16,20},{20,24},{24,28},{28,0},{1,5},{5... | collective-permute-start | bytes 1327112 | tf_op jit(solution)/shard_map/ppermute | solution.py:23
  46.9 19.5 %collective-permute-start.21 = (bf16[128,4096]{1,0:T(8,128)(2,1)S(1)}, bf16[128,4096]{1,0:T(8,128)(2,1)S(1)}, u32[]{:S(2)}, u32[]{:S(2)}) collective-permute-start(bf16[128,4096]{1,0:T(8,128)(2,1)S(1)} %collective-permute-done.18.xn), channel_id=1, source_target_pairs={{0,2},{2,0},{1,3},{3,1},{4,6},{6,4},{5,7},{7,5},{8,10},{10,8},{9,1... | collective-permute-start | bytes 3145736 | tf_op jit(solution)/shard_map/ppermute | solution.py:35
  52.0 14.4 %collective-permute-start.19 = (bf16[656,384]{1,0:T(8,128)(2,1)S(1)}, bf16[656,384]{1,0:T(8,128)(2,1)S(1)}, u32[]{:S(2)}, u32[]{:S(2)}) collective-permute-start(bf16[656,384]{1,0:T(8,128)(2,1)S(1)} %get-tuple-element.101), channel_id=1, source_target_pairs={{0,64},{64,128},{128,192},{192,0},{1,65},{65,129},{129,193},{193,1... | collective-permute-start | bytes 1511432 | tf_op jit(solution)/shard_map/ppermute | solution.py:23
  52.6 11.3 %collective-permute-start.20 = (bf16[568,384]{1,0:T(8,128)(2,1)S(1)}, bf16[568,384]{1,0:T(8,128)(2,1)S(1)}, u32[]{:S(2)}, u32[]{:S(2)}) collective-permute-start(bf16[568,384]{1,0:T(8,128)(2,1)S(1)} %constant_dynamic-update-slice_fusion.22), channel_id=1, source_target_pairs={{0,192},{64,0},{128,64},{192,128},{1,193},{65,1},{129,65},{193,129... | collective-permute-start | bytes 1308680 | tf_op jit(solution)/shard_map/ppermute | solution.py:23
  54.9 13.3 %collective-permute-start.28 = (bf16[512,384]{1,0:T(8,128)(2,1)S(1)}, bf16[512,384]{1,0:T(8,128)(2,1)S(1)}, u32[]{:S(2)}, u32[]{:S(2)}) collective-permute-start(bf16[512,384]{1,0:T(8,128)(2,1)S(1)} %slice.219), channel_id=1, source_target_pairs={{0,4},{4,8},{8,12},{12,16},{16,20},{20,24},{24,28},{28,0},{1,5},{5... | collective-permute-start | bytes 1179656 | tf_op jit(solution)/shard_map/ppermute | solution.py:23
  55.7 12.5 %collective-permute-start.29 = (bf16[512,384]{1,0:T(8,128)(2,1)S(1)}, bf16[512,384]{1,0:T(8,128)(2,1)S(1)}, u32[]{:S(2)}, u32[]{:S(2)}) collective-permute-start(bf16[512,384]{1,0:T(8,128)(2,1)S(1)} %slice.220), channel_id=1, source_target_pairs={{0,28},{4,0},{8,4},{12,8},{16,12},{20,16},{24,20},{28,24},{1,29},{... | collective-permute-start | bytes 1179656 | tf_op jit(solution)/shard_map/ppermute | solution.py:23
  63.9 9.6 %collective-permute-start.24 = (bf16[136,384]{1,0:T(8,128)(2,1)S(1)}, bf16[136,384]{1,0:T(8,128)(2,1)S(1)}, u32[]{:S(2)}, u32[]{:S(2)}) collective-permute-start(bf16[136,384]{1,0:T(8,128)(2,1)S(1)} %pad_maximum_fusion.7.last.refs_2_), channel_id=1, source_target_pairs={{0,128},{64,192},{128,0},{192,64},{1,129},{65,193},{129,1},{193,65... | collective-permute-start | bytes 313352 | tf_op jit(solution)/shard_map/ppermute | solution.py:23
  66.4 8.0 %collective-permute-start.23 = (bf16[280,384]{1,0:T(8,128)(2,1)S(1)}, bf16[280,384]{1,0:T(8,128)(2,1)S(1)}, u32[]{:S(2)}, u32[]{:S(2)}) collective-permute-start(bf16[280,384]{1,0:T(8,128)(2,1)S(1)} %pad_maximum_fusion.3), channel_id=1, source_target_pairs={{0,192},{64,0},{128,64},{192,128},{1,193},{65,1},{129,65},{193,129... | collective-permute-start | bytes 645128 | tf_op jit(solution)/shard_map/ppermute | solution.py:23
  68.2 11.5 %collective-permute-start.30 = (bf16[256,384]{1,0:T(8,128)(2,1)S(1)}, bf16[256,384]{1,0:T(8,128)(2,1)S(1)}, u32[]{:S(2)}, u32[]{:S(2)}) collective-permute-start(bf16[256,384]{1,0:T(8,128)(2,1)S(1)} %slice.221), channel_id=1, source_target_pairs={{0,4},{4,8},{8,12},{12,16},{16,20},{20,24},{24,28},{28,0},{1,5},{5... | collective-permute-start | bytes 589832 | tf_op jit(solution)/shard_map/ppermute | solution.py:23
  69.1 10.6 %collective-permute-start.31 = (bf16[256,384]{1,0:T(8,128)(2,1)S(1)}, bf16[256,384]{1,0:T(8,128)(2,1)S(1)}, u32[]{:S(2)}, u32[]{:S(2)}) collective-permute-start(bf16[256,384]{1,0:T(8,128)(2,1)S(1)} %slice.222), channel_id=1, source_target_pairs={{0,28},{4,0},{8,4},{12,8},{16,12},{20,16},{24,20},{28,24},{1,29},{... | collective-permute-start | bytes 589832 | tf_op jit(solution)/shard_map/ppermute | solution.py:23
  76.6 7.1 %collective-permute-start.26 = (bf16[256,192]{1,0:T(8,128)(2,1)S(1)}, bf16[256,192]{1,0:T(8,128)(2,1)S(1)}, u32[]{:S(2)}, u32[]{:S(2)}) collective-permute-start(bf16[256,192]{1,0:T(8,128)(2,1)S(1)} %get-tuple-element.76.own), channel_id=1, source_target_pairs={{0,1},{1,0},{2,3},{3,2},{4,5},{5,4},{6,7},{7,6},{8,9},{9,8},{10,11... | collective-permute-start | bytes 294920 | tf_op jit(solution)/shard_map/ppermute | solution.py:43
  (10 other events, 52.4 us)

commit v10 on v9

--- a/solution.py
+++ b/solution.py
@@ -63,12 +63,7 @@
     chosen = jnp.max(jnp.where(hit, 1.0, 0.0), axis=0, keepdims=True)
     route = jnp.sum(jnp.where(hit, rw[...], 0.0), axis=0, keepdims=True)
     n = chosen.shape[1]
-    row = lax.broadcasted_iota(I32, (n, n), 0)
-    col = lax.broadcasted_iota(I32, (n, n), 1)
-    before = jnp.where(row < col, 1.0, 0.0).astype(BF16)
-    ones = jnp.broadcast_to(chosen, (16, n)).astype(BF16)
-    position = jnp.dot(ones, before, preferred_element_type=F32)[:1]
-    info[0:1, :] = position
+    info[0:1, :] = jnp.zeros((1, n), F32)
     info[1:2, :] = chosen
     info[2:3, :] = route
     info[3:8, :] = jnp.zeros((5, n), F32)
@@ -103,13 +98,21 @@
     return (info[0:1, :] == slot) & (info[1:2, :] > 0.5)
 
 
-def gather_body(where, tokens, info, out, slot_route, near, arrive):
+def gather_body(where, tokens, routed, out, slot_route, info, near, arrive):
     n, width = near.shape[1:]
     copies = [
         pltpu.make_async_copy(tokens.at[:, i * width : (i + 1) * width], near.at[i], arrive.at[i]) for i in range(NY)
     ]
     for copy in copies:
         copy.start()
+    chosen = routed[1:2, :]
+    row = lax.broadcasted_iota(I32, (n, n), 0)
+    col = lax.broadcasted_iota(I32, (n, n), 1)
+    before = jnp.where(row < col, 1.0, 0.0).astype(BF16)
+    ones = jnp.broadcast_to(chosen, (16, n)).astype(BF16)
+    position = jnp.dot(ones, before, preferred_element_type=F32)[:1]
+    info[0:1, :] = position
+    info[1:8, :] = routed[1:8, :]
     picked = table(info)
     got = jnp.sum(jnp.where(picked, info[2:3, :], 0.0), axis=1, keepdims=True)
     slot_route[...] = jnp.broadcast_to(got, slot_route.shape)
@@ -130,9 +133,13 @@
     n, d = tokens.shape
     return pl.pallas_call(
         gather_body,
-        out_shape=(jax.ShapeDtypeStruct((CAP, d), BF16), jax.ShapeDtypeStruct((CAP, 128), F32)),
+        out_shape=(
+            jax.ShapeDtypeStruct((CAP, d), BF16),
+            jax.ShapeDtypeStruct((CAP, 128), F32),
+            jax.ShapeDtypeStruct(info.shape, F32),
+        ),
         in_specs=[whole(pltpu.SMEM), whole(pltpu.HBM), whole()],
-        out_specs=(whole(), whole()),
+        out_specs=(whole(), whole(), whole()),
         scratch_shapes=[VMEM((NY, n, d // NY), tokens.dtype), pltpu.SemaphoreType.DMA((NY,))],
         compiler_params=pltpu.CompilerParams(vmem_limit_bytes=16 << 20),
         cost_estimate=pl.CostEstimate(flops=2 * CAP * n * d, bytes_accessed=2 * n * d, transcendentals=0),
@@ -279,9 +286,15 @@
                 one_hot[:, t : t + 256], scaled, (((0,), (0,)), ((), ())), preferred_element_type=F32
             )
             done[y, t : t + 256, :] = mixed.astype(BF16)
-        at = pl.multiple_of(y * 1024 + column * 512, 512)
-        copies.append(pltpu.make_async_copy(done.at[y], out.at[:, pl.ds(at, 512)], sent.at[y]))
-        copies[-1].start()
+            if t % 512 == 256:
+                part = pl.ds(t - 256, 512)
+                at = pl.multiple_of(y * 1024 + column * 512, 512)
+                copies.append(
+                    pltpu.make_async_copy(
+                        done.at[y, part, :], out.at[part, pl.ds(at, 512)], sent.at[2 * y + t // 512]
+                    )
+                )
+                copies[-1].start()
     for copy in copies:
         copy.wait()
 
@@ -294,7 +307,7 @@
         out_shape=jax.ShapeDtypeStruct((n, 2048), BF16),
         in_specs=[whole(pltpu.SMEM)] + [whole()] * 4 + [whole(pltpu.HBM)] * len(extra),
         out_specs=whole(pltpu.HBM),
-        scratch_shapes=[VMEM((2, n, 512), BF16), pltpu.SemaphoreType.DMA((2,))],
+        scratch_shapes=[VMEM((2, n, 512), BF16), pltpu.SemaphoreType.DMA((4,))],
         input_output_aliases={} if half is None else {5: 0},
         compiler_params=pltpu.CompilerParams(vmem_limit_bytes=12 << 20),
         cost_estimate=pl.CostEstimate(flops=2 * n * CAP * 1024, bytes_accessed=3 << 20, transcendentals=0),
@@ -326,7 +339,7 @@
     tiles = [packed[0], C(packed[1]), XL(packed[2]), lax.ppermute(packed[3], ("xl", "c"), both)]
     tiles = [jnp.where(c == 0, tiles[k], tiles[k ^ 1]) for k in range(4)]
     arrived = jnp.stack([jnp.where(xl == 0, tiles[k], tiles[k ^ 2]) for k in range(4)])
-    slot_rows, slot_route = gather_rows(where, pltpu.with_memory_space_constraint(tokens, pltpu.HBM), info)
+    slot_rows, slot_route, info = gather_rows(where, pltpu.with_memory_space_constraint(tokens, pltpu.HBM), info)
 
     lane = lax.broadcasted_iota(I32, (8, 384), 1)
     tile = jnp.zeros((8, 384), BF16)

time: 98.6 us -> 98.5 us (level)
  no operation moved by 1% of the time
where the time goes in v10:
time: 98.5 us; the launch traced here: 98.1 us
  starting transfers between devices  53.2 us (54%)
  waiting for transfers between devices  25 us (25%)
  Pallas kernels  17.6 us (18%)
  local copies, waits for them, and re-layouts  1 us (1%)
    ppermute x22, starting transfers between devices, ring(): return lambda a: lax.ppermute(a, axis, [(i, (i + k) % n) for i in range(n)])  30.7 us
    ppermute x22, waiting for transfers between devices, ring(): return lambda a: lax.ppermute(a, axis, [(i, (i + k) % n) for i in range(n)])  18.1 us
    ppermute x5, starting transfers between devices, C(): return lax.ppermute(a, 'c', [(0, 1), (1, 0)])  13.3 us
    ppermute x2, starting transfers between devices, HA(): return lax.ppermute(a, 'ha', [(0, 1), (1, 0)])  5.84 us
    pallas_call x1, Pallas kernels, gather_rows(): pl.pallas_call(gather_body, out_shape=(jax.ShapeDtypeStruct((CAP, d), BF1...  4.99 us
    pallas_call x2, Pallas kernels, mix(): pl.pallas_call(functools.partial(mix_body, half is not None), out_shape=j...  4.51 us
    ppermute x2, waiting for transfers between devices, HA(): return lax.ppermute(a, 'ha', [(0, 1), (1, 0)])  3.94 us
    pallas_call x1, Pallas kernels, down(): pl.pallas_call(down_body, out_shape=jax.ShapeDtypeStruct((256, 1024), F32...  2.86 us
  transfers between devices with their start and end apart: 34, of which 11 were waited for; matrix products, arithmetic and copies ran while one was open for 1% of the time, Pallas kernels for 11%

profile of v10, /device:TPU:1, one launch (start us, length us, event | category | flops | bytes accessed | tf_op | source)
XLA Modules:
  0.0 98.1 jit_solution(5662308120276078343)
XLA Ops:
  1.8 3.3 %collective-permute-start = (bf16[104,384]{1,0:T(8,128)(2,1)S(1)}, bf16[104,384]{1,0:T(8,128)(2,1)S(1)}, u32[]{:S(2)}, u32[]{:S(2)}) collective-permute-start(bf16[104,384]{1,0:T(8,128)(2,1)S(1)} %get-tuple-element.112), channel_id=1, source_target_pairs={{0,2},{2,0},{1,3},{3,1},{4,6},{6,4},{5,7},{7,5},{8,10},{10,8},{9,1... | collective-permute-start | bytes 239624 | tf_op jit(solution)/shard_map/ppermute | solution.py:35
  6.8 5.0 %gather_rows.1 = (bf16[128,4096]{1,0:T(8,128)(2,1)S(1)}, f32[128,128]{1,0:T(8,128)S(1)}, f32[8,1024]{1,0:T(8,128)S(1)}) custom-call(s32[6]{0:T(128)S(1)} %stack.38.refs_0_.where, bf16[1024,4096]{1,0:T(8,128)(2,1)} %tokens.1, f32[8,1024]{1,0:T(8,128)S(1)} %get-tuple-element.53.routed), custom_call_target="tpu_custom_call" | custom-call | flops 1073741824 | bytes 8388608 | tf_op jit(solution)/shard_map/gather_rows/pallas_call | solution.py:134
  12.1 2.7 %collective-permute-start.6 = (bf16[128,384]{1,0:T(8,128)(2,1)S(1)}, bf16[128,384]{1,0:T(8,128)(2,1)S(1)}, u32[]{:S(2)}, u32[]{:S(2)}) collective-permute-start(bf16[128,384]{1,0:T(8,128)(2,1)S(1)} %pad_maximum_fusion.9), channel_id=1, source_target_pairs={{0,192},{64,0},{128,64},{192,128},{1,193},{65,1},{129,65},{193,129... | collective-permute-start | bytes 294920 | tf_op jit(solution)/shard_map/ppermute | solution.py:23
  16.5 4.0 %collective-permute-start.4 = (bf16[136,384]{1,0:T(8,128)(2,1)S(1)}, bf16[136,384]{1,0:T(8,128)(2,1)S(1)}, u32[]{:S(2)}, u32[]{:S(2)}) collective-permute-start(bf16[136,384]{1,0:T(8,128)(2,1)S(1)} %pad_maximum_fusion.8), channel_id=1, source_target_pairs={{0,28},{4,0},{8,4},{12,8},{16,12},{20,16},{24,20},{28,24},{1,29},{... | collective-permute-start | bytes 313352 | tf_op jit(solution)/shard_map/ppermute | solution.py:23
  22.8 2.8 %collective-permute-start.10 = (bf16[256,384]{1,0:T(8,128)(2,1)S(1)}, bf16[256,384]{1,0:T(8,128)(2,1)S(1)}, u32[]{:S(2)}, u32[]{:S(2)}) collective-permute-start(bf16[256,384]{1,0:T(8,128)(2,1)S(1)} %pad_maximum_fusion.6), channel_id=1, source_target_pairs={{0,1},{1,0},{2,3},{3,2},{4,5},{5,4},{6,7},{7,6},{8,9},{9,8},{10,11... | collective-permute-start | bytes 589832 | tf_op jit(solution)/shard_map/ppermute | solution.py:43
  25.6 2.8 %collective-permute-start.9 = (bf16[136,384]{1,0:T(8,128)(2,1)S(1)}, bf16[136,384]{1,0:T(8,128)(2,1)S(1)}, u32[]{:S(2)}, u32[]{:S(2)}) collective-permute-start(bf16[136,384]{1,0:T(8,128)(2,1)S(1)} %collective-permute-done.4), channel_id=1, source_target_pairs={{0,28},{4,0},{8,4},{12,8},{16,12},{20,16},{24,20},{28,24},{1,29},{... | collective-permute-start | bytes 313352 | tf_op jit(solution)/shard_map/ppermute | solution.py:23
  28.5 2.2 %collective-permute-done.8 = bf16[136,384]{1,0:T(8,128)(2,1)S(1)} collective-permute-done((bf16[136,384]{1,0:T(8,128)(2,1)S(1)}, bf16[136,384]{1,0:T(8,128)(2,1)S(1)}, u32[]{:S(2)}, u32[]{:S(2)}) %collective-permute-start.8) | collective-permute-done | bytes 104480 | tf_op jit(solution)/shard_map/ppermute | solution.py:23
  31.7 2.8 %collective-permute-start.13 = (bf16[648,384]{1,0:T(8,128)(2,1)S(1)}, bf16[648,384]{1,0:T(8,128)(2,1)S(1)}, u32[]{:S(2)}, u32[]{:S(2)}) collective-permute-start(bf16[648,384]{1,0:T(8,128)(2,1)S(1)} %constant_dynamic-update-slice_fusion.6), channel_id=1, source_target_pairs={{0,28},{4,0},{8,4},{12,8},{16,12},{20,16},{24,20},{28,24},{1,29},{... | collective-permute-start | bytes 1493000 | tf_op jit(solution)/shard_map/ppermute | solution.py:23
  35.1 2.2 %collective-permute-start.17 = (bf16[680,384]{1,0:T(8,128)(2,1)S(1)}, bf16[680,384]{1,0:T(8,128)(2,1)S(1)}, u32[]{:S(2)}, u32[]{:S(2)}) collective-permute-start(bf16[680,384]{1,0:T(8,128)(2,1)S(1)} %constant_dynamic-update-slice_fusion.12.first.refs_0_), channel_id=1, source_target_pairs={{0,192},{64,0},{128,64},{192,128},{1,193},{65,1},{129,65},{193,129... | collective-permute-start | bytes 1566728 | tf_op jit(solution)/shard_map/ppermute | solution.py:23
  37.3 5.1 %collective-permute-done.13.refs_1_ = bf16[648,384]{1,0:T(8,128)(2,1)S(1)} collective-permute-done((bf16[648,384]{1,0:T(8,128)(2,1)S(1)}, bf16[648,384]{1,0:T(8,128)(2,1)S(1)}, u32[]{:S(2)}, u32[]{:S(2)}) %collective-permute-start.13) | collective-permute-done | bytes 497696 | tf_op jit(solution)/shard_map/ppermute | solution.py:23
  42.4 2.7 %collective-permute-done.12.refs_7_ = bf16[648,384]{1,0:T(8,128)(2,1)S(1)} collective-permute-done((bf16[648,384]{1,0:T(8,128)(2,1)S(1)}, bf16[648,384]{1,0:T(8,128)(2,1)S(1)}, u32[]{:S(2)}, u32[]{:S(2)}) %collective-permute-start.12) | collective-permute-done | bytes 497696 | tf_op jit(solution)/shard_map/ppermute | solution.py:23
  47.0 5.0 %collective-permute-start.21 = (bf16[128,4096]{1,0:T(8,128)(2,1)S(1)}, bf16[128,4096]{1,0:T(8,128)(2,1)S(1)}, u32[]{:S(2)}, u32[]{:S(2)}) collective-permute-start(bf16[128,4096]{1,0:T(8,128)(2,1)S(1)} %collective-permute-done.18.xn), channel_id=1, source_target_pairs={{0,2},{2,0},{1,3},{3,1},{4,6},{6,4},{5,7},{7,5},{8,10},{10,8},{9,1... | collective-permute-start | bytes 3145736 | tf_op jit(solution)/shard_map/ppermute | solution.py:35
  52.7 2.2 %collective-permute-start.20 = (bf16[568,384]{1,0:T(8,128)(2,1)S(1)}, bf16[568,384]{1,0:T(8,128)(2,1)S(1)}, u32[]{:S(2)}, u32[]{:S(2)}) collective-permute-start(bf16[568,384]{1,0:T(8,128)(2,1)S(1)} %constant_dynamic-update-slice_fusion.22), channel_id=1, source_target_pairs={{0,192},{64,0},{128,64},{192,128},{1,193},{65,1},{129,65},{193,129... | collective-permute-start | bytes 1308680 | tf_op jit(solution)/shard_map/ppermute | solution.py:23
  55.9 1.9 %collective-permute-start.29 = (bf16[512,384]{1,0:T(8,128)(2,1)S(1)}, bf16[512,384]{1,0:T(8,128)(2,1)S(1)}, u32[]{:S(2)}, u32[]{:S(2)}) collective-permute-start(bf16[512,384]{1,0:T(8,128)(2,1)S(1)} %slice.220), channel_id=1, source_target_pairs={{0,28},{4,0},{8,4},{12,8},{16,12},{20,16},{24,20},{28,24},{1,29},{... | collective-permute-start | bytes 1179656 | tf_op jit(solution)/shard_map/ppermute | solution.py:23
  57.8 6.2 %collective-permute-done.20.g_ahead.refs_6_ = bf16[568,384]{1,0:T(8,128)(2,1)S(1)} collective-permute-done((bf16[568,384]{1,0:T(8,128)(2,1)S(1)}, bf16[568,384]{1,0:T(8,128)(2,1)S(1)}, u32[]{:S(2)}, u32[]{:S(2)}) %collective-permute-start.20) | collective-permute-done | bytes 436256 | tf_op jit(solution)/shard_map/ppermute | solution.py:23
  64.1 2.1 %collective-permute-start.24 = (bf16[136,384]{1,0:T(8,128)(2,1)S(1)}, bf16[136,384]{1,0:T(8,128)(2,1)S(1)}, u32[]{:S(2)}, u32[]{:S(2)}) collective-permute-start(bf16[136,384]{1,0:T(8,128)(2,1)S(1)} %pad_maximum_fusion.7.last.refs_2_), channel_id=1, source_target_pairs={{0,128},{64,192},{128,0},{192,64},{1,129},{65,193},{129,1},{193,65... | collective-permute-start | bytes 313352 | tf_op jit(solution)/shard_map/ppermute | solution.py:23
  69.2 2.2 %collective-permute-start.31 = (bf16[256,384]{1,0:T(8,128)(2,1)S(1)}, bf16[256,384]{1,0:T(8,128)(2,1)S(1)}, u32[]{:S(2)}, u32[]{:S(2)}) collective-permute-start(bf16[256,384]{1,0:T(8,128)(2,1)S(1)} %slice.222), channel_id=1, source_target_pairs={{0,28},{4,0},{8,4},{12,8},{16,12},{20,16},{24,20},{28,24},{1,29},{... | collective-permute-start | bytes 589832 | tf_op jit(solution)/shard_map/ppermute | solution.py:23
  71.5 2.2 %gate_up_near.1 = (f32[512,384]{1,0:T(8,128)S(1)}, bf16[512,640]{1,0:T(8,128)(2,1)S(1)}) custom-call(bf16[680,384]{1,0:T(8,128)(2,1)S(1)} %constant_dynamic-update-slice_fusion.12.first.refs_0_, bf16[272,384]{1,0:T(8,128)(2,1)S(1)} %pad_maximum_fusion.4.second.refs_1_, bf16[136,384]{1,0:T(8,128)(2,1)S(1)} %pad_maximum_fusion.7.last.refs_2_, ...), custom_call_target="tpu_custom_call" | custom-call | flops 1358954496 | bytes 8388608 | tf_op jit(solution)/shard_map/gate_up_near/pallas_call | solution.py:174
  76.8 3.0 %collective-permute-start.26 = (bf16[256,192]{1,0:T(8,128)(2,1)S(1)}, bf16[256,192]{1,0:T(8,128)(2,1)S(1)}, u32[]{:S(2)}, u32[]{:S(2)}) collective-permute-start(bf16[256,192]{1,0:T(8,128)(2,1)S(1)} %get-tuple-element.77.own), channel_id=1, source_target_pairs={{0,1},{1,0},{2,3},{3,2},{4,5},{5,4},{6,7},{7,6},{8,9},{9,8},{10,11... | collective-permute-start | bytes 294920 | tf_op jit(solution)/shard_map/ppermute | solution.py:43
  79.9 3.9 %collective-permute-done.26.ha = bf16[256,192]{1,0:T(8,128)(2,1)S(1)} collective-permute-done((bf16[256,192]{1,0:T(8,128)(2,1)S(1)}, bf16[256,192]{1,0:T(8,128)(2,1)S(1)}, u32[]{:S(2)}, u32[]{:S(2)}) %collective-permute-start.26) | collective-permute-done | bytes 98336 | tf_op jit(solution)/shard_map/ppermute | solution.py:43
  85.5 3.3 %collective-permute-start.32 = (bf16[256,768]{1,0:T(8,128)(2,1)S(1)}, bf16[256,768]{1,0:T(8,128)(2,1)S(1)}, u32[]{:S(2)}, u32[]{:S(2)}) collective-permute-start(bf16[256,768]{1,0:T(8,128)(2,1)S(1)} %pad_maximum_fusion.1), channel_id=1, source_target_pairs={{0,2},{2,0},{1,3},{3,1},{4,6},{6,4},{5,7},{7,5},{8,10},{10,8},{9,1... | collective-permute-start | bytes 1179656 | tf_op jit(solution)/shard_map/ppermute | solution.py:35
  90.1 2.9 %down.1.rows = f32[256,1024]{1,0:T(8,128)S(1)} custom-call(s32[6]{0:T(128)S(1)} %stack.38.refs_0_.where, bf16[256,192]{1,0:T(8,128)(2,1)S(1)} %get-tuple-element.77.own, bf16[256,192]{1,0:T(8,128)(2,1)S(1)} %collective-permute-done.25.near, bf16[256,192]{1,0:T(8,128)(2,1)S(1)} %collective-permute-done.26.ha, ...), custom_call_target="tpu_custom_call" | custom-call | flops 805306368 | bytes 5242880 | tf_op jit(solution)/shard_map/down/pallas_call | solution.py:262
  93.4 2.3 %mix_own.1.refs_0_ = bf16[1024,2048]{1,0:T(8,128)(2,1)} custom-call(s32[6]{0:T(128)S(1)} %stack.38.refs_0_.where, f32[256,1024]{1,0:T(8,128)S(1)} %down.1.rows, f32[8,1024]{1,0:T(8,128)S(1)} %get-tuple-element.86.info, f32[128,128]{1,0:T(8,128)S(1)} %get-tuple-element.87.slot_route, f32[8,128]{1,0:T(8,128)S(1)} %get-tuple-element.88.limit), custom_call_target="tpu_custom_call" | custom-call | flops 268435456 | bytes 3145728 | tf_op jit(solution)/shard_map/mix_own/pallas_call | solution.py:305
  95.6 2.3 %mix_rest.1 = bf16[1024,2048]{1,0:T(8,128)(2,1)} custom-call(s32[6]{0:T(128)S(1)} %stack.38.refs_0_.where, f32[128,1024]{1,0:T(8,128)S(1)} %collective-permute-done.33.rows, f32[8,1024]{1,0:T(8,128)S(1)} %get-tuple-element.86.info, f32[128,128]{1,0:T(8,128)S(1)} %get-tuple-element.87.slot_route, ...), custom_call_target="tpu_custom_call", output_to_operand_aliasing={{}: (5, {})} | custom-call | flops 268435456 | bytes 3145728 | tf_op jit(solution)/shard_map/mix_rest/pallas_call | solution.py:305
  (113 shorter events, 22.3 us)
Async XLA Ops:
  1.8 10.1 %collective-permute-start = (bf16[104,384]{1,0:T(8,128)(2,1)S(1)}, bf16[104,384]{1,0:T(8,128)(2,1)S(1)}, u32[]{:S(2)}, u32[]{:S(2)}) collective-permute-start(bf16[104,384]{1,0:T(8,128)(2,1)S(1)} %get-tuple-element.112), channel_id=1, source_target_pairs={{0,2},{2,0},{1,3},{3,1},{4,6},{6,4},{5,7},{7,5},{8,10},{10,8},{9,1... | collective-permute-start | bytes 239624 | tf_op jit(solution)/shard_map/ppermute | solution.py:35
  12.0 8.5 %collective-permute-start.5 = (bf16[128,384]{1,0:T(8,128)(2,1)S(1)}, bf16[128,384]{1,0:T(8,128)(2,1)S(1)}, u32[]{:S(2)}, u32[]{:S(2)}) collective-permute-start(bf16[128,384]{1,0:T(8,128)(2,1)S(1)} %pad_maximum_fusion.9), channel_id=1, source_target_pairs={{0,64},{64,128},{128,192},{192,0},{1,65},{65,129},{129,193},{193,1... | collective-permute-start | bytes 294920 | tf_op jit(solution)/shard_map/ppermute | solution.py:23
  12.1 9.8 %collective-permute-start.6 = (bf16[128,384]{1,0:T(8,128)(2,1)S(1)}, bf16[128,384]{1,0:T(8,128)(2,1)S(1)}, u32[]{:S(2)}, u32[]{:S(2)}) collective-permute-start(bf16[128,384]{1,0:T(8,128)(2,1)S(1)} %pad_maximum_fusion.9), channel_id=1, source_target_pairs={{0,192},{64,0},{128,64},{192,128},{1,193},{65,1},{129,65},{193,129... | collective-permute-start | bytes 294920 | tf_op jit(solution)/shard_map/ppermute | solution.py:23
  14.8 7.2 %collective-permute-start.7 = (bf16[128,384]{1,0:T(8,128)(2,1)S(1)}, bf16[128,384]{1,0:T(8,128)(2,1)S(1)}, u32[]{:S(2)}, u32[]{:S(2)}) collective-permute-start(bf16[128,384]{1,0:T(8,128)(2,1)S(1)} %pad_maximum_fusion.9), channel_id=1, source_target_pairs={{0,128},{64,192},{128,0},{192,64},{1,129},{65,193},{129,1},{193,65... | collective-permute-start | bytes 294920 | tf_op jit(solution)/shard_map/ppermute | solution.py:23
  14.9 7.7 %collective-permute-start.3 = (bf16[136,384]{1,0:T(8,128)(2,1)S(1)}, bf16[136,384]{1,0:T(8,128)(2,1)S(1)}, u32[]{:S(2)}, u32[]{:S(2)}) collective-permute-start(bf16[136,384]{1,0:T(8,128)(2,1)S(1)} %pad_maximum_fusion.8), channel_id=1, source_target_pairs={{0,4},{4,8},{8,12},{12,16},{16,20},{20,24},{24,28},{28,0},{1,5},{5... | collective-permute-start | bytes 313352 | tf_op jit(solution)/shard_map/ppermute | solution.py:23
  20.6 10.2 %collective-permute-start.11 = (bf16[128,4096]{1,0:T(8,128)(2,1)S(1)}, bf16[128,4096]{1,0:T(8,128)(2,1)S(1)}, u32[]{:S(2)}, u32[]{:S(2)}) collective-permute-start(bf16[128,4096]{1,0:T(8,128)(2,1)S(1)} %get-tuple-element.62.xo), channel_id=1, source_target_pairs={{0,2},{2,0},{1,3},{3,1},{4,6},{6,4},{5,7},{7,5},{8,10},{10,8},{9,1... | collective-permute-start | bytes 3145736 | tf_op jit(solution)/shard_map/ppermute | solution.py:35
  22.8 8.0 %collective-permute-start.10 = (bf16[256,384]{1,0:T(8,128)(2,1)S(1)}, bf16[256,384]{1,0:T(8,128)(2,1)S(1)}, u32[]{:S(2)}, u32[]{:S(2)}) collective-permute-start(bf16[256,384]{1,0:T(8,128)(2,1)S(1)} %pad_maximum_fusion.6), channel_id=1, source_target_pairs={{0,1},{1,0},{2,3},{3,2},{4,5},{5,4},{6,7},{7,6},{8,9},{9,8},{10,11... | collective-permute-start | bytes 589832 | tf_op jit(solution)/shard_map/ppermute | solution.py:43
  31.0 16.0 %collective-permute-start.18 = (bf16[128,4096]{1,0:T(8,128)(2,1)S(1)}, bf16[128,4096]{1,0:T(8,128)(2,1)S(1)}, u32[]{:S(2)}, u32[]{:S(2)}) collective-permute-start(bf16[128,4096]{1,0:T(8,128)(2,1)S(1)} %get-tuple-element.62.xo), channel_id=1, source_target_pairs={{0,32},{2,35},{32,1},{34,2},{1,33},{3,34},{33,0},{35,3},{4,36},{6,... | collective-permute-start | bytes 3145736 | tf_op jit(solution)/shard_map/ppermute | solution.py:51
  31.7 10.7 %collective-permute-start.13 = (bf16[648,384]{1,0:T(8,128)(2,1)S(1)}, bf16[648,384]{1,0:T(8,128)(2,1)S(1)}, u32[]{:S(2)}, u32[]{:S(2)}) collective-permute-start(bf16[648,384]{1,0:T(8,128)(2,1)S(1)} %constant_dynamic-update-slice_fusion.6), channel_id=1, source_target_pairs={{0,28},{4,0},{8,4},{12,8},{16,12},{20,16},{24,20},{28,24},{1,29},{... | collective-permute-start | bytes 1493000 | tf_op jit(solution)/shard_map/ppermute | solution.py:23
  34.5 10.6 %collective-permute-start.12 = (bf16[648,384]{1,0:T(8,128)(2,1)S(1)}, bf16[648,384]{1,0:T(8,128)(2,1)S(1)}, u32[]{:S(2)}, u32[]{:S(2)}) collective-permute-start(bf16[648,384]{1,0:T(8,128)(2,1)S(1)} %constant_dynamic-update-slice_fusion), channel_id=1, source_target_pairs={{0,4},{4,8},{8,12},{12,16},{16,20},{20,24},{24,28},{28,0},{1,5},{5... | collective-permute-start | bytes 1493000 | tf_op jit(solution)/shard_map/ppermute | solution.py:23
  34.5 12.5 %collective-permute-start.16 = (bf16[680,384]{1,0:T(8,128)(2,1)S(1)}, bf16[680,384]{1,0:T(8,128)(2,1)S(1)}, u32[]{:S(2)}, u32[]{:S(2)}) collective-permute-start(bf16[680,384]{1,0:T(8,128)(2,1)S(1)} %constant_dynamic-update-slice_fusion.12.first.refs_0_), channel_id=1, source_target_pairs={{0,64},{64,128},{128,192},{192,0},{1,65},{65,129},{129,193},{193,1... | collective-permute-start | bytes 1566728 | tf_op jit(solution)/shard_map/ppermute | solution.py:23
  35.1 11.9 %collective-permute-start.17 = (bf16[680,384]{1,0:T(8,128)(2,1)S(1)}, bf16[680,384]{1,0:T(8,128)(2,1)S(1)}, u32[]{:S(2)}, u32[]{:S(2)}) collective-permute-start(bf16[680,384]{1,0:T(8,128)(2,1)S(1)} %constant_dynamic-update-slice_fusion.12.first.refs_0_), channel_id=1, source_target_pairs={{0,192},{64,0},{128,64},{192,128},{1,193},{65,1},{129,65},{193,129... | collective-permute-start | bytes 1566728 | tf_op jit(solution)/shard_map/ppermute | solution.py:23
  45.2 9.7 %collective-permute-start.15 = (bf16[584,384]{1,0:T(8,128)(2,1)S(1)}, bf16[584,384]{1,0:T(8,128)(2,1)S(1)}, u32[]{:S(2)}, u32[]{:S(2)}) collective-permute-start(bf16[584,384]{1,0:T(8,128)(2,1)S(1)} %pad_maximum_fusion), channel_id=1, source_target_pairs={{0,28},{4,0},{8,4},{12,8},{16,12},{20,16},{24,20},{28,24},{1,29},{... | collective-permute-start | bytes 1345544 | tf_op jit(solution)/shard_map/ppermute | solution.py:23
  45.6 9.3 %collective-permute-start.14 = (bf16[576,384]{1,0:T(8,128)(2,1)S(1)}, bf16[576,384]{1,0:T(8,128)(2,1)S(1)}, u32[]{:S(2)}, u32[]{:S(2)}) collective-permute-start(bf16[576,384]{1,0:T(8,128)(2,1)S(1)} %slice.194), channel_id=1, source_target_pairs={{0,4},{4,8},{8,12},{12,16},{16,20},{20,24},{24,28},{28,0},{1,5},{5... | collective-permute-start | bytes 1327112 | tf_op jit(solution)/shard_map/ppermute | solution.py:23
  47.0 19.5 %collective-permute-start.21 = (bf16[128,4096]{1,0:T(8,128)(2,1)S(1)}, bf16[128,4096]{1,0:T(8,128)(2,1)S(1)}, u32[]{:S(2)}, u32[]{:S(2)}) collective-permute-start(bf16[128,4096]{1,0:T(8,128)(2,1)S(1)} %collective-permute-done.18.xn), channel_id=1, source_target_pairs={{0,2},{2,0},{1,3},{3,1},{4,6},{6,4},{5,7},{7,5},{8,10},{10,8},{9,1... | collective-permute-start | bytes 3145736 | tf_op jit(solution)/shard_map/ppermute | solution.py:35
  52.1 14.4 %collective-permute-start.19 = (bf16[656,384]{1,0:T(8,128)(2,1)S(1)}, bf16[656,384]{1,0:T(8,128)(2,1)S(1)}, u32[]{:S(2)}, u32[]{:S(2)}) collective-permute-start(bf16[656,384]{1,0:T(8,128)(2,1)S(1)} %get-tuple-element.103), channel_id=1, source_target_pairs={{0,64},{64,128},{128,192},{192,0},{1,65},{65,129},{129,193},{193,1... | collective-permute-start | bytes 1511432 | tf_op jit(solution)/shard_map/ppermute | solution.py:23
  52.7 11.3 %collective-permute-start.20 = (bf16[568,384]{1,0:T(8,128)(2,1)S(1)}, bf16[568,384]{1,0:T(8,128)(2,1)S(1)}, u32[]{:S(2)}, u32[]{:S(2)}) collective-permute-start(bf16[568,384]{1,0:T(8,128)(2,1)S(1)} %constant_dynamic-update-slice_fusion.22), channel_id=1, source_target_pairs={{0,192},{64,0},{128,64},{192,128},{1,193},{65,1},{129,65},{193,129... | collective-permute-start | bytes 1308680 | tf_op jit(solution)/shard_map/ppermute | solution.py:23
  55.0 13.3 %collective-permute-start.28 = (bf16[512,384]{1,0:T(8,128)(2,1)S(1)}, bf16[512,384]{1,0:T(8,128)(2,1)S(1)}, u32[]{:S(2)}, u32[]{:S(2)}) collective-permute-start(bf16[512,384]{1,0:T(8,128)(2,1)S(1)} %slice.219), channel_id=1, source_target_pairs={{0,4},{4,8},{8,12},{12,16},{16,20},{20,24},{24,28},{28,0},{1,5},{5... | collective-permute-start | bytes 1179656 | tf_op jit(solution)/shard_map/ppermute | solution.py:23
  55.9 12.5 %collective-permute-start.29 = (bf16[512,384]{1,0:T(8,128)(2,1)S(1)}, bf16[512,384]{1,0:T(8,128)(2,1)S(1)}, u32[]{:S(2)}, u32[]{:S(2)}) collective-permute-start(bf16[512,384]{1,0:T(8,128)(2,1)S(1)} %slice.220), channel_id=1, source_target_pairs={{0,28},{4,0},{8,4},{12,8},{16,12},{20,16},{24,20},{28,24},{1,29},{... | collective-permute-start | bytes 1179656 | tf_op jit(solution)/shard_map/ppermute | solution.py:23
  64.1 9.6 %collective-permute-start.24 = (bf16[136,384]{1,0:T(8,128)(2,1)S(1)}, bf16[136,384]{1,0:T(8,128)(2,1)S(1)}, u32[]{:S(2)}, u32[]{:S(2)}) collective-permute-start(bf16[136,384]{1,0:T(8,128)(2,1)S(1)} %pad_maximum_fusion.7.last.refs_2_), channel_id=1, source_target_pairs={{0,128},{64,192},{128,0},{192,64},{1,129},{65,193},{129,1},{193,65... | collective-permute-start | bytes 313352 | tf_op jit(solution)/shard_map/ppermute | solution.py:23
  66.6 8.0 %collective-permute-start.23 = (bf16[280,384]{1,0:T(8,128)(2,1)S(1)}, bf16[280,384]{1,0:T(8,128)(2,1)S(1)}, u32[]{:S(2)}, u32[]{:S(2)}) collective-permute-start(bf16[280,384]{1,0:T(8,128)(2,1)S(1)} %pad_maximum_fusion.3), channel_id=1, source_target_pairs={{0,192},{64,0},{128,64},{192,128},{1,193},{65,1},{129,65},{193,129... | collective-permute-start | bytes 645128 | tf_op jit(solution)/shard_map/ppermute | solution.py:23
  68.4 11.5 %collective-permute-start.30 = (bf16[256,384]{1,0:T(8,128)(2,1)S(1)}, bf16[256,384]{1,0:T(8,128)(2,1)S(1)}, u32[]{:S(2)}, u32[]{:S(2)}) collective-permute-start(bf16[256,384]{1,0:T(8,128)(2,1)S(1)} %slice.221), channel_id=1, source_target_pairs={{0,4},{4,8},{8,12},{12,16},{16,20},{20,24},{24,28},{28,0},{1,5},{5... | collective-permute-start | bytes 589832 | tf_op jit(solution)/shard_map/ppermute | solution.py:23
  69.2 10.6 %collective-permute-start.31 = (bf16[256,384]{1,0:T(8,128)(2,1)S(1)}, bf16[256,384]{1,0:T(8,128)(2,1)S(1)}, u32[]{:S(2)}, u32[]{:S(2)}) collective-permute-start(bf16[256,384]{1,0:T(8,128)(2,1)S(1)} %slice.222), channel_id=1, source_target_pairs={{0,28},{4,0},{8,4},{12,8},{16,12},{20,16},{24,20},{28,24},{1,29},{... | collective-permute-start | bytes 589832 | tf_op jit(solution)/shard_map/ppermute | solution.py:23
  76.8 7.0 %collective-permute-start.26 = (bf16[256,192]{1,0:T(8,128)(2,1)S(1)}, bf16[256,192]{1,0:T(8,128)(2,1)S(1)}, u32[]{:S(2)}, u32[]{:S(2)}) collective-permute-start(bf16[256,192]{1,0:T(8,128)(2,1)S(1)} %get-tuple-element.77.own), channel_id=1, source_target_pairs={{0,1},{1,0},{2,3},{3,2},{4,5},{5,4},{6,7},{7,6},{8,9},{9,8},{10,11... | collective-permute-start | bytes 294920 | tf_op jit(solution)/shard_map/ppermute | solution.py:43
  (10 other events, 53.0 us)

commit v11 on v9

--- a/solution.py
+++ b/solution.py
@@ -279,9 +279,15 @@
                 one_hot[:, t : t + 256], scaled, (((0,), (0,)), ((), ())), preferred_element_type=F32
             )
             done[y, t : t + 256, :] = mixed.astype(BF16)
-        at = pl.multiple_of(y * 1024 + column * 512, 512)
-        copies.append(pltpu.make_async_copy(done.at[y], out.at[:, pl.ds(at, 512)], sent.at[y]))
-        copies[-1].start()
+            if t % 512 == 256:
+                part = pl.ds(t - 256, 512)
+                at = pl.multiple_of(y * 1024 + column * 512, 512)
+                copies.append(
+                    pltpu.make_async_copy(
+                        done.at[y, part, :], out.at[part, pl.ds(at, 512)], sent.at[2 * y + t // 512]
+                    )
+                )
+                copies[-1].start()
     for copy in copies:
         copy.wait()
 
@@ -294,7 +300,7 @@
         out_shape=jax.ShapeDtypeStruct((n, 2048), BF16),
         in_specs=[whole(pltpu.SMEM)] + [whole()] * 4 + [whole(pltpu.HBM)] * len(extra),
         out_specs=whole(pltpu.HBM),
-        scratch_shapes=[VMEM((2, n, 512), BF16), pltpu.SemaphoreType.DMA((2,))],
+        scratch_shapes=[VMEM((2, n, 512), BF16), pltpu.SemaphoreType.DMA((4,))],
         input_output_aliases={} if half is None else {5: 0},
         compiler_params=pltpu.CompilerParams(vmem_limit_bytes=12 << 20),
         cost_estimate=pl.CostEstimate(flops=2 * n * CAP * 1024, bytes_accessed=3 << 20, transcendentals=0),
@@ -369,7 +375,7 @@
     g_back = Y(1)(jnp.concatenate([second[:256], f_back[:384], second[256:]], axis=0))
     g_ahead = Y(-1)(jnp.concatenate([second[:256], f_ahead[384:640], second[256:], f_ahead[640:]], axis=0))
     far_rows = C(neighbour_rows)
-    up2, dn2 = together(up2, dn2)
+    up2, dn2, far_rows = together(up2, dn2, far_rows)
     g_back, g_ahead, far_rows = together(g_back, g_ahead, far_rows)
 
     last = jnp.concatenate([up2[512:], dn2[512:]], axis=0)

time: 98.6 us -> 103 us (1.045)
  waiting for transfers between devices: 25 us -> 29.9 us
    ppermute x22, starting transfers between devices: 30.7 us -> 26.3 us  [ring(): return lambda a: lax.ppermute(a, axis, [(i, (i + k) % n) for i in range(n)])]
    ppermute x22, waiting for transfers between devices: 18.1 us -> 21.5 us  [ring(): return lambda a: lax.ppermute(a, axis, [(i, (i + k) % n) for i in range(n)])]
    ppermute x5, starting transfers between devices: 13.3 us -> 15.9 us  [C(): return lax.ppermute(a, 'c', [(0, 1), (1, 0)])]
    ppermute x2, waiting for transfers between devices: 3.93 us -> 5.75 us  [HA(): return lax.ppermute(a, 'ha', [(0, 1), (1, 0)])]
    ppermute x1, starting transfers between devices: 0.69 us -> 2.48 us  [across_x(): return lax.ppermute(a, ('xl', 'c', 'ha'), pairs)]
    ppermute x1, starting transfers between devices: 1.73 us -> 0.01 us  [per_device(): lax.ppermute(packed[3], ('xl', 'c'), both)]
    ppermute x1, starting transfers between devices: 0.1 us -> 1.35 us  [HIDDEN_FAR(): return lax.ppermute(a, ('xl', 'ha'), pairs)]
  transfers between devices with their start and end apart: 34 -> 34, of which waited for: 11 -> 13; matrix products, arithmetic and copies ran while one was open for 1% -> 1% of each run, Pallas kernels for 11% -> 10%
where the time goes in v11:
time: 103 us
  starting transfers between devices  52.9 us (51%)
  waiting for transfers between devices  29.9 us (29%)
  Pallas kernels  17.4 us (17%)
    ppermute x22, starting transfers between devices, ring(): return lambda a: lax.ppermute(a, axis, [(i, (i + k) % n) for i in range(n)])  26.3 us
    ppermute x22, waiting for transfers between devices, ring(): return lambda a: lax.ppermute(a, axis, [(i, (i + k) % n) for i in range(n)])  21.5 us
    ppermute x5, starting transfers between devices, C(): return lax.ppermute(a, 'c', [(0, 1), (1, 0)])  15.9 us
    ppermute x2, waiting for transfers between devices, HA(): return lax.ppermute(a, 'ha', [(0, 1), (1, 0)])  5.75 us
    ppermute x2, starting transfers between devices, HA(): return lax.ppermute(a, 'ha', [(0, 1), (1, 0)])  5.42 us
    pallas_call x1, Pallas kernels, gather_rows(): pl.pallas_call(gather_body, out_shape=(jax.ShapeDtypeStruct((CAP, d), BF1...  4.64 us
    pallas_call x2, Pallas kernels, mix(): pl.pallas_call(functools.partial(mix_body, half is not None), out_shape=j...  4.52 us
    pallas_call x1, Pallas kernels, down(): pl.pallas_call(down_body, out_shape=jax.ShapeDtypeStruct((256, 1024), F32...  2.86 us
  transfers between devices with their start and end apart: 34, of which 13 were waited for; matrix products, arithmetic and copies ran while one was open for 1% of the time, Pallas kernels for 10%

profile of v11, /device:TPU:1, one launch (start us, length us, event | category | flops | bytes accessed | tf_op | source)
XLA Modules:
  0.0 102.6 jit_solution(18015610577111465412)
XLA Ops:
  1.9 3.3 %collective-permute-start = (bf16[104,384]{1,0:T(8,128)(2,1)S(1)}, bf16[104,384]{1,0:T(8,128)(2,1)S(1)}, u32[]{:S(2)}, u32[]{:S(2)}) collective-permute-start(bf16[104,384]{1,0:T(8,128)(2,1)S(1)} %get-tuple-element.112), channel_id=1, source_target_pairs={{0,2},{2,0},{1,3},{3,1},{4,6},{6,4},{5,7},{7,5},{8,10},{10,8},{9,1... | collective-permute-start | bytes 239624 | tf_op jit(solution)/shard_map/ppermute | solution.py:35
  6.7 4.6 %gather_rows.1 = (bf16[128,4096]{1,0:T(8,128)(2,1)S(1)}, f32[128,128]{1,0:T(8,128)S(1)}) custom-call(s32[6]{0:T(128)S(1)} %stack.38.refs_0_.where, bf16[1024,4096]{1,0:T(8,128)(2,1)} %tokens.1, f32[8,1024]{1,0:T(8,128)S(1)} %get-tuple-element.53.info), custom_call_target="tpu_custom_call" | custom-call | flops 1073741824 | bytes 8388608 | tf_op jit(solution)/shard_map/gather_rows/pallas_call | solution.py:131
  14.4 5.7 %collective-permute-start.4 = (bf16[136,384]{1,0:T(8,128)(2,1)S(1)}, bf16[136,384]{1,0:T(8,128)(2,1)S(1)}, u32[]{:S(2)}, u32[]{:S(2)}) collective-permute-start(bf16[136,384]{1,0:T(8,128)(2,1)S(1)} %pad_maximum_fusion.8), channel_id=1, source_target_pairs={{0,28},{4,0},{8,4},{12,8},{16,12},{20,16},{24,20},{28,24},{1,29},{... | collective-permute-start | bytes 313352 | tf_op jit(solution)/shard_map/ppermute | solution.py:23
  22.0 2.8 %collective-permute-done.3 = bf16[136,384]{1,0:T(8,128)(2,1)S(1)} collective-permute-done((bf16[136,384]{1,0:T(8,128)(2,1)S(1)}, bf16[136,384]{1,0:T(8,128)(2,1)S(1)}, u32[]{:S(2)}, u32[]{:S(2)}) %collective-permute-start.3) | collective-permute-done | bytes 104480 | tf_op jit(solution)/shard_map/ppermute | solution.py:23
  25.1 2.7 %collective-permute-start.9 = (bf16[136,384]{1,0:T(8,128)(2,1)S(1)}, bf16[136,384]{1,0:T(8,128)(2,1)S(1)}, u32[]{:S(2)}, u32[]{:S(2)}) collective-permute-start(bf16[136,384]{1,0:T(8,128)(2,1)S(1)} %collective-permute-done.4), channel_id=1, source_target_pairs={{0,28},{4,0},{8,4},{12,8},{16,12},{20,16},{24,20},{28,24},{1,29},{... | collective-permute-start | bytes 313352 | tf_op jit(solution)/shard_map/ppermute | solution.py:23
  27.8 2.8 %collective-permute-start.10 = (bf16[256,384]{1,0:T(8,128)(2,1)S(1)}, bf16[256,384]{1,0:T(8,128)(2,1)S(1)}, u32[]{:S(2)}, u32[]{:S(2)}) collective-permute-start(bf16[256,384]{1,0:T(8,128)(2,1)S(1)} %pad_maximum_fusion.6), channel_id=1, source_target_pairs={{0,1},{1,0},{2,3},{3,2},{4,5},{5,4},{6,7},{7,6},{8,9},{9,8},{10,11... | collective-permute-start | bytes 589832 | tf_op jit(solution)/shard_map/ppermute | solution.py:43
  30.8 3.1 %collective-permute-done.10 = bf16[256,384]{1,0:T(8,128)(2,1)S(1)} collective-permute-done((bf16[256,384]{1,0:T(8,128)(2,1)S(1)}, bf16[256,384]{1,0:T(8,128)(2,1)S(1)}, u32[]{:S(2)}, u32[]{:S(2)}) %collective-permute-start.10) | collective-permute-done | bytes 196640 | tf_op jit(solution)/shard_map/ppermute | solution.py:43
  35.7 2.5 %collective-permute-start.18 = (bf16[128,4096]{1,0:T(8,128)(2,1)S(1)}, bf16[128,4096]{1,0:T(8,128)(2,1)S(1)}, u32[]{:S(2)}, u32[]{:S(2)}) collective-permute-start(bf16[128,4096]{1,0:T(8,128)(2,1)S(1)} %get-tuple-element.60.xo), channel_id=1, source_target_pairs={{0,32},{2,35},{32,1},{34,2},{1,33},{3,34},{33,0},{35,3},{4,36},{6,... | collective-permute-start | bytes 3145736 | tf_op jit(solution)/shard_map/ppermute | solution.py:51
  38.2 2.1 %collective-permute-start.17 = (bf16[680,384]{1,0:T(8,128)(2,1)S(1)}, bf16[680,384]{1,0:T(8,128)(2,1)S(1)}, u32[]{:S(2)}, u32[]{:S(2)}) collective-permute-start(bf16[680,384]{1,0:T(8,128)(2,1)S(1)} %constant_dynamic-update-slice_fusion.12.first.refs_0_), channel_id=1, source_target_pairs={{0,192},{64,0},{128,64},{192,128},{1,193},{65,1},{129,65},{193,129... | collective-permute-start | bytes 1566728 | tf_op jit(solution)/shard_map/ppermute | solution.py:23
  40.2 2.1 %collective-permute-done.13.refs_1_ = bf16[648,384]{1,0:T(8,128)(2,1)S(1)} collective-permute-done((bf16[648,384]{1,0:T(8,128)(2,1)S(1)}, bf16[648,384]{1,0:T(8,128)(2,1)S(1)}, u32[]{:S(2)}, u32[]{:S(2)}) %collective-permute-start.13) | collective-permute-done | bytes 497696 | tf_op jit(solution)/shard_map/ppermute | solution.py:23
  44.1 2.7 %collective-permute-start.15 = (bf16[584,384]{1,0:T(8,128)(2,1)S(1)}, bf16[584,384]{1,0:T(8,128)(2,1)S(1)}, u32[]{:S(2)}, u32[]{:S(2)}) collective-permute-start(bf16[584,384]{1,0:T(8,128)(2,1)S(1)} %pad_maximum_fusion), channel_id=1, source_target_pairs={{0,28},{4,0},{8,4},{12,8},{16,12},{20,16},{24,20},{28,24},{1,29},{... | collective-permute-start | bytes 1345544 | tf_op jit(solution)/shard_map/ppermute | solution.py:23
  47.4 2.9 %collective-permute-done.16.f_back.refs_3_ = bf16[680,384]{1,0:T(8,128)(2,1)S(1)} collective-permute-done((bf16[680,384]{1,0:T(8,128)(2,1)S(1)}, bf16[680,384]{1,0:T(8,128)(2,1)S(1)}, u32[]{:S(2)}, u32[]{:S(2)}) %collective-permute-start.16) | collective-permute-done | bytes 522272 | tf_op jit(solution)/shard_map/ppermute | solution.py:23
  50.3 6.7 %collective-permute-start.19 = (bf16[128,4096]{1,0:T(8,128)(2,1)S(1)}, bf16[128,4096]{1,0:T(8,128)(2,1)S(1)}, u32[]{:S(2)}, u32[]{:S(2)}) collective-permute-start(bf16[128,4096]{1,0:T(8,128)(2,1)S(1)} %collective-permute-done.18.xn), channel_id=1, source_target_pairs={{0,2},{2,0},{1,3},{3,1},{4,6},{6,4},{5,7},{7,5},{8,10},{10,8},{9,1... | collective-permute-start | bytes 3145736 | tf_op jit(solution)/shard_map/ppermute | solution.py:35
  57.5 2.3 %collective-permute-start.21 = (bf16[568,384]{1,0:T(8,128)(2,1)S(1)}, bf16[568,384]{1,0:T(8,128)(2,1)S(1)}, u32[]{:S(2)}, u32[]{:S(2)}) collective-permute-start(bf16[568,384]{1,0:T(8,128)(2,1)S(1)} %constant_dynamic-update-slice_fusion.22), channel_id=1, source_target_pairs={{0,192},{64,0},{128,64},{192,128},{1,193},{65,1},{129,65},{193,129... | collective-permute-start | bytes 1308680 | tf_op jit(solution)/shard_map/ppermute | solution.py:23
  61.6 7.4 %collective-permute-done.21.g_ahead.refs_6_ = bf16[568,384]{1,0:T(8,128)(2,1)S(1)} collective-permute-done((bf16[568,384]{1,0:T(8,128)(2,1)S(1)}, bf16[568,384]{1,0:T(8,128)(2,1)S(1)}, u32[]{:S(2)}, u32[]{:S(2)}) %collective-permute-start.21) | collective-permute-done | bytes 436256 | tf_op jit(solution)/shard_map/ppermute | solution.py:23
  69.0 2.5 %collective-permute-done.20.g_back.refs_5_ = bf16[656,384]{1,0:T(8,128)(2,1)S(1)} collective-permute-done((bf16[656,384]{1,0:T(8,128)(2,1)S(1)}, bf16[656,384]{1,0:T(8,128)(2,1)S(1)}, u32[]{:S(2)}, u32[]{:S(2)}) %collective-permute-start.20) | collective-permute-done | bytes 503840 | tf_op jit(solution)/shard_map/ppermute | solution.py:23
  71.7 2.7 %collective-permute-start.23 = (bf16[280,384]{1,0:T(8,128)(2,1)S(1)}, bf16[280,384]{1,0:T(8,128)(2,1)S(1)}, u32[]{:S(2)}, u32[]{:S(2)}) collective-permute-start(bf16[280,384]{1,0:T(8,128)(2,1)S(1)} %pad_maximum_fusion.3), channel_id=1, source_target_pairs={{0,192},{64,0},{128,64},{192,128},{1,193},{65,1},{129,65},{193,129... | collective-permute-start | bytes 645128 | tf_op jit(solution)/shard_map/ppermute | solution.py:23
  76.1 2.2 %gate_up_near.1 = (f32[512,384]{1,0:T(8,128)S(1)}, bf16[512,640]{1,0:T(8,128)(2,1)S(1)}) custom-call(bf16[680,384]{1,0:T(8,128)(2,1)S(1)} %constant_dynamic-update-slice_fusion.12.first.refs_0_, bf16[272,384]{1,0:T(8,128)(2,1)S(1)} %pad_maximum_fusion.4.second.refs_1_, bf16[136,384]{1,0:T(8,128)(2,1)S(1)} %pad_maximum_fusion.7.last.refs_2_, ...), custom_call_target="tpu_custom_call" | custom-call | flops 1358954496 | bytes 8388608 | tf_op jit(solution)/shard_map/gate_up_near/pallas_call | solution.py:167
  83.0 2.6 %collective-permute-start.26 = (bf16[256,192]{1,0:T(8,128)(2,1)S(1)}, bf16[256,192]{1,0:T(8,128)(2,1)S(1)}, u32[]{:S(2)}, u32[]{:S(2)}) collective-permute-start(bf16[256,192]{1,0:T(8,128)(2,1)S(1)} %get-tuple-element.78.own), channel_id=1, source_target_pairs={{0,1},{1,0},{2,3},{3,2},{4,5},{5,4},{6,7},{7,6},{8,9},{9,8},{10,11... | collective-permute-start | bytes 294920 | tf_op jit(solution)/shard_map/ppermute | solution.py:43
  86.8 2.6 %collective-permute-done.26.ha = bf16[256,192]{1,0:T(8,128)(2,1)S(1)} collective-permute-done((bf16[256,192]{1,0:T(8,128)(2,1)S(1)}, bf16[256,192]{1,0:T(8,128)(2,1)S(1)}, u32[]{:S(2)}, u32[]{:S(2)}) %collective-permute-start.26) | collective-permute-done | bytes 98336 | tf_op jit(solution)/shard_map/ppermute | solution.py:43
  89.6 3.7 %collective-permute-start.32 = (bf16[256,768]{1,0:T(8,128)(2,1)S(1)}, bf16[256,768]{1,0:T(8,128)(2,1)S(1)}, u32[]{:S(2)}, u32[]{:S(2)}) collective-permute-start(bf16[256,768]{1,0:T(8,128)(2,1)S(1)} %pad_maximum_fusion.1), channel_id=1, source_target_pairs={{0,2},{2,0},{1,3},{3,1},{4,6},{6,4},{5,7},{7,5},{8,10},{10,8},{9,1... | collective-permute-start | bytes 1179656 | tf_op jit(solution)/shard_map/ppermute | solution.py:35
  94.6 2.9 %down.1.rows = f32[256,1024]{1,0:T(8,128)S(1)} custom-call(s32[6]{0:T(128)S(1)} %stack.38.refs_0_.where, bf16[256,192]{1,0:T(8,128)(2,1)S(1)} %get-tuple-element.78.own, bf16[256,192]{1,0:T(8,128)(2,1)S(1)} %collective-permute-done.25.near, bf16[256,192]{1,0:T(8,128)(2,1)S(1)} %collective-permute-done.26.ha, ...), custom_call_target="tpu_custom_call" | custom-call | flops 805306368 | bytes 5242880 | tf_op jit(solution)/shard_map/down/pallas_call | solution.py:255
  97.9 2.3 %mix_own.1.refs_0_ = bf16[1024,2048]{1,0:T(8,128)(2,1)} custom-call(s32[6]{0:T(128)S(1)} %stack.38.refs_0_.where, f32[256,1024]{1,0:T(8,128)S(1)} %down.1.rows, f32[8,1024]{1,0:T(8,128)S(1)} %get-tuple-element.53.info, f32[128,128]{1,0:T(8,128)S(1)} %get-tuple-element.87.slot_route, f32[8,128]{1,0:T(8,128)S(1)} %get-tuple-element.88.limit), custom_call_target="tpu_custom_call" | custom-call | flops 268435456 | bytes 3145728 | tf_op jit(solution)/shard_map/mix_own/pallas_call | solution.py:298
  100.1 2.3 %mix_rest.1 = bf16[1024,2048]{1,0:T(8,128)(2,1)} custom-call(s32[6]{0:T(128)S(1)} %stack.38.refs_0_.where, f32[128,1024]{1,0:T(8,128)S(1)} %collective-permute-done.33.rows, f32[8,1024]{1,0:T(8,128)S(1)} %get-tuple-element.53.info, f32[128,128]{1,0:T(8,128)S(1)} %get-tuple-element.87.slot_route, ...), custom_call_target="tpu_custom_call", output_to_operand_aliasing={{}: (5, {})} | custom-call | flops 268435456 | bytes 3145728 | tf_op jit(solution)/shard_map/mix_rest/pallas_call | solution.py:298
  (113 shorter events, 24.4 us)
Async XLA Ops:
  1.9 9.5 %collective-permute-start = (bf16[104,384]{1,0:T(8,128)(2,1)S(1)}, bf16[104,384]{1,0:T(8,128)(2,1)S(1)}, u32[]{:S(2)}, u32[]{:S(2)}) collective-permute-start(bf16[104,384]{1,0:T(8,128)(2,1)S(1)} %get-tuple-element.112), channel_id=1, source_target_pairs={{0,2},{2,0},{1,3},{3,1},{4,6},{6,4},{5,7},{7,5},{8,10},{10,8},{9,1... | collective-permute-start | bytes 239624 | tf_op jit(solution)/shard_map/ppermute | solution.py:35
  5.3 6.1 %collective-permute-start.1 = (bf16[104,384]{1,0:T(8,128)(2,1)S(1)}, bf16[104,384]{1,0:T(8,128)(2,1)S(1)}, u32[]{:S(2)}, u32[]{:S(2)}) collective-permute-start(bf16[104,384]{1,0:T(8,128)(2,1)S(1)} %get-tuple-element.114), channel_id=1, source_target_pairs={{0,32},{32,0},{1,33},{33,1},{2,34},{34,2},{3,35},{35,3},{4,36},{36... | collective-permute-start | bytes 239624 | tf_op jit(solution)/shard_map/ppermute | solution.py:39
  11.6 8.4 %collective-permute-start.7 = (bf16[128,384]{1,0:T(8,128)(2,1)S(1)}, bf16[128,384]{1,0:T(8,128)(2,1)S(1)}, u32[]{:S(2)}, u32[]{:S(2)}) collective-permute-start(bf16[128,384]{1,0:T(8,128)(2,1)S(1)} %pad_maximum_fusion.9), channel_id=1, source_target_pairs={{0,128},{64,192},{128,0},{192,64},{1,129},{65,193},{129,1},{193,65... | collective-permute-start | bytes 294920 | tf_op jit(solution)/shard_map/ppermute | solution.py:23
  12.9 9.1 %collective-permute-start.6 = (bf16[128,384]{1,0:T(8,128)(2,1)S(1)}, bf16[128,384]{1,0:T(8,128)(2,1)S(1)}, u32[]{:S(2)}, u32[]{:S(2)}) collective-permute-start(bf16[128,384]{1,0:T(8,128)(2,1)S(1)} %pad_maximum_fusion.9), channel_id=1, source_target_pairs={{0,192},{64,0},{128,64},{192,128},{1,193},{65,1},{129,65},{193,129... | collective-permute-start | bytes 294920 | tf_op jit(solution)/shard_map/ppermute | solution.py:23
  13.7 8.3 %collective-permute-start.5 = (bf16[128,384]{1,0:T(8,128)(2,1)S(1)}, bf16[128,384]{1,0:T(8,128)(2,1)S(1)}, u32[]{:S(2)}, u32[]{:S(2)}) collective-permute-start(bf16[128,384]{1,0:T(8,128)(2,1)S(1)} %pad_maximum_fusion.9), channel_id=1, source_target_pairs={{0,64},{64,128},{128,192},{192,0},{1,65},{65,129},{129,193},{193,1... | collective-permute-start | bytes 294920 | tf_op jit(solution)/shard_map/ppermute | solution.py:23
  14.4 7.6 %collective-permute-start.4 = (bf16[136,384]{1,0:T(8,128)(2,1)S(1)}, bf16[136,384]{1,0:T(8,128)(2,1)S(1)}, u32[]{:S(2)}, u32[]{:S(2)}) collective-permute-start(bf16[136,384]{1,0:T(8,128)(2,1)S(1)} %pad_maximum_fusion.8), channel_id=1, source_target_pairs={{0,28},{4,0},{8,4},{12,8},{16,12},{20,16},{24,20},{28,24},{1,29},{... | collective-permute-start | bytes 313352 | tf_op jit(solution)/shard_map/ppermute | solution.py:23
  20.1 13.8 %collective-permute-start.11 = (bf16[128,4096]{1,0:T(8,128)(2,1)S(1)}, bf16[128,4096]{1,0:T(8,128)(2,1)S(1)}, u32[]{:S(2)}, u32[]{:S(2)}) collective-permute-start(bf16[128,4096]{1,0:T(8,128)(2,1)S(1)} %get-tuple-element.60.xo), channel_id=1, source_target_pairs={{0,2},{2,0},{1,3},{3,1},{4,6},{6,4},{5,7},{7,5},{8,10},{10,8},{9,1... | collective-permute-start | bytes 3145736 | tf_op jit(solution)/shard_map/ppermute | solution.py:35
  34.1 8.2 %collective-permute-start.13 = (bf16[648,384]{1,0:T(8,128)(2,1)S(1)}, bf16[648,384]{1,0:T(8,128)(2,1)S(1)}, u32[]{:S(2)}, u32[]{:S(2)}) collective-permute-start(bf16[648,384]{1,0:T(8,128)(2,1)S(1)} %constant_dynamic-update-slice_fusion.6), channel_id=1, source_target_pairs={{0,28},{4,0},{8,4},{12,8},{16,12},{20,16},{24,20},{28,24},{1,29},{... | collective-permute-start | bytes 1493000 | tf_op jit(solution)/shard_map/ppermute | solution.py:23
  34.2 9.6 %collective-permute-start.12 = (bf16[648,384]{1,0:T(8,128)(2,1)S(1)}, bf16[648,384]{1,0:T(8,128)(2,1)S(1)}, u32[]{:S(2)}, u32[]{:S(2)}) collective-permute-start(bf16[648,384]{1,0:T(8,128)(2,1)S(1)} %constant_dynamic-update-slice_fusion), channel_id=1, source_target_pairs={{0,4},{4,8},{8,12},{12,16},{16,20},{20,24},{24,28},{28,0},{1,5},{5... | collective-permute-start | bytes 1493000 | tf_op jit(solution)/shard_map/ppermute | solution.py:23
  35.7 14.6 %collective-permute-start.18 = (bf16[128,4096]{1,0:T(8,128)(2,1)S(1)}, bf16[128,4096]{1,0:T(8,128)(2,1)S(1)}, u32[]{:S(2)}, u32[]{:S(2)}) collective-permute-start(bf16[128,4096]{1,0:T(8,128)(2,1)S(1)} %get-tuple-element.60.xo), channel_id=1, source_target_pairs={{0,32},{2,35},{32,1},{34,2},{1,33},{3,34},{33,0},{35,3},{4,36},{6,... | collective-permute-start | bytes 3145736 | tf_op jit(solution)/shard_map/ppermute | solution.py:51
  38.2 9.2 %collective-permute-start.17 = (bf16[680,384]{1,0:T(8,128)(2,1)S(1)}, bf16[680,384]{1,0:T(8,128)(2,1)S(1)}, u32[]{:S(2)}, u32[]{:S(2)}) collective-permute-start(bf16[680,384]{1,0:T(8,128)(2,1)S(1)} %constant_dynamic-update-slice_fusion.12.first.refs_0_), channel_id=1, source_target_pairs={{0,192},{64,0},{128,64},{192,128},{1,193},{65,1},{129,65},{193,129... | collective-permute-start | bytes 1566728 | tf_op jit(solution)/shard_map/ppermute | solution.py:23
  40.2 10.0 %collective-permute-start.16 = (bf16[680,384]{1,0:T(8,128)(2,1)S(1)}, bf16[680,384]{1,0:T(8,128)(2,1)S(1)}, u32[]{:S(2)}, u32[]{:S(2)}) collective-permute-start(bf16[680,384]{1,0:T(8,128)(2,1)S(1)} %constant_dynamic-update-slice_fusion.12.first.refs_0_), channel_id=1, source_target_pairs={{0,64},{64,128},{128,192},{192,0},{1,65},{65,129},{129,193},{193,1... | collective-permute-start | bytes 1566728 | tf_op jit(solution)/shard_map/ppermute | solution.py:23
  44.0 15.9 %collective-permute-start.14 = (bf16[576,384]{1,0:T(8,128)(2,1)S(1)}, bf16[576,384]{1,0:T(8,128)(2,1)S(1)}, u32[]{:S(2)}, u32[]{:S(2)}) collective-permute-start(bf16[576,384]{1,0:T(8,128)(2,1)S(1)} %slice.194), channel_id=1, source_target_pairs={{0,4},{4,8},{8,12},{12,16},{16,20},{20,24},{24,28},{28,0},{1,5},{5... | collective-permute-start | bytes 1327112 | tf_op jit(solution)/shard_map/ppermute | solution.py:23
  44.1 15.8 %collective-permute-start.15 = (bf16[584,384]{1,0:T(8,128)(2,1)S(1)}, bf16[584,384]{1,0:T(8,128)(2,1)S(1)}, u32[]{:S(2)}, u32[]{:S(2)}) collective-permute-start(bf16[584,384]{1,0:T(8,128)(2,1)S(1)} %pad_maximum_fusion), channel_id=1, source_target_pairs={{0,28},{4,0},{8,4},{12,8},{16,12},{20,16},{24,20},{28,24},{1,29},{... | collective-permute-start | bytes 1345544 | tf_op jit(solution)/shard_map/ppermute | solution.py:23
  50.3 9.6 %collective-permute-start.19 = (bf16[128,4096]{1,0:T(8,128)(2,1)S(1)}, bf16[128,4096]{1,0:T(8,128)(2,1)S(1)}, u32[]{:S(2)}, u32[]{:S(2)}) collective-permute-start(bf16[128,4096]{1,0:T(8,128)(2,1)S(1)} %collective-permute-done.18.xn), channel_id=1, source_target_pairs={{0,2},{2,0},{1,3},{3,1},{4,6},{6,4},{5,7},{7,5},{8,10},{10,8},{9,1... | collective-permute-start | bytes 3145736 | tf_op jit(solution)/shard_map/ppermute | solution.py:35
  57.1 14.4 %collective-permute-start.20 = (bf16[656,384]{1,0:T(8,128)(2,1)S(1)}, bf16[656,384]{1,0:T(8,128)(2,1)S(1)}, u32[]{:S(2)}, u32[]{:S(2)}) collective-permute-start(bf16[656,384]{1,0:T(8,128)(2,1)S(1)} %get-tuple-element.103), channel_id=1, source_target_pairs={{0,64},{64,128},{128,192},{192,0},{1,65},{65,129},{129,193},{193,1... | collective-permute-start | bytes 1511432 | tf_op jit(solution)/shard_map/ppermute | solution.py:23
  57.5 11.4 %collective-permute-start.21 = (bf16[568,384]{1,0:T(8,128)(2,1)S(1)}, bf16[568,384]{1,0:T(8,128)(2,1)S(1)}, u32[]{:S(2)}, u32[]{:S(2)}) collective-permute-start(bf16[568,384]{1,0:T(8,128)(2,1)S(1)} %constant_dynamic-update-slice_fusion.22), channel_id=1, source_target_pairs={{0,192},{64,0},{128,64},{192,128},{1,193},{65,1},{129,65},{193,129... | collective-permute-start | bytes 1308680 | tf_op jit(solution)/shard_map/ppermute | solution.py:23
  60.0 14.5 %collective-permute-start.29 = (bf16[512,384]{1,0:T(8,128)(2,1)S(1)}, bf16[512,384]{1,0:T(8,128)(2,1)S(1)}, u32[]{:S(2)}, u32[]{:S(2)}) collective-permute-start(bf16[512,384]{1,0:T(8,128)(2,1)S(1)} %slice.220), channel_id=1, source_target_pairs={{0,28},{4,0},{8,4},{12,8},{16,12},{20,16},{24,20},{28,24},{1,29},{... | collective-permute-start | bytes 1179656 | tf_op jit(solution)/shard_map/ppermute | solution.py:23
  61.3 13.2 %collective-permute-start.28 = (bf16[512,384]{1,0:T(8,128)(2,1)S(1)}, bf16[512,384]{1,0:T(8,128)(2,1)S(1)}, u32[]{:S(2)}, u32[]{:S(2)}) collective-permute-start(bf16[512,384]{1,0:T(8,128)(2,1)S(1)} %slice.219), channel_id=1, source_target_pairs={{0,4},{4,8},{8,12},{12,16},{16,20},{20,24},{24,28},{28,0},{1,5},{5... | collective-permute-start | bytes 1179656 | tf_op jit(solution)/shard_map/ppermute | solution.py:23
  71.5 8.7 %collective-permute-start.22 = (bf16[264,384]{1,0:T(8,128)(2,1)S(1)}, bf16[264,384]{1,0:T(8,128)(2,1)S(1)}, u32[]{:S(2)}, u32[]{:S(2)}) collective-permute-start(bf16[264,384]{1,0:T(8,128)(2,1)S(1)} %pad_maximum_fusion.5), channel_id=1, source_target_pairs={{0,64},{64,128},{128,192},{192,0},{1,65},{65,129},{129,193},{193,1... | collective-permute-start | bytes 608264 | tf_op jit(solution)/shard_map/ppermute | solution.py:23
  71.7 8.6 %collective-permute-start.23 = (bf16[280,384]{1,0:T(8,128)(2,1)S(1)}, bf16[280,384]{1,0:T(8,128)(2,1)S(1)}, u32[]{:S(2)}, u32[]{:S(2)}) collective-permute-start(bf16[280,384]{1,0:T(8,128)(2,1)S(1)} %pad_maximum_fusion.3), channel_id=1, source_target_pairs={{0,192},{64,0},{128,64},{192,128},{1,193},{65,1},{129,65},{193,129... | collective-permute-start | bytes 645128 | tf_op jit(solution)/shard_map/ppermute | solution.py:23
  74.6 14.8 %collective-permute-start.31 = (bf16[256,384]{1,0:T(8,128)(2,1)S(1)}, bf16[256,384]{1,0:T(8,128)(2,1)S(1)}, u32[]{:S(2)}, u32[]{:S(2)}) collective-permute-start(bf16[256,384]{1,0:T(8,128)(2,1)S(1)} %slice.222), channel_id=1, source_target_pairs={{0,28},{4,0},{8,4},{12,8},{16,12},{20,16},{24,20},{28,24},{1,29},{... | collective-permute-start | bytes 589832 | tf_op jit(solution)/shard_map/ppermute | solution.py:23
  75.9 13.6 %collective-permute-start.30 = (bf16[256,384]{1,0:T(8,128)(2,1)S(1)}, bf16[256,384]{1,0:T(8,128)(2,1)S(1)}, u32[]{:S(2)}, u32[]{:S(2)}) collective-permute-start(bf16[256,384]{1,0:T(8,128)(2,1)S(1)} %slice.221), channel_id=1, source_target_pairs={{0,4},{4,8},{8,12},{12,16},{16,20},{20,24},{24,28},{28,0},{1,5},{5... | collective-permute-start | bytes 589832 | tf_op jit(solution)/shard_map/ppermute | solution.py:23
  83.0 6.5 %collective-permute-start.26 = (bf16[256,192]{1,0:T(8,128)(2,1)S(1)}, bf16[256,192]{1,0:T(8,128)(2,1)S(1)}, u32[]{:S(2)}, u32[]{:S(2)}) collective-permute-start(bf16[256,192]{1,0:T(8,128)(2,1)S(1)} %get-tuple-element.78.own), channel_id=1, source_target_pairs={{0,1},{1,0},{2,3},{3,2},{4,5},{5,4},{6,7},{7,6},{8,9},{9,8},{10,11... | collective-permute-start | bytes 294920 | tf_op jit(solution)/shard_map/ppermute | solution.py:43
  (10 other events, 50.8 us)
